TPU v7x, 256 devices: a whole 4x4x8 slice. The times are simulated.
256 devices in a mesh: ctx: 8 (over y, z_lo), exp: 16 (over z_hi, x), rep: 2 (over core).
Axes of the slice: x: 4, y: 4, z: 8 (z_hi: 4, z_lo: 2; z = z_hi * 2 + z_lo), core: 2. Of those that a mesh axis runs over, the one named last changes fastest.
Arguments:
- hidden_in: bfloat16 [8192, 4096], P(('rep', 'ctx', 'exp')), parts along dimension 0, may hold values from -6 to 6
- queries: bfloat16 [8192, 8192], P(('rep', 'ctx'), 'exp'), parts along dimension 0, may hold values from -64 to 64
- keys: bfloat16 [8192, 512], P(('rep', 'ctx')), parts along dimension 0, may hold values from -8 to 8
- values: bfloat16 [8192, 512], P(('rep', 'ctx')), parts along dimension 0, may hold values from -6 to 6
- out_proj: bfloat16 [8192, 4096], P('exp'), may hold values from -0.0625 to 0.0625
- norm_gain: float32 [4096], replicated, may hold values from 0.1 to 1.9
- expert_ids: int32 [8192, 8], P(('rep', 'ctx', 'exp')), parts along dimension 0, may hold values from 0 to 127, all different within a row; in each aligned block of 32 rows (0 to 31, 32 to 63, ...) at most 2 rows name the same one
- gate_fixed: int32 [8192, 8], P(('rep', 'ctx', 'exp')), parts along dimension 0, may hold values from 1 to 4096
- live_counts: int32 [256], P(('rep', 'ctx', 'exp')), parts along dimension 0, may hold values from 16 to 32, as said below
- gate_proj: bfloat16 [16, 4096, 1536], P('exp', None, 'ctx'), may hold values from -0.09375 to 0.09375
- up_proj: bfloat16 [16, 4096, 1536], P('exp', None, 'ctx'), may hold values from -0.09375 to 0.09375
- down_proj: bfloat16 [16, 1536, 4096], P('exp', 'ctx'), may hold values from -0.4375 to 0.4375
Outputs:
- mixed: bfloat16 [8192, 4096], P(('rep', 'ctx', 'exp')), parts along dimension 0
- expert_sum: bfloat16 [8192, 4096], P(('rep', 'ctx', 'exp')), parts along dimension 0
There are 2 independent parts, one for each index of `rep`. A program takes and returns all parts, laid end to end along the dimension named above; an argument that names none is the same for every part. Nothing has to cross between parts.
Inputs may be any that keep to these rules, and one draw needn't show every extreme that they name: `expert_ids`: each row names 8 different experts; among the 32 rows of one device no expert is named by more than 2 rows. `live_counts`: some device has all of its rows live.
All inputs are finite; a program needn't handle non-finite values.
Results may differ from a plain program's by a relative error of at most 0.023.
Values may be sent and summed in bfloat16 or wider, within the bound.
No kernel may reach another device: no remote copies, remote signals or barrier semaphores. Data moves between devices by JAX's collectives and lax.ppermute only.
A program may use at most 64 MiB of HBM per device.

v0:
```python
import functools
import math

import jax
import jax.numpy as jnp
from jax import lax
from jax.experimental import pallas as pl
from jax.experimental.pallas import tpu as pltpu
from jax.sharding import PartitionSpec as P

D = 4096
HEADS = 64
KV_HEADS = 4
HEAD_DIM = 128
TOPK = 8
CAP = 2
N_X = 4
N_Z = 4
N_Y = 4
TOKENS = 32
BF16 = jnp.bfloat16
F32 = jnp.float32
LOWEST = -1e30
EXP2_SCALE = HEAD_DIM ** (-0.5) * math.log2(math.e)
VMEM = pltpu.VMEM
SMEM = pltpu.SMEM


def params(limit_mib=8):
    return pltpu.CompilerParams(vmem_limit_bytes=limit_mib << 20)


def whole():
    return pl.BlockSpec(memory_space=VMEM)


def shift_x(a, d):
    pairs = [(z * N_X + x, z * N_X + (x + d) % N_X) for z in range(N_Z) for x in range(N_X)]
    return lax.ppermute(a, "exp", pairs)


def shift_z(a, d):
    pairs = [(z * N_X + x, (z + d) % N_Z * N_X + x) for z in range(N_Z) for x in range(N_X)]
    return lax.ppermute(a, "exp", pairs)


def shift_y(a, d):
    pairs = [(y * 2 + k, (y + d) % N_Y * 2 + k) for y in range(N_Y) for k in range(2)]
    return lax.ppermute(a, "ctx", pairs)


def swap_l(a):
    return lax.ppermute(a, "ctx", [(i, i ^ 1) for i in range(2 * N_Y)])


def swap_core(a):
    return lax.ppermute(a, "rep", [(0, 1), (1, 0)])


def pick_head(where_am, keys, values):
    rows = keys.shape[0]

    def kernel(where_ref, key_ref, value_ref, out_ref):
        out_ref[0:rows, :] = key_ref[...]
        out_ref[rows:, :] = value_ref[...]

    column = pl.BlockSpec((rows, HEAD_DIM), lambda i, w: (0, w[0]))
    return pl.pallas_call(
        kernel,
        grid_spec=pltpu.PrefetchScalarGridSpec(
            num_scalar_prefetch=1,
            grid=(1,),
            in_specs=[column, column],
            out_specs=pl.BlockSpec((2 * rows, HEAD_DIM), lambda i, w: (0, 0)),
        ),
        out_shape=jax.ShapeDtypeStruct((2 * rows, HEAD_DIM), BF16),
        compiler_params=params(),
        name="pick_head",
    )(where_am, keys, values)


def pick_weights(place, out_proj):
    rows, cols = out_proj.shape[0] // 2, out_proj.shape[1] // N_X

    def kernel(place_ref, *refs):
        for source, target in zip(refs[:3], refs[3:]):
            target[...] = source[...]

    def block(d):
        return pl.BlockSpec((rows, cols), lambda i, w: (w[0], lax.rem(w[1] + d, N_X)))

    return pl.pallas_call(
        kernel,
        grid_spec=pltpu.PrefetchScalarGridSpec(
            num_scalar_prefetch=1,
            grid=(1,),
            in_specs=[block(d) for d in range(1, N_X)],
            out_specs=[pl.BlockSpec((rows, cols), lambda i, w: (0, 0))] * 3,
        ),
        out_shape=[jax.ShapeDtypeStruct((rows, cols), BF16)] * 3,
        compiler_params=params(),
        name="pick_weights",
    )(place, out_proj, out_proj, out_proj)


def attend(queries, blocks, bias, state, last):
    rows, heads = queries.shape[0], queries.shape[1] // HEAD_DIM
    n = len(blocks)
    first = state is None
    tile = 128

    def kernel(*refs):
        bias_ref, q_ref = refs[0], refs[1]
        kv_refs = refs[2 : 2 + n]
        rest = refs[2 + n :]
        if not first:
            acc_in, top_in = rest[0], rest[1]
            rest = rest[2:]
        key = jnp.concatenate([r[0:rows, :] for r in kv_refs], axis=0)
        ones = jnp.ones((rows, HEAD_DIM), BF16)
        value = jnp.concatenate(
            [jnp.concatenate([r[rows:, :], ones], axis=1) for r in kv_refs], axis=0
        )
        for part in range(rows // tile):
            at = pl.ds(part * tile, tile)
            seen = n * rows
            scores = lax.dot_general(
                q_ref[at, :], key[:seen], (((1,), (1,)), ((), ())), preferred_element_type=F32
            )
            if first:
                i = lax.broadcasted_iota(jnp.int32, (tile, rows), 0) + part * tile
                j = lax.broadcasted_iota(jnp.int32, (tile, rows), 1)
                diagonal = jnp.where(j <= i, scores[:, :rows], LOWEST)
                scores = jnp.concatenate([diagonal, scores[:, rows:]], axis=1)
                newest = jnp.full((tile, HEAD_DIM), LOWEST, F32)
            else:
                before = top_in[0, at, :]
                newest = before
            for b in range(n):
                highest = jnp.max(scores[:, b * rows : (b + 1) * rows], axis=1, keepdims=True)
                newest = jnp.maximum(newest, highest + bias_ref[b])
            offsets = [(newest - bias_ref[b]) * EXP2_SCALE for b in range(n)]
            pieces = []
            for lane in range(0, seen, HEAD_DIM):
                pieces.append(
                    jnp.exp2(
                        scores[:, lane : lane + HEAD_DIM] * EXP2_SCALE - offsets[lane // rows]
                    ).astype(BF16)
                )
            total = jnp.dot(
                jnp.concatenate(pieces, axis=1), value[:seen], preferred_element_type=F32
            )
            if not first:
                factor = jnp.exp2((before - newest) * EXP2_SCALE)
                total = acc_in[0, at, :] * jnp.concatenate([factor, factor], axis=1) + total
            if last:
                rest[0][at, :] = (total[:, :HEAD_DIM] / total[:, HEAD_DIM:]).astype(BF16)
            else:
                rest[0][0, at, :] = total
                rest[1][0, at, :] = newest

    q_spec = pl.BlockSpec((rows, HEAD_DIM), lambda h, f: (0, h))
    kv_spec = pl.BlockSpec((2 * rows, HEAD_DIM), lambda h, f: (0, 0))
    state_specs = [
        pl.BlockSpec((1, rows, 2 * HEAD_DIM), lambda h, f: (h, 0, 0)),
        pl.BlockSpec((1, rows, HEAD_DIM), lambda h, f: (h, 0, 0)),
    ]
    state_shapes = [
        jax.ShapeDtypeStruct((heads, rows, 2 * HEAD_DIM), F32),
        jax.ShapeDtypeStruct((heads, rows, HEAD_DIM), F32),
    ]
    return pl.pallas_call(
        kernel,
        grid_spec=pltpu.PrefetchScalarGridSpec(
            num_scalar_prefetch=1,
            grid=(heads,),
            in_specs=[q_spec] + [kv_spec] * n + ([] if first else state_specs),
            out_specs=q_spec if last else state_specs,
        ),
        out_shape=jax.ShapeDtypeStruct(queries.shape, BF16) if last else state_shapes,
        compiler_params=params(20),
        cost_estimate=pl.CostEstimate(
            flops=heads * n * rows * rows * HEAD_DIM * 4,
            transcendentals=heads * n * rows * rows,
            bytes_accessed=4 << 20,
        ),
        name="attend",
    )(bias, queries, *blocks, *(() if first else state))


def rows_of(place_ref, left_ref, dz, columns):
    row = lax.rem(place_ref[0] + dz, N_Z) * (N_X * TOKENS)
    return left_ref[pl.ds(pl.multiple_of(row, N_X * TOKENS), N_X * TOKENS), columns]


def project_near(place, own, out_proj, lefts, fetched, other):
    n = len(lefts)
    rows = own.shape[1]
    cols = out_proj.shape[1] // N_X

    def kernel(place_ref, own_ref, weight_ref, *refs):
        left_refs, fetched_refs, other_ref, out_refs = refs[:n], refs[n : 2 * n], refs[2 * n], refs[2 * n + 1 :]
        for dz in range(N_Z):
            total = jnp.dot(
                rows_of(place_ref, own_ref, dz, slice(None)),
                weight_ref[...],
                preferred_element_type=F32,
            )
            for k in range(n):
                total = total + fetched_part(
                    place_ref, left_refs[k], fetched_refs[k], other_ref, (0, 2)[k], dz
                )
            out_refs[dz][...] = total

    fixed = lambda i, w: (0, 0)
    square = pl.BlockSpec(own.shape, fixed)
    return pl.pallas_call(
        kernel,
        grid_spec=pltpu.PrefetchScalarGridSpec(
            num_scalar_prefetch=1,
            grid=(1,),
            in_specs=[square, pl.BlockSpec((rows, cols), lambda i, w: (0, w[1]))]
            + [square] * n
            + [pl.BlockSpec((rows // 2, cols), fixed)] * n
            + [pl.BlockSpec(other.shape, fixed)],
            out_specs=[pl.BlockSpec((N_X * TOKENS, cols), fixed)] * N_Z,
        ),
        out_shape=[jax.ShapeDtypeStruct((N_X * TOKENS, cols), F32)] * N_Z,
        compiler_params=params(28),
        name="project_near",
    )(place, own, out_proj, *lefts, *fetched, other)


def fetched_part(place_ref, left_ref, fetched_ref, other_ref, at, dz):
    half = fetched_ref.shape[0]
    core = place_ref[2]
    mine = pl.ds(pl.multiple_of(core * half, half), half)
    theirs = pl.ds(pl.multiple_of((1 - core) * half, half), half)
    return jnp.dot(
        rows_of(place_ref, left_ref, dz, mine), fetched_ref[...], preferred_element_type=F32
    ) + jnp.dot(
        rows_of(place_ref, left_ref, dz, theirs),
        other_ref[at * half : (at + 1) * half, :],
        preferred_element_type=F32,
    )


def project_far(place, near, left, fetched, other):
    shape = near[0].shape
    middle = shape[1] // 2

    def kernel(place_ref, left_ref, fetched_ref, other_ref, *refs):
        near_refs, out_refs = refs[:4], refs[4:]
        for dz in (2, 1, 3, 0):
            total = near_refs[dz][...] + fetched_part(
                place_ref, left_ref, fetched_ref, other_ref, 1, dz
            )
            total = total.astype(BF16)
            if dz == 2:
                out_refs[3][...] = total[:, :middle]
                out_refs[4][...] = total[:, middle:]
            else:
                out_refs[{0: 0, 1: 1, 3: 2}[dz]][...] = total

    return pl.pallas_call(
        kernel,
        in_specs=[pl.BlockSpec(memory_space=SMEM)] + [whole()] * 7,
        out_specs=[whole()] * 5,
        out_shape=[jax.ShapeDtypeStruct(shape, BF16)] * 3
        + [jax.ShapeDtypeStruct((shape[0], middle), BF16)] * 2,
        compiler_params=params(),
        name="project_far",
    )(place, left, fetched, other, *near)


def pick_hidden(place, live, hidden_in, ids):
    cols = D // N_X

    def kernel(place_ref, live_ref, hidden_ref, id_ref, *out_refs):
        x = place_ref[1]
        t = lax.broadcasted_iota(jnp.int32, (TOPK, TOKENS), 1)
        alive = jnp.where(t < live_ref[0], id_ref[...] + 1, 0).astype(F32)
        for d in range(N_X):
            column = pl.ds(pl.multiple_of(lax.rem(x + N_X - d, N_X) * cols, cols), cols)
            out_refs[d][0:TOKENS, :] = hidden_ref[:, column]
            place_at = (
                lax.broadcasted_iota(jnp.int32, (TOKENS, cols), 1)
                == lax.broadcasted_iota(jnp.int32, (TOKENS, cols), 0) + x * TOKENS
            ).astype(F32)
            out_refs[d][TOKENS:, :] = jnp.dot(
                alive, place_at, preferred_element_type=F32
            ).astype(BF16)

    return pl.pallas_call(
        kernel,
        in_specs=[pl.BlockSpec(memory_space=SMEM)] * 2 + [whole()] * 2,
        out_specs=[whole()] * N_X,
        out_shape=[jax.ShapeDtypeStruct((TOKENS + TOPK, cols), BF16)] * N_X,
        compiler_params=params(),
        name="pick_hidden",
    )(place, live, hidden_in, ids)


def route(place, hidden):
    slots = N_Z * N_X * N_X * CAP
    tokens = N_X * TOKENS

    def kernel(place_ref, *refs):
        z = place_ref[0]
        s = lax.broadcasted_iota(jnp.int32, (slots, tokens), 0)
        t = lax.broadcasted_iota(jnp.int32, (slots, tokens), 1)
        dz, expert_x, owner, cap = s // 32, (s // 8) % 4, (s // 2) % 4, s % 2
        expert = ((z + dz) % N_Z) * N_X + expert_x
        wanted = jnp.where(owner == t // TOKENS, expert + 1, -1).astype(F32)
        ids = sum(r[TOKENS:, 0:tokens].astype(F32) for r in refs[:4])
        present = jnp.zeros((slots, tokens), F32)
        for k in range(TOPK):
            present = present + (ids[k : k + 1, :] == wanted).astype(F32)
        earlier = (
            lax.broadcasted_iota(jnp.int32, (tokens, tokens), 0)
            < lax.broadcasted_iota(jnp.int32, (tokens, tokens), 1)
        ).astype(F32)
        rank = jnp.dot(present, earlier, preferred_element_type=F32)
        fits = jnp.abs(rank - cap.astype(F32)) < 0.5
        refs[4][...] = jnp.where(fits, present, 0.0).astype(BF16)

    return pl.pallas_call(
        kernel,
        in_specs=[pl.BlockSpec(memory_space=SMEM)] + [whole()] * 4,
        out_specs=whole(),
        out_shape=jax.ShapeDtypeStruct((slots, tokens), BF16),
        compiler_params=params(),
        name="route",
    )(place, *hidden)


def route_weights(place, ids, gates, live):
    slots = N_X * N_Z * CAP

    def kernel(place_ref, live_ref, id_ref, gate_ref, weight_ref):
        z = place_ref[0]
        s = lax.broadcasted_iota(jnp.int32, (slots, TOKENS), 0)
        t = lax.broadcasted_iota(jnp.int32, (slots, TOKENS), 1)
        expert_x, dz, cap = s // (N_Z * CAP), (s // CAP) % N_Z, s % CAP
        expert = ((z + dz) % N_Z) * N_X + expert_x
        present = jnp.zeros((slots, TOKENS), F32)
        weight = jnp.zeros((slots, TOKENS), F32)
        for k in range(TOPK):
            hit = ((id_ref[k : k + 1, :] == expert) & (t < live_ref[0])).astype(F32)
            present = present + hit
            weight = weight + hit * gate_ref[k : k + 1, :].astype(F32)
        earlier = (
            lax.broadcasted_iota(jnp.int32, (TOKENS, TOKENS), 0)
            < lax.broadcasted_iota(jnp.int32, (TOKENS, TOKENS), 1)
        ).astype(F32)
        rank = jnp.dot(present, earlier, preferred_element_type=F32)
        weight_ref[...] = jnp.where(jnp.abs(rank - cap.astype(F32)) < 0.5, weight, 0.0) / 4096.0

    return pl.pallas_call(
        kernel,
        in_specs=[pl.BlockSpec(memory_space=SMEM)] * 2 + [whole()] * 2,
        out_specs=whole(),
        out_shape=jax.ShapeDtypeStruct((slots, TOKENS), F32),
        compiler_params=params(),
        name="route_weights",
    )(place, live, ids, gates)


def finish_rows(place, hidden, sums, pick):
    cols = sums[0].shape[1]

    def kernel(place_ref, h0, h1, h2, h3, s0, s1, s2, pick_ref, *refs):
        mixed_ref, send_refs = refs[0], refs[1:5]
        for d, h in enumerate((h0, h1, h2, h3)):
            at = pl.ds(pl.multiple_of(lax.rem(place_ref[1] + d, N_X) * TOKENS, TOKENS), TOKENS)
            mixed_ref[at, :] = (
                h[0:TOKENS, :].astype(F32)
                + (s0[at, :].astype(F32) + s1[at, :].astype(F32) + s2[at, :].astype(F32))
            ).astype(BF16)
        send = jnp.dot(pick_ref[...], mixed_ref[...], preferred_element_type=F32).astype(BF16)
        for dz in range(N_Z):
            send_refs[dz][...] = send[dz * 32 : dz * 32 + 32, :]

    return pl.pallas_call(
        kernel,
        in_specs=[pl.BlockSpec(memory_space=SMEM)] + [whole()] * 8,
        out_specs=[whole()] * 5,
        out_shape=[jax.ShapeDtypeStruct((N_X * TOKENS, cols), BF16)]
        + [jax.ShapeDtypeStruct((32, cols), BF16)] * 4,
        compiler_params=params(),
        name="finish_rows",
    )(place, *hidden, *sums, pick)


def by_columns(groups, mixed):
    cols = mixed.shape[1]

    def kernel(*refs):
        held = [r[...] for r in refs[:4]]
        for x in range(N_X):
            refs[5][x, 0:32, :] = jnp.concatenate([h[x * 8 : x * 8 + 8, :] for h in held], axis=0)
            refs[5][x, 32:64, :] = refs[4][x * TOKENS : (x + 1) * TOKENS, :]

    return pl.pallas_call(
        kernel,
        in_specs=[whole()] * 5,
        out_specs=whole(),
        out_shape=jax.ShapeDtypeStruct((N_X, 64, cols), BF16),
        compiler_params=params(),
        name="by_columns",
    )(*groups, mixed)


def join_columns(pieces, gain):
    cols = pieces.shape[2]

    def kernel(piece_ref, gain_ref, block_ref, mixed_ref):
        values = [piece_ref[x, 0:32, :].astype(F32) for x in range(N_X)]
        square = sum(jnp.sum(v * v, axis=1, keepdims=True) for v in values)
        scale = lax.rsqrt(square / D + 1e-06)
        for x, value in enumerate(values):
            column = slice(x * cols, (x + 1) * cols)
            block_ref[:, column] = (value * scale * gain_ref[:, column]).astype(BF16)
            mixed_ref[:, column] = piece_ref[x, 32:64, :]

    return pl.pallas_call(
        kernel,
        in_specs=[whole()] * 2,
        out_specs=[whole()] * 2,
        out_shape=[jax.ShapeDtypeStruct((32, D), BF16)] * 2,
        compiler_params=params(),
        name="join_columns",
    )(pieces, gain)


def regroup(groups):
    rows = 4 * 4 * CAP

    def kernel(*refs):
        held = jnp.concatenate([r[...] for r in refs[:4]], axis=0)
        to = lax.broadcasted_iota(jnp.int32, (rows, rows), 0)
        come = lax.broadcasted_iota(jnp.int32, (rows, rows), 1)
        b, a, cap = to // 8, (to // CAP) % 4, to % CAP
        order = (come == a * 8 + b * CAP + cap).astype(BF16)
        moved = jnp.dot(order, held, preferred_element_type=F32).astype(BF16)
        for i in range(4):
            refs[4][i] = moved[i * 8 : i * 8 + 8, :]

    return pl.pallas_call(
        kernel,
        in_specs=[whole()] * 4,
        out_specs=whole(),
        out_shape=jax.ShapeDtypeStruct((4, 8, D), BF16),
        compiler_params=params(),
        name="regroup",
    )(*groups)


def run_expert(blocks, gate, up, down):
    n = len(blocks)

    def kernel(*refs):
        in_refs, (gate_ref, up_ref, down_ref), out_refs = refs[:n], refs[n : n + 3], refs[n + 3 :]
        rows = jnp.concatenate([r[...] for r in in_refs], axis=0)
        last = (((1,), (1,)), ((), ()))
        gate_part = lax.dot_general(rows, gate_ref[...], last, preferred_element_type=F32)
        up_part = lax.dot_general(rows, up_ref[...], last, preferred_element_type=F32)
        hidden = (gate_part / (1.0 + jnp.exp(-gate_part)) * up_part).astype(BF16)
        result = jnp.dot(hidden, down_ref[...], preferred_element_type=F32).astype(BF16)
        at = 0
        for r in out_refs:
            r[...] = result[at : at + r.shape[0], :]
            at += r.shape[0]

    return pl.pallas_call(
        kernel,
        in_specs=[whole()] * (n + 3),
        out_specs=[whole()] * n,
        out_shape=[jax.ShapeDtypeStruct(b.shape, BF16) for b in blocks],
        compiler_params=params(24),
        name="run_expert",
    )(*blocks, gate, up, down)


def combine(weight, groups):
    def kernel(weight_ref, *refs):
        held = jnp.concatenate([refs[0][i] for i in range(4)], axis=0).astype(F32)
        refs[1][...] = lax.dot_general(
            weight_ref[...],
            held,
            (((0,), (0,)), ((), ())),
            precision=lax.Precision.HIGHEST,
            preferred_element_type=F32,
        ).astype(BF16)

    return pl.pallas_call(
        kernel,
        in_specs=[whole()] * 2,
        out_specs=whole(),
        out_shape=jax.ShapeDtypeStruct((TOKENS, D), BF16),
        compiler_params=params(),
        name="combine",
    )(weight, groups)


def tie(values, *others):
    n = len(values)
    return lax.optimization_barrier((*values, *others))[:n]


def add(*arrays):
    return sum(a.astype(F32) for a in arrays).astype(BF16)


def exchange_x(a):
    groups = [[z * N_X + x for x in range(N_X)] for z in range(N_Z)]
    return lax.all_to_all(a, "exp", 0, 0, tiled=True, axis_index_groups=groups)


def scatter_ctx(parts):
    own, swapped, below, above, below_swapped, below_two, above_swapped, far = parts
    got_far = swap_l(far)
    got_below_swapped = swap_l(below_swapped)
    got_above_swapped = shift_y(above_swapped, 1)
    got_two = shift_y(add(below_two, got_far), -1)
    got_above = shift_y(above, 1)
    got_swapped = swap_l(add(swapped, got_above_swapped))
    got_below = shift_y(add(below, got_two, got_below_swapped), -1)
    return add(own, got_above, got_below, got_swapped)


def on_device(
    hidden_in,
    queries,
    keys,
    values,
    out_proj,
    norm_gain,
    expert_ids,
    gate_fixed,
    live_counts,
    gate_proj,
    up_proj,
    down_proj,
):
    exp_index = lax.axis_index("exp")
    ctx_index = lax.axis_index("ctx")
    rep_index = lax.axis_index("rep")
    z, x = exp_index // N_X, exp_index % N_X
    y, side = ctx_index // 2, ctx_index % 2
    place = jnp.stack([z, x, rep_index]).astype(jnp.int32)
    seq_rows = queries.shape[0]
    local_heads = queries.shape[1] // HEAD_DIM
    kv_index = exp_index * local_heads // (HEADS // KV_HEADS)

    def bias(*steps):
        owners = jnp.stack([((y + dy) % N_Y) * 2 + (side ^ flip) for dy, flip in steps])
        return jnp.where(owners < ctx_index, 0.0, LOWEST).astype(F32)

    own = pick_head(kv_index.astype(jnp.int32)[None], keys, values)
    swapped = swap_l(own)
    below = shift_y(own, 1)
    above = shift_y(own, -1)
    out_proj = pltpu.with_memory_space_constraint(out_proj, pltpu.HBM)
    away = pick_weights(jnp.stack([rep_index, x]).astype(jnp.int32), out_proj)
    fetched = [shift_x(away[0], 1), None, shift_x(away[2], 3)]
    swapped, below, above = tie((swapped, below, above), *away)
    below_two = shift_y(below, 1)
    below_swapped = swap_l(below)
    above_swapped = shift_y(swapped, -1)
    state = attend(
        queries,
        [own, swapped, below, above],
        jnp.concatenate([jnp.zeros((1,), F32), bias((0, 1), (-1, 0), (1, 0))]),
        None,
        False,
    )
    below_two, below_swapped, above_swapped = tie(
        (below_two, below_swapped, above_swapped), *state
    )
    far = swap_l(below_two)
    (away_far,) = tie((away[1],), *state)
    fetched[1] = shift_x(away_far, 2)
    below_swapped, above_swapped, *state = tie(
        (below_swapped, above_swapped, *state), fetched[0], fetched[2]
    )
    state = attend(
        queries,
        [below_swapped, below_two, above_swapped],
        bias((-1, 1), (-2, 0), (1, 1)),
        state,
        False,
    )
    (far,) = tie((far,), *state)
    attended = attend(queries, [far], bias((-2, 1)), state, True)

    half = seq_rows // 2
    from_left = shift_x(attended, 1)
    from_right = shift_x(attended, -1)
    ids = expert_ids.T
    hidden_in, later_place = tie((hidden_in, place), attended)
    hidden = pick_hidden(later_place, live_counts, hidden_in, ids)
    from_left, from_right = tie((from_left, from_right), *hidden)
    far_a = shift_x(from_left[:half], 1)
    far_b = shift_x(from_right[half:], -1)
    fetched = tie(fetched, from_left)
    other = swap_core(jnp.concatenate(fetched, axis=0))
    hidden = [hidden[0]] + [shift_x(hidden[d], -d) for d in range(1, N_X)]
    pick = route(place, hidden)
    weight = route_weights(later_place, ids, gate_fixed.T, live_counts)
    from_left, from_right = tie((from_left, from_right), pick, weight)
    near = project_near(
        place, attended, out_proj, [from_left, from_right], [fetched[0], fetched[2]], other
    )
    far_a, far_b = tie((far_a, far_b), *near)
    from_far = jnp.concatenate([far_a, far_b], axis=0)
    mine, up_chunk, down_chunk, low, high = project_far(place, near, from_far, fetched[1], other)

    middle = low.shape[1]
    got_low = shift_z(low, 1)
    got_high = shift_z(high, -1)
    up_chunk = jnp.concatenate([add(up_chunk[:, :middle], got_low), up_chunk[:, middle:]], axis=1)
    down_chunk = jnp.concatenate(
        [down_chunk[:, :middle], add(down_chunk[:, middle:], got_high)], axis=1
    )
    got_up = shift_z(up_chunk, 1)
    got_down = shift_z(down_chunk, -1)
    mixed, *send = finish_rows(place, hidden, [mine, got_up, got_down], pick)

    by_z = [send[0]] + [shift_z(send[d], d) for d in range(1, N_Z)]
    block, mixed = join_columns(exchange_x(by_columns(by_z, mixed)), norm_gain.reshape(1, D))
    swapped = swap_l(block)
    below = shift_y(block, 1)
    above = shift_y(block, -1)
    below_two = shift_y(below, 1)
    below_swapped = swap_l(below)
    above_swapped = shift_y(swapped, -1)
    far = swap_l(below_two)
    parts = run_expert(
        [block, swapped, below, above, below_swapped, below_two, above_swapped, far],
        gate_proj[0].T,
        up_proj[0].T,
        down_proj[0],
    )

    result = scatter_ctx(parts)
    back_z = [result[:8]] + [shift_z(result[8 * d : 8 * d + 8], -d) for d in range(1, N_Z)]
    return (mixed, combine(weight, exchange_x(regroup(back_z))))


def solution(mesh):
    in_specs = (
        P(("rep", "ctx", "exp"), None),
        P(("rep", "ctx"), "exp"),
        P(("rep", "ctx"), None),
        P(("rep", "ctx"), None),
        P("exp", None),
        P(),
        P(("rep", "ctx", "exp"), None),
        P(("rep", "ctx", "exp"), None),
        P(("rep", "ctx", "exp")),
        P("exp", None, "ctx"),
        P("exp", None, "ctx"),
        P("exp", "ctx", None),
    )
    out_specs = (P(("rep", "ctx", "exp"), None), P(("rep", "ctx", "exp"), None))
    return jax.shard_map(
        on_device, mesh=mesh, in_specs=in_specs, out_specs=out_specs, check_vma=False
    )
```

profile of v0, /device:TPU:24, one launch (start us, length us, event | category | flops | bytes accessed | tf_op | source)
XLA Modules:
  0.0 223.8 jit_solution(14670137739196806565)
XLA Ops:
  3.6 2.5 %collective-permute-start.1 = (bf16[1024,128]{1,0:T(8,128)(2,1)S(1)}, bf16[1024,128]{1,0:T(8,128)(2,1)S(1)}, u32[]{:S(2)}, u32[]{:S(2)}) collective-permute-start(bf16[1024,128]{1,0:T(8,128)(2,1)S(1)} %pick_head.1.refs_2_), channel_id=1, source_target_pairs={{0,64},{32,96},{64,128},{96,160},{128,192},{160,224},{192,0},{224,... | collective-permute-start | bytes 786440 | tf_op jit(solution)/shard_map/ppermute | solution.py:49
  6.1 1.9 collective-permute-start
  8.1 2.8 %pick_weights.1 = (bf16[256,1024]{1,0:T(8,128)(2,1)S(1)}, bf16[256,1024]{1,0:T(8,128)(2,1)}, bf16[256,1024]{1,0:T(8,128)(2,1)S(1)}) custom-call(s32[2]{0:T(128)S(1)} %pad_add_fusion.1.place_ref, bf16[512,4096]{1,0:T(8,128)(2,1)} %weight_ref.1, bf16[512,4096]{1,0:T(8,128)(2,1)} %weight_ref.1, bf16[512,4096]{1,0:T(8,128)(2,1)} %weight_ref.1), custom_call_target="tpu_custom_call" | custom-call | tf_op jit(solution)/shard_map/pick_weights/pallas_call | solution.py:92
  10.9 1.5 collective-permute-start.7
  12.4 1.7 collective-permute-start.8
  14.2 1.4 collective-permute-start.4
  15.6 1.4 collective-permute-start.3
  17.7 9.4 %attend.3 = (f32[4,512,256]{2,1,0:T(8,128)S(1)}, f32[4,512,128]{2,1,0:T(8,128)S(1)}) custom-call(f32[4]{0:T(128)S(1)} %pad_maximum_fusion.4.refs_0_, bf16[512,512]{1,0:T(8,128)(2,1)S(1)} %copy-done.5, bf16[1024,128]{1,0:T(8,128)(2,1)S(1)} %pick_head.1.refs_2_, bf16[1024,128]{1,0:T(8,128)(2,1)} %collective-permute-done.refs_3_, ...), custom_call_target="tpu_custom_call" | custom-call | flops 2147483648 | bytes 4194304 | tf_op jit(solution)/shard_map/attend/pallas_call | solution.py:172
  28.0 7.0 %attend.4 = (f32[4,512,256]{2,1,0:T(8,128)S(1)}, f32[4,512,128]{2,1,0:T(8,128)S(1)}) custom-call(f32[3]{0:T(128)S(1)} %compare_select_fusion.refs_0_, bf16[512,512]{1,0:T(8,128)(2,1)S(1)} %copy-done.5, bf16[1024,128]{1,0:T(8,128)(2,1)S(1)} %collective-permute-done.4.refs_2_, bf16[1024,128]{1,0:T(8,128)(2,1)S(1)} %collective-permute-done.3.refs_3_, ...), custom_call_target="tpu_custom_call" | custom-call | flops 1610612736 | bytes 4194304 | tf_op jit(solution)/shard_map/attend/pallas_call | solution.py:172
  35.1 3.1 %attend.5.own_ref = bf16[512,512]{1,0:T(8,128)(2,1)S(1)} custom-call(f32[1]{0:T(128)} %bitcast.3.refs_0_, bf16[512,512]{1,0:T(8,128)(2,1)S(1)} %copy-done.5, bf16[1024,128]{1,0:T(8,128)(2,1)S(1)} %collective-permute-done.6.refs_2_, f32[4,512,256]{2,1,0:T(8,128)S(1)} %get-tuple-element.75.refs_3_, f32[4,512,128]{2,1,0:T(8,128)S(1)} %get-tuple-element.76.refs_4_), custom_call_target="tpu_custom_call" | custom-call | flops 536870912 | bytes 4194304 | tf_op jit(solution)/shard_map/attend/pallas_call | solution.py:172
  38.1 2.4 %collective-permute-start.13 = (bf16[512,512]{1,0:T(8,128)(2,1)S(1)}, bf16[512,512]{1,0:T(8,128)(2,1)S(1)}, u32[]{:S(2)}, u32[]{:S(2)}) collective-permute-start(bf16[512,512]{1,0:T(8,128)(2,1)S(1)} %attend.5.own_ref), channel_id=1, source_target_pairs={{0,6},{2,0},{4,2},{6,4},{8,14},{10,8},{12,10},{14,12},{16,22},{18,... | collective-permute-start | bytes 1572872 | tf_op jit(solution)/shard_map/ppermute | solution.py:39
  40.6 2.5 %collective-permute-start.16 = (bf16[256,1024]{1,0:T(8,128)(2,1)}, bf16[256,1024]{1,0:T(8,128)(2,1)S(1)}, u32[]{:S(2)}, u32[]{:S(2)}) collective-permute-start(bf16[256,1024]{1,0:T(8,128)(2,1)} %get-tuple-element.88), channel_id=1, source_target_pairs={{0,4},{2,6},{4,0},{6,2},{8,12},{10,14},{12,8},{14,10},{16,20},{18,... | collective-permute-start | bytes 1572872 | tf_op jit(solution)/shard_map/ppermute | solution.py:39
  44.5 16.1 %collective-permute-done.13.refs_1_ = bf16[512,512]{1,0:T(8,128)(2,1)S(1)} collective-permute-done((bf16[512,512]{1,0:T(8,128)(2,1)S(1)}, bf16[512,512]{1,0:T(8,128)(2,1)S(1)}, u32[]{:S(2)}, u32[]{:S(2)}) %collective-permute-start.13) | collective-permute-done | bytes 524320 | tf_op jit(solution)/shard_map/ppermute | solution.py:39
  60.6 3.4 %collective-permute-done.12.refs_0_ = bf16[512,512]{1,0:T(8,128)(2,1)S(1)} collective-permute-done((bf16[512,512]{1,0:T(8,128)(2,1)S(1)}, bf16[512,512]{1,0:T(8,128)(2,1)S(1)}, u32[]{:S(2)}, u32[]{:S(2)}) %collective-permute-start.12) | collective-permute-done | bytes 524320 | tf_op jit(solution)/shard_map/ppermute | solution.py:39
  64.4 3.2 %collective-permute-start.15 = (bf16[256,512]{1,0:T(8,128)(2,1)S(1)}, bf16[256,512]{1,0:T(8,128)(2,1)S(1)}, u32[]{:S(2)}, u32[]{:S(2)}) collective-permute-start(bf16[256,512]{1,0:T(8,128)(2,1)S(1)} %slice.31), channel_id=1, source_target_pairs={{0,6},{2,0},{4,2},{6,4},{8,14},{10,8},{12,10},{14,12},{16,22},{18,... | collective-permute-start | bytes 786440 | tf_op jit(solution)/shard_map/ppermute | solution.py:39
  68.5 8.5 %collective-permute-done.9.refs_1_.h1 = bf16[40,1024]{1,0:T(8,128)(2,1)S(1)} collective-permute-done((bf16[40,1024]{1,0:T(8,128)(2,1)S(1)}, bf16[40,1024]{1,0:T(8,128)(2,1)S(1)}, u32[]{:S(2)}, u32[]{:S(2)}) %collective-permute-start.9) | collective-permute-done | bytes 81952 | tf_op jit(solution)/shard_map/ppermute | solution.py:39
  77.7 5.4 %collective-permute-done.11.refs_3_.h3 = bf16[40,1024]{1,0:T(8,128)(2,1)S(1)} collective-permute-done((bf16[40,1024]{1,0:T(8,128)(2,1)S(1)}, bf16[40,1024]{1,0:T(8,128)(2,1)S(1)}, u32[]{:S(2)}, u32[]{:S(2)}) %collective-permute-start.11) | collective-permute-done | bytes 81952 | tf_op jit(solution)/shard_map/ppermute | solution.py:39
  83.9 3.6 %project_near.1 = (f32[128,1024]{1,0:T(8,128)S(1)}, f32[128,1024]{1,0:T(8,128)S(1)}, f32[128,1024]{1,0:T(8,128)S(1)}, f32[128,1024]{1,0:T(8,128)S(1)}) custom-call(s32[3]{0:T(128)S(1)} %pad_add_fusion.place_ref, bf16[512,512]{1,0:T(8,128)(2,1)S(1)} %attend.5.own_ref, bf16[512,4096]{1,0:T(8,128)(2,1)} %weight_ref.1, ...), custom_call_target="tpu_custom_call" | custom-call | tf_op jit(solution)/shard_map/project_near/pallas_call | solution.py:217
  88.9 6.0 %collective-permute-start.20 = (bf16[128,512]{1,0:T(8,128)(2,1)S(1)}, bf16[128,512]{1,0:T(8,128)(2,1)S(1)}, u32[]{:S(2)}, u32[]{:S(2)}) collective-permute-start(bf16[128,512]{1,0:T(8,128)(2,1)S(1)} %get-tuple-element.102), channel_id=1, source_target_pairs={{0,24},{2,26},{4,28},{6,30},{8,0},{10,2},{12,4},{14,6},{16,8},{18,... | collective-permute-start | bytes 393224 | tf_op jit(solution)/shard_map/ppermute | solution.py:44
  95.0 4.2 %collective-permute-done.20 = bf16[128,512]{1,0:T(8,128)(2,1)S(1)} collective-permute-done((bf16[128,512]{1,0:T(8,128)(2,1)S(1)}, bf16[128,512]{1,0:T(8,128)(2,1)S(1)}, u32[]{:S(2)}, u32[]{:S(2)}) %collective-permute-start.20) | collective-permute-done | bytes 131104 | tf_op jit(solution)/shard_map/ppermute | solution.py:44
  99.4 4.8 %collective-permute-start.21 = (bf16[128,1024]{1,0:T(8,128)(2,1)S(1)}, bf16[128,1024]{1,0:T(8,128)(2,1)S(1)}, u32[]{:S(2)}, u32[]{:S(2)}) collective-permute-start(bf16[128,1024]{1,0:T(8,128)(2,1)S(1)} %pad_maximum_fusion.3), channel_id=1, source_target_pairs={{0,24},{2,26},{4,28},{6,30},{8,0},{10,2},{12,4},{14,6},{16,8},{18,... | collective-permute-start | bytes 786440 | tf_op jit(solution)/shard_map/ppermute | solution.py:44
  104.3 7.6 %collective-permute-done.21.s2 = bf16[128,1024]{1,0:T(8,128)(2,1)S(1)} collective-permute-done((bf16[128,1024]{1,0:T(8,128)(2,1)S(1)}, bf16[128,1024]{1,0:T(8,128)(2,1)S(1)}, u32[]{:S(2)}, u32[]{:S(2)}) %collective-permute-start.21) | collective-permute-done | bytes 262176 | tf_op jit(solution)/shard_map/ppermute | solution.py:44
  111.9 4.4 %collective-permute-done.19.s1 = bf16[128,1024]{1,0:T(8,128)(2,1)S(1)} collective-permute-done((bf16[128,1024]{1,0:T(8,128)(2,1)S(1)}, bf16[128,1024]{1,0:T(8,128)(2,1)S(1)}, u32[]{:S(2)}, u32[]{:S(2)}) %collective-permute-start.19) | collective-permute-done | bytes 262176 | tf_op jit(solution)/shard_map/ppermute | solution.py:44
  117.3 3.8 %collective-permute-start.23 = (bf16[32,1024]{1,0:T(8,128)(2,1)S(1)}, bf16[32,1024]{1,0:T(8,128)(2,1)S(1)}, u32[]{:S(2)}, u32[]{:S(2)}) collective-permute-start(bf16[32,1024]{1,0:T(8,128)(2,1)S(1)} %get-tuple-element.105), channel_id=1, source_target_pairs={{0,16},{2,18},{4,20},{6,22},{8,24},{10,26},{12,28},{14,30},{16,0},... | collective-permute-start | bytes 196616 | tf_op jit(solution)/shard_map/ppermute | solution.py:44
  121.1 13.3 %collective-permute-start.24 = (bf16[32,1024]{1,0:T(8,128)(2,1)S(1)}, bf16[32,1024]{1,0:T(8,128)(2,1)S(1)}, u32[]{:S(2)}, u32[]{:S(2)}) collective-permute-start(bf16[32,1024]{1,0:T(8,128)(2,1)S(1)} %get-tuple-element.106), channel_id=1, source_target_pairs={{0,24},{2,26},{4,28},{6,30},{8,0},{10,2},{12,4},{14,6},{16,8},{18,... | collective-permute-start | bytes 196616 | tf_op jit(solution)/shard_map/ppermute | solution.py:44
  134.4 2.3 %collective-permute-done.24.refs_3_ = bf16[32,1024]{1,0:T(8,128)(2,1)S(1)} collective-permute-done((bf16[32,1024]{1,0:T(8,128)(2,1)S(1)}, bf16[32,1024]{1,0:T(8,128)(2,1)S(1)}, u32[]{:S(2)}, u32[]{:S(2)}) %collective-permute-start.24) | collective-permute-done | bytes 65568 | tf_op jit(solution)/shard_map/ppermute | solution.py:44
  136.8 11.0 %all_to_all.10.piece_ref = bf16[4,64,1024]{2,1,0:T(8,128)(2,1)S(1)} all-to-all(bf16[4,64,1024]{2,1,0:T(8,128)(2,1)S(1)} %by_columns.1), channel_id=1, replica_groups={{0,2,4,6},{8,10,12,14},{16,18,20,22},{24,26,28,30},{1,3,5,7},{9,11,13,1..., dimensions={0} | all-to-all | bytes 1048576 | tf_op jit(solution)/shard_map/all_to_all | solution.py:517
  148.6 3.5 %collective-permute-start.26 = (bf16[32,4096]{1,0:T(8,128)(2,1)S(1)}, bf16[32,4096]{1,0:T(8,128)(2,1)S(1)}, u32[]{:S(2)}, u32[]{:S(2)}) collective-permute-start(bf16[32,4096]{1,0:T(8,128)(2,1)S(1)} %get-tuple-element.109.refs_0_), channel_id=1, source_target_pairs={{0,64},{32,96},{64,128},{96,160},{128,192},{160,224},{192,0},{224,... | collective-permute-start | bytes 786440 | tf_op jit(solution)/shard_map/ppermute | solution.py:49
  152.1 1.5 collective-permute-start.25
  153.6 4.6 %collective-permute-done.26.refs_2_ = bf16[32,4096]{1,0:T(8,128)(2,1)S(1)} collective-permute-done((bf16[32,4096]{1,0:T(8,128)(2,1)S(1)}, bf16[32,4096]{1,0:T(8,128)(2,1)S(1)}, u32[]{:S(2)}, u32[]{:S(2)}) %collective-permute-start.26) | collective-permute-done | bytes 262176 | tf_op jit(solution)/shard_map/ppermute | solution.py:49
  158.2 3.7 %collective-permute-start.29 = (bf16[32,4096]{1,0:T(8,128)(2,1)S(1)}, bf16[32,4096]{1,0:T(8,128)(2,1)S(1)}, u32[]{:S(2)}, u32[]{:S(2)}) collective-permute-start(bf16[32,4096]{1,0:T(8,128)(2,1)S(1)} %collective-permute-done.26.refs_2_), channel_id=1, source_target_pairs={{0,64},{32,96},{64,128},{96,160},{128,192},{160,224},{192,0},{224,... | collective-permute-start | bytes 786440 | tf_op jit(solution)/shard_map/ppermute | solution.py:49
  162.0 3.8 %collective-permute-done.29.refs_5_ = bf16[32,4096]{1,0:T(8,128)(2,1)S(1)} collective-permute-done((bf16[32,4096]{1,0:T(8,128)(2,1)S(1)}, bf16[32,4096]{1,0:T(8,128)(2,1)S(1)}, u32[]{:S(2)}, u32[]{:S(2)}) %collective-permute-start.29) | collective-permute-done | bytes 262176 | tf_op jit(solution)/shard_map/ppermute | solution.py:49
  165.8 3.7 %collective-permute-done.27.refs_3_ = bf16[32,4096]{1,0:T(8,128)(2,1)S(1)} collective-permute-done((bf16[32,4096]{1,0:T(8,128)(2,1)S(1)}, bf16[32,4096]{1,0:T(8,128)(2,1)S(1)}, u32[]{:S(2)}, u32[]{:S(2)}) %collective-permute-start.27) | collective-permute-done | bytes 262176 | tf_op jit(solution)/shard_map/ppermute | solution.py:49
  169.5 2.8 %collective-permute-done.30.refs_6_ = bf16[32,4096]{1,0:T(8,128)(2,1)S(1)} collective-permute-done((bf16[32,4096]{1,0:T(8,128)(2,1)S(1)}, bf16[32,4096]{1,0:T(8,128)(2,1)S(1)}, u32[]{:S(2)}, u32[]{:S(2)}) %collective-permute-start.30) | collective-permute-done | bytes 262176 | tf_op jit(solution)/shard_map/ppermute | solution.py:49
  172.3 2.7 %collective-permute-done.31.refs_7_ = bf16[32,4096]{1,0:T(8,128)(2,1)S(1)} collective-permute-done((bf16[32,4096]{1,0:T(8,128)(2,1)S(1)}, bf16[32,4096]{1,0:T(8,128)(2,1)S(1)}, u32[]{:S(2)}, u32[]{:S(2)}) %collective-permute-start.31) | collective-permute-done | bytes 262176 | tf_op jit(solution)/shard_map/ppermute | solution.py:53
  175.0 1.9 run_expert.1
  177.0 3.7 %collective-permute-start.32 = (bf16[32,4096]{1,0:T(8,128)(2,1)S(1)}, bf16[32,4096]{1,0:T(8,128)(2,1)S(1)}, u32[]{:S(2)}, u32[]{:S(2)}) collective-permute-start(bf16[32,4096]{1,0:T(8,128)(2,1)S(1)} %get-tuple-element.111), channel_id=1, source_target_pairs={{0,64},{32,96},{64,128},{96,160},{128,192},{160,224},{192,0},{224,... | collective-permute-start | bytes 786440 | tf_op jit(solution)/shard_map/ppermute | solution.py:49
  180.7 1.9 collective-permute-start.35
  182.7 1.9 collective-permute-done.33
  184.8 4.2 %collective-permute-done.37 = bf16[32,4096]{1,0:T(8,128)(2,1)S(1)} collective-permute-done((bf16[32,4096]{1,0:T(8,128)(2,1)S(1)}, bf16[32,4096]{1,0:T(8,128)(2,1)S(1)}, u32[]{:S(2)}, u32[]{:S(2)}) %collective-permute-start.37) | collective-permute-done | bytes 262176 | tf_op jit(solution)/shard_map/ppermute | solution.py:49
  189.5 2.8 %collective-permute-done.34 = bf16[32,4096]{1,0:T(8,128)(2,1)S(1)} collective-permute-done((bf16[32,4096]{1,0:T(8,128)(2,1)S(1)}, bf16[32,4096]{1,0:T(8,128)(2,1)S(1)}, u32[]{:S(2)}, u32[]{:S(2)}) %collective-permute-start.34) | collective-permute-done | bytes 262176 | tf_op jit(solution)/shard_map/ppermute | solution.py:49
  192.5 4.7 %collective-permute-done.38 = bf16[32,4096]{1,0:T(8,128)(2,1)S(1)} collective-permute-done((bf16[32,4096]{1,0:T(8,128)(2,1)S(1)}, bf16[32,4096]{1,0:T(8,128)(2,1)S(1)}, u32[]{:S(2)}, u32[]{:S(2)}) %collective-permute-start.38) | collective-permute-done | bytes 262176 | tf_op jit(solution)/shard_map/ppermute | solution.py:53
  197.2 2.9 %collective-permute-done.36 = bf16[32,4096]{1,0:T(8,128)(2,1)S(1)} collective-permute-done((bf16[32,4096]{1,0:T(8,128)(2,1)S(1)}, bf16[32,4096]{1,0:T(8,128)(2,1)S(1)}, u32[]{:S(2)}, u32[]{:S(2)}) %collective-permute-start.36) | collective-permute-done | bytes 262176 | tf_op jit(solution)/shard_map/ppermute | solution.py:49
  200.3 4.2 %collective-permute-start.41 = (bf16[8,4096]{1,0:T(8,128)(2,1)S(1)}, bf16[8,4096]{1,0:T(8,128)(2,1)S(1)}, u32[]{:S(2)}, u32[]{:S(2)}) collective-permute-start(bf16[8,4096]{1,0:T(8,128)(2,1)S(1)} %get-tuple-element.118), channel_id=1, source_target_pairs={{0,8},{2,10},{4,12},{6,14},{8,16},{10,18},{12,20},{14,22},{16,24},... | collective-permute-start | bytes 196616 | tf_op jit(solution)/shard_map/ppermute | solution.py:44
  204.5 1.7 collective-permute-start.40
  206.2 1.9 collective-permute-start.39
  208.1 4.8 %collective-permute-done.40.refs_2_ = bf16[8,4096]{1,0:T(8,128)(2,1)S(1)} collective-permute-done((bf16[8,4096]{1,0:T(8,128)(2,1)S(1)}, bf16[8,4096]{1,0:T(8,128)(2,1)S(1)}, u32[]{:S(2)}, u32[]{:S(2)}) %collective-permute-start.40) | collective-permute-done | bytes 65568 | tf_op jit(solution)/shard_map/ppermute | solution.py:44
  213.2 9.1 %all_to_all.11.refs_0_ = bf16[4,8,4096]{2,1,0:T(8,128)(2,1)S(1)} all-to-all(bf16[4,8,4096]{2,1,0:T(8,128)(2,1)S(1)} %regroup.1), channel_id=1, replica_groups={{0,2,4,6},{8,10,12,14},{16,18,20,22},{24,26,28,30},{1,3,5,7},{9,11,13,1..., dimensions={0} | all-to-all | bytes 524288 | tf_op jit(solution)/shard_map/all_to_all | solution.py:517
  (94 shorter events, 14.5 us)
Async XLA Ops:
  2.8 11.4 %collective-permute-start.2 = (bf16[1024,128]{1,0:T(8,128)(2,1)S(1)}, bf16[1024,128]{1,0:T(8,128)(2,1)}, u32[]{:S(2)}, u32[]{:S(2)}) collective-permute-start(bf16[1024,128]{1,0:T(8,128)(2,1)S(1)} %pick_head.1.refs_2_), channel_id=1, source_target_pairs={{0,192},{32,224},{64,0},{96,32},{128,64},{160,96},{192,128},{224,1... | collective-permute-start | bytes 786440 | tf_op jit(solution)/shard_map/ppermute | solution.py:49
  3.6 10.6 %collective-permute-start.1 = (bf16[1024,128]{1,0:T(8,128)(2,1)S(1)}, bf16[1024,128]{1,0:T(8,128)(2,1)S(1)}, u32[]{:S(2)}, u32[]{:S(2)}) collective-permute-start(bf16[1024,128]{1,0:T(8,128)(2,1)S(1)} %pick_head.1.refs_2_), channel_id=1, source_target_pairs={{0,64},{32,96},{64,128},{96,160},{128,192},{160,224},{192,0},{224,... | collective-permute-start | bytes 786440 | tf_op jit(solution)/shard_map/ppermute | solution.py:49
  6.1 8.1 %collective-permute-start = (bf16[1024,128]{1,0:T(8,128)(2,1)S(1)}, bf16[1024,128]{1,0:T(8,128)(2,1)}, u32[]{:S(2)}, u32[]{:S(2)}) collective-permute-start(bf16[1024,128]{1,0:T(8,128)(2,1)S(1)} %pick_head.1.refs_2_), channel_id=1, source_target_pairs={{0,32},{32,0},{64,96},{96,64},{128,160},{160,128},{192,224},{224,1... | collective-permute-start | bytes 786440 | tf_op jit(solution)/shard_map/ppermute | solution.py:53
  8.1 9.6 %copy-start.5 = (bf16[512,512]{1,0:T(8,128)(2,1)S(1)}, bf16[512,512]{1,0:T(8,128)(2,1)}, u32[]{:S(2)}) copy-start(bf16[512,512]{1,0:T(8,128)(2,1)} %refs_1_.7) | copy-start | bytes 1572868
  10.9 17.1 %collective-permute-start.7 = (bf16[256,1024]{1,0:T(8,128)(2,1)S(1)}, bf16[256,1024]{1,0:T(8,128)(2,1)S(1)}, u32[]{:S(2)}, u32[]{:S(2)}) collective-permute-start(bf16[256,1024]{1,0:T(8,128)(2,1)S(1)} %get-tuple-element.60), channel_id=1, source_target_pairs={{0,2},{2,4},{4,6},{6,0},{8,10},{10,12},{12,14},{14,8},{16,18},{18,... | collective-permute-start | bytes 1572872 | tf_op jit(solution)/shard_map/ppermute | solution.py:39
  12.4 15.7 %collective-permute-start.8 = (bf16[256,1024]{1,0:T(8,128)(2,1)S(1)}, bf16[256,1024]{1,0:T(8,128)(2,1)S(1)}, u32[]{:S(2)}, u32[]{:S(2)}) collective-permute-start(bf16[256,1024]{1,0:T(8,128)(2,1)S(1)} %get-tuple-element.62), channel_id=1, source_target_pairs={{0,6},{2,0},{4,2},{6,4},{8,14},{10,8},{12,10},{14,12},{16,22},{18,... | collective-permute-start | bytes 1572872 | tf_op jit(solution)/shard_map/ppermute | solution.py:39
  14.2 12.9 %collective-permute-start.4 = (bf16[1024,128]{1,0:T(8,128)(2,1)S(1)}, bf16[1024,128]{1,0:T(8,128)(2,1)S(1)}, u32[]{:S(2)}, u32[]{:S(2)}) collective-permute-start(bf16[1024,128]{1,0:T(8,128)(2,1)S(1)} %collective-permute-done.1.refs_4_), channel_id=1, source_target_pairs={{0,32},{32,0},{64,96},{96,64},{128,160},{160,128},{192,224},{224,1... | collective-permute-start | bytes 786440 | tf_op jit(solution)/shard_map/ppermute | solution.py:53
  15.6 11.5 %collective-permute-start.3 = (bf16[1024,128]{1,0:T(8,128)(2,1)S(1)}, bf16[1024,128]{1,0:T(8,128)(2,1)S(1)}, u32[]{:S(2)}, u32[]{:S(2)}) collective-permute-start(bf16[1024,128]{1,0:T(8,128)(2,1)S(1)} %collective-permute-done.1.refs_4_), channel_id=1, source_target_pairs={{0,64},{32,96},{64,128},{96,160},{128,192},{160,224},{192,0},{224,... | collective-permute-start | bytes 786440 | tf_op jit(solution)/shard_map/ppermute | solution.py:49
  17.0 10.1 %collective-permute-start.5 = (bf16[1024,128]{1,0:T(8,128)(2,1)}, bf16[1024,128]{1,0:T(8,128)(2,1)S(1)}, u32[]{:S(2)}, u32[]{:S(2)}) collective-permute-start(bf16[1024,128]{1,0:T(8,128)(2,1)} %collective-permute-done.refs_3_), channel_id=1, source_target_pairs={{0,192},{32,224},{64,0},{96,32},{128,64},{160,96},{192,128},{224,1... | collective-permute-start | bytes 786440 | tf_op jit(solution)/shard_map/ppermute | solution.py:49
  27.1 7.9 %collective-permute-start.6 = (bf16[1024,128]{1,0:T(8,128)(2,1)S(1)}, bf16[1024,128]{1,0:T(8,128)(2,1)S(1)}, u32[]{:S(2)}, u32[]{:S(2)}) collective-permute-start(bf16[1024,128]{1,0:T(8,128)(2,1)S(1)} %collective-permute-done.3.refs_3_), channel_id=1, source_target_pairs={{0,32},{32,0},{64,96},{96,64},{128,160},{160,128},{192,224},{224,1... | collective-permute-start | bytes 786440 | tf_op jit(solution)/shard_map/ppermute | solution.py:53
  38.1 22.4 %collective-permute-start.13 = (bf16[512,512]{1,0:T(8,128)(2,1)S(1)}, bf16[512,512]{1,0:T(8,128)(2,1)S(1)}, u32[]{:S(2)}, u32[]{:S(2)}) collective-permute-start(bf16[512,512]{1,0:T(8,128)(2,1)S(1)} %attend.5.own_ref), channel_id=1, source_target_pairs={{0,6},{2,0},{4,2},{6,4},{8,14},{10,8},{12,10},{14,12},{16,22},{18,... | collective-permute-start | bytes 1572872 | tf_op jit(solution)/shard_map/ppermute | solution.py:39
  40.6 23.4 %collective-permute-start.12 = (bf16[512,512]{1,0:T(8,128)(2,1)S(1)}, bf16[512,512]{1,0:T(8,128)(2,1)S(1)}, u32[]{:S(2)}, u32[]{:S(2)}) collective-permute-start(bf16[512,512]{1,0:T(8,128)(2,1)S(1)} %attend.5.own_ref), channel_id=1, source_target_pairs={{0,2},{2,4},{4,6},{6,0},{8,10},{10,12},{12,14},{14,8},{16,18},{18,... | collective-permute-start | bytes 1572872 | tf_op jit(solution)/shard_map/ppermute | solution.py:39
  40.6 23.4 %collective-permute-start.16 = (bf16[256,1024]{1,0:T(8,128)(2,1)}, bf16[256,1024]{1,0:T(8,128)(2,1)S(1)}, u32[]{:S(2)}, u32[]{:S(2)}) collective-permute-start(bf16[256,1024]{1,0:T(8,128)(2,1)} %get-tuple-element.88), channel_id=1, source_target_pairs={{0,4},{2,6},{4,0},{6,2},{8,12},{10,14},{12,8},{14,10},{16,20},{18,... | collective-permute-start | bytes 1572872 | tf_op jit(solution)/shard_map/ppermute | solution.py:39
  64.0 13.1 %copy-start.9 = (s32[32,8]{0,1:T(8,128)S(1)}, s32[32,8]{0,1:T(8,128)}, u32[]{:S(2)}) copy-start(s32[32,8]{0,1:T(8,128)} %param.19) | copy-start | bytes 3076
  64.1 19.8 %collective-permute-start.17 = (bf16[768,1024]{1,0:T(8,128)(2,1)S(1)}, bf16[768,1024]{1,0:T(8,128)(2,1)S(1)}, u32[]{:S(2)}, u32[]{:S(2)}) collective-permute-start(bf16[768,1024]{1,0:T(8,128)(2,1)S(1)} %pad_maximum_fusion), channel_id=1, source_target_pairs={{0,1},{1,0},{2,3},{3,2},{4,5},{5,4},{6,7},{7,6},{8,9},{9,8},{10,11... | collective-permute-start | bytes 4718600 | tf_op jit(solution)/shard_map/ppermute | solution.py:57
  64.3 23.2 %collective-permute-start.14 = (bf16[256,512]{1,0:T(8,128)(2,1)S(1)}, bf16[256,512]{1,0:T(8,128)(2,1)S(1)}, u32[]{:S(2)}, u32[]{:S(2)}) collective-permute-start(bf16[256,512]{1,0:T(8,128)(2,1)S(1)} %slice.30), channel_id=1, source_target_pairs={{0,2},{2,4},{4,6},{6,0},{8,10},{10,12},{12,14},{14,8},{16,18},{18,... | collective-permute-start | bytes 786440 | tf_op jit(solution)/shard_map/ppermute | solution.py:39
  64.4 23.2 %collective-permute-start.15 = (bf16[256,512]{1,0:T(8,128)(2,1)S(1)}, bf16[256,512]{1,0:T(8,128)(2,1)S(1)}, u32[]{:S(2)}, u32[]{:S(2)}) collective-permute-start(bf16[256,512]{1,0:T(8,128)(2,1)S(1)} %slice.31), channel_id=1, source_target_pairs={{0,6},{2,0},{4,2},{6,4},{8,14},{10,8},{12,10},{14,12},{16,22},{18,... | collective-permute-start | bytes 786440 | tf_op jit(solution)/shard_map/ppermute | solution.py:39
  67.6 9.5 %collective-permute-start.9 = (bf16[40,1024]{1,0:T(8,128)(2,1)S(1)}, bf16[40,1024]{1,0:T(8,128)(2,1)S(1)}, u32[]{:S(2)}, u32[]{:S(2)}) collective-permute-start(bf16[40,1024]{1,0:T(8,128)(2,1)S(1)} %get-tuple-element.81), channel_id=1, source_target_pairs={{0,6},{2,0},{4,2},{6,4},{8,14},{10,8},{12,10},{14,12},{16,22},{18,... | collective-permute-start | bytes 245768 | tf_op jit(solution)/shard_map/ppermute | solution.py:39
  67.6 10.1 %collective-permute-start.10 = (bf16[40,1024]{1,0:T(8,128)(2,1)S(1)}, bf16[40,1024]{1,0:T(8,128)(2,1)S(1)}, u32[]{:S(2)}, u32[]{:S(2)}) collective-permute-start(bf16[40,1024]{1,0:T(8,128)(2,1)S(1)} %get-tuple-element.82), channel_id=1, source_target_pairs={{0,4},{2,6},{4,0},{6,2},{8,12},{10,14},{12,8},{14,10},{16,20},{18,... | collective-permute-start | bytes 245768 | tf_op jit(solution)/shard_map/ppermute | solution.py:39
  77.0 6.1 %collective-permute-start.11 = (bf16[40,1024]{1,0:T(8,128)(2,1)S(1)}, bf16[40,1024]{1,0:T(8,128)(2,1)S(1)}, u32[]{:S(2)}, u32[]{:S(2)}) collective-permute-start(bf16[40,1024]{1,0:T(8,128)(2,1)S(1)} %get-tuple-element.83), channel_id=1, source_target_pairs={{0,2},{2,4},{4,6},{6,0},{8,10},{10,12},{12,14},{14,8},{16,18},{18,... | collective-permute-start | bytes 245768 | tf_op jit(solution)/shard_map/ppermute | solution.py:39
  88.9 10.4 %collective-permute-start.20 = (bf16[128,512]{1,0:T(8,128)(2,1)S(1)}, bf16[128,512]{1,0:T(8,128)(2,1)S(1)}, u32[]{:S(2)}, u32[]{:S(2)}) collective-permute-start(bf16[128,512]{1,0:T(8,128)(2,1)S(1)} %get-tuple-element.102), channel_id=1, source_target_pairs={{0,24},{2,26},{4,28},{6,30},{8,0},{10,2},{12,4},{14,6},{16,8},{18,... | collective-permute-start | bytes 393224 | tf_op jit(solution)/shard_map/ppermute | solution.py:44
  94.9 9.2 %collective-permute-start.18 = (bf16[128,512]{1,0:T(8,128)(2,1)S(1)}, bf16[128,512]{1,0:T(8,128)(2,1)S(1)}, u32[]{:S(2)}, u32[]{:S(2)}) collective-permute-start(bf16[128,512]{1,0:T(8,128)(2,1)S(1)} %get-tuple-element.100), channel_id=1, source_target_pairs={{0,8},{2,10},{4,12},{6,14},{8,16},{10,18},{12,20},{14,22},{16,24},... | collective-permute-start | bytes 393224 | tf_op jit(solution)/shard_map/ppermute | solution.py:44
  99.3 48.5 %copy-start.8 = (f32[4096]{0:T(1024)S(1)}, f32[4096]{0:T(1024)}, u32[]{:S(2)}) copy-start(f32[4096]{0:T(1024)} %param.17) | copy-start | bytes 49156
  99.4 12.6 %collective-permute-start.21 = (bf16[128,1024]{1,0:T(8,128)(2,1)S(1)}, bf16[128,1024]{1,0:T(8,128)(2,1)S(1)}, u32[]{:S(2)}, u32[]{:S(2)}) collective-permute-start(bf16[128,1024]{1,0:T(8,128)(2,1)S(1)} %pad_maximum_fusion.3), channel_id=1, source_target_pairs={{0,24},{2,26},{4,28},{6,30},{8,0},{10,2},{12,4},{14,6},{16,8},{18,... | collective-permute-start | bytes 786440 | tf_op jit(solution)/shard_map/ppermute | solution.py:44
  104.1 70.8 %copy-start.2 = (bf16[1,192,4096]{2,1,0:T(8,128)(2,1)S(1)}, bf16[1,192,4096]{2,1,0:T(8,128)(2,1)}, u32[]{:S(2)}) copy-start(bf16[1,192,4096]{2,1,0:T(8,128)(2,1)} %param.23) | copy-start | bytes 4718596
  104.2 12.1 %collective-permute-start.19 = (bf16[128,1024]{1,0:T(8,128)(2,1)S(1)}, bf16[128,1024]{1,0:T(8,128)(2,1)S(1)}, u32[]{:S(2)}, u32[]{:S(2)}) collective-permute-start(bf16[128,1024]{1,0:T(8,128)(2,1)S(1)} %pad_maximum_fusion.2), channel_id=1, source_target_pairs={{0,8},{2,10},{4,12},{6,14},{8,16},{10,18},{12,20},{14,22},{16,24},... | collective-permute-start | bytes 786440 | tf_op jit(solution)/shard_map/ppermute | solution.py:44
  116.3 58.7 %copy-start.1 = (bf16[1,4096,192]{1,2,0:T(8,128)(2,1)S(1)}, bf16[1,4096,192]{1,2,0:T(8,128)(2,1)}, u32[]{:S(2)}) copy-start(bf16[1,4096,192]{1,2,0:T(8,128)(2,1)} %param.22) | copy-start | bytes 4718596
  117.2 57.8 %copy-start = (bf16[1,4096,192]{1,2,0:T(8,128)(2,1)S(1)}, bf16[1,4096,192]{1,2,0:T(8,128)(2,1)}, u32[]{:S(2)}) copy-start(bf16[1,4096,192]{1,2,0:T(8,128)(2,1)} %param.21) | copy-start | bytes 4718596
  117.2 17.2 %collective-permute-start.22 = (bf16[32,1024]{1,0:T(8,128)(2,1)S(1)}, bf16[32,1024]{1,0:T(8,128)(2,1)S(1)}, u32[]{:S(2)}, u32[]{:S(2)}) collective-permute-start(bf16[32,1024]{1,0:T(8,128)(2,1)S(1)} %get-tuple-element.104), channel_id=1, source_target_pairs={{0,8},{2,10},{4,12},{6,14},{8,16},{10,18},{12,20},{14,22},{16,24},... | collective-permute-start | bytes 196616 | tf_op jit(solution)/shard_map/ppermute | solution.py:44
  117.3 17.1 %collective-permute-start.23 = (bf16[32,1024]{1,0:T(8,128)(2,1)S(1)}, bf16[32,1024]{1,0:T(8,128)(2,1)S(1)}, u32[]{:S(2)}, u32[]{:S(2)}) collective-permute-start(bf16[32,1024]{1,0:T(8,128)(2,1)S(1)} %get-tuple-element.105), channel_id=1, source_target_pairs={{0,16},{2,18},{4,20},{6,22},{8,24},{10,26},{12,28},{14,30},{16,0},... | collective-permute-start | bytes 196616 | tf_op jit(solution)/shard_map/ppermute | solution.py:44
  121.1 15.7 %collective-permute-start.24 = (bf16[32,1024]{1,0:T(8,128)(2,1)S(1)}, bf16[32,1024]{1,0:T(8,128)(2,1)S(1)}, u32[]{:S(2)}, u32[]{:S(2)}) collective-permute-start(bf16[32,1024]{1,0:T(8,128)(2,1)S(1)} %get-tuple-element.106), channel_id=1, source_target_pairs={{0,24},{2,26},{4,28},{6,30},{8,0},{10,2},{12,4},{14,6},{16,8},{18,... | collective-permute-start | bytes 196616 | tf_op jit(solution)/shard_map/ppermute | solution.py:44
  148.6 9.6 %collective-permute-start.26 = (bf16[32,4096]{1,0:T(8,128)(2,1)S(1)}, bf16[32,4096]{1,0:T(8,128)(2,1)S(1)}, u32[]{:S(2)}, u32[]{:S(2)}) collective-permute-start(bf16[32,4096]{1,0:T(8,128)(2,1)S(1)} %get-tuple-element.109.refs_0_), channel_id=1, source_target_pairs={{0,64},{32,96},{64,128},{96,160},{128,192},{160,224},{192,0},{224,... | collective-permute-start | bytes 786440 | tf_op jit(solution)/shard_map/ppermute | solution.py:49
  152.1 9.8 %collective-permute-start.25 = (bf16[32,4096]{1,0:T(8,128)(2,1)S(1)}, bf16[32,4096]{1,0:T(8,128)(2,1)S(1)}, u32[]{:S(2)}, u32[]{:S(2)}) collective-permute-start(bf16[32,4096]{1,0:T(8,128)(2,1)S(1)} %get-tuple-element.109.refs_0_), channel_id=1, source_target_pairs={{0,32},{32,0},{64,96},{96,64},{128,160},{160,128},{192,224},{224,1... | collective-permute-start | bytes 786440 | tf_op jit(solution)/shard_map/ppermute | solution.py:53
  158.2 7.6 %collective-permute-start.29 = (bf16[32,4096]{1,0:T(8,128)(2,1)S(1)}, bf16[32,4096]{1,0:T(8,128)(2,1)S(1)}, u32[]{:S(2)}, u32[]{:S(2)}) collective-permute-start(bf16[32,4096]{1,0:T(8,128)(2,1)S(1)} %collective-permute-done.26.refs_2_), channel_id=1, source_target_pairs={{0,64},{32,96},{64,128},{96,160},{128,192},{160,224},{192,0},{224,... | collective-permute-start | bytes 786440 | tf_op jit(solution)/shard_map/ppermute | solution.py:49
  161.9 7.6 %collective-permute-start.27 = (bf16[32,4096]{1,0:T(8,128)(2,1)S(1)}, bf16[32,4096]{1,0:T(8,128)(2,1)S(1)}, u32[]{:S(2)}, u32[]{:S(2)}) collective-permute-start(bf16[32,4096]{1,0:T(8,128)(2,1)S(1)} %get-tuple-element.109.refs_0_), channel_id=1, source_target_pairs={{0,192},{32,224},{64,0},{96,32},{128,64},{160,96},{192,128},{224,1... | collective-permute-start | bytes 786440 | tf_op jit(solution)/shard_map/ppermute | solution.py:49
  161.9 7.6 %collective-permute-start.28 = (bf16[32,4096]{1,0:T(8,128)(2,1)S(1)}, bf16[32,4096]{1,0:T(8,128)(2,1)S(1)}, u32[]{:S(2)}, u32[]{:S(2)}) collective-permute-start(bf16[32,4096]{1,0:T(8,128)(2,1)S(1)} %collective-permute-done.26.refs_2_), channel_id=1, source_target_pairs={{0,32},{32,0},{64,96},{96,64},{128,160},{160,128},{192,224},{224,1... | collective-permute-start | bytes 786440 | tf_op jit(solution)/shard_map/ppermute | solution.py:53
  161.9 10.4 %collective-permute-start.30 = (bf16[32,4096]{1,0:T(8,128)(2,1)S(1)}, bf16[32,4096]{1,0:T(8,128)(2,1)S(1)}, u32[]{:S(2)}, u32[]{:S(2)}) collective-permute-start(bf16[32,4096]{1,0:T(8,128)(2,1)S(1)} %collective-permute-done.25.refs_1_), channel_id=1, source_target_pairs={{0,192},{32,224},{64,0},{96,32},{128,64},{160,96},{192,128},{224,1... | collective-permute-start | bytes 786440 | tf_op jit(solution)/shard_map/ppermute | solution.py:49
  165.8 9.2 %collective-permute-start.31 = (bf16[32,4096]{1,0:T(8,128)(2,1)S(1)}, bf16[32,4096]{1,0:T(8,128)(2,1)S(1)}, u32[]{:S(2)}, u32[]{:S(2)}) collective-permute-start(bf16[32,4096]{1,0:T(8,128)(2,1)S(1)} %collective-permute-done.29.refs_5_), channel_id=1, source_target_pairs={{0,32},{32,0},{64,96},{96,64},{128,160},{160,128},{192,224},{224,1... | collective-permute-start | bytes 786440 | tf_op jit(solution)/shard_map/ppermute | solution.py:53
  176.9 7.7 %collective-permute-start.33 = (bf16[32,4096]{1,0:T(8,128)(2,1)S(1)}, bf16[32,4096]{1,0:T(8,128)(2,1)S(1)}, u32[]{:S(2)}, u32[]{:S(2)}) collective-permute-start(bf16[32,4096]{1,0:T(8,128)(2,1)S(1)} %get-tuple-element.114), channel_id=1, source_target_pairs={{0,32},{32,0},{64,96},{96,64},{128,160},{160,128},{192,224},{224,1... | collective-permute-start | bytes 786440 | tf_op jit(solution)/shard_map/ppermute | solution.py:53
  177.0 15.5 %collective-permute-start.32 = (bf16[32,4096]{1,0:T(8,128)(2,1)S(1)}, bf16[32,4096]{1,0:T(8,128)(2,1)S(1)}, u32[]{:S(2)}, u32[]{:S(2)}) collective-permute-start(bf16[32,4096]{1,0:T(8,128)(2,1)S(1)} %get-tuple-element.111), channel_id=1, source_target_pairs={{0,64},{32,96},{64,128},{96,160},{128,192},{160,224},{192,0},{224,... | collective-permute-start | bytes 786440 | tf_op jit(solution)/shard_map/ppermute | solution.py:49
  180.7 8.8 %collective-permute-start.35 = (bf16[32,4096]{1,0:T(8,128)(2,1)S(1)}, bf16[32,4096]{1,0:T(8,128)(2,1)S(1)}, u32[]{:S(2)}, u32[]{:S(2)}) collective-permute-start(bf16[32,4096]{1,0:T(8,128)(2,1)S(1)} %get-tuple-element.115), channel_id=1, source_target_pairs={{0,32},{32,0},{64,96},{96,64},{128,160},{160,128},{192,224},{224,1... | collective-permute-start | bytes 786440 | tf_op jit(solution)/shard_map/ppermute | solution.py:53
  182.7 6.4 %collective-permute-start.37 = (bf16[32,4096]{1,0:T(8,128)(2,1)S(1)}, bf16[32,4096]{1,0:T(8,128)(2,1)S(1)}, u32[]{:S(2)}, u32[]{:S(2)}) collective-permute-start(bf16[32,4096]{1,0:T(8,128)(2,1)S(1)} %get-tuple-element.117), channel_id=1, source_target_pairs={{0,64},{32,96},{64,128},{96,160},{128,192},{160,224},{192,0},{224,... | collective-permute-start | bytes 786440 | tf_op jit(solution)/shard_map/ppermute | solution.py:49
  184.7 7.7 %collective-permute-start.34 = (bf16[32,4096]{1,0:T(8,128)(2,1)S(1)}, bf16[32,4096]{1,0:T(8,128)(2,1)S(1)}, u32[]{:S(2)}, u32[]{:S(2)}) collective-permute-start(bf16[32,4096]{1,0:T(8,128)(2,1)S(1)} %add_convert_fusion.3), channel_id=1, source_target_pairs={{0,192},{32,224},{64,0},{96,32},{128,64},{160,96},{192,128},{224,1... | collective-permute-start | bytes 786440 | tf_op jit(solution)/shard_map/ppermute | solution.py:49
  189.1 8.1 %collective-permute-start.38 = (bf16[32,4096]{1,0:T(8,128)(2,1)S(1)}, bf16[32,4096]{1,0:T(8,128)(2,1)S(1)}, u32[]{:S(2)}, u32[]{:S(2)}) collective-permute-start(bf16[32,4096]{1,0:T(8,128)(2,1)S(1)} %add_convert_fusion.1), channel_id=1, source_target_pairs={{0,32},{32,0},{64,96},{96,64},{128,160},{160,128},{192,224},{224,1... | collective-permute-start | bytes 786440 | tf_op jit(solution)/shard_map/ppermute | solution.py:53
  192.4 7.7 %collective-permute-start.36 = (bf16[32,4096]{1,0:T(8,128)(2,1)S(1)}, bf16[32,4096]{1,0:T(8,128)(2,1)S(1)}, u32[]{:S(2)}, u32[]{:S(2)}) collective-permute-start(bf16[32,4096]{1,0:T(8,128)(2,1)S(1)} %add_convert_fusion.2), channel_id=1, source_target_pairs={{0,192},{32,224},{64,0},{96,32},{128,64},{160,96},{192,128},{224,1... | collective-permute-start | bytes 786440 | tf_op jit(solution)/shard_map/ppermute | solution.py:49
  200.3 7.9 %collective-permute-start.41 = (bf16[8,4096]{1,0:T(8,128)(2,1)S(1)}, bf16[8,4096]{1,0:T(8,128)(2,1)S(1)}, u32[]{:S(2)}, u32[]{:S(2)}) collective-permute-start(bf16[8,4096]{1,0:T(8,128)(2,1)S(1)} %get-tuple-element.118), channel_id=1, source_target_pairs={{0,8},{2,10},{4,12},{6,14},{8,16},{10,18},{12,20},{14,22},{16,24},... | collective-permute-start | bytes 196616 | tf_op jit(solution)/shard_map/ppermute | solution.py:44
  204.5 8.5 %collective-permute-start.40 = (bf16[8,4096]{1,0:T(8,128)(2,1)S(1)}, bf16[8,4096]{1,0:T(8,128)(2,1)S(1)}, u32[]{:S(2)}, u32[]{:S(2)}) collective-permute-start(bf16[8,4096]{1,0:T(8,128)(2,1)S(1)} %get-tuple-element.119), channel_id=1, source_target_pairs={{0,16},{2,18},{4,20},{6,22},{8,24},{10,26},{12,28},{14,30},{16,0},... | collective-permute-start | bytes 196616 | tf_op jit(solution)/shard_map/ppermute | solution.py:44
  206.2 6.8 %collective-permute-start.39 = (bf16[8,4096]{1,0:T(8,128)(2,1)S(1)}, bf16[8,4096]{1,0:T(8,128)(2,1)S(1)}, u32[]{:S(2)}, u32[]{:S(2)}) collective-permute-start(bf16[8,4096]{1,0:T(8,128)(2,1)S(1)} %get-tuple-element.120), channel_id=1, source_target_pairs={{0,24},{2,26},{4,28},{6,30},{8,0},{10,2},{12,4},{14,6},{16,8},{18,... | collective-permute-start | bytes 196616 | tf_op jit(solution)/shard_map/ppermute | solution.py:44
  (4 other events, 19.6 us)
where the time goes:
time: 228 us; the launch traced here: 224 us
  waiting for transfers between devices  90.9 us (40%)
  starting transfers between devices  73.3 us (32%)
  Pallas kernels  34.5 us (15%)
  blocking collectives  20 us (9%)
    ppermute x10, starting transfers between devices, shift_z(): return lax.ppermute(a, 'exp', pairs)  36.1 us
    ppermute x10, waiting for transfers between devices, shift_x(): return lax.ppermute(a, 'exp', pairs)  33.4 us
    ppermute x12, waiting for transfers between devices, shift_y(): return lax.ppermute(a, 'ctx', pairs)  24.8 us
    ppermute x10, waiting for transfers between devices, shift_z(): return lax.ppermute(a, 'exp', pairs)  23.5 us
    all_to_all x2, blocking collectives, exchange_x(): return lax.all_to_all(a, 'exp', 0, 0, tiled=True, axis_index_groups=groups)  20 us
    pallas_call x3, Pallas kernels, attend(): pl.pallas_call(kernel, grid_spec=pltpu.PrefetchScalarGridSpec(num_scalar_...  19.5 us
    ppermute x12, starting transfers between devices, shift_y(): return lax.ppermute(a, 'ctx', pairs)  16.6 us
    ppermute x10, starting transfers between devices, shift_x(): return lax.ppermute(a, 'exp', pairs)  12.5 us
  transfers between devices with their start and end apart: 42, of which 19 were waited for; matrix products, arithmetic and copies ran while one was open for 0% of the time, Pallas kernels for 11%

commit v1 on v0

--- a/solution.py
+++ b/solution.py
@@ -18,6 +18,7 @@
 N_Z = 4
 N_Y = 4
 TOKENS = 32
+RIDER = 2 * (TOKENS + TOPK)
 BF16 = jnp.bfloat16
 F32 = jnp.float32
 LOWEST = -1e30
@@ -103,19 +104,29 @@
     )(place, out_proj, out_proj, out_proj)
 
 
-def attend(queries, blocks, bias, state, last):
+def attend(queries, blocks, bias, state, riders=None):
     rows, heads = queries.shape[0], queries.shape[1] // HEAD_DIM
-    n = len(blocks)
+    calls = len(blocks)
+    n = sum(b.shape[0] for b in blocks) // (2 * rows)
     first = state is None
+    last = riders is not None
     tile = 128
 
     def kernel(*refs):
         bias_ref, q_ref = refs[0], refs[1]
-        kv_refs = refs[2 : 2 + n]
-        rest = refs[2 + n :]
+        kv_refs = [
+            r.at[first_row : first_row + 2 * rows]
+            for r in refs[2 : 2 + calls]
+            for first_row in range(0, r.shape[0], 2 * rows)
+        ]
+        rest = refs[2 + calls :]
         if not first:
             acc_in, top_in = rest[0], rest[1]
             rest = rest[2:]
+        if last:
+            rider_refs, rest = rest[:3], rest[3:]
+            for rider, target in zip(rider_refs, rest):
+                target[rows:, :] = rider[...]
         key = jnp.concatenate([r[0:rows, :] for r in kv_refs], axis=0)
         ones = jnp.ones((rows, HEAD_DIM), BF16)
         value = jnp.concatenate(
@@ -154,13 +165,17 @@
                 factor = jnp.exp2((before - newest) * EXP2_SCALE)
                 total = acc_in[0, at, :] * jnp.concatenate([factor, factor], axis=1) + total
             if last:
-                rest[0][at, :] = (total[:, :HEAD_DIM] / total[:, HEAD_DIM:]).astype(BF16)
+                done = (total[:, :HEAD_DIM] / total[:, HEAD_DIM:]).astype(BF16)
+                for target in rest:
+                    target[at, :] = done
             else:
                 rest[0][0, at, :] = total
                 rest[1][0, at, :] = newest
 
     q_spec = pl.BlockSpec((rows, HEAD_DIM), lambda h, f: (0, h))
-    kv_spec = pl.BlockSpec((2 * rows, HEAD_DIM), lambda h, f: (0, 0))
+    kv_specs = [pl.BlockSpec(b.shape, lambda h, f: (0, 0)) for b in blocks]
+    rider_spec = pl.BlockSpec((RIDER, HEAD_DIM), lambda h, f: (0, h))
+    message_spec = pl.BlockSpec((rows + RIDER, HEAD_DIM), lambda h, f: (0, h))
     state_specs = [
         pl.BlockSpec((1, rows, 2 * HEAD_DIM), lambda h, f: (h, 0, 0)),
         pl.BlockSpec((1, rows, HEAD_DIM), lambda h, f: (h, 0, 0)),
@@ -174,10 +189,15 @@
         grid_spec=pltpu.PrefetchScalarGridSpec(
             num_scalar_prefetch=1,
             grid=(heads,),
-            in_specs=[q_spec] + [kv_spec] * n + ([] if first else state_specs),
-            out_specs=q_spec if last else state_specs,
+            in_specs=[q_spec]
+            + kv_specs
+            + ([] if first else state_specs)
+            + ([rider_spec] * 3 if last else []),
+            out_specs=[message_spec] * 3 if last else state_specs,
         ),
-        out_shape=jax.ShapeDtypeStruct(queries.shape, BF16) if last else state_shapes,
+        out_shape=[jax.ShapeDtypeStruct((rows + RIDER, queries.shape[1]), BF16)] * 3
+        if last
+        else state_shapes,
         compiler_params=params(20),
         cost_estimate=pl.CostEstimate(
             flops=heads * n * rows * rows * HEAD_DIM * 4,
@@ -185,7 +205,7 @@
             bytes_accessed=4 << 20,
         ),
         name="attend",
-    )(bias, queries, *blocks, *(() if first else state))
+    )(bias, queries, *blocks, *(() if first else state), *(riders if last else ()))
 
 
 def rows_of(place_ref, left_ref, dz, columns):
@@ -195,7 +215,6 @@
 
 def project_near(place, own, out_proj, lefts, fetched, other):
     n = len(lefts)
-    rows = own.shape[1]
     cols = out_proj.shape[1] // N_X
 
     def kernel(place_ref, own_ref, weight_ref, *refs):
@@ -219,9 +238,9 @@
         grid_spec=pltpu.PrefetchScalarGridSpec(
             num_scalar_prefetch=1,
             grid=(1,),
-            in_specs=[square, pl.BlockSpec((rows, cols), lambda i, w: (0, w[1]))]
+            in_specs=[square, pl.BlockSpec((out_proj.shape[0], cols), lambda i, w: (0, w[1]))]
             + [square] * n
-            + [pl.BlockSpec((rows // 2, cols), fixed)] * n
+            + [pl.BlockSpec(fetched[0].shape, fixed)] * n
             + [pl.BlockSpec(other.shape, fixed)],
             out_specs=[pl.BlockSpec((N_X * TOKENS, cols), fixed)] * N_Z,
         ),
@@ -274,28 +293,31 @@
 
 
 def pick_hidden(place, live, hidden_in, ids):
-    cols = D // N_X
+    cols = D // N_X // 2
 
     def kernel(place_ref, live_ref, hidden_ref, id_ref, *out_refs):
         x = place_ref[1]
         t = lax.broadcasted_iota(jnp.int32, (TOPK, TOKENS), 1)
         alive = jnp.where(t < live_ref[0], id_ref[...] + 1, 0).astype(F32)
+        lanes = (
+            lax.broadcasted_iota(jnp.int32, (TOKENS, cols), 1)
+            == lax.broadcasted_iota(jnp.int32, (TOKENS, cols), 0) + x * TOKENS
+        ).astype(F32)
+        alive = jnp.dot(alive, lanes, preferred_element_type=F32)
         for d in range(N_X):
-            column = pl.ds(pl.multiple_of(lax.rem(x + N_X - d, N_X) * cols, cols), cols)
-            out_refs[d][0:TOKENS, :] = hidden_ref[:, column]
-            place_at = (
-                lax.broadcasted_iota(jnp.int32, (TOKENS, cols), 1)
-                == lax.broadcasted_iota(jnp.int32, (TOKENS, cols), 0) + x * TOKENS
-            ).astype(F32)
-            out_refs[d][TOKENS:, :] = jnp.dot(
-                alive, place_at, preferred_element_type=F32
-            ).astype(BF16)
+            for side in range(2):
+                column = pl.multiple_of(lax.rem(x + d, N_X) * (2 * cols) + side * cols, cols)
+                top = side * (TOKENS + TOPK)
+                out_refs[d][top : top + TOKENS, :] = hidden_ref[:, pl.ds(column, cols)]
+                out_refs[d][top + TOKENS : top + TOKENS + TOPK, :] = (
+                    alive if side == 0 else jnp.zeros_like(alive)
+                ).astype(BF16)
 
     return pl.pallas_call(
         kernel,
         in_specs=[pl.BlockSpec(memory_space=SMEM)] * 2 + [whole()] * 2,
         out_specs=[whole()] * N_X,
-        out_shape=[jax.ShapeDtypeStruct((TOKENS + TOPK, cols), BF16)] * N_X,
+        out_shape=[jax.ShapeDtypeStruct((RIDER, cols), BF16)] * N_X,
         compiler_params=params(),
         name="pick_hidden",
     )(place, live, hidden_in, ids)
@@ -312,7 +334,10 @@
         dz, expert_x, owner, cap = s // 32, (s // 8) % 4, (s // 2) % 4, s % 2
         expert = ((z + dz) % N_Z) * N_X + expert_x
         wanted = jnp.where(owner == t // TOKENS, expert + 1, -1).astype(F32)
-        ids = sum(r[TOKENS:, 0:tokens].astype(F32) for r in refs[:4])
+        ids = sum(
+            r[r.shape[0] - RIDER + TOKENS : r.shape[0] - RIDER + TOKENS + TOPK, 0:tokens].astype(F32)
+            for r in refs[:4]
+        )
         present = jnp.zeros((slots, tokens), F32)
         for k in range(TOPK):
             present = present + (ids[k : k + 1, :] == wanted).astype(F32)
@@ -372,9 +397,14 @@
     def kernel(place_ref, h0, h1, h2, h3, s0, s1, s2, pick_ref, *refs):
         mixed_ref, send_refs = refs[0], refs[1:5]
         for d, h in enumerate((h0, h1, h2, h3)):
-            at = pl.ds(pl.multiple_of(lax.rem(place_ref[1] + d, N_X) * TOKENS, TOKENS), TOKENS)
+            row = lax.rem(place_ref[1] + N_X - d, N_X) * TOKENS
+            at = pl.ds(pl.multiple_of(row, TOKENS), TOKENS)
+            top = h.shape[0] - RIDER
+            rows = jnp.concatenate(
+                [h[top : top + TOKENS, :], h[top + TOKENS + TOPK : top + 2 * TOKENS + TOPK, :]], axis=1
+            )
             mixed_ref[at, :] = (
-                h[0:TOKENS, :].astype(F32)
+                rows.astype(F32)
                 + (s0[at, :].astype(F32) + s1[at, :].astype(F32) + s2[at, :].astype(F32))
             ).astype(BF16)
         send = jnp.dot(pick_ref[...], mixed_ref[...], preferred_element_type=F32).astype(BF16)
@@ -557,68 +587,56 @@
         owners = jnp.stack([((y + dy) % N_Y) * 2 + (side ^ flip) for dy, flip in steps])
         return jnp.where(owners < ctx_index, 0.0, LOWEST).astype(F32)
 
+    keys, values, out_proj = [
+        pltpu.with_memory_space_constraint(a, pltpu.HBM) for a in (keys, values, out_proj)
+    ]
     own = pick_head(kv_index.astype(jnp.int32)[None], keys, values)
     swapped = swap_l(own)
-    below = shift_y(own, 1)
-    above = shift_y(own, -1)
-    out_proj = pltpu.with_memory_space_constraint(out_proj, pltpu.HBM)
     away = pick_weights(jnp.stack([rep_index, x]).astype(jnp.int32), out_proj)
-    fetched = [shift_x(away[0], 1), None, shift_x(away[2], 3)]
-    swapped, below, above = tie((swapped, below, above), *away)
-    below_two = shift_y(below, 1)
-    below_swapped = swap_l(below)
-    above_swapped = shift_y(swapped, -1)
+    fetched = [shift_x(away[d - 1], d) for d in range(1, N_X)]
+    (swapped,) = tie((swapped,), *away)
+    pair = jnp.concatenate([own, swapped], axis=0)
+    below = shift_y(pair, 1)
+    above = shift_y(pair, -1)
     state = attend(
         queries,
-        [own, swapped, below, above],
-        jnp.concatenate([jnp.zeros((1,), F32), bias((0, 1), (-1, 0), (1, 0))]),
+        [pair],
+        jnp.concatenate([jnp.zeros((1,), F32), bias((0, 1))]),
         None,
-        False,
-    )
-    below_two, below_swapped, above_swapped = tie(
-        (below_two, below_swapped, above_swapped), *state
-    )
-    far = swap_l(below_two)
-    (away_far,) = tie((away[1],), *state)
-    fetched[1] = shift_x(away_far, 2)
-    below_swapped, above_swapped, *state = tie(
-        (below_swapped, above_swapped, *state), fetched[0], fetched[2]
-    )
+    )
+    riders = pick_hidden(place, live_counts, hidden_in, expert_ids.T)
+    below, above = tie((below, above), *state, *riders)
+    block = own.shape[0]
+    far_a = shift_y(below[:block], 1)
+    far_b = shift_y(above[block:], -1)
     state = attend(
-        queries,
-        [below_swapped, below_two, above_swapped],
-        bias((-1, 1), (-2, 0), (1, 1)),
-        state,
-        False,
-    )
-    (far,) = tie((far,), *state)
-    attended = attend(queries, [far], bias((-2, 1)), state, True)
-
-    half = seq_rows // 2
-    from_left = shift_x(attended, 1)
-    from_right = shift_x(attended, -1)
-    ids = expert_ids.T
-    hidden_in, later_place = tie((hidden_in, place), attended)
-    hidden = pick_hidden(later_place, live_counts, hidden_in, ids)
-    from_left, from_right = tie((from_left, from_right), *hidden)
-    far_a = shift_x(from_left[:half], 1)
-    far_b = shift_x(from_right[half:], -1)
-    fetched = tie(fetched, from_left)
+        queries, [below, above], bias((-1, 0), (-1, 1), (1, 0), (1, 1)), state
+    )
+    far_a, far_b = tie((far_a, far_b), *state, *fetched)
+    messages = attend(
+        queries, [far_a, far_b], bias((-2, 0), (-2, 1)), state, riders[1:]
+    )
+
+    from_left = shift_x(messages[0], 1)
+    from_right = shift_x(messages[2], 3)
+    from_far = shift_x(messages[1], 2)
+    weight = route_weights(
+        tie((place,), from_left)[0], live=live_counts, ids=expert_ids.T, gates=gate_fixed.T
+    )
+    fetched = tie(fetched, from_left, from_right)
     other = swap_core(jnp.concatenate(fetched, axis=0))
-    hidden = [hidden[0]] + [shift_x(hidden[d], -d) for d in range(1, N_X)]
-    pick = route(place, hidden)
-    weight = route_weights(later_place, ids, gate_fixed.T, live_counts)
-    from_left, from_right = tie((from_left, from_right), pick, weight)
     near = project_near(
-        place, attended, out_proj, [from_left, from_right], [fetched[0], fetched[2]], other
-    )
-    far_a, far_b = tie((far_a, far_b), *near)
-    from_far = jnp.concatenate([far_a, far_b], axis=0)
+        place, messages[0], out_proj, [from_left, from_right], [fetched[0], fetched[2]], other
+    )
+    from_far, *near = tie((from_far, *near))
+    hidden = [riders[0], from_left, from_far, from_right]
     mine, up_chunk, down_chunk, low, high = project_far(place, near, from_far, fetched[1], other)
 
     middle = low.shape[1]
     got_low = shift_z(low, 1)
     got_high = shift_z(high, -1)
+    pick = route(place, hidden)
+    got_low, got_high = tie((got_low, got_high), pick)
     up_chunk = jnp.concatenate([add(up_chunk[:, :middle], got_low), up_chunk[:, middle:]], axis=1)
     down_chunk = jnp.concatenate(
         [down_chunk[:, :middle], add(down_chunk[:, middle:], got_high)], axis=1

time: 228 us -> 210 us (0.921); the launches traced: 224 us -> 209 us
  starting transfers between devices: 73.3 us -> 60.9 us
  blocking collectives: 20 us -> 11 us
  waiting for transfers between devices: 90.9 us -> 95.8 us
  Pallas kernels: 34.5 us -> 37.4 us
    ppermute x10, starting transfers between devices: 36.1 us -> 25.8 us  [shift_z(): return lax.ppermute(a, 'exp', pairs)]
    all_to_all x2 -> x1, blocking collectives: 20 us -> 11 us  [exchange_x(): return lax.all_to_all(a, 'exp', 0, 0, tiled=True, axis_index_groups=groups)]
    all_to_all x0 -> x1, waiting for transfers between devices: none -> 5.94 us  [exchange_x(): return lax.all_to_all(a, 'exp', 0, 0, tiled=True, axis_index_groups=groups)]
    ppermute x10 -> x6, waiting for transfers between devices: 33.4 us -> 28.2 us  [shift_x(): return lax.ppermute(a, 'exp', pairs)]
    ppermute x10 -> x6, starting transfers between devices: 12.5 us -> 8.09 us  [shift_x(): return lax.ppermute(a, 'exp', pairs)]
    ppermute x12, starting transfers between devices: 16.6 us -> 12.9 us  [shift_y(): return lax.ppermute(a, 'ctx', pairs)]
    all_to_all x0 -> x1, starting transfers between devices: none -> 3.41 us  [exchange_x(): return lax.all_to_all(a, 'exp', 0, 0, tiled=True, axis_index_groups=groups)]
    ppermute x1, waiting for transfers between devices: 0.01 us -> 3.3 us  [swap_core(): return lax.ppermute(a, 'rep', [(0, 1), (1, 0)])]
  transfers between devices with their start and end apart: 42 -> 37, of which waited for: 19 -> 26; matrix products, arithmetic and copies ran while one was open for 0% -> 1% of each run, Pallas kernels for 11% -> 11%
where the time goes in v1:
time: 210 us; the launch traced here: 209 us
  waiting for transfers between devices  95.8 us (46%)
  starting transfers between devices  60.9 us (29%)
  Pallas kernels  37.4 us (18%)
  blocking collectives  11 us (5%)
    ppermute x6, waiting for transfers between devices, shift_x(): return lax.ppermute(a, 'exp', pairs)  28.2 us
    ppermute x10, waiting for transfers between devices, shift_z(): return lax.ppermute(a, 'exp', pairs)  26.1 us
    ppermute x10, starting transfers between devices, shift_z(): return lax.ppermute(a, 'exp', pairs)  25.8 us
    ppermute x12, waiting for transfers between devices, shift_y(): return lax.ppermute(a, 'ctx', pairs)  25.1 us
    pallas_call x3, Pallas kernels, attend(): pl.pallas_call(kernel, grid_spec=pltpu.PrefetchScalarGridSpec(num_scalar_...  20.2 us
    ppermute x12, starting transfers between devices, shift_y(): return lax.ppermute(a, 'ctx', pairs)  12.9 us
    all_to_all x1, blocking collectives, exchange_x(): return lax.all_to_all(a, 'exp', 0, 0, tiled=True, axis_index_groups=groups)  11 us
    ppermute x7, starting transfers between devices, swap_l(): return lax.ppermute(a, 'ctx', [(i, i ^ 1) for i in range(2 * N_Y)])  10.5 us
  transfers between devices with their start and end apart: 37, of which 26 were waited for; matrix products, arithmetic and copies ran while one was open for 1% of the time, Pallas kernels for 11%

profile of v1, /device:TPU:24, one launch (start us, length us, event | category | flops | bytes accessed | tf_op | source)
XLA Modules:
  0.0 208.7 jit_solution(199868505857841473)
XLA Ops:
  1.6 2.0 collective-permute-start
  3.7 3.1 %pick_weights.1 = (bf16[256,1024]{1,0:T(8,128)(2,1)}, bf16[256,1024]{1,0:T(8,128)(2,1)}, bf16[256,1024]{1,0:T(8,128)(2,1)}) custom-call(s32[2]{0:T(128)S(1)} %pad_add_fusion.1.place_ref, bf16[512,4096]{1,0:T(8,128)(2,1)} %weight_ref.1, bf16[512,4096]{1,0:T(8,128)(2,1)} %weight_ref.1, bf16[512,4096]{1,0:T(8,128)(2,1)} %weight_ref.1), custom_call_target="tpu_custom_call" | custom-call | tf_op jit(solution)/shard_map/pick_weights/pallas_call | solution.py:93
  6.8 3.1 %collective-permute-done = bf16[1024,128]{1,0:T(8,128)(2,1)S(1)} collective-permute-done((bf16[1024,128]{1,0:T(8,128)(2,1)S(1)}, bf16[1024,128]{1,0:T(8,128)(2,1)S(1)}, u32[]{:S(2)}, u32[]{:S(2)}) %collective-permute-start) | collective-permute-done | bytes 262176 | tf_op jit(solution)/shard_map/ppermute | solution.py:54
  10.8 2.5 %collective-permute-start.1 = (bf16[2048,128]{1,0:T(8,128)(2,1)S(1)}, bf16[2048,128]{1,0:T(8,128)(2,1)}, u32[]{:S(2)}, u32[]{:S(2)}) collective-permute-start(bf16[2048,128]{1,0:T(8,128)(2,1)S(1)} %pad_maximum_fusion.1.refs_2_), channel_id=1, source_target_pairs={{0,64},{32,96},{64,128},{96,160},{128,192},{160,224},{192,0},{224,... | collective-permute-start | bytes 1572872 | tf_op jit(solution)/shard_map/ppermute | solution.py:50
  13.3 1.5 collective-permute-start.5
  14.8 2.7 %collective-permute-start.6 = (bf16[256,1024]{1,0:T(8,128)(2,1)}, bf16[256,1024]{1,0:T(8,128)(2,1)S(1)}, u32[]{:S(2)}, u32[]{:S(2)}) collective-permute-start(bf16[256,1024]{1,0:T(8,128)(2,1)} %get-tuple-element.58), channel_id=1, source_target_pairs={{0,4},{2,6},{4,0},{6,2},{8,12},{10,14},{12,8},{14,10},{16,20},{18,... | collective-permute-start | bytes 1572872 | tf_op jit(solution)/shard_map/ppermute | solution.py:40
  17.5 1.4 collective-permute-start.7
  20.5 5.0 %attend.3 = (f32[4,512,256]{2,1,0:T(8,128)S(1)}, f32[4,512,128]{2,1,0:T(8,128)S(1)}) custom-call(f32[2]{0:T(128)S(1)} %pad_maximum_fusion.4.refs_0_, bf16[512,512]{1,0:T(8,128)(2,1)S(1)} %copy-done.3, bf16[2048,128]{1,0:T(8,128)(2,1)S(1)} %pad_maximum_fusion.1.refs_2_), custom_call_target="tpu_custom_call" | custom-call | flops 1073741824 | bytes 4194304 | tf_op jit(solution)/shard_map/attend/pallas_call | solution.py:187
  26.6 1.8 collective-permute-start.3
  28.8 9.5 %attend.4 = (f32[4,512,256]{2,1,0:T(8,128)S(1)}, f32[4,512,128]{2,1,0:T(8,128)S(1)}) custom-call(f32[4]{0:T(128)S(1)} %compare_select_fusion.refs_0_, bf16[512,512]{1,0:T(8,128)(2,1)S(1)} %copy-done.3, bf16[2048,128]{1,0:T(8,128)(2,1)} %collective-permute-done.1.refs_2_, bf16[2048,128]{1,0:T(8,128)(2,1)S(1)} %collective-permute-done.2.refs_3_, ...), custom_call_target="tpu_custom_call" | custom-call | flops 2147483648 | bytes 4194304 | tf_op jit(solution)/shard_map/attend/pallas_call | solution.py:187
  39.4 5.7 %attend.5 = (bf16[592,512]{1,0:T(8,128)(2,1)S(1)}, bf16[592,512]{1,0:T(8,128)(2,1)S(1)}, bf16[592,512]{1,0:T(8,128)(2,1)S(1)}) custom-call(f32[2]{0:T(128)S(1)} %compare_select_fusion.1.refs_0_, bf16[512,512]{1,0:T(8,128)(2,1)S(1)} %copy-done.3, bf16[1024,128]{1,0:T(8,128)(2,1)S(1)} %collective-permute-done.3.refs_2_, ...), custom_call_target="tpu_custom_call" | custom-call | flops 1073741824 | bytes 4194304 | tf_op jit(solution)/shard_map/attend/pallas_call | solution.py:187
  45.1 2.3 %collective-permute-start.10 = (bf16[592,512]{1,0:T(8,128)(2,1)S(1)}, bf16[592,512]{1,0:T(8,128)(2,1)S(1)}, u32[]{:S(2)}, u32[]{:S(2)}) collective-permute-start(bf16[592,512]{1,0:T(8,128)(2,1)S(1)} %get-tuple-element.74), channel_id=1, source_target_pairs={{0,6},{2,0},{4,2},{6,4},{8,14},{10,8},{12,10},{14,12},{16,22},{18,... | collective-permute-start | bytes 1818632 | tf_op jit(solution)/shard_map/ppermute | solution.py:40
  47.4 13.1 %collective-permute-done.10.refs_1_.refs_3_.h3 = bf16[592,512]{1,0:T(8,128)(2,1)S(1)} collective-permute-done((bf16[592,512]{1,0:T(8,128)(2,1)S(1)}, bf16[592,512]{1,0:T(8,128)(2,1)S(1)}, u32[]{:S(2)}, u32[]{:S(2)}) %collective-permute-start.10) | collective-permute-done | bytes 606240 | tf_op jit(solution)/shard_map/ppermute | solution.py:40
  60.5 3.4 %collective-permute-done.8.refs_0_.refs_1_.h1 = bf16[592,512]{1,0:T(8,128)(2,1)S(1)} collective-permute-done((bf16[592,512]{1,0:T(8,128)(2,1)S(1)}, bf16[592,512]{1,0:T(8,128)(2,1)S(1)}, u32[]{:S(2)}, u32[]{:S(2)}) %collective-permute-start.8) | collective-permute-done | bytes 606240 | tf_op jit(solution)/shard_map/ppermute | solution.py:40
  64.5 3.3 %collective-permute-done.11.refs_4_.other_ref = bf16[768,1024]{1,0:T(8,128)(2,1)S(1)} collective-permute-done((bf16[768,1024]{1,0:T(8,128)(2,1)S(1)}, bf16[768,1024]{1,0:T(8,128)(2,1)S(1)}, u32[]{:S(2)}, u32[]{:S(2)}) %collective-permute-start.11) | collective-permute-done | bytes 1572896 | tf_op jit(solution)/shard_map/ppermute | solution.py:58
  67.7 3.7 %project_near.1 = (f32[128,1024]{1,0:T(8,128)S(1)}, f32[128,1024]{1,0:T(8,128)S(1)}, f32[128,1024]{1,0:T(8,128)S(1)}, f32[128,1024]{1,0:T(8,128)S(1)}) custom-call(s32[3]{0:T(128)S(1)} %pad_add_fusion.place_ref, bf16[592,512]{1,0:T(8,128)(2,1)S(1)} %get-tuple-element.72.own_ref, bf16[512,4096]{1,0:T(8,128)(2,1)} %weight_ref.1, ...), custom_call_target="tpu_custom_call" | custom-call | tf_op jit(solution)/shard_map/project_near/pallas_call | solution.py:236
  71.4 10.5 %collective-permute-done.9.left_ref.refs_2_.h2 = bf16[592,512]{1,0:T(8,128)(2,1)S(1)} collective-permute-done((bf16[592,512]{1,0:T(8,128)(2,1)S(1)}, bf16[592,512]{1,0:T(8,128)(2,1)S(1)}, u32[]{:S(2)}, u32[]{:S(2)}) %collective-permute-start.9) | collective-permute-done | bytes 606240 | tf_op jit(solution)/shard_map/ppermute | solution.py:40
  83.3 3.4 %collective-permute-start.12 = (bf16[128,512]{1,0:T(8,128)(2,1)S(1)}, bf16[128,512]{1,0:T(8,128)(2,1)S(1)}, u32[]{:S(2)}, u32[]{:S(2)}) collective-permute-start(bf16[128,512]{1,0:T(8,128)(2,1)S(1)} %get-tuple-element.89), channel_id=1, source_target_pairs={{0,8},{2,10},{4,12},{6,14},{8,16},{10,18},{12,20},{14,22},{16,24},... | collective-permute-start | bytes 393224 | tf_op jit(solution)/shard_map/ppermute | solution.py:45
  86.7 2.7 %collective-permute-start.13 = (bf16[128,512]{1,0:T(8,128)(2,1)S(1)}, bf16[128,512]{1,0:T(8,128)(2,1)S(1)}, u32[]{:S(2)}, u32[]{:S(2)}) collective-permute-start(bf16[128,512]{1,0:T(8,128)(2,1)S(1)} %get-tuple-element.90), channel_id=1, source_target_pairs={{0,24},{2,26},{4,28},{6,30},{8,0},{10,2},{12,4},{14,6},{16,8},{18,... | collective-permute-start | bytes 393224 | tf_op jit(solution)/shard_map/ppermute | solution.py:45
  90.2 3.0 %collective-permute-done.12 = bf16[128,512]{1,0:T(8,128)(2,1)S(1)} collective-permute-done((bf16[128,512]{1,0:T(8,128)(2,1)S(1)}, bf16[128,512]{1,0:T(8,128)(2,1)S(1)}, u32[]{:S(2)}, u32[]{:S(2)}) %collective-permute-start.12) | collective-permute-done | bytes 131104 | tf_op jit(solution)/shard_map/ppermute | solution.py:45
  93.2 3.4 %collective-permute-done.13 = bf16[128,512]{1,0:T(8,128)(2,1)S(1)} collective-permute-done((bf16[128,512]{1,0:T(8,128)(2,1)S(1)}, bf16[128,512]{1,0:T(8,128)(2,1)S(1)}, u32[]{:S(2)}, u32[]{:S(2)}) %collective-permute-start.13) | collective-permute-done | bytes 131104 | tf_op jit(solution)/shard_map/ppermute | solution.py:45
  96.7 2.8 %collective-permute-start.15 = (bf16[128,1024]{1,0:T(8,128)(2,1)S(1)}, bf16[128,1024]{1,0:T(8,128)(2,1)S(1)}, u32[]{:S(2)}, u32[]{:S(2)}) collective-permute-start(bf16[128,1024]{1,0:T(8,128)(2,1)S(1)} %pad_maximum_fusion.3), channel_id=1, source_target_pairs={{0,24},{2,26},{4,28},{6,30},{8,0},{10,2},{12,4},{14,6},{16,8},{18,... | collective-permute-start | bytes 786440 | tf_op jit(solution)/shard_map/ppermute | solution.py:45
  100.7 10.3 %collective-permute-done.15.s2 = bf16[128,1024]{1,0:T(8,128)(2,1)S(1)} collective-permute-done((bf16[128,1024]{1,0:T(8,128)(2,1)S(1)}, bf16[128,1024]{1,0:T(8,128)(2,1)S(1)}, u32[]{:S(2)}, u32[]{:S(2)}) %collective-permute-start.15) | collective-permute-done | bytes 262176 | tf_op jit(solution)/shard_map/ppermute | solution.py:45
  111.0 2.7 %collective-permute-done.14.s1 = bf16[128,1024]{1,0:T(8,128)(2,1)S(1)} collective-permute-done((bf16[128,1024]{1,0:T(8,128)(2,1)S(1)}, bf16[128,1024]{1,0:T(8,128)(2,1)S(1)}, u32[]{:S(2)}, u32[]{:S(2)}) %collective-permute-start.14) | collective-permute-done | bytes 262176 | tf_op jit(solution)/shard_map/ppermute | solution.py:45
  115.5 2.7 %collective-permute-start.17 = (bf16[32,1024]{1,0:T(8,128)(2,1)S(1)}, bf16[32,1024]{1,0:T(8,128)(2,1)S(1)}, u32[]{:S(2)}, u32[]{:S(2)}) collective-permute-start(bf16[32,1024]{1,0:T(8,128)(2,1)S(1)} %get-tuple-element.96), channel_id=1, source_target_pairs={{0,16},{2,18},{4,20},{6,22},{8,24},{10,26},{12,28},{14,30},{16,0},... | collective-permute-start | bytes 196616 | tf_op jit(solution)/shard_map/ppermute | solution.py:45
  118.2 3.6 %collective-permute-start.18 = (bf16[32,1024]{1,0:T(8,128)(2,1)S(1)}, bf16[32,1024]{1,0:T(8,128)(2,1)S(1)}, u32[]{:S(2)}, u32[]{:S(2)}) collective-permute-start(bf16[32,1024]{1,0:T(8,128)(2,1)S(1)} %get-tuple-element.97), channel_id=1, source_target_pairs={{0,24},{2,26},{4,28},{6,30},{8,0},{10,2},{12,4},{14,6},{16,8},{18,... | collective-permute-start | bytes 196616 | tf_op jit(solution)/shard_map/ppermute | solution.py:45
  123.9 11.0 %all_to_all.10.piece_ref = bf16[4,64,1024]{2,1,0:T(8,128)(2,1)S(1)} all-to-all(bf16[4,64,1024]{2,1,0:T(8,128)(2,1)S(1)} %by_columns.1), channel_id=1, replica_groups={{0,2,4,6},{8,10,12,14},{16,18,20,22},{24,26,28,30},{1,3,5,7},{9,11,13,1..., dimensions={0} | all-to-all | bytes 1048576 | tf_op jit(solution)/shard_map/all_to_all | solution.py:547
  136.0 2.2 %collective-permute-start.19 = (bf16[32,4096]{1,0:T(8,128)(2,1)S(1)}, bf16[32,4096]{1,0:T(8,128)(2,1)S(1)}, u32[]{:S(2)}, u32[]{:S(2)}) collective-permute-start(bf16[32,4096]{1,0:T(8,128)(2,1)S(1)} %get-tuple-element.101.refs_0_), channel_id=1, source_target_pairs={{0,32},{32,0},{64,96},{96,64},{128,160},{160,128},{192,224},{224,1... | collective-permute-start | bytes 786440 | tf_op jit(solution)/shard_map/ppermute | solution.py:54
  138.2 4.7 %collective-permute-done.20.refs_2_ = bf16[32,4096]{1,0:T(8,128)(2,1)S(1)} collective-permute-done((bf16[32,4096]{1,0:T(8,128)(2,1)S(1)}, bf16[32,4096]{1,0:T(8,128)(2,1)S(1)}, u32[]{:S(2)}, u32[]{:S(2)}) %collective-permute-start.20) | collective-permute-done | bytes 262176 | tf_op jit(solution)/shard_map/ppermute | solution.py:50
  144.9 1.4 collective-permute-start.22
  147.2 2.1 collective-permute-done.23.refs_5_
  149.2 1.4 collective-permute-start.25
  150.7 1.4 collective-permute-done.21.refs_3_
  152.9 2.0 collective-permute-done.24.refs_6_
  155.7 1.9 run_expert.1
  157.7 1.5 collective-permute-start.27
  159.2 3.8 %collective-permute-start.26 = (bf16[32,4096]{1,0:T(8,128)(2,1)S(1)}, bf16[32,4096]{1,0:T(8,128)(2,1)S(1)}, u32[]{:S(2)}, u32[]{:S(2)}) collective-permute-start(bf16[32,4096]{1,0:T(8,128)(2,1)S(1)} %get-tuple-element.103), channel_id=1, source_target_pairs={{0,64},{32,96},{64,128},{96,160},{128,192},{160,224},{192,0},{224,... | collective-permute-start | bytes 786440 | tf_op jit(solution)/shard_map/ppermute | solution.py:50
  163.2 1.7 collective-permute-done.27
  165.3 4.4 %collective-permute-done.31 = bf16[32,4096]{1,0:T(8,128)(2,1)S(1)} collective-permute-done((bf16[32,4096]{1,0:T(8,128)(2,1)S(1)}, bf16[32,4096]{1,0:T(8,128)(2,1)S(1)}, u32[]{:S(2)}, u32[]{:S(2)}) %collective-permute-start.31) | collective-permute-done | bytes 262176 | tf_op jit(solution)/shard_map/ppermute | solution.py:50
  169.8 1.8 collective-permute-start.32
  171.6 3.7 %collective-permute-done.28 = bf16[32,4096]{1,0:T(8,128)(2,1)S(1)} collective-permute-done((bf16[32,4096]{1,0:T(8,128)(2,1)S(1)}, bf16[32,4096]{1,0:T(8,128)(2,1)S(1)}, u32[]{:S(2)}, u32[]{:S(2)}) %collective-permute-start.28) | collective-permute-done | bytes 262176 | tf_op jit(solution)/shard_map/ppermute | solution.py:50
  176.3 6.8 %collective-permute-done.30 = bf16[32,4096]{1,0:T(8,128)(2,1)S(1)} collective-permute-done((bf16[32,4096]{1,0:T(8,128)(2,1)S(1)}, bf16[32,4096]{1,0:T(8,128)(2,1)S(1)}, u32[]{:S(2)}, u32[]{:S(2)}) %collective-permute-start.30) | collective-permute-done | bytes 262176 | tf_op jit(solution)/shard_map/ppermute | solution.py:50
  183.3 4.9 %collective-permute-start.35 = (bf16[8,4096]{1,0:T(8,128)(2,1)S(1)}, bf16[8,4096]{1,0:T(8,128)(2,1)S(1)}, u32[]{:S(2)}, u32[]{:S(2)}) collective-permute-start(bf16[8,4096]{1,0:T(8,128)(2,1)S(1)} %get-tuple-element.110), channel_id=1, source_target_pairs={{0,8},{2,10},{4,12},{6,14},{8,16},{10,18},{12,20},{14,22},{16,24},... | collective-permute-start | bytes 196616 | tf_op jit(solution)/shard_map/ppermute | solution.py:45
  188.2 2.1 %collective-permute-start.34 = (bf16[8,4096]{1,0:T(8,128)(2,1)S(1)}, bf16[8,4096]{1,0:T(8,128)(2,1)S(1)}, u32[]{:S(2)}, u32[]{:S(2)}) collective-permute-start(bf16[8,4096]{1,0:T(8,128)(2,1)S(1)} %get-tuple-element.111), channel_id=1, source_target_pairs={{0,16},{2,18},{4,20},{6,22},{8,24},{10,26},{12,28},{14,30},{16,0},... | collective-permute-start | bytes 196616 | tf_op jit(solution)/shard_map/ppermute | solution.py:45
  190.3 1.5 collective-permute-start.33
  191.9 4.5 %collective-permute-done.34.refs_2_ = bf16[8,4096]{1,0:T(8,128)(2,1)S(1)} collective-permute-done((bf16[8,4096]{1,0:T(8,128)(2,1)S(1)}, bf16[8,4096]{1,0:T(8,128)(2,1)S(1)}, u32[]{:S(2)}, u32[]{:S(2)}) %collective-permute-start.34) | collective-permute-done | bytes 65568 | tf_op jit(solution)/shard_map/ppermute | solution.py:45
  197.3 3.4 %all-to-all-start.1 = ((bf16[4,8,4096]{2,1,0:T(8,128)(2,1)}), bf16[4,8,4096]{2,1,0:T(8,128)(2,1)S(1)}, u32[]{:S(2)}, u32[]{:S(2)}) async-start(bf16[4,8,4096]{2,1,0:T(8,128)(2,1)} %regroup.1), calls=%async_computation.1 | async-start | bytes 524288 | tf_op jit(solution)/shard_map/all_to_all | solution.py:547
  201.5 5.9 %all-to-all-done.1.refs_0_ = bf16[4,8,4096]{2,1,0:T(8,128)(2,1)S(1)} async-done(((bf16[4,8,4096]{2,1,0:T(8,128)(2,1)}), bf16[4,8,4096]{2,1,0:T(8,128)(2,1)S(1)}, u32[]{:S(2)}, u32[]{:S(2)}) %all-to-all-start.1) | async-done | bytes 262176 | tf_op jit(solution)/shard_map/all_to_all | solution.py:547
  (79 shorter events, 23.4 us)
Async XLA Ops:
  1.6 8.3 %collective-permute-start = (bf16[1024,128]{1,0:T(8,128)(2,1)S(1)}, bf16[1024,128]{1,0:T(8,128)(2,1)S(1)}, u32[]{:S(2)}, u32[]{:S(2)}) collective-permute-start(bf16[1024,128]{1,0:T(8,128)(2,1)S(1)} %pick_head.1), channel_id=1, source_target_pairs={{0,32},{32,0},{64,96},{96,64},{128,160},{160,128},{192,224},{224,1... | collective-permute-start | bytes 786440 | tf_op jit(solution)/shard_map/ppermute | solution.py:54
  3.7 16.0 %copy-start.4 = (bf16[32,4096]{1,0:T(8,128)(2,1)S(1)}, bf16[32,4096]{1,0:T(8,128)(2,1)}, u32[]{:S(2)}) copy-start(bf16[32,4096]{1,0:T(8,128)(2,1)} %hidden_ref.1) | copy-start | bytes 786436
  3.7 16.0 %copy-start.5 = (s32[32,8]{0,1:T(8,128)S(1)}, s32[32,8]{0,1:T(8,128)}, u32[]{:S(2)}) copy-start(s32[32,8]{0,1:T(8,128)} %param.18) | copy-start | bytes 3076
  3.7 16.8 %copy-start.3 = (bf16[512,512]{1,0:T(8,128)(2,1)S(1)}, bf16[512,512]{1,0:T(8,128)(2,1)}, u32[]{:S(2)}) copy-start(bf16[512,512]{1,0:T(8,128)(2,1)} %refs_1_.7) | copy-start | bytes 1572868
  10.0 15.6 %collective-permute-start.2 = (bf16[2048,128]{1,0:T(8,128)(2,1)S(1)}, bf16[2048,128]{1,0:T(8,128)(2,1)S(1)}, u32[]{:S(2)}, u32[]{:S(2)}) collective-permute-start(bf16[2048,128]{1,0:T(8,128)(2,1)S(1)} %pad_maximum_fusion.1.refs_2_), channel_id=1, source_target_pairs={{0,192},{32,224},{64,0},{96,32},{128,64},{160,96},{192,128},{224,1... | collective-permute-start | bytes 1572872 | tf_op jit(solution)/shard_map/ppermute | solution.py:50
  10.8 14.8 %collective-permute-start.1 = (bf16[2048,128]{1,0:T(8,128)(2,1)S(1)}, bf16[2048,128]{1,0:T(8,128)(2,1)}, u32[]{:S(2)}, u32[]{:S(2)}) collective-permute-start(bf16[2048,128]{1,0:T(8,128)(2,1)S(1)} %pad_maximum_fusion.1.refs_2_), channel_id=1, source_target_pairs={{0,64},{32,96},{64,128},{96,160},{128,192},{160,224},{192,0},{224,... | collective-permute-start | bytes 1572872 | tf_op jit(solution)/shard_map/ppermute | solution.py:50
  13.3 24.9 %collective-permute-start.5 = (bf16[256,1024]{1,0:T(8,128)(2,1)}, bf16[256,1024]{1,0:T(8,128)(2,1)S(1)}, u32[]{:S(2)}, u32[]{:S(2)}) collective-permute-start(bf16[256,1024]{1,0:T(8,128)(2,1)} %get-tuple-element.57), channel_id=1, source_target_pairs={{0,2},{2,4},{4,6},{6,0},{8,10},{10,12},{12,14},{14,8},{16,18},{18,... | collective-permute-start | bytes 1572872 | tf_op jit(solution)/shard_map/ppermute | solution.py:40
  14.8 24.6 %collective-permute-start.6 = (bf16[256,1024]{1,0:T(8,128)(2,1)}, bf16[256,1024]{1,0:T(8,128)(2,1)S(1)}, u32[]{:S(2)}, u32[]{:S(2)}) collective-permute-start(bf16[256,1024]{1,0:T(8,128)(2,1)} %get-tuple-element.58), channel_id=1, source_target_pairs={{0,4},{2,6},{4,0},{6,2},{8,12},{10,14},{12,8},{14,10},{16,20},{18,... | collective-permute-start | bytes 1572872 | tf_op jit(solution)/shard_map/ppermute | solution.py:40
  17.5 21.9 %collective-permute-start.7 = (bf16[256,1024]{1,0:T(8,128)(2,1)}, bf16[256,1024]{1,0:T(8,128)(2,1)S(1)}, u32[]{:S(2)}, u32[]{:S(2)}) collective-permute-start(bf16[256,1024]{1,0:T(8,128)(2,1)} %get-tuple-element.59), channel_id=1, source_target_pairs={{0,6},{2,0},{4,2},{6,4},{8,14},{10,8},{12,10},{14,12},{16,22},{18,... | collective-permute-start | bytes 1572872 | tf_op jit(solution)/shard_map/ppermute | solution.py:40
  26.6 12.8 %collective-permute-start.3 = (bf16[1024,128]{1,0:T(8,128)(2,1)S(1)}, bf16[1024,128]{1,0:T(8,128)(2,1)S(1)}, u32[]{:S(2)}, u32[]{:S(2)}) collective-permute-start(bf16[1024,128]{1,0:T(8,128)(2,1)S(1)} %slice.30), channel_id=1, source_target_pairs={{0,64},{32,96},{64,128},{96,160},{128,192},{160,224},{192,0},{224,... | collective-permute-start | bytes 786440 | tf_op jit(solution)/shard_map/ppermute | solution.py:50
  28.4 11.0 %collective-permute-start.4 = (bf16[1024,128]{1,0:T(8,128)(2,1)S(1)}, bf16[1024,128]{1,0:T(8,128)(2,1)S(1)}, u32[]{:S(2)}, u32[]{:S(2)}) collective-permute-start(bf16[1024,128]{1,0:T(8,128)(2,1)S(1)} %slice.31), channel_id=1, source_target_pairs={{0,192},{32,224},{64,0},{96,32},{128,64},{160,96},{192,128},{224,1... | collective-permute-start | bytes 786440 | tf_op jit(solution)/shard_map/ppermute | solution.py:50
  45.1 15.5 %collective-permute-start.10 = (bf16[592,512]{1,0:T(8,128)(2,1)S(1)}, bf16[592,512]{1,0:T(8,128)(2,1)S(1)}, u32[]{:S(2)}, u32[]{:S(2)}) collective-permute-start(bf16[592,512]{1,0:T(8,128)(2,1)S(1)} %get-tuple-element.74), channel_id=1, source_target_pairs={{0,6},{2,0},{4,2},{6,4},{8,14},{10,8},{12,10},{14,12},{16,22},{18,... | collective-permute-start | bytes 1818632 | tf_op jit(solution)/shard_map/ppermute | solution.py:40
  47.4 16.5 %collective-permute-start.8 = (bf16[592,512]{1,0:T(8,128)(2,1)S(1)}, bf16[592,512]{1,0:T(8,128)(2,1)S(1)}, u32[]{:S(2)}, u32[]{:S(2)}) collective-permute-start(bf16[592,512]{1,0:T(8,128)(2,1)S(1)} %get-tuple-element.72.own_ref), channel_id=1, source_target_pairs={{0,2},{2,4},{4,6},{6,0},{8,10},{10,12},{12,14},{14,8},{16,18},{18,... | collective-permute-start | bytes 1818632 | tf_op jit(solution)/shard_map/ppermute | solution.py:40
  64.1 3.7 %collective-permute-start.11 = (bf16[768,1024]{1,0:T(8,128)(2,1)S(1)}, bf16[768,1024]{1,0:T(8,128)(2,1)S(1)}, u32[]{:S(2)}, u32[]{:S(2)}) collective-permute-start(bf16[768,1024]{1,0:T(8,128)(2,1)S(1)} %pad_maximum_fusion), channel_id=1, source_target_pairs={{0,1},{1,0},{2,3},{3,2},{4,5},{5,4},{6,7},{7,6},{8,9},{9,8},{10,11... | collective-permute-start | bytes 4718600 | tf_op jit(solution)/shard_map/ppermute | solution.py:58
  64.3 17.6 %collective-permute-start.9 = (bf16[592,512]{1,0:T(8,128)(2,1)S(1)}, bf16[592,512]{1,0:T(8,128)(2,1)S(1)}, u32[]{:S(2)}, u32[]{:S(2)}) collective-permute-start(bf16[592,512]{1,0:T(8,128)(2,1)S(1)} %get-tuple-element.73), channel_id=1, source_target_pairs={{0,4},{2,6},{4,0},{6,2},{8,12},{10,14},{12,8},{14,10},{16,20},{18,... | collective-permute-start | bytes 1818632 | tf_op jit(solution)/shard_map/ppermute | solution.py:40
  83.3 9.9 %collective-permute-start.12 = (bf16[128,512]{1,0:T(8,128)(2,1)S(1)}, bf16[128,512]{1,0:T(8,128)(2,1)S(1)}, u32[]{:S(2)}, u32[]{:S(2)}) collective-permute-start(bf16[128,512]{1,0:T(8,128)(2,1)S(1)} %get-tuple-element.89), channel_id=1, source_target_pairs={{0,8},{2,10},{4,12},{6,14},{8,16},{10,18},{12,20},{14,22},{16,24},... | collective-permute-start | bytes 393224 | tf_op jit(solution)/shard_map/ppermute | solution.py:45
  86.7 9.9 %collective-permute-start.13 = (bf16[128,512]{1,0:T(8,128)(2,1)S(1)}, bf16[128,512]{1,0:T(8,128)(2,1)S(1)}, u32[]{:S(2)}, u32[]{:S(2)}) collective-permute-start(bf16[128,512]{1,0:T(8,128)(2,1)S(1)} %get-tuple-element.90), channel_id=1, source_target_pairs={{0,24},{2,26},{4,28},{6,30},{8,0},{10,2},{12,4},{14,6},{16,8},{18,... | collective-permute-start | bytes 393224 | tf_op jit(solution)/shard_map/ppermute | solution.py:45
  96.7 14.3 %collective-permute-start.15 = (bf16[128,1024]{1,0:T(8,128)(2,1)S(1)}, bf16[128,1024]{1,0:T(8,128)(2,1)S(1)}, u32[]{:S(2)}, u32[]{:S(2)}) collective-permute-start(bf16[128,1024]{1,0:T(8,128)(2,1)S(1)} %pad_maximum_fusion.3), channel_id=1, source_target_pairs={{0,24},{2,26},{4,28},{6,30},{8,0},{10,2},{12,4},{14,6},{16,8},{18,... | collective-permute-start | bytes 786440 | tf_op jit(solution)/shard_map/ppermute | solution.py:45
  99.5 14.2 %collective-permute-start.14 = (bf16[128,1024]{1,0:T(8,128)(2,1)S(1)}, bf16[128,1024]{1,0:T(8,128)(2,1)S(1)}, u32[]{:S(2)}, u32[]{:S(2)}) collective-permute-start(bf16[128,1024]{1,0:T(8,128)(2,1)S(1)} %pad_maximum_fusion.2), channel_id=1, source_target_pairs={{0,8},{2,10},{4,12},{6,14},{8,16},{10,18},{12,20},{14,22},{16,24},... | collective-permute-start | bytes 786440 | tf_op jit(solution)/shard_map/ppermute | solution.py:45
  113.7 42.0 %copy-start.1 = (bf16[1,4096,192]{1,2,0:T(8,128)(2,1)S(1)}, bf16[1,4096,192]{1,2,0:T(8,128)(2,1)}, u32[]{:S(2)}) copy-start(bf16[1,4096,192]{1,2,0:T(8,128)(2,1)} %param.22) | copy-start | bytes 4718596
  113.7 42.0 %copy-start.2 = (bf16[1,192,4096]{2,1,0:T(8,128)(2,1)S(1)}, bf16[1,192,4096]{2,1,0:T(8,128)(2,1)}, u32[]{:S(2)}) copy-start(bf16[1,192,4096]{2,1,0:T(8,128)(2,1)} %param.23) | copy-start | bytes 4718596
  114.6 20.3 %copy-start.6 = (f32[4096]{0:T(1024)S(1)}, f32[4096]{0:T(1024)}, u32[]{:S(2)}) copy-start(f32[4096]{0:T(1024)} %param.17) | copy-start | bytes 49156
  114.6 41.1 %copy-start = (bf16[1,4096,192]{1,2,0:T(8,128)(2,1)S(1)}, bf16[1,4096,192]{1,2,0:T(8,128)(2,1)}, u32[]{:S(2)}) copy-start(bf16[1,4096,192]{1,2,0:T(8,128)(2,1)} %param.21) | copy-start | bytes 4718596
  114.6 8.3 %collective-permute-start.16 = (bf16[32,1024]{1,0:T(8,128)(2,1)S(1)}, bf16[32,1024]{1,0:T(8,128)(2,1)S(1)}, u32[]{:S(2)}, u32[]{:S(2)}) collective-permute-start(bf16[32,1024]{1,0:T(8,128)(2,1)S(1)} %get-tuple-element.95), channel_id=1, source_target_pairs={{0,8},{2,10},{4,12},{6,14},{8,16},{10,18},{12,20},{14,22},{16,24},... | collective-permute-start | bytes 196616 | tf_op jit(solution)/shard_map/ppermute | solution.py:45
  115.5 8.3 %collective-permute-start.17 = (bf16[32,1024]{1,0:T(8,128)(2,1)S(1)}, bf16[32,1024]{1,0:T(8,128)(2,1)S(1)}, u32[]{:S(2)}, u32[]{:S(2)}) collective-permute-start(bf16[32,1024]{1,0:T(8,128)(2,1)S(1)} %get-tuple-element.96), channel_id=1, source_target_pairs={{0,16},{2,18},{4,20},{6,22},{8,24},{10,26},{12,28},{14,30},{16,0},... | collective-permute-start | bytes 196616 | tf_op jit(solution)/shard_map/ppermute | solution.py:45
  118.2 5.7 %collective-permute-start.18 = (bf16[32,1024]{1,0:T(8,128)(2,1)S(1)}, bf16[32,1024]{1,0:T(8,128)(2,1)S(1)}, u32[]{:S(2)}, u32[]{:S(2)}) collective-permute-start(bf16[32,1024]{1,0:T(8,128)(2,1)S(1)} %get-tuple-element.97), channel_id=1, source_target_pairs={{0,24},{2,26},{4,28},{6,30},{8,0},{10,2},{12,4},{14,6},{16,8},{18,... | collective-permute-start | bytes 196616 | tf_op jit(solution)/shard_map/ppermute | solution.py:45
  135.7 7.1 %collective-permute-start.20 = (bf16[32,4096]{1,0:T(8,128)(2,1)S(1)}, bf16[32,4096]{1,0:T(8,128)(2,1)S(1)}, u32[]{:S(2)}, u32[]{:S(2)}) collective-permute-start(bf16[32,4096]{1,0:T(8,128)(2,1)S(1)} %get-tuple-element.101.refs_0_), channel_id=1, source_target_pairs={{0,64},{32,96},{64,128},{96,160},{128,192},{160,224},{192,0},{224,... | collective-permute-start | bytes 786440 | tf_op jit(solution)/shard_map/ppermute | solution.py:50
  136.0 10.3 %collective-permute-start.19 = (bf16[32,4096]{1,0:T(8,128)(2,1)S(1)}, bf16[32,4096]{1,0:T(8,128)(2,1)S(1)}, u32[]{:S(2)}, u32[]{:S(2)}) collective-permute-start(bf16[32,4096]{1,0:T(8,128)(2,1)S(1)} %get-tuple-element.101.refs_0_), channel_id=1, source_target_pairs={{0,32},{32,0},{64,96},{96,64},{128,160},{160,128},{192,224},{224,1... | collective-permute-start | bytes 786440 | tf_op jit(solution)/shard_map/ppermute | solution.py:54
  142.9 6.4 %collective-permute-start.23 = (bf16[32,4096]{1,0:T(8,128)(2,1)S(1)}, bf16[32,4096]{1,0:T(8,128)(2,1)S(1)}, u32[]{:S(2)}, u32[]{:S(2)}) collective-permute-start(bf16[32,4096]{1,0:T(8,128)(2,1)S(1)} %collective-permute-done.20.refs_2_), channel_id=1, source_target_pairs={{0,64},{32,96},{64,128},{96,160},{128,192},{160,224},{192,0},{224,... | collective-permute-start | bytes 786440 | tf_op jit(solution)/shard_map/ppermute | solution.py:50
  143.6 8.5 %collective-permute-start.21 = (bf16[32,4096]{1,0:T(8,128)(2,1)S(1)}, bf16[32,4096]{1,0:T(8,128)(2,1)S(1)}, u32[]{:S(2)}, u32[]{:S(2)}) collective-permute-start(bf16[32,4096]{1,0:T(8,128)(2,1)S(1)} %get-tuple-element.101.refs_0_), channel_id=1, source_target_pairs={{0,192},{32,224},{64,0},{96,32},{128,64},{160,96},{192,128},{224,1... | collective-permute-start | bytes 786440 | tf_op jit(solution)/shard_map/ppermute | solution.py:50
  144.9 8.0 %collective-permute-start.22 = (bf16[32,4096]{1,0:T(8,128)(2,1)S(1)}, bf16[32,4096]{1,0:T(8,128)(2,1)S(1)}, u32[]{:S(2)}, u32[]{:S(2)}) collective-permute-start(bf16[32,4096]{1,0:T(8,128)(2,1)S(1)} %collective-permute-done.20.refs_2_), channel_id=1, source_target_pairs={{0,32},{32,0},{64,96},{96,64},{128,160},{160,128},{192,224},{224,1... | collective-permute-start | bytes 786440 | tf_op jit(solution)/shard_map/ppermute | solution.py:54
  146.3 8.6 %collective-permute-start.24 = (bf16[32,4096]{1,0:T(8,128)(2,1)S(1)}, bf16[32,4096]{1,0:T(8,128)(2,1)S(1)}, u32[]{:S(2)}, u32[]{:S(2)}) collective-permute-start(bf16[32,4096]{1,0:T(8,128)(2,1)S(1)} %collective-permute-done.19.refs_1_), channel_id=1, source_target_pairs={{0,192},{32,224},{64,0},{96,32},{128,64},{160,96},{192,128},{224,1... | collective-permute-start | bytes 786440 | tf_op jit(solution)/shard_map/ppermute | solution.py:50
  149.2 6.5 %collective-permute-start.25 = (bf16[32,4096]{1,0:T(8,128)(2,1)S(1)}, bf16[32,4096]{1,0:T(8,128)(2,1)S(1)}, u32[]{:S(2)}, u32[]{:S(2)}) collective-permute-start(bf16[32,4096]{1,0:T(8,128)(2,1)S(1)} %collective-permute-done.23.refs_5_), channel_id=1, source_target_pairs={{0,32},{32,0},{64,96},{96,64},{128,160},{160,128},{192,224},{224,1... | collective-permute-start | bytes 786440 | tf_op jit(solution)/shard_map/ppermute | solution.py:54
  157.7 7.3 %collective-permute-start.27 = (bf16[32,4096]{1,0:T(8,128)(2,1)S(1)}, bf16[32,4096]{1,0:T(8,128)(2,1)S(1)}, u32[]{:S(2)}, u32[]{:S(2)}) collective-permute-start(bf16[32,4096]{1,0:T(8,128)(2,1)S(1)} %get-tuple-element.106), channel_id=1, source_target_pairs={{0,32},{32,0},{64,96},{96,64},{128,160},{160,128},{192,224},{224,1... | collective-permute-start | bytes 786440 | tf_op jit(solution)/shard_map/ppermute | solution.py:54
  159.2 16.3 %collective-permute-start.26 = (bf16[32,4096]{1,0:T(8,128)(2,1)S(1)}, bf16[32,4096]{1,0:T(8,128)(2,1)S(1)}, u32[]{:S(2)}, u32[]{:S(2)}) collective-permute-start(bf16[32,4096]{1,0:T(8,128)(2,1)S(1)} %get-tuple-element.103), channel_id=1, source_target_pairs={{0,64},{32,96},{64,128},{96,160},{128,192},{160,224},{192,0},{224,... | collective-permute-start | bytes 786440 | tf_op jit(solution)/shard_map/ppermute | solution.py:50
  163.0 8.6 %collective-permute-start.29 = (bf16[32,4096]{1,0:T(8,128)(2,1)S(1)}, bf16[32,4096]{1,0:T(8,128)(2,1)S(1)}, u32[]{:S(2)}, u32[]{:S(2)}) collective-permute-start(bf16[32,4096]{1,0:T(8,128)(2,1)S(1)} %get-tuple-element.107), channel_id=1, source_target_pairs={{0,32},{32,0},{64,96},{96,64},{128,160},{160,128},{192,224},{224,1... | collective-permute-start | bytes 786440 | tf_op jit(solution)/shard_map/ppermute | solution.py:54
  163.1 6.6 %collective-permute-start.31 = (bf16[32,4096]{1,0:T(8,128)(2,1)S(1)}, bf16[32,4096]{1,0:T(8,128)(2,1)S(1)}, u32[]{:S(2)}, u32[]{:S(2)}) collective-permute-start(bf16[32,4096]{1,0:T(8,128)(2,1)S(1)} %get-tuple-element.109), channel_id=1, source_target_pairs={{0,64},{32,96},{64,128},{96,160},{128,192},{160,224},{192,0},{224,... | collective-permute-start | bytes 786440 | tf_op jit(solution)/shard_map/ppermute | solution.py:50
  165.0 10.3 %collective-permute-start.28 = (bf16[32,4096]{1,0:T(8,128)(2,1)S(1)}, bf16[32,4096]{1,0:T(8,128)(2,1)S(1)}, u32[]{:S(2)}, u32[]{:S(2)}) collective-permute-start(bf16[32,4096]{1,0:T(8,128)(2,1)S(1)} %add_convert_fusion.3), channel_id=1, source_target_pairs={{0,192},{32,224},{64,0},{96,32},{128,64},{160,96},{192,128},{224,1... | collective-permute-start | bytes 786440 | tf_op jit(solution)/shard_map/ppermute | solution.py:50
  169.8 6.5 %collective-permute-start.32 = (bf16[32,4096]{1,0:T(8,128)(2,1)S(1)}, bf16[32,4096]{1,0:T(8,128)(2,1)S(1)}, u32[]{:S(2)}, u32[]{:S(2)}) collective-permute-start(bf16[32,4096]{1,0:T(8,128)(2,1)S(1)} %add_convert_fusion.1), channel_id=1, source_target_pairs={{0,32},{32,0},{64,96},{96,64},{128,160},{160,128},{192,224},{224,1... | collective-permute-start | bytes 786440 | tf_op jit(solution)/shard_map/ppermute | solution.py:54
  175.4 25.3 %copy-start.7 = (s32[32,8]{0,1:T(8,128)S(1)}, s32[32,8]{0,1:T(8,128)}, u32[]{:S(2)}) copy-start(s32[32,8]{0,1:T(8,128)} %param.19) | copy-start | bytes 3076
  175.4 7.7 %collective-permute-start.30 = (bf16[32,4096]{1,0:T(8,128)(2,1)S(1)}, bf16[32,4096]{1,0:T(8,128)(2,1)S(1)}, u32[]{:S(2)}, u32[]{:S(2)}) collective-permute-start(bf16[32,4096]{1,0:T(8,128)(2,1)S(1)} %add_convert_fusion.2), channel_id=1, source_target_pairs={{0,192},{32,224},{64,0},{96,32},{128,64},{160,96},{192,128},{224,1... | collective-permute-start | bytes 786440 | tf_op jit(solution)/shard_map/ppermute | solution.py:50
  183.3 8.6 %collective-permute-start.35 = (bf16[8,4096]{1,0:T(8,128)(2,1)S(1)}, bf16[8,4096]{1,0:T(8,128)(2,1)S(1)}, u32[]{:S(2)}, u32[]{:S(2)}) collective-permute-start(bf16[8,4096]{1,0:T(8,128)(2,1)S(1)} %get-tuple-element.110), channel_id=1, source_target_pairs={{0,8},{2,10},{4,12},{6,14},{8,16},{10,18},{12,20},{14,22},{16,24},... | collective-permute-start | bytes 196616 | tf_op jit(solution)/shard_map/ppermute | solution.py:45
  188.2 8.2 %collective-permute-start.34 = (bf16[8,4096]{1,0:T(8,128)(2,1)S(1)}, bf16[8,4096]{1,0:T(8,128)(2,1)S(1)}, u32[]{:S(2)}, u32[]{:S(2)}) collective-permute-start(bf16[8,4096]{1,0:T(8,128)(2,1)S(1)} %get-tuple-element.111), channel_id=1, source_target_pairs={{0,16},{2,18},{4,20},{6,22},{8,24},{10,26},{12,28},{14,30},{16,0},... | collective-permute-start | bytes 196616 | tf_op jit(solution)/shard_map/ppermute | solution.py:45
  190.3 6.1 %collective-permute-start.33 = (bf16[8,4096]{1,0:T(8,128)(2,1)S(1)}, bf16[8,4096]{1,0:T(8,128)(2,1)S(1)}, u32[]{:S(2)}, u32[]{:S(2)}) collective-permute-start(bf16[8,4096]{1,0:T(8,128)(2,1)S(1)} %get-tuple-element.112), channel_id=1, source_target_pairs={{0,24},{2,26},{4,28},{6,30},{8,0},{10,2},{12,4},{14,6},{16,8},{18,... | collective-permute-start | bytes 196616 | tf_op jit(solution)/shard_map/ppermute | solution.py:45
  197.3 10.1 %all-to-all-start.1 = ((bf16[4,8,4096]{2,1,0:T(8,128)(2,1)}), bf16[4,8,4096]{2,1,0:T(8,128)(2,1)S(1)}, u32[]{:S(2)}, u32[]{:S(2)}) async-start(bf16[4,8,4096]{2,1,0:T(8,128)(2,1)} %regroup.1), calls=%async_computation.1 | async-start | bytes 524288 | tf_op jit(solution)/shard_map/all_to_all | solution.py:547

commit v2 on v1

--- a/solution.py
+++ b/solution.py
@@ -104,7 +104,7 @@
     )(place, out_proj, out_proj, out_proj)
 
 
-def attend(queries, blocks, bias, state, riders=None):
+def attend(queries, blocks, spot, steps, state, riders=None):
     rows, heads = queries.shape[0], queries.shape[1] // HEAD_DIM
     calls = len(blocks)
     n = sum(b.shape[0] for b in blocks) // (2 * rows)
@@ -113,13 +113,18 @@
     tile = 128
 
     def kernel(*refs):
-        bias_ref, q_ref = refs[0], refs[1]
+        spot_ref, q_ref = refs[0], refs[1]
+        bias = []
+        for dy, flip in steps:
+            side = 1 - spot_ref[1] if flip else spot_ref[1]
+            owner = lax.rem(spot_ref[0] + N_Y + dy, N_Y) * 2 + side
+            bias.append(jnp.where(owner <= spot_ref[2], 0.0, LOWEST).astype(F32))
         kv_refs = [
             r.at[first_row : first_row + 2 * rows]
             for r in refs[2 : 2 + calls]
             for first_row in range(0, r.shape[0], 2 * rows)
         ]
-        rest = refs[2 + calls :]
+        rest, (key_ref, value_ref) = refs[2 + calls : -2], refs[-2:]
         if not first:
             acc_in, top_in = rest[0], rest[1]
             rest = rest[2:]
@@ -127,85 +132,87 @@
             rider_refs, rest = rest[:3], rest[3:]
             for rider, target in zip(rider_refs, rest):
                 target[rows:, :] = rider[...]
-        key = jnp.concatenate([r[0:rows, :] for r in kv_refs], axis=0)
-        ones = jnp.ones((rows, HEAD_DIM), BF16)
-        value = jnp.concatenate(
-            [jnp.concatenate([r[rows:, :], ones], axis=1) for r in kv_refs], axis=0
-        )
-        for part in range(rows // tile):
-            at = pl.ds(part * tile, tile)
-            seen = n * rows
-            scores = lax.dot_general(
-                q_ref[at, :], key[:seen], (((1,), (1,)), ((), ())), preferred_element_type=F32
-            )
-            if first:
-                i = lax.broadcasted_iota(jnp.int32, (tile, rows), 0) + part * tile
-                j = lax.broadcasted_iota(jnp.int32, (tile, rows), 1)
-                diagonal = jnp.where(j <= i, scores[:, :rows], LOWEST)
-                scores = jnp.concatenate([diagonal, scores[:, rows:]], axis=1)
-                newest = jnp.full((tile, HEAD_DIM), LOWEST, F32)
-            else:
-                before = top_in[0, at, :]
-                newest = before
-            for b in range(n):
-                highest = jnp.max(scores[:, b * rows : (b + 1) * rows], axis=1, keepdims=True)
-                newest = jnp.maximum(newest, highest + bias_ref[b])
-            offsets = [(newest - bias_ref[b]) * EXP2_SCALE for b in range(n)]
-            pieces = []
-            for lane in range(0, seen, HEAD_DIM):
-                pieces.append(
-                    jnp.exp2(
-                        scores[:, lane : lane + HEAD_DIM] * EXP2_SCALE - offsets[lane // rows]
-                    ).astype(BF16)
+        for b, r in enumerate(kv_refs):
+            at = slice(b * rows, (b + 1) * rows)
+            key_ref[at, :] = r[0:rows, :]
+            value_ref[at, 0:HEAD_DIM] = r[rows:, :]
+        value_ref[:, HEAD_DIM:] = jnp.ones((n * rows, HEAD_DIM), BF16)
+
+        def head(h, carry):
+            lanes = pl.ds(pl.multiple_of(h * HEAD_DIM, HEAD_DIM), HEAD_DIM)
+
+            def score(part):
+                return lax.dot_general(
+                    q_ref[pl.ds(part * tile, tile), lanes],
+                    key_ref[...],
+                    (((1,), (1,)), ((), ())),
+                    preferred_element_type=F32,
                 )
-            total = jnp.dot(
-                jnp.concatenate(pieces, axis=1), value[:seen], preferred_element_type=F32
-            )
-            if not first:
-                factor = jnp.exp2((before - newest) * EXP2_SCALE)
-                total = acc_in[0, at, :] * jnp.concatenate([factor, factor], axis=1) + total
-            if last:
-                done = (total[:, :HEAD_DIM] / total[:, HEAD_DIM:]).astype(BF16)
-                for target in rest:
-                    target[at, :] = done
-            else:
-                rest[0][0, at, :] = total
-                rest[1][0, at, :] = newest
-
-    q_spec = pl.BlockSpec((rows, HEAD_DIM), lambda h, f: (0, h))
-    kv_specs = [pl.BlockSpec(b.shape, lambda h, f: (0, 0)) for b in blocks]
-    rider_spec = pl.BlockSpec((RIDER, HEAD_DIM), lambda h, f: (0, h))
-    message_spec = pl.BlockSpec((rows + RIDER, HEAD_DIM), lambda h, f: (0, h))
-    state_specs = [
-        pl.BlockSpec((1, rows, 2 * HEAD_DIM), lambda h, f: (h, 0, 0)),
-        pl.BlockSpec((1, rows, HEAD_DIM), lambda h, f: (h, 0, 0)),
-    ]
+
+            upcoming = score(0)
+            for part in range(rows // tile):
+                at = pl.ds(part * tile, tile)
+                scores = upcoming
+                if (part + 1) * tile < rows:
+                    upcoming = score(part + 1)
+                if first:
+                    i = lax.broadcasted_iota(jnp.int32, (tile, rows), 0) + part * tile
+                    j = lax.broadcasted_iota(jnp.int32, (tile, rows), 1)
+                    diagonal = jnp.where(j <= i, scores[:, :rows], LOWEST)
+                    scores = jnp.concatenate([diagonal, scores[:, rows:]], axis=1)
+                    newest = jnp.full((tile, HEAD_DIM), LOWEST, F32)
+                else:
+                    before = top_in[h, at, :]
+                    newest = before
+                for b in range(n):
+                    highest = jnp.max(scores[:, b * rows : (b + 1) * rows], axis=1, keepdims=True)
+                    newest = jnp.maximum(newest, highest + bias[b])
+                offsets = [(newest - bias[b]) * EXP2_SCALE for b in range(n)]
+                pieces = []
+                for lane in range(0, n * rows, HEAD_DIM):
+                    pieces.append(
+                        jnp.exp2(
+                            scores[:, lane : lane + HEAD_DIM] * EXP2_SCALE - offsets[lane // rows]
+                        ).astype(BF16)
+                    )
+                total = jnp.dot(
+                    jnp.concatenate(pieces, axis=1), value_ref[...], preferred_element_type=F32
+                )
+                if not first:
+                    factor = jnp.exp2((before - newest) * EXP2_SCALE)
+                    total = acc_in[h, at, :] * jnp.concatenate([factor, factor], axis=1) + total
+                if last:
+                    done = (total[:, :HEAD_DIM] / total[:, HEAD_DIM:]).astype(BF16)
+                    for target in rest:
+                        target[at, lanes] = done
+                else:
+                    rest[0][h, at, :] = total
+                    rest[1][h, at, :] = newest
+            return carry
+
+        lax.fori_loop(0, heads, head, 0)
+
     state_shapes = [
         jax.ShapeDtypeStruct((heads, rows, 2 * HEAD_DIM), F32),
         jax.ShapeDtypeStruct((heads, rows, HEAD_DIM), F32),
     ]
     return pl.pallas_call(
         kernel,
-        grid_spec=pltpu.PrefetchScalarGridSpec(
-            num_scalar_prefetch=1,
-            grid=(heads,),
-            in_specs=[q_spec]
-            + kv_specs
-            + ([] if first else state_specs)
-            + ([rider_spec] * 3 if last else []),
-            out_specs=[message_spec] * 3 if last else state_specs,
-        ),
+        in_specs=[pl.BlockSpec(memory_space=SMEM)]
+        + [whole()] * (1 + calls + (0 if first else 2) + (3 if last else 0)),
+        out_specs=[whole()] * (3 if last else 2),
         out_shape=[jax.ShapeDtypeStruct((rows + RIDER, queries.shape[1]), BF16)] * 3
         if last
         else state_shapes,
-        compiler_params=params(20),
+        scratch_shapes=[VMEM((n * rows, HEAD_DIM), BF16), VMEM((n * rows, 2 * HEAD_DIM), BF16)],
+        compiler_params=params(16),
         cost_estimate=pl.CostEstimate(
             flops=heads * n * rows * rows * HEAD_DIM * 4,
             transcendentals=heads * n * rows * rows,
             bytes_accessed=4 << 20,
         ),
         name="attend",
-    )(bias, queries, *blocks, *(() if first else state), *(riders if last else ()))
+    )(spot, queries, *blocks, *(() if first else state), *(riders if last else ()))
 
 
 def rows_of(place_ref, left_ref, dz, columns):
@@ -246,6 +253,7 @@
         ),
         out_shape=[jax.ShapeDtypeStruct((N_X * TOKENS, cols), F32)] * N_Z,
         compiler_params=params(28),
+        cost_estimate=pl.CostEstimate(flops=1, transcendentals=0, bytes_accessed=1),
         name="project_near",
     )(place, own, out_proj, *lefts, *fetched, other)
 
@@ -531,6 +539,25 @@
         compiler_params=params(),
         name="combine",
     )(weight, groups)
+
+
+def stack(arrays):
+    rows = sum(a.shape[0] for a in arrays)
+
+    def kernel(*refs):
+        at = 0
+        for r in refs[:-1]:
+            refs[-1][at : at + r.shape[0], :] = r[...]
+            at += r.shape[0]
+
+    return pl.pallas_call(
+        kernel,
+        in_specs=[whole()] * len(arrays),
+        out_specs=whole(),
+        out_shape=jax.ShapeDtypeStruct((rows, arrays[0].shape[1]), BF16),
+        compiler_params=params(4),
+        name="stack",
+    )(*arrays)
 
 
 def tie(values, *others):
@@ -583,9 +610,7 @@
     local_heads = queries.shape[1] // HEAD_DIM
     kv_index = exp_index * local_heads // (HEADS // KV_HEADS)
 
-    def bias(*steps):
-        owners = jnp.stack([((y + dy) % N_Y) * 2 + (side ^ flip) for dy, flip in steps])
-        return jnp.where(owners < ctx_index, 0.0, LOWEST).astype(F32)
+    spot = jnp.stack([y, side, ctx_index]).astype(jnp.int32)
 
     keys, values, out_proj = [
         pltpu.with_memory_space_constraint(a, pltpu.HBM) for a in (keys, values, out_proj)
@@ -595,26 +620,21 @@
     away = pick_weights(jnp.stack([rep_index, x]).astype(jnp.int32), out_proj)
     fetched = [shift_x(away[d - 1], d) for d in range(1, N_X)]
     (swapped,) = tie((swapped,), *away)
-    pair = jnp.concatenate([own, swapped], axis=0)
+    pair = stack([own, swapped])
     below = shift_y(pair, 1)
     above = shift_y(pair, -1)
-    state = attend(
-        queries,
-        [pair],
-        jnp.concatenate([jnp.zeros((1,), F32), bias((0, 1))]),
-        None,
-    )
+    state = attend(queries, [pair], spot, [(0, 0), (0, 1)], None)
     riders = pick_hidden(place, live_counts, hidden_in, expert_ids.T)
     below, above = tie((below, above), *state, *riders)
     block = own.shape[0]
     far_a = shift_y(below[:block], 1)
     far_b = shift_y(above[block:], -1)
     state = attend(
-        queries, [below, above], bias((-1, 0), (-1, 1), (1, 0), (1, 1)), state
-    )
-    far_a, far_b = tie((far_a, far_b), *state, *fetched)
+        queries, [below, above], spot, [(-1, 0), (-1, 1), (1, 0), (1, 1)], state
+    )
+    far_a, far_b, *fetched = tie((far_a, far_b, *fetched), *state)
     messages = attend(
-        queries, [far_a, far_b], bias((-2, 0), (-2, 1)), state, riders[1:]
+        queries, [far_a, far_b], spot, [(-2, 0), (-2, 1)], state, riders[1:]
     )
 
     from_left = shift_x(messages[0], 1)
@@ -623,8 +643,7 @@
     weight = route_weights(
         tie((place,), from_left)[0], live=live_counts, ids=expert_ids.T, gates=gate_fixed.T
     )
-    fetched = tie(fetched, from_left, from_right)
-    other = swap_core(jnp.concatenate(fetched, axis=0))
+    other = swap_core(stack(fetched))
     near = project_near(
         place, messages[0], out_proj, [from_left, from_right], [fetched[0], fetched[2]], other
     )

time: 210 us -> 209 us (level)
  Pallas kernels: 37.4 us -> 35 us
    ppermute x7, waiting for transfers between devices: 7.19 us -> 15.1 us  [swap_l(): return lax.ppermute(a, 'ctx', [(i, i ^ 1) for i in range(2 * N_Y)])]
    ppermute x10, waiting for transfers between devices: 26.1 us -> 20.6 us  [shift_z(): return lax.ppermute(a, 'exp', pairs)]
    ppermute x10, starting transfers between devices: 25.8 us -> 30.6 us  [shift_z(): return lax.ppermute(a, 'exp', pairs)]
    ppermute x7, starting transfers between devices: 10.5 us -> 6.31 us  [swap_l(): return lax.ppermute(a, 'ctx', [(i, i ^ 1) for i in range(2 * N_Y)])]
    ppermute x1, waiting for transfers between devices: 3.3 us -> 0.01 us  [swap_core(): return lax.ppermute(a, 'rep', [(0, 1), (1, 0)])]
    pallas_call x3 -> x5, Pallas kernels: 20.2 us -> 17.8 us  [the longest x3 17.7 us: attend(): pl.pallas_call(kernel, in_specs=[pl.BlockSpec(memory_space=SMEM)] + [whol...]
    ppermute x6, starting transfers between devices: 8.09 us -> 10.4 us  [shift_x(): return lax.ppermute(a, 'exp', pairs)]
    ppermute x6, waiting for transfers between devices: 28.2 us -> 30.3 us  [shift_x(): return lax.ppermute(a, 'exp', pairs)]
  transfers between devices with their start and end apart: 37 -> 37, of which waited for: 26 -> 22; matrix products, arithmetic and copies ran while one was open for 1% -> 1% of each run, Pallas kernels for 11% -> 13%
where the time goes in v2:
time: 209 us; the launch traced here: 208 us
  waiting for transfers between devices  96.7 us (46%)
  starting transfers between devices  62.8 us (30%)
  Pallas kernels  35 us (17%)
  blocking collectives  10.5 us (5%)
    ppermute x10, starting transfers between devices, shift_z(): return lax.ppermute(a, 'exp', pairs)  30.6 us
    ppermute x6, waiting for transfers between devices, shift_x(): return lax.ppermute(a, 'exp', pairs)  30.3 us
    ppermute x12, waiting for transfers between devices, shift_y(): return lax.ppermute(a, 'ctx', pairs)  24.7 us
    ppermute x10, waiting for transfers between devices, shift_z(): return lax.ppermute(a, 'exp', pairs)  20.6 us
    pallas_call x3, Pallas kernels, attend(): pl.pallas_call(kernel, in_specs=[pl.BlockSpec(memory_space=SMEM)] + [whol...  17.7 us
    ppermute x7, waiting for transfers between devices, swap_l(): return lax.ppermute(a, 'ctx', [(i, i ^ 1) for i in range(2 * N_Y)])  15.1 us
    ppermute x12, starting transfers between devices, shift_y(): return lax.ppermute(a, 'ctx', pairs)  11.2 us
    all_to_all x1, blocking collectives, exchange_x(): return lax.all_to_all(a, 'exp', 0, 0, tiled=True, axis_index_groups=groups)  10.5 us
  transfers between devices with their start and end apart: 37, of which 22 were waited for; matrix products, arithmetic and copies ran while one was open for 1% of the time, Pallas kernels for 13%

profile of v2, /device:TPU:24, one launch (start us, length us, event | category | flops | bytes accessed | tf_op | source)
XLA Modules:
  0.0 208.2 jit_solution(771299921025415025)
XLA Ops:
  1.6 2.0 collective-permute-start
  3.7 3.1 %pick_weights.1 = (bf16[256,1024]{1,0:T(8,128)(2,1)}, bf16[256,1024]{1,0:T(8,128)(2,1)}, bf16[256,1024]{1,0:T(8,128)(2,1)}) custom-call(s32[2]{0:T(128)S(1)} %pad_add_fusion.2.place_ref, bf16[512,4096]{1,0:T(8,128)(2,1)} %weight_ref.1, bf16[512,4096]{1,0:T(8,128)(2,1)} %weight_ref.1, bf16[512,4096]{1,0:T(8,128)(2,1)} %weight_ref.1), custom_call_target="tpu_custom_call" | custom-call | tf_op jit(solution)/shard_map/pick_weights/pallas_call | solution.py:93
  6.8 3.1 %collective-permute-done.refs_1_ = bf16[1024,128]{1,0:T(8,128)(2,1)S(1)} collective-permute-done((bf16[1024,128]{1,0:T(8,128)(2,1)S(1)}, bf16[1024,128]{1,0:T(8,128)(2,1)S(1)}, u32[]{:S(2)}, u32[]{:S(2)}) %collective-permute-start) | collective-permute-done | bytes 262176 | tf_op jit(solution)/shard_map/ppermute | solution.py:54
  10.8 2.5 %collective-permute-start.1 = (bf16[2048,128]{1,0:T(8,128)(2,1)S(1)}, bf16[2048,128]{1,0:T(8,128)(2,1)}, u32[]{:S(2)}, u32[]{:S(2)}) collective-permute-start(bf16[2048,128]{1,0:T(8,128)(2,1)S(1)} %stack.40.refs_2_), channel_id=1, source_target_pairs={{0,64},{32,96},{64,128},{96,160},{128,192},{160,224},{192,0},{224,... | collective-permute-start | bytes 1572872 | tf_op jit(solution)/shard_map/ppermute | solution.py:50
  13.3 1.5 collective-permute-start.5
  14.8 2.7 %collective-permute-start.6 = (bf16[256,1024]{1,0:T(8,128)(2,1)}, bf16[256,1024]{1,0:T(8,128)(2,1)S(1)}, u32[]{:S(2)}, u32[]{:S(2)}) collective-permute-start(bf16[256,1024]{1,0:T(8,128)(2,1)} %get-tuple-element.58), channel_id=1, source_target_pairs={{0,4},{2,6},{4,0},{6,2},{8,12},{10,14},{12,8},{14,10},{16,20},{18,... | collective-permute-start | bytes 1572872 | tf_op jit(solution)/shard_map/ppermute | solution.py:40
  20.5 4.6 %attend.3 = (f32[4,512,256]{2,1,0:T(8,128)S(1)}, f32[4,512,128]{2,1,0:T(8,128)S(1)}) custom-call(s32[3]{0:T(128)S(1)} %pad_add_fusion.1.refs_0_, bf16[512,512]{1,0:T(8,128)(2,1)S(1)} %copy-done.3, bf16[2048,128]{1,0:T(8,128)(2,1)S(1)} %stack.40.refs_2_), custom_call_target="tpu_custom_call" | custom-call | flops 1073741824 | bytes 4194304 | tf_op jit(solution)/shard_map/attend/pallas_call | solution.py:199
  26.1 2.3 %collective-permute-start.3 = (bf16[1024,128]{1,0:T(8,128)(2,1)S(1)}, bf16[1024,128]{1,0:T(8,128)(2,1)S(1)}, u32[]{:S(2)}, u32[]{:S(2)}) collective-permute-start(bf16[1024,128]{1,0:T(8,128)(2,1)S(1)} %slice.30), channel_id=1, source_target_pairs={{0,64},{32,96},{64,128},{96,160},{128,192},{160,224},{192,0},{224,... | collective-permute-start | bytes 786440 | tf_op jit(solution)/shard_map/ppermute | solution.py:50
  28.4 8.2 %attend.4 = (f32[4,512,256]{2,1,0:T(8,128)S(1)}, f32[4,512,128]{2,1,0:T(8,128)S(1)}) custom-call(s32[3]{0:T(128)S(1)} %pad_add_fusion.1.refs_0_, bf16[512,512]{1,0:T(8,128)(2,1)S(1)} %copy-done.3, bf16[2048,128]{1,0:T(8,128)(2,1)} %collective-permute-done.1.refs_2_, bf16[2048,128]{1,0:T(8,128)(2,1)S(1)} %collective-permute-done.2.refs_3_, ...), custom_call_target="tpu_custom_call" | custom-call | flops 2147483648 | bytes 4194304 | tf_op jit(solution)/shard_map/attend/pallas_call | solution.py:199
  36.6 2.7 %collective-permute-done.6.refs_1_.fetched_ref = bf16[256,1024]{1,0:T(8,128)(2,1)S(1)} collective-permute-done((bf16[256,1024]{1,0:T(8,128)(2,1)}, bf16[256,1024]{1,0:T(8,128)(2,1)S(1)}, u32[]{:S(2)}, u32[]{:S(2)}) %collective-permute-start.6) | collective-permute-done | bytes 524320 | tf_op jit(solution)/shard_map/ppermute | solution.py:40
  39.6 4.9 %attend.5 = (bf16[592,512]{1,0:T(8,128)(2,1)S(1)}, bf16[592,512]{1,0:T(8,128)(2,1)S(1)}, bf16[592,512]{1,0:T(8,128)(2,1)S(1)}) custom-call(s32[3]{0:T(128)S(1)} %pad_add_fusion.1.refs_0_, bf16[512,512]{1,0:T(8,128)(2,1)S(1)} %copy-done.3, bf16[1024,128]{1,0:T(8,128)(2,1)S(1)} %collective-permute-done.3.refs_2_, ...), custom_call_target="tpu_custom_call" | custom-call | flops 1073741824 | bytes 4194304 | tf_op jit(solution)/shard_map/attend/pallas_call | solution.py:199
  44.5 2.3 %collective-permute-start.10 = (bf16[592,512]{1,0:T(8,128)(2,1)S(1)}, bf16[592,512]{1,0:T(8,128)(2,1)S(1)}, u32[]{:S(2)}, u32[]{:S(2)}) collective-permute-start(bf16[592,512]{1,0:T(8,128)(2,1)S(1)} %get-tuple-element.74), channel_id=1, source_target_pairs={{0,6},{2,0},{4,2},{6,4},{8,14},{10,8},{12,10},{14,12},{16,22},{18,... | collective-permute-start | bytes 1818632 | tf_op jit(solution)/shard_map/ppermute | solution.py:40
  46.8 2.4 %collective-permute-start.9 = (bf16[592,512]{1,0:T(8,128)(2,1)S(1)}, bf16[592,512]{1,0:T(8,128)(2,1)S(1)}, u32[]{:S(2)}, u32[]{:S(2)}) collective-permute-start(bf16[592,512]{1,0:T(8,128)(2,1)S(1)} %get-tuple-element.73), channel_id=1, source_target_pairs={{0,4},{2,6},{4,0},{6,2},{8,12},{10,14},{12,8},{14,10},{16,20},{18,... | collective-permute-start | bytes 1818632 | tf_op jit(solution)/shard_map/ppermute | solution.py:40
  49.2 24.2 %collective-permute-done.10.refs_1_.refs_3_.h3 = bf16[592,512]{1,0:T(8,128)(2,1)S(1)} collective-permute-done((bf16[592,512]{1,0:T(8,128)(2,1)S(1)}, bf16[592,512]{1,0:T(8,128)(2,1)S(1)}, u32[]{:S(2)}, u32[]{:S(2)}) %collective-permute-start.10) | collective-permute-done | bytes 606240 | tf_op jit(solution)/shard_map/ppermute | solution.py:40
  73.4 3.4 %collective-permute-done.8.refs_0_.refs_1_.h1 = bf16[592,512]{1,0:T(8,128)(2,1)S(1)} collective-permute-done((bf16[592,512]{1,0:T(8,128)(2,1)S(1)}, bf16[592,512]{1,0:T(8,128)(2,1)S(1)}, u32[]{:S(2)}, u32[]{:S(2)}) %collective-permute-start.8) | collective-permute-done | bytes 606240 | tf_op jit(solution)/shard_map/ppermute | solution.py:40
  76.8 3.7 %project_near.1 = (f32[128,1024]{1,0:T(8,128)S(1)}, f32[128,1024]{1,0:T(8,128)S(1)}, f32[128,1024]{1,0:T(8,128)S(1)}, f32[128,1024]{1,0:T(8,128)S(1)}) custom-call(s32[3]{0:T(128)S(1)} %pad_add_fusion.place_ref, bf16[592,512]{1,0:T(8,128)(2,1)S(1)} %get-tuple-element.72.own_ref, bf16[512,4096]{1,0:T(8,128)(2,1)} %weight_ref.1, ...), custom_call_target="tpu_custom_call" | custom-call | flops 1 | bytes 1 | tf_op jit(solution)/shard_map/project_near/pallas_call | solution.py:243
  81.8 3.3 %collective-permute-start.12 = (bf16[128,512]{1,0:T(8,128)(2,1)S(1)}, bf16[128,512]{1,0:T(8,128)(2,1)S(1)}, u32[]{:S(2)}, u32[]{:S(2)}) collective-permute-start(bf16[128,512]{1,0:T(8,128)(2,1)S(1)} %get-tuple-element.89), channel_id=1, source_target_pairs={{0,8},{2,10},{4,12},{6,14},{8,16},{10,18},{12,20},{14,22},{16,24},... | collective-permute-start | bytes 393224 | tf_op jit(solution)/shard_map/ppermute | solution.py:45
  85.2 2.8 %collective-permute-start.13 = (bf16[128,512]{1,0:T(8,128)(2,1)S(1)}, bf16[128,512]{1,0:T(8,128)(2,1)S(1)}, u32[]{:S(2)}, u32[]{:S(2)}) collective-permute-start(bf16[128,512]{1,0:T(8,128)(2,1)S(1)} %get-tuple-element.90), channel_id=1, source_target_pairs={{0,24},{2,26},{4,28},{6,30},{8,0},{10,2},{12,4},{14,6},{16,8},{18,... | collective-permute-start | bytes 393224 | tf_op jit(solution)/shard_map/ppermute | solution.py:45
  88.7 2.1 %collective-permute-done.12 = bf16[128,512]{1,0:T(8,128)(2,1)S(1)} collective-permute-done((bf16[128,512]{1,0:T(8,128)(2,1)S(1)}, bf16[128,512]{1,0:T(8,128)(2,1)S(1)}, u32[]{:S(2)}, u32[]{:S(2)}) %collective-permute-start.12) | collective-permute-done | bytes 131104 | tf_op jit(solution)/shard_map/ppermute | solution.py:45
  90.9 2.7 %collective-permute-done.13 = bf16[128,512]{1,0:T(8,128)(2,1)S(1)} collective-permute-done((bf16[128,512]{1,0:T(8,128)(2,1)S(1)}, bf16[128,512]{1,0:T(8,128)(2,1)S(1)}, u32[]{:S(2)}, u32[]{:S(2)}) %collective-permute-start.13) | collective-permute-done | bytes 131104 | tf_op jit(solution)/shard_map/ppermute | solution.py:45
  93.7 3.1 %collective-permute-start.15 = (bf16[128,1024]{1,0:T(8,128)(2,1)S(1)}, bf16[128,1024]{1,0:T(8,128)(2,1)S(1)}, u32[]{:S(2)}, u32[]{:S(2)}) collective-permute-start(bf16[128,1024]{1,0:T(8,128)(2,1)S(1)} %pad_maximum_fusion.1), channel_id=1, source_target_pairs={{0,24},{2,26},{4,28},{6,30},{8,0},{10,2},{12,4},{14,6},{16,8},{18,... | collective-permute-start | bytes 786440 | tf_op jit(solution)/shard_map/ppermute | solution.py:45
  96.8 1.9 collective-permute-start.14
  98.7 5.7 %collective-permute-done.15.s2 = bf16[128,1024]{1,0:T(8,128)(2,1)S(1)} collective-permute-done((bf16[128,1024]{1,0:T(8,128)(2,1)S(1)}, bf16[128,1024]{1,0:T(8,128)(2,1)S(1)}, u32[]{:S(2)}, u32[]{:S(2)}) %collective-permute-start.15) | collective-permute-done | bytes 262176 | tf_op jit(solution)/shard_map/ppermute | solution.py:45
  104.4 3.8 %collective-permute-done.14.s1 = bf16[128,1024]{1,0:T(8,128)(2,1)S(1)} collective-permute-done((bf16[128,1024]{1,0:T(8,128)(2,1)S(1)}, bf16[128,1024]{1,0:T(8,128)(2,1)S(1)}, u32[]{:S(2)}, u32[]{:S(2)}) %collective-permute-start.14) | collective-permute-done | bytes 262176 | tf_op jit(solution)/shard_map/ppermute | solution.py:45
  109.1 4.1 %collective-permute-start.16 = (bf16[32,1024]{1,0:T(8,128)(2,1)S(1)}, bf16[32,1024]{1,0:T(8,128)(2,1)S(1)}, u32[]{:S(2)}, u32[]{:S(2)}) collective-permute-start(bf16[32,1024]{1,0:T(8,128)(2,1)S(1)} %get-tuple-element.95), channel_id=1, source_target_pairs={{0,8},{2,10},{4,12},{6,14},{8,16},{10,18},{12,20},{14,22},{16,24},... | collective-permute-start | bytes 196616 | tf_op jit(solution)/shard_map/ppermute | solution.py:45
  113.2 4.1 %collective-permute-start.17 = (bf16[32,1024]{1,0:T(8,128)(2,1)S(1)}, bf16[32,1024]{1,0:T(8,128)(2,1)S(1)}, u32[]{:S(2)}, u32[]{:S(2)}) collective-permute-start(bf16[32,1024]{1,0:T(8,128)(2,1)S(1)} %get-tuple-element.96), channel_id=1, source_target_pairs={{0,16},{2,18},{4,20},{6,22},{8,24},{10,26},{12,28},{14,30},{16,0},... | collective-permute-start | bytes 196616 | tf_op jit(solution)/shard_map/ppermute | solution.py:45
  117.3 4.0 %collective-permute-start.18 = (bf16[32,1024]{1,0:T(8,128)(2,1)S(1)}, bf16[32,1024]{1,0:T(8,128)(2,1)S(1)}, u32[]{:S(2)}, u32[]{:S(2)}) collective-permute-start(bf16[32,1024]{1,0:T(8,128)(2,1)S(1)} %get-tuple-element.97), channel_id=1, source_target_pairs={{0,24},{2,26},{4,28},{6,30},{8,0},{10,2},{12,4},{14,6},{16,8},{18,... | collective-permute-start | bytes 196616 | tf_op jit(solution)/shard_map/ppermute | solution.py:45
  121.4 1.9 collective-permute-done.18.refs_3_
  123.3 10.5 %all_to_all.10.piece_ref = bf16[4,64,1024]{2,1,0:T(8,128)(2,1)S(1)} all-to-all(bf16[4,64,1024]{2,1,0:T(8,128)(2,1)S(1)} %by_columns.1), channel_id=1, replica_groups={{0,2,4,6},{8,10,12,14},{16,18,20,22},{24,26,28,30},{1,3,5,7},{9,11,13,1..., dimensions={0} | all-to-all | bytes 1048576 | tf_op jit(solution)/shard_map/all_to_all | solution.py:574
  135.1 2.1 collective-permute-start.19
  137.2 6.5 %collective-permute-done.20.refs_2_ = bf16[32,4096]{1,0:T(8,128)(2,1)S(1)} collective-permute-done((bf16[32,4096]{1,0:T(8,128)(2,1)S(1)}, bf16[32,4096]{1,0:T(8,128)(2,1)S(1)}, u32[]{:S(2)}, u32[]{:S(2)}) %collective-permute-start.20) | collective-permute-done | bytes 262176 | tf_op jit(solution)/shard_map/ppermute | solution.py:50
  143.6 2.0 collective-permute-start.21
  146.0 4.0 %collective-permute-done.23.refs_5_ = bf16[32,4096]{1,0:T(8,128)(2,1)S(1)} collective-permute-done((bf16[32,4096]{1,0:T(8,128)(2,1)S(1)}, bf16[32,4096]{1,0:T(8,128)(2,1)S(1)}, u32[]{:S(2)}, u32[]{:S(2)}) %collective-permute-start.23) | collective-permute-done | bytes 262176 | tf_op jit(solution)/shard_map/ppermute | solution.py:50
  152.0 2.0 collective-permute-done.24.refs_6_
  154.0 5.0 %collective-permute-done.25.refs_7_ = bf16[32,4096]{1,0:T(8,128)(2,1)S(1)} collective-permute-done((bf16[32,4096]{1,0:T(8,128)(2,1)S(1)}, bf16[32,4096]{1,0:T(8,128)(2,1)S(1)}, u32[]{:S(2)}, u32[]{:S(2)}) %collective-permute-start.25) | collective-permute-done | bytes 262176 | tf_op jit(solution)/shard_map/ppermute | solution.py:54
  159.1 1.9 run_expert.1
  161.1 2.4 %collective-permute-start.26 = (bf16[32,4096]{1,0:T(8,128)(2,1)S(1)}, bf16[32,4096]{1,0:T(8,128)(2,1)S(1)}, u32[]{:S(2)}, u32[]{:S(2)}) collective-permute-start(bf16[32,4096]{1,0:T(8,128)(2,1)S(1)} %get-tuple-element.103), channel_id=1, source_target_pairs={{0,64},{32,96},{64,128},{96,160},{128,192},{160,224},{192,0},{224,... | collective-permute-start | bytes 786440 | tf_op jit(solution)/shard_map/ppermute | solution.py:50
  163.7 4.2 %collective-permute-done.27 = bf16[32,4096]{1,0:T(8,128)(2,1)S(1)} collective-permute-done((bf16[32,4096]{1,0:T(8,128)(2,1)S(1)}, bf16[32,4096]{1,0:T(8,128)(2,1)S(1)}, u32[]{:S(2)}, u32[]{:S(2)}) %collective-permute-start.27) | collective-permute-done | bytes 262176 | tf_op jit(solution)/shard_map/ppermute | solution.py:54
  168.1 2.3 %collective-permute-done.31 = bf16[32,4096]{1,0:T(8,128)(2,1)S(1)} collective-permute-done((bf16[32,4096]{1,0:T(8,128)(2,1)S(1)}, bf16[32,4096]{1,0:T(8,128)(2,1)S(1)}, u32[]{:S(2)}, u32[]{:S(2)}) %collective-permute-start.31) | collective-permute-done | bytes 262176 | tf_op jit(solution)/shard_map/ppermute | solution.py:50
  170.4 2.0 collective-permute-start.32
  172.4 3.1 %collective-permute-done.28 = bf16[32,4096]{1,0:T(8,128)(2,1)S(1)} collective-permute-done((bf16[32,4096]{1,0:T(8,128)(2,1)S(1)}, bf16[32,4096]{1,0:T(8,128)(2,1)S(1)}, u32[]{:S(2)}, u32[]{:S(2)}) %collective-permute-start.28) | collective-permute-done | bytes 262176 | tf_op jit(solution)/shard_map/ppermute | solution.py:50
  175.8 2.0 collective-permute-done.32
  177.8 5.6 %collective-permute-done.30 = bf16[32,4096]{1,0:T(8,128)(2,1)S(1)} collective-permute-done((bf16[32,4096]{1,0:T(8,128)(2,1)S(1)}, bf16[32,4096]{1,0:T(8,128)(2,1)S(1)}, u32[]{:S(2)}, u32[]{:S(2)}) %collective-permute-start.30) | collective-permute-done | bytes 262176 | tf_op jit(solution)/shard_map/ppermute | solution.py:50
  183.5 3.3 %collective-permute-start.35 = (bf16[8,4096]{1,0:T(8,128)(2,1)S(1)}, bf16[8,4096]{1,0:T(8,128)(2,1)S(1)}, u32[]{:S(2)}, u32[]{:S(2)}) collective-permute-start(bf16[8,4096]{1,0:T(8,128)(2,1)S(1)} %get-tuple-element.110), channel_id=1, source_target_pairs={{0,8},{2,10},{4,12},{6,14},{8,16},{10,18},{12,20},{14,22},{16,24},... | collective-permute-start | bytes 196616 | tf_op jit(solution)/shard_map/ppermute | solution.py:45
  186.8 2.6 %collective-permute-start.34 = (bf16[8,4096]{1,0:T(8,128)(2,1)S(1)}, bf16[8,4096]{1,0:T(8,128)(2,1)S(1)}, u32[]{:S(2)}, u32[]{:S(2)}) collective-permute-start(bf16[8,4096]{1,0:T(8,128)(2,1)S(1)} %get-tuple-element.111), channel_id=1, source_target_pairs={{0,16},{2,18},{4,20},{6,22},{8,24},{10,26},{12,28},{14,30},{16,0},... | collective-permute-start | bytes 196616 | tf_op jit(solution)/shard_map/ppermute | solution.py:45
  190.7 4.3 %collective-permute-done.34.refs_2_ = bf16[8,4096]{1,0:T(8,128)(2,1)S(1)} collective-permute-done((bf16[8,4096]{1,0:T(8,128)(2,1)S(1)}, bf16[8,4096]{1,0:T(8,128)(2,1)S(1)}, u32[]{:S(2)}, u32[]{:S(2)}) %collective-permute-start.34) | collective-permute-done | bytes 65568 | tf_op jit(solution)/shard_map/ppermute | solution.py:45
  196.0 4.2 %all-to-all-start.1 = ((bf16[4,8,4096]{2,1,0:T(8,128)(2,1)}), bf16[4,8,4096]{2,1,0:T(8,128)(2,1)S(1)}, u32[]{:S(2)}, u32[]{:S(2)}) async-start(bf16[4,8,4096]{2,1,0:T(8,128)(2,1)} %regroup.1), calls=%async_computation.1 | async-start | bytes 524288 | tf_op jit(solution)/shard_map/all_to_all | solution.py:574
  200.9 6.0 %all-to-all-done.1.refs_0_ = bf16[4,8,4096]{2,1,0:T(8,128)(2,1)S(1)} async-done(((bf16[4,8,4096]{2,1,0:T(8,128)(2,1)}), bf16[4,8,4096]{2,1,0:T(8,128)(2,1)S(1)}, u32[]{:S(2)}, u32[]{:S(2)}) %all-to-all-start.1) | async-done | bytes 262176 | tf_op jit(solution)/shard_map/all_to_all | solution.py:574
  (77 shorter events, 17.4 us)
Async XLA Ops:
  1.6 8.3 %collective-permute-start = (bf16[1024,128]{1,0:T(8,128)(2,1)S(1)}, bf16[1024,128]{1,0:T(8,128)(2,1)S(1)}, u32[]{:S(2)}, u32[]{:S(2)}) collective-permute-start(bf16[1024,128]{1,0:T(8,128)(2,1)S(1)} %pick_head.1.refs_0_), channel_id=1, source_target_pairs={{0,32},{32,0},{64,96},{96,64},{128,160},{160,128},{192,224},{224,1... | collective-permute-start | bytes 786440 | tf_op jit(solution)/shard_map/ppermute | solution.py:54
  3.7 16.0 %copy-start.4 = (bf16[32,4096]{1,0:T(8,128)(2,1)S(1)}, bf16[32,4096]{1,0:T(8,128)(2,1)}, u32[]{:S(2)}) copy-start(bf16[32,4096]{1,0:T(8,128)(2,1)} %hidden_ref.1) | copy-start | bytes 786436
  3.7 16.0 %copy-start.5 = (s32[32,8]{0,1:T(8,128)S(1)}, s32[32,8]{0,1:T(8,128)}, u32[]{:S(2)}) copy-start(s32[32,8]{0,1:T(8,128)} %param.18) | copy-start | bytes 3076
  3.7 16.7 %copy-start.3 = (bf16[512,512]{1,0:T(8,128)(2,1)S(1)}, bf16[512,512]{1,0:T(8,128)(2,1)}, u32[]{:S(2)}) copy-start(bf16[512,512]{1,0:T(8,128)(2,1)} %refs_1_.7) | copy-start | bytes 1572868
  10.0 15.1 %collective-permute-start.2 = (bf16[2048,128]{1,0:T(8,128)(2,1)S(1)}, bf16[2048,128]{1,0:T(8,128)(2,1)S(1)}, u32[]{:S(2)}, u32[]{:S(2)}) collective-permute-start(bf16[2048,128]{1,0:T(8,128)(2,1)S(1)} %stack.40.refs_2_), channel_id=1, source_target_pairs={{0,192},{32,224},{64,0},{96,32},{128,64},{160,96},{192,128},{224,1... | collective-permute-start | bytes 1572872 | tf_op jit(solution)/shard_map/ppermute | solution.py:50
  10.8 14.3 %collective-permute-start.1 = (bf16[2048,128]{1,0:T(8,128)(2,1)S(1)}, bf16[2048,128]{1,0:T(8,128)(2,1)}, u32[]{:S(2)}, u32[]{:S(2)}) collective-permute-start(bf16[2048,128]{1,0:T(8,128)(2,1)S(1)} %stack.40.refs_2_), channel_id=1, source_target_pairs={{0,64},{32,96},{64,128},{96,160},{128,192},{160,224},{192,0},{224,... | collective-permute-start | bytes 1572872 | tf_op jit(solution)/shard_map/ppermute | solution.py:50
  13.3 23.3 %collective-permute-start.5 = (bf16[256,1024]{1,0:T(8,128)(2,1)}, bf16[256,1024]{1,0:T(8,128)(2,1)S(1)}, u32[]{:S(2)}, u32[]{:S(2)}) collective-permute-start(bf16[256,1024]{1,0:T(8,128)(2,1)} %get-tuple-element.57), channel_id=1, source_target_pairs={{0,2},{2,4},{4,6},{6,0},{8,10},{10,12},{12,14},{14,8},{16,18},{18,... | collective-permute-start | bytes 1572872 | tf_op jit(solution)/shard_map/ppermute | solution.py:40
  14.8 24.6 %collective-permute-start.6 = (bf16[256,1024]{1,0:T(8,128)(2,1)}, bf16[256,1024]{1,0:T(8,128)(2,1)S(1)}, u32[]{:S(2)}, u32[]{:S(2)}) collective-permute-start(bf16[256,1024]{1,0:T(8,128)(2,1)} %get-tuple-element.58), channel_id=1, source_target_pairs={{0,4},{2,6},{4,0},{6,2},{8,12},{10,14},{12,8},{14,10},{16,20},{18,... | collective-permute-start | bytes 1572872 | tf_op jit(solution)/shard_map/ppermute | solution.py:40
  17.5 21.9 %collective-permute-start.7 = (bf16[256,1024]{1,0:T(8,128)(2,1)}, bf16[256,1024]{1,0:T(8,128)(2,1)S(1)}, u32[]{:S(2)}, u32[]{:S(2)}) collective-permute-start(bf16[256,1024]{1,0:T(8,128)(2,1)} %get-tuple-element.59), channel_id=1, source_target_pairs={{0,6},{2,0},{4,2},{6,4},{8,14},{10,8},{12,10},{14,12},{16,22},{18,... | collective-permute-start | bytes 1572872 | tf_op jit(solution)/shard_map/ppermute | solution.py:40
  26.1 13.3 %collective-permute-start.3 = (bf16[1024,128]{1,0:T(8,128)(2,1)S(1)}, bf16[1024,128]{1,0:T(8,128)(2,1)S(1)}, u32[]{:S(2)}, u32[]{:S(2)}) collective-permute-start(bf16[1024,128]{1,0:T(8,128)(2,1)S(1)} %slice.30), channel_id=1, source_target_pairs={{0,64},{32,96},{64,128},{96,160},{128,192},{160,224},{192,0},{224,... | collective-permute-start | bytes 786440 | tf_op jit(solution)/shard_map/ppermute | solution.py:50
  28.4 11.0 %collective-permute-start.4 = (bf16[1024,128]{1,0:T(8,128)(2,1)S(1)}, bf16[1024,128]{1,0:T(8,128)(2,1)S(1)}, u32[]{:S(2)}, u32[]{:S(2)}) collective-permute-start(bf16[1024,128]{1,0:T(8,128)(2,1)S(1)} %slice.31), channel_id=1, source_target_pairs={{0,192},{32,224},{64,0},{96,32},{128,64},{160,96},{192,128},{224,1... | collective-permute-start | bytes 786440 | tf_op jit(solution)/shard_map/ppermute | solution.py:50
  39.5 37.3 %collective-permute-start.11 = (bf16[768,1024]{1,0:T(8,128)(2,1)S(1)}, bf16[768,1024]{1,0:T(8,128)(2,1)S(1)}, u32[]{:S(2)}, u32[]{:S(2)}) collective-permute-start(bf16[768,1024]{1,0:T(8,128)(2,1)S(1)} %stack.41), channel_id=1, source_target_pairs={{0,1},{1,0},{2,3},{3,2},{4,5},{5,4},{6,7},{7,6},{8,9},{9,8},{10,11... | collective-permute-start | bytes 4718600 | tf_op jit(solution)/shard_map/ppermute | solution.py:58
  44.5 29.0 %collective-permute-start.10 = (bf16[592,512]{1,0:T(8,128)(2,1)S(1)}, bf16[592,512]{1,0:T(8,128)(2,1)S(1)}, u32[]{:S(2)}, u32[]{:S(2)}) collective-permute-start(bf16[592,512]{1,0:T(8,128)(2,1)S(1)} %get-tuple-element.74), channel_id=1, source_target_pairs={{0,6},{2,0},{4,2},{6,4},{8,14},{10,8},{12,10},{14,12},{16,22},{18,... | collective-permute-start | bytes 1818632 | tf_op jit(solution)/shard_map/ppermute | solution.py:40
  46.8 30.0 %collective-permute-start.8 = (bf16[592,512]{1,0:T(8,128)(2,1)S(1)}, bf16[592,512]{1,0:T(8,128)(2,1)S(1)}, u32[]{:S(2)}, u32[]{:S(2)}) collective-permute-start(bf16[592,512]{1,0:T(8,128)(2,1)S(1)} %get-tuple-element.72.own_ref), channel_id=1, source_target_pairs={{0,2},{2,4},{4,6},{6,0},{8,10},{10,12},{12,14},{14,8},{16,18},{18,... | collective-permute-start | bytes 1818632 | tf_op jit(solution)/shard_map/ppermute | solution.py:40
  46.8 33.7 %collective-permute-start.9 = (bf16[592,512]{1,0:T(8,128)(2,1)S(1)}, bf16[592,512]{1,0:T(8,128)(2,1)S(1)}, u32[]{:S(2)}, u32[]{:S(2)}) collective-permute-start(bf16[592,512]{1,0:T(8,128)(2,1)S(1)} %get-tuple-element.73), channel_id=1, source_target_pairs={{0,4},{2,6},{4,0},{6,2},{8,12},{10,14},{12,8},{14,10},{16,20},{18,... | collective-permute-start | bytes 1818632 | tf_op jit(solution)/shard_map/ppermute | solution.py:40
  81.8 9.0 %collective-permute-start.12 = (bf16[128,512]{1,0:T(8,128)(2,1)S(1)}, bf16[128,512]{1,0:T(8,128)(2,1)S(1)}, u32[]{:S(2)}, u32[]{:S(2)}) collective-permute-start(bf16[128,512]{1,0:T(8,128)(2,1)S(1)} %get-tuple-element.89), channel_id=1, source_target_pairs={{0,8},{2,10},{4,12},{6,14},{8,16},{10,18},{12,20},{14,22},{16,24},... | collective-permute-start | bytes 393224 | tf_op jit(solution)/shard_map/ppermute | solution.py:45
  85.2 8.4 %collective-permute-start.13 = (bf16[128,512]{1,0:T(8,128)(2,1)S(1)}, bf16[128,512]{1,0:T(8,128)(2,1)S(1)}, u32[]{:S(2)}, u32[]{:S(2)}) collective-permute-start(bf16[128,512]{1,0:T(8,128)(2,1)S(1)} %get-tuple-element.90), channel_id=1, source_target_pairs={{0,24},{2,26},{4,28},{6,30},{8,0},{10,2},{12,4},{14,6},{16,8},{18,... | collective-permute-start | bytes 393224 | tf_op jit(solution)/shard_map/ppermute | solution.py:45
  93.7 10.7 %collective-permute-start.15 = (bf16[128,1024]{1,0:T(8,128)(2,1)S(1)}, bf16[128,1024]{1,0:T(8,128)(2,1)S(1)}, u32[]{:S(2)}, u32[]{:S(2)}) collective-permute-start(bf16[128,1024]{1,0:T(8,128)(2,1)S(1)} %pad_maximum_fusion.1), channel_id=1, source_target_pairs={{0,24},{2,26},{4,28},{6,30},{8,0},{10,2},{12,4},{14,6},{16,8},{18,... | collective-permute-start | bytes 786440 | tf_op jit(solution)/shard_map/ppermute | solution.py:45
  96.8 11.4 %collective-permute-start.14 = (bf16[128,1024]{1,0:T(8,128)(2,1)S(1)}, bf16[128,1024]{1,0:T(8,128)(2,1)S(1)}, u32[]{:S(2)}, u32[]{:S(2)}) collective-permute-start(bf16[128,1024]{1,0:T(8,128)(2,1)S(1)} %pad_maximum_fusion), channel_id=1, source_target_pairs={{0,8},{2,10},{4,12},{6,14},{8,16},{10,18},{12,20},{14,22},{16,24},... | collective-permute-start | bytes 786440 | tf_op jit(solution)/shard_map/ppermute | solution.py:45
  108.2 50.9 %copy-start.1 = (bf16[1,4096,192]{1,2,0:T(8,128)(2,1)S(1)}, bf16[1,4096,192]{1,2,0:T(8,128)(2,1)}, u32[]{:S(2)}) copy-start(bf16[1,4096,192]{1,2,0:T(8,128)(2,1)} %param.22) | copy-start | bytes 4718596
  108.2 50.9 %copy-start.2 = (bf16[1,192,4096]{2,1,0:T(8,128)(2,1)S(1)}, bf16[1,192,4096]{2,1,0:T(8,128)(2,1)}, u32[]{:S(2)}) copy-start(bf16[1,192,4096]{2,1,0:T(8,128)(2,1)} %param.23) | copy-start | bytes 4718596
  109.1 24.7 %copy-start.6 = (f32[4096]{0:T(1024)S(1)}, f32[4096]{0:T(1024)}, u32[]{:S(2)}) copy-start(f32[4096]{0:T(1024)} %param.17) | copy-start | bytes 49156
  109.1 50.0 %copy-start = (bf16[1,4096,192]{1,2,0:T(8,128)(2,1)S(1)}, bf16[1,4096,192]{1,2,0:T(8,128)(2,1)}, u32[]{:S(2)}) copy-start(bf16[1,4096,192]{1,2,0:T(8,128)(2,1)} %param.21) | copy-start | bytes 4718596
  109.1 12.3 %collective-permute-start.16 = (bf16[32,1024]{1,0:T(8,128)(2,1)S(1)}, bf16[32,1024]{1,0:T(8,128)(2,1)S(1)}, u32[]{:S(2)}, u32[]{:S(2)}) collective-permute-start(bf16[32,1024]{1,0:T(8,128)(2,1)S(1)} %get-tuple-element.95), channel_id=1, source_target_pairs={{0,8},{2,10},{4,12},{6,14},{8,16},{10,18},{12,20},{14,22},{16,24},... | collective-permute-start | bytes 196616 | tf_op jit(solution)/shard_map/ppermute | solution.py:45
  113.2 8.2 %collective-permute-start.17 = (bf16[32,1024]{1,0:T(8,128)(2,1)S(1)}, bf16[32,1024]{1,0:T(8,128)(2,1)S(1)}, u32[]{:S(2)}, u32[]{:S(2)}) collective-permute-start(bf16[32,1024]{1,0:T(8,128)(2,1)S(1)} %get-tuple-element.96), channel_id=1, source_target_pairs={{0,16},{2,18},{4,20},{6,22},{8,24},{10,26},{12,28},{14,30},{16,0},... | collective-permute-start | bytes 196616 | tf_op jit(solution)/shard_map/ppermute | solution.py:45
  117.3 5.9 %collective-permute-start.18 = (bf16[32,1024]{1,0:T(8,128)(2,1)S(1)}, bf16[32,1024]{1,0:T(8,128)(2,1)S(1)}, u32[]{:S(2)}, u32[]{:S(2)}) collective-permute-start(bf16[32,1024]{1,0:T(8,128)(2,1)S(1)} %get-tuple-element.97), channel_id=1, source_target_pairs={{0,24},{2,26},{4,28},{6,30},{8,0},{10,2},{12,4},{14,6},{16,8},{18,... | collective-permute-start | bytes 196616 | tf_op jit(solution)/shard_map/ppermute | solution.py:45
  134.6 9.0 %collective-permute-start.20 = (bf16[32,4096]{1,0:T(8,128)(2,1)S(1)}, bf16[32,4096]{1,0:T(8,128)(2,1)S(1)}, u32[]{:S(2)}, u32[]{:S(2)}) collective-permute-start(bf16[32,4096]{1,0:T(8,128)(2,1)S(1)} %get-tuple-element.101.refs_0_), channel_id=1, source_target_pairs={{0,64},{32,96},{64,128},{96,160},{128,192},{160,224},{192,0},{224,... | collective-permute-start | bytes 786440 | tf_op jit(solution)/shard_map/ppermute | solution.py:50
  135.1 10.6 %collective-permute-start.19 = (bf16[32,4096]{1,0:T(8,128)(2,1)S(1)}, bf16[32,4096]{1,0:T(8,128)(2,1)S(1)}, u32[]{:S(2)}, u32[]{:S(2)}) collective-permute-start(bf16[32,4096]{1,0:T(8,128)(2,1)S(1)} %get-tuple-element.101.refs_0_), channel_id=1, source_target_pairs={{0,32},{32,0},{64,96},{96,64},{128,160},{160,128},{192,224},{224,1... | collective-permute-start | bytes 786440 | tf_op jit(solution)/shard_map/ppermute | solution.py:54
  143.6 6.4 %collective-permute-start.23 = (bf16[32,4096]{1,0:T(8,128)(2,1)S(1)}, bf16[32,4096]{1,0:T(8,128)(2,1)S(1)}, u32[]{:S(2)}, u32[]{:S(2)}) collective-permute-start(bf16[32,4096]{1,0:T(8,128)(2,1)S(1)} %collective-permute-done.20.refs_2_), channel_id=1, source_target_pairs={{0,64},{32,96},{64,128},{96,160},{128,192},{160,224},{192,0},{224,... | collective-permute-start | bytes 786440 | tf_op jit(solution)/shard_map/ppermute | solution.py:50
  143.6 7.6 %collective-permute-start.21 = (bf16[32,4096]{1,0:T(8,128)(2,1)S(1)}, bf16[32,4096]{1,0:T(8,128)(2,1)S(1)}, u32[]{:S(2)}, u32[]{:S(2)}) collective-permute-start(bf16[32,4096]{1,0:T(8,128)(2,1)S(1)} %get-tuple-element.101.refs_0_), channel_id=1, source_target_pairs={{0,192},{32,224},{64,0},{96,32},{128,64},{160,96},{192,128},{224,1... | collective-permute-start | bytes 786440 | tf_op jit(solution)/shard_map/ppermute | solution.py:50
  145.7 6.4 %collective-permute-start.22 = (bf16[32,4096]{1,0:T(8,128)(2,1)S(1)}, bf16[32,4096]{1,0:T(8,128)(2,1)S(1)}, u32[]{:S(2)}, u32[]{:S(2)}) collective-permute-start(bf16[32,4096]{1,0:T(8,128)(2,1)S(1)} %collective-permute-done.20.refs_2_), channel_id=1, source_target_pairs={{0,32},{32,0},{64,96},{96,64},{128,160},{160,128},{192,224},{224,1... | collective-permute-start | bytes 786440 | tf_op jit(solution)/shard_map/ppermute | solution.py:54
  145.7 8.4 %collective-permute-start.24 = (bf16[32,4096]{1,0:T(8,128)(2,1)S(1)}, bf16[32,4096]{1,0:T(8,128)(2,1)S(1)}, u32[]{:S(2)}, u32[]{:S(2)}) collective-permute-start(bf16[32,4096]{1,0:T(8,128)(2,1)S(1)} %collective-permute-done.19.refs_1_), channel_id=1, source_target_pairs={{0,192},{32,224},{64,0},{96,32},{128,64},{160,96},{192,128},{224,1... | collective-permute-start | bytes 786440 | tf_op jit(solution)/shard_map/ppermute | solution.py:50
  150.0 9.0 %collective-permute-start.25 = (bf16[32,4096]{1,0:T(8,128)(2,1)S(1)}, bf16[32,4096]{1,0:T(8,128)(2,1)S(1)}, u32[]{:S(2)}, u32[]{:S(2)}) collective-permute-start(bf16[32,4096]{1,0:T(8,128)(2,1)S(1)} %collective-permute-done.23.refs_5_), channel_id=1, source_target_pairs={{0,32},{32,0},{64,96},{96,64},{128,160},{160,128},{192,224},{224,1... | collective-permute-start | bytes 786440 | tf_op jit(solution)/shard_map/ppermute | solution.py:54
  161.0 6.8 %collective-permute-start.27 = (bf16[32,4096]{1,0:T(8,128)(2,1)S(1)}, bf16[32,4096]{1,0:T(8,128)(2,1)S(1)}, u32[]{:S(2)}, u32[]{:S(2)}) collective-permute-start(bf16[32,4096]{1,0:T(8,128)(2,1)S(1)} %get-tuple-element.106), channel_id=1, source_target_pairs={{0,32},{32,0},{64,96},{96,64},{128,160},{160,128},{192,224},{224,1... | collective-permute-start | bytes 786440 | tf_op jit(solution)/shard_map/ppermute | solution.py:54
  161.1 14.7 %collective-permute-start.26 = (bf16[32,4096]{1,0:T(8,128)(2,1)S(1)}, bf16[32,4096]{1,0:T(8,128)(2,1)S(1)}, u32[]{:S(2)}, u32[]{:S(2)}) collective-permute-start(bf16[32,4096]{1,0:T(8,128)(2,1)S(1)} %get-tuple-element.103), channel_id=1, source_target_pairs={{0,64},{32,96},{64,128},{96,160},{128,192},{160,224},{192,0},{224,... | collective-permute-start | bytes 786440 | tf_op jit(solution)/shard_map/ppermute | solution.py:50
  163.5 9.0 %collective-permute-start.29 = (bf16[32,4096]{1,0:T(8,128)(2,1)S(1)}, bf16[32,4096]{1,0:T(8,128)(2,1)S(1)}, u32[]{:S(2)}, u32[]{:S(2)}) collective-permute-start(bf16[32,4096]{1,0:T(8,128)(2,1)S(1)} %get-tuple-element.107), channel_id=1, source_target_pairs={{0,32},{32,0},{64,96},{96,64},{128,160},{160,128},{192,224},{224,1... | collective-permute-start | bytes 786440 | tf_op jit(solution)/shard_map/ppermute | solution.py:54
  163.6 6.7 %collective-permute-start.31 = (bf16[32,4096]{1,0:T(8,128)(2,1)S(1)}, bf16[32,4096]{1,0:T(8,128)(2,1)S(1)}, u32[]{:S(2)}, u32[]{:S(2)}) collective-permute-start(bf16[32,4096]{1,0:T(8,128)(2,1)S(1)} %get-tuple-element.109), channel_id=1, source_target_pairs={{0,64},{32,96},{64,128},{96,160},{128,192},{160,224},{192,0},{224,... | collective-permute-start | bytes 786440 | tf_op jit(solution)/shard_map/ppermute | solution.py:50
  167.9 7.7 %collective-permute-start.28 = (bf16[32,4096]{1,0:T(8,128)(2,1)S(1)}, bf16[32,4096]{1,0:T(8,128)(2,1)S(1)}, u32[]{:S(2)}, u32[]{:S(2)}) collective-permute-start(bf16[32,4096]{1,0:T(8,128)(2,1)S(1)} %add_convert_fusion.3), channel_id=1, source_target_pairs={{0,192},{32,224},{64,0},{96,32},{128,64},{160,96},{192,128},{224,1... | collective-permute-start | bytes 786440 | tf_op jit(solution)/shard_map/ppermute | solution.py:50
  170.4 7.4 %collective-permute-start.32 = (bf16[32,4096]{1,0:T(8,128)(2,1)S(1)}, bf16[32,4096]{1,0:T(8,128)(2,1)S(1)}, u32[]{:S(2)}, u32[]{:S(2)}) collective-permute-start(bf16[32,4096]{1,0:T(8,128)(2,1)S(1)} %add_convert_fusion.1), channel_id=1, source_target_pairs={{0,32},{32,0},{64,96},{96,64},{128,160},{160,128},{192,224},{224,1... | collective-permute-start | bytes 786440 | tf_op jit(solution)/shard_map/ppermute | solution.py:54
  175.7 24.6 %copy-start.7 = (s32[32,8]{0,1:T(8,128)S(1)}, s32[32,8]{0,1:T(8,128)}, u32[]{:S(2)}) copy-start(s32[32,8]{0,1:T(8,128)} %param.19) | copy-start | bytes 3076
  175.7 7.7 %collective-permute-start.30 = (bf16[32,4096]{1,0:T(8,128)(2,1)S(1)}, bf16[32,4096]{1,0:T(8,128)(2,1)S(1)}, u32[]{:S(2)}, u32[]{:S(2)}) collective-permute-start(bf16[32,4096]{1,0:T(8,128)(2,1)S(1)} %add_convert_fusion.2), channel_id=1, source_target_pairs={{0,192},{32,224},{64,0},{96,32},{128,64},{160,96},{192,128},{224,1... | collective-permute-start | bytes 786440 | tf_op jit(solution)/shard_map/ppermute | solution.py:50
  183.5 7.2 %collective-permute-start.35 = (bf16[8,4096]{1,0:T(8,128)(2,1)S(1)}, bf16[8,4096]{1,0:T(8,128)(2,1)S(1)}, u32[]{:S(2)}, u32[]{:S(2)}) collective-permute-start(bf16[8,4096]{1,0:T(8,128)(2,1)S(1)} %get-tuple-element.110), channel_id=1, source_target_pairs={{0,8},{2,10},{4,12},{6,14},{8,16},{10,18},{12,20},{14,22},{16,24},... | collective-permute-start | bytes 196616 | tf_op jit(solution)/shard_map/ppermute | solution.py:45
  186.8 8.2 %collective-permute-start.34 = (bf16[8,4096]{1,0:T(8,128)(2,1)S(1)}, bf16[8,4096]{1,0:T(8,128)(2,1)S(1)}, u32[]{:S(2)}, u32[]{:S(2)}) collective-permute-start(bf16[8,4096]{1,0:T(8,128)(2,1)S(1)} %get-tuple-element.111), channel_id=1, source_target_pairs={{0,16},{2,18},{4,20},{6,22},{8,24},{10,26},{12,28},{14,30},{16,0},... | collective-permute-start | bytes 196616 | tf_op jit(solution)/shard_map/ppermute | solution.py:45
  189.4 5.6 %collective-permute-start.33 = (bf16[8,4096]{1,0:T(8,128)(2,1)S(1)}, bf16[8,4096]{1,0:T(8,128)(2,1)S(1)}, u32[]{:S(2)}, u32[]{:S(2)}) collective-permute-start(bf16[8,4096]{1,0:T(8,128)(2,1)S(1)} %get-tuple-element.112), channel_id=1, source_target_pairs={{0,24},{2,26},{4,28},{6,30},{8,0},{10,2},{12,4},{14,6},{16,8},{18,... | collective-permute-start | bytes 196616 | tf_op jit(solution)/shard_map/ppermute | solution.py:45
  196.0 10.9 %all-to-all-start.1 = ((bf16[4,8,4096]{2,1,0:T(8,128)(2,1)}), bf16[4,8,4096]{2,1,0:T(8,128)(2,1)S(1)}, u32[]{:S(2)}, u32[]{:S(2)}) async-start(bf16[4,8,4096]{2,1,0:T(8,128)(2,1)} %regroup.1), calls=%async_computation.1 | async-start | bytes 524288 | tf_op jit(solution)/shard_map/all_to_all | solution.py:574

commit v3 on v2

--- a/solution.py
+++ b/solution.py
@@ -110,6 +110,7 @@
     n = sum(b.shape[0] for b in blocks) // (2 * rows)
     first = state is None
     last = riders is not None
+    passengers = [r for group in riders for r in group] if last else []
     tile = 128
 
     def kernel(*refs):
@@ -129,9 +130,10 @@
             acc_in, top_in = rest[0], rest[1]
             rest = rest[2:]
         if last:
-            rider_refs, rest = rest[:3], rest[3:]
-            for rider, target in zip(rider_refs, rest):
-                target[rows:, :] = rider[...]
+            rider_refs, rest = list(rest[: len(passengers)]), rest[len(passengers) :]
+            for group, target in zip(riders, rest):
+                for at in range(rows, rows + RIDER * len(group), RIDER):
+                    target[at : at + RIDER, :] = rider_refs.pop(0)[...]
         for b, r in enumerate(kv_refs):
             at = slice(b * rows, (b + 1) * rows)
             key_ref[at, :] = r[0:rows, :]
@@ -199,9 +201,12 @@
     return pl.pallas_call(
         kernel,
         in_specs=[pl.BlockSpec(memory_space=SMEM)]
-        + [whole()] * (1 + calls + (0 if first else 2) + (3 if last else 0)),
-        out_specs=[whole()] * (3 if last else 2),
-        out_shape=[jax.ShapeDtypeStruct((rows + RIDER, queries.shape[1]), BF16)] * 3
+        + [whole()] * (1 + calls + (0 if first else 2) + len(passengers)),
+        out_specs=[whole()] * 2,
+        out_shape=[
+            jax.ShapeDtypeStruct((rows + RIDER * len(group), queries.shape[1]), BF16)
+            for group in riders
+        ]
         if last
         else state_shapes,
         scratch_shapes=[VMEM((n * rows, HEAD_DIM), BF16), VMEM((n * rows, 2 * HEAD_DIM), BF16)],
@@ -212,7 +217,7 @@
             bytes_accessed=4 << 20,
         ),
         name="attend",
-    )(spot, queries, *blocks, *(() if first else state), *(riders if last else ()))
+    )(spot, queries, *blocks, *(() if first else state), *passengers)
 
 
 def rows_of(place_ref, left_ref, dz, columns):
@@ -225,8 +230,9 @@
     cols = out_proj.shape[1] // N_X
 
     def kernel(place_ref, own_ref, weight_ref, *refs):
-        left_refs, fetched_refs, other_ref, out_refs = refs[:n], refs[n : 2 * n], refs[2 * n], refs[2 * n + 1 :]
-        for dz in range(N_Z):
+        left_refs, fetched_refs, other_ref, out_ref = refs[:n], refs[n : 2 * n], refs[2 * n], refs[-1]
+
+        def chunk(dz, carry):
             total = jnp.dot(
                 rows_of(place_ref, own_ref, dz, slice(None)),
                 weight_ref[...],
@@ -236,7 +242,10 @@
                 total = total + fetched_part(
                     place_ref, left_refs[k], fetched_refs[k], other_ref, (0, 2)[k], dz
                 )
-            out_refs[dz][...] = total
+            out_ref[dz] = total
+            return carry
+
+        lax.fori_loop(0, N_Z, chunk, 0)
 
     fixed = lambda i, w: (0, 0)
     square = pl.BlockSpec(own.shape, fixed)
@@ -246,12 +255,12 @@
             num_scalar_prefetch=1,
             grid=(1,),
             in_specs=[square, pl.BlockSpec((out_proj.shape[0], cols), lambda i, w: (0, w[1]))]
-            + [square] * n
+            + [pl.BlockSpec(left.shape, fixed) for left in lefts]
             + [pl.BlockSpec(fetched[0].shape, fixed)] * n
             + [pl.BlockSpec(other.shape, fixed)],
-            out_specs=[pl.BlockSpec((N_X * TOKENS, cols), fixed)] * N_Z,
+            out_specs=pl.BlockSpec((N_Z, N_X * TOKENS, cols), lambda i, w: (0, 0, 0)),
         ),
-        out_shape=[jax.ShapeDtypeStruct((N_X * TOKENS, cols), F32)] * N_Z,
+        out_shape=jax.ShapeDtypeStruct((N_Z, N_X * TOKENS, cols), F32),
         compiler_params=params(28),
         cost_estimate=pl.CostEstimate(flops=1, transcendentals=0, bytes_accessed=1),
         name="project_near",
@@ -272,14 +281,35 @@
     )
 
 
-def project_far(place, near, left, fetched, other):
-    shape = near[0].shape
+def forward(message, first, rows, riders):
+    attended = message.shape[0] // 512 * 512
+
+    def kernel(message_ref, out_ref):
+        out_ref[0:rows, :] = message_ref[first : first + rows, :]
+        if riders:
+            out_ref[rows:, :] = message_ref[attended : attended + riders, :]
+
+    return pl.pallas_call(
+        kernel,
+        in_specs=[whole()],
+        out_specs=whole(),
+        out_shape=jax.ShapeDtypeStruct((rows + riders, message.shape[1]), BF16),
+        compiler_params=params(4),
+        name="forward",
+    )(message)
+
+
+def project_far(place, near, lefts, fetched, other):
+    shape = near.shape[1:]
     middle = shape[1] // 2
 
-    def kernel(place_ref, left_ref, fetched_ref, other_ref, *refs):
-        near_refs, out_refs = refs[:4], refs[4:]
+    def kernel(place_ref, upper_ref, lower_ref, fetched_ref, other_ref, *refs):
+        near_ref, out_refs, left_ref = refs[0], refs[1:-1], refs[-1]
+        half = left_ref.shape[0] // 2
+        left_ref[:half, :] = upper_ref[:half, :]
+        left_ref[half:, :] = lower_ref[...]
         for dz in (2, 1, 3, 0):
-            total = near_refs[dz][...] + fetched_part(
+            total = near_ref[dz] + fetched_part(
                 place_ref, left_ref, fetched_ref, other_ref, 1, dz
             )
             total = total.astype(BF16)
@@ -291,13 +321,14 @@
 
     return pl.pallas_call(
         kernel,
-        in_specs=[pl.BlockSpec(memory_space=SMEM)] + [whole()] * 7,
+        in_specs=[pl.BlockSpec(memory_space=SMEM)] + [whole()] * 5,
         out_specs=[whole()] * 5,
+        scratch_shapes=[VMEM((2 * lefts[1].shape[0], lefts[1].shape[1]), BF16)],
         out_shape=[jax.ShapeDtypeStruct(shape, BF16)] * 3
         + [jax.ShapeDtypeStruct((shape[0], middle), BF16)] * 2,
         compiler_params=params(),
         name="project_far",
-    )(place, left, fetched, other, *near)
+    )(place, *lefts, fetched, other, near)
 
 
 def pick_hidden(place, live, hidden_in, ids):
@@ -634,12 +665,14 @@
     )
     far_a, far_b, *fetched = tie((far_a, far_b, *fetched), *state)
     messages = attend(
-        queries, [far_a, far_b], spot, [(-2, 0), (-2, 1)], state, riders[1:]
+        queries, [far_a, far_b], spot, [(-2, 0), (-2, 1)], state, [[riders[2], riders[1]], [riders[3]]]
     )
 
     from_left = shift_x(messages[0], 1)
-    from_right = shift_x(messages[2], 3)
-    from_far = shift_x(messages[1], 2)
+    from_right = shift_x(messages[1], 3)
+    half = seq_rows // 2
+    far_a = shift_x(forward(from_left, 0, half, RIDER), 1)
+    far_b = shift_x(forward(from_right, half, half, 0), 3)
     weight = route_weights(
         tie((place,), from_left)[0], live=live_counts, ids=expert_ids.T, gates=gate_fixed.T
     )
@@ -647,9 +680,11 @@
     near = project_near(
         place, messages[0], out_proj, [from_left, from_right], [fetched[0], fetched[2]], other
     )
-    from_far, *near = tie((from_far, *near))
-    hidden = [riders[0], from_left, from_far, from_right]
-    mine, up_chunk, down_chunk, low, high = project_far(place, near, from_far, fetched[1], other)
+    far_a, far_b, near = tie((far_a, far_b, near))
+    hidden = [riders[0], from_left, far_a, from_right]
+    mine, up_chunk, down_chunk, low, high = project_far(
+        place, near, [far_a, far_b], fetched[1], other
+    )
 
     middle = low.shape[1]
     got_low = shift_z(low, 1)

time: 209 us -> 202 us (0.967)
  waiting for transfers between devices: 96.7 us -> 92.4 us
  starting transfers between devices: 62.8 us -> 60.1 us
    ppermute x6 -> x7, waiting for transfers between devices: 30.3 us -> 21.8 us  [shift_x(): return lax.ppermute(a, 'exp', pairs)]
    ppermute x10, waiting for transfers between devices: 20.6 us -> 25.7 us  [shift_z(): return lax.ppermute(a, 'exp', pairs)]
    ppermute x10, starting transfers between devices: 30.6 us -> 26.3 us  [shift_z(): return lax.ppermute(a, 'exp', pairs)]
    ppermute x6 -> x7, starting transfers between devices: 10.4 us -> 12.5 us  [shift_x(): return lax.ppermute(a, 'exp', pairs)]
  transfers between devices with their start and end apart: 37 -> 38, of which waited for: 22 -> 24; matrix products, arithmetic and copies ran while one was open for 1% -> 1% of each run, Pallas kernels for 13% -> 13%
where the time goes in v3:
time: 202 us
  waiting for transfers between devices  92.4 us (46%)
  starting transfers between devices  60.1 us (30%)
  Pallas kernels  35.6 us (18%)
  blocking collectives  10.5 us (5%)
    ppermute x10, starting transfers between devices, shift_z(): return lax.ppermute(a, 'exp', pairs)  26.3 us
    ppermute x10, waiting for transfers between devices, shift_z(): return lax.ppermute(a, 'exp', pairs)  25.7 us
    ppermute x12, waiting for transfers between devices, shift_y(): return lax.ppermute(a, 'ctx', pairs)  25.1 us
    ppermute x7, waiting for transfers between devices, shift_x(): return lax.ppermute(a, 'exp', pairs)  21.8 us
    pallas_call x3, Pallas kernels, attend(): pl.pallas_call(kernel, in_specs=[pl.BlockSpec(memory_space=SMEM)] + [whol...  17.6 us
    ppermute x7, waiting for transfers between devices, swap_l(): return lax.ppermute(a, 'ctx', [(i, i ^ 1) for i in range(2 * N_Y)])  13.8 us
    ppermute x7, starting transfers between devices, shift_x(): return lax.ppermute(a, 'exp', pairs)  12.5 us
    ppermute x12, starting transfers between devices, shift_y(): return lax.ppermute(a, 'ctx', pairs)  11.5 us
  transfers between devices with their start and end apart: 38, of which 24 were waited for; matrix products, arithmetic and copies ran while one was open for 1% of the time, Pallas kernels for 13%

profile of v3, /device:TPU:24, one launch (start us, length us, event | category | flops | bytes accessed | tf_op | source)
XLA Modules:
  0.0 201.8 jit_solution(832378604877848348)
XLA Ops:
  1.6 2.0 collective-permute-start
  3.7 3.1 %pick_weights.1 = (bf16[256,1024]{1,0:T(8,128)(2,1)}, bf16[256,1024]{1,0:T(8,128)(2,1)}, bf16[256,1024]{1,0:T(8,128)(2,1)}) custom-call(s32[2]{0:T(128)S(1)} %pad_add_fusion.2.place_ref, bf16[512,4096]{1,0:T(8,128)(2,1)} %weight_ref.1, bf16[512,4096]{1,0:T(8,128)(2,1)} %weight_ref.1, bf16[512,4096]{1,0:T(8,128)(2,1)} %weight_ref.1), custom_call_target="tpu_custom_call" | custom-call | tf_op jit(solution)/shard_map/pick_weights/pallas_call | solution.py:93
  6.8 3.1 %collective-permute-done.refs_1_ = bf16[1024,128]{1,0:T(8,128)(2,1)S(1)} collective-permute-done((bf16[1024,128]{1,0:T(8,128)(2,1)S(1)}, bf16[1024,128]{1,0:T(8,128)(2,1)S(1)}, u32[]{:S(2)}, u32[]{:S(2)}) %collective-permute-start) | collective-permute-done | bytes 262176 | tf_op jit(solution)/shard_map/ppermute | solution.py:54
  10.8 2.5 %collective-permute-start.1 = (bf16[2048,128]{1,0:T(8,128)(2,1)S(1)}, bf16[2048,128]{1,0:T(8,128)(2,1)}, u32[]{:S(2)}, u32[]{:S(2)}) collective-permute-start(bf16[2048,128]{1,0:T(8,128)(2,1)S(1)} %stack.40.refs_2_), channel_id=1, source_target_pairs={{0,64},{32,96},{64,128},{96,160},{128,192},{160,224},{192,0},{224,... | collective-permute-start | bytes 1572872 | tf_op jit(solution)/shard_map/ppermute | solution.py:50
  13.3 1.5 collective-permute-start.5
  14.8 2.7 %collective-permute-start.6 = (bf16[256,1024]{1,0:T(8,128)(2,1)}, bf16[256,1024]{1,0:T(8,128)(2,1)S(1)}, u32[]{:S(2)}, u32[]{:S(2)}) collective-permute-start(bf16[256,1024]{1,0:T(8,128)(2,1)} %get-tuple-element.51), channel_id=1, source_target_pairs={{0,4},{2,6},{4,0},{6,2},{8,12},{10,14},{12,8},{14,10},{16,20},{18,... | collective-permute-start | bytes 1572872 | tf_op jit(solution)/shard_map/ppermute | solution.py:40
  17.5 1.4 collective-permute-start.7
  20.5 4.6 %attend.3 = (f32[4,512,256]{2,1,0:T(8,128)S(1)}, f32[4,512,128]{2,1,0:T(8,128)S(1)}) custom-call(s32[3]{0:T(128)S(1)} %pad_add_fusion.1.refs_0_, bf16[512,512]{1,0:T(8,128)(2,1)S(1)} %copy-done.3, bf16[2048,128]{1,0:T(8,128)(2,1)S(1)} %stack.40.refs_2_), custom_call_target="tpu_custom_call" | custom-call | flops 1073741824 | bytes 4194304 | tf_op jit(solution)/shard_map/attend/pallas_call | solution.py:201
  26.1 2.3 %collective-permute-start.3 = (bf16[1024,128]{1,0:T(8,128)(2,1)S(1)}, bf16[1024,128]{1,0:T(8,128)(2,1)S(1)}, u32[]{:S(2)}, u32[]{:S(2)}) collective-permute-start(bf16[1024,128]{1,0:T(8,128)(2,1)S(1)} %slice.30), channel_id=1, source_target_pairs={{0,64},{32,96},{64,128},{96,160},{128,192},{160,224},{192,0},{224,... | collective-permute-start | bytes 786440 | tf_op jit(solution)/shard_map/ppermute | solution.py:50
  28.4 8.2 %attend.4 = (f32[4,512,256]{2,1,0:T(8,128)S(1)}, f32[4,512,128]{2,1,0:T(8,128)S(1)}) custom-call(s32[3]{0:T(128)S(1)} %pad_add_fusion.1.refs_0_, bf16[512,512]{1,0:T(8,128)(2,1)S(1)} %copy-done.3, bf16[2048,128]{1,0:T(8,128)(2,1)} %collective-permute-done.1.refs_2_, bf16[2048,128]{1,0:T(8,128)(2,1)S(1)} %collective-permute-done.2.refs_3_, ...), custom_call_target="tpu_custom_call" | custom-call | flops 2147483648 | bytes 4194304 | tf_op jit(solution)/shard_map/attend/pallas_call | solution.py:201
  36.7 2.7 %collective-permute-done.6.refs_1_.fetched_ref = bf16[256,1024]{1,0:T(8,128)(2,1)S(1)} collective-permute-done((bf16[256,1024]{1,0:T(8,128)(2,1)}, bf16[256,1024]{1,0:T(8,128)(2,1)S(1)}, u32[]{:S(2)}, u32[]{:S(2)}) %collective-permute-start.6) | collective-permute-done | bytes 524320 | tf_op jit(solution)/shard_map/ppermute | solution.py:40
  39.6 4.8 %attend.5 = (bf16[672,512]{1,0:T(8,128)(2,1)S(1)}, bf16[592,512]{1,0:T(8,128)(2,1)S(1)}) custom-call(s32[3]{0:T(128)S(1)} %pad_add_fusion.1.refs_0_, bf16[512,512]{1,0:T(8,128)(2,1)S(1)} %copy-done.3, bf16[1024,128]{1,0:T(8,128)(2,1)S(1)} %collective-permute-done.3.refs_2_, bf16[1024,128]{1,0:T(8,128)(2,1)S(1)} %collective-permute-done.4.refs_3_, ...), custom_call_target="tpu_custom_call" | custom-call | flops 1073741824 | bytes 4194304 | tf_op jit(solution)/shard_map/attend/pallas_call | solution.py:201
  44.4 1.4 collective-permute-start.8
  45.8 1.9 collective-permute-start.10
  47.7 15.8 %collective-permute-done.8.message_ref.refs_0_.refs_1_.h1 = bf16[672,512]{1,0:T(8,128)(2,1)S(1)} collective-permute-done((bf16[672,512]{1,0:T(8,128)(2,1)S(1)}, bf16[672,512]{1,0:T(8,128)(2,1)S(1)}, u32[]{:S(2)}, u32[]{:S(2)}) %collective-permute-start.8) | collective-permute-done | bytes 688160 | tf_op jit(solution)/shard_map/ppermute | solution.py:40
  64.0 3.2 %collective-permute-start.11 = (bf16[256,512]{1,0:T(8,128)(2,1)S(1)}, bf16[256,512]{1,0:T(8,128)(2,1)S(1)}, u32[]{:S(2)}, u32[]{:S(2)}) collective-permute-start(bf16[256,512]{1,0:T(8,128)(2,1)S(1)} %forward.3), channel_id=1, source_target_pairs={{0,6},{2,0},{4,2},{6,4},{8,14},{10,8},{12,10},{14,12},{16,22},{18,... | collective-permute-start | bytes 786440 | tf_op jit(solution)/shard_map/ppermute | solution.py:40
  67.2 4.3 %project_near.1.refs_0_ = f32[4,128,1024]{2,1,0:T(8,128)S(1)} custom-call(s32[3]{0:T(128)S(1)} %pad_add_fusion.place_ref, bf16[672,512]{1,0:T(8,128)(2,1)S(1)} %get-tuple-element.65.own_ref, bf16[512,4096]{1,0:T(8,128)(2,1)} %weight_ref.1, bf16[672,512]{1,0:T(8,128)(2,1)S(1)} %collective-permute-done.8.message_ref.refs_0_.refs_1_.h1, ...), custom_call_target="tpu_custom_call" | custom-call | flops 1 | bytes 1 | tf_op jit(solution)/shard_map/project_near/pallas_call | solution.py:252
  72.3 2.4 %collective-permute-done.9.upper_ref.refs_2_.h2 = bf16[336,512]{1,0:T(8,128)(2,1)S(1)} collective-permute-done((bf16[336,512]{1,0:T(8,128)(2,1)S(1)}, bf16[336,512]{1,0:T(8,128)(2,1)S(1)}, u32[]{:S(2)}, u32[]{:S(2)}) %collective-permute-start.9) | collective-permute-done | bytes 344096 | tf_op jit(solution)/shard_map/ppermute | solution.py:40
  76.1 3.4 %collective-permute-start.13 = (bf16[128,512]{1,0:T(8,128)(2,1)S(1)}, bf16[128,512]{1,0:T(8,128)(2,1)S(1)}, u32[]{:S(2)}, u32[]{:S(2)}) collective-permute-start(bf16[128,512]{1,0:T(8,128)(2,1)S(1)} %get-tuple-element.75), channel_id=1, source_target_pairs={{0,8},{2,10},{4,12},{6,14},{8,16},{10,18},{12,20},{14,22},{16,24},... | collective-permute-start | bytes 393224 | tf_op jit(solution)/shard_map/ppermute | solution.py:45
  79.4 2.7 %collective-permute-start.14 = (bf16[128,512]{1,0:T(8,128)(2,1)S(1)}, bf16[128,512]{1,0:T(8,128)(2,1)S(1)}, u32[]{:S(2)}, u32[]{:S(2)}) collective-permute-start(bf16[128,512]{1,0:T(8,128)(2,1)S(1)} %get-tuple-element.76), channel_id=1, source_target_pairs={{0,24},{2,26},{4,28},{6,30},{8,0},{10,2},{12,4},{14,6},{16,8},{18,... | collective-permute-start | bytes 393224 | tf_op jit(solution)/shard_map/ppermute | solution.py:45
  83.0 2.3 %collective-permute-done.13 = bf16[128,512]{1,0:T(8,128)(2,1)S(1)} collective-permute-done((bf16[128,512]{1,0:T(8,128)(2,1)S(1)}, bf16[128,512]{1,0:T(8,128)(2,1)S(1)}, u32[]{:S(2)}, u32[]{:S(2)}) %collective-permute-start.13) | collective-permute-done | bytes 131104 | tf_op jit(solution)/shard_map/ppermute | solution.py:45
  85.3 3.2 %collective-permute-done.14 = bf16[128,512]{1,0:T(8,128)(2,1)S(1)} collective-permute-done((bf16[128,512]{1,0:T(8,128)(2,1)S(1)}, bf16[128,512]{1,0:T(8,128)(2,1)S(1)}, u32[]{:S(2)}, u32[]{:S(2)}) %collective-permute-start.14) | collective-permute-done | bytes 131104 | tf_op jit(solution)/shard_map/ppermute | solution.py:45
  88.6 2.8 %collective-permute-start.16 = (bf16[128,1024]{1,0:T(8,128)(2,1)S(1)}, bf16[128,1024]{1,0:T(8,128)(2,1)S(1)}, u32[]{:S(2)}, u32[]{:S(2)}) collective-permute-start(bf16[128,1024]{1,0:T(8,128)(2,1)S(1)} %pad_maximum_fusion.1), channel_id=1, source_target_pairs={{0,24},{2,26},{4,28},{6,30},{8,0},{10,2},{12,4},{14,6},{16,8},{18,... | collective-permute-start | bytes 786440 | tf_op jit(solution)/shard_map/ppermute | solution.py:45
  92.5 9.8 %collective-permute-done.16.s2 = bf16[128,1024]{1,0:T(8,128)(2,1)S(1)} collective-permute-done((bf16[128,1024]{1,0:T(8,128)(2,1)S(1)}, bf16[128,1024]{1,0:T(8,128)(2,1)S(1)}, u32[]{:S(2)}, u32[]{:S(2)}) %collective-permute-start.16) | collective-permute-done | bytes 262176 | tf_op jit(solution)/shard_map/ppermute | solution.py:45
  102.2 2.0 collective-permute-done.15.s1
  106.5 3.0 %collective-permute-start.18 = (bf16[32,1024]{1,0:T(8,128)(2,1)S(1)}, bf16[32,1024]{1,0:T(8,128)(2,1)S(1)}, u32[]{:S(2)}, u32[]{:S(2)}) collective-permute-start(bf16[32,1024]{1,0:T(8,128)(2,1)S(1)} %get-tuple-element.82), channel_id=1, source_target_pairs={{0,16},{2,18},{4,20},{6,22},{8,24},{10,26},{12,28},{14,30},{16,0},... | collective-permute-start | bytes 196616 | tf_op jit(solution)/shard_map/ppermute | solution.py:45
  109.5 4.0 %collective-permute-start.19 = (bf16[32,1024]{1,0:T(8,128)(2,1)S(1)}, bf16[32,1024]{1,0:T(8,128)(2,1)S(1)}, u32[]{:S(2)}, u32[]{:S(2)}) collective-permute-start(bf16[32,1024]{1,0:T(8,128)(2,1)S(1)} %get-tuple-element.83), channel_id=1, source_target_pairs={{0,24},{2,26},{4,28},{6,30},{8,0},{10,2},{12,4},{14,6},{16,8},{18,... | collective-permute-start | bytes 196616 | tf_op jit(solution)/shard_map/ppermute | solution.py:45
  113.5 1.8 collective-permute-done.18.refs_2_
  116.4 10.5 %all_to_all.10.piece_ref = bf16[4,64,1024]{2,1,0:T(8,128)(2,1)S(1)} all-to-all(bf16[4,64,1024]{2,1,0:T(8,128)(2,1)S(1)} %by_columns.1), channel_id=1, replica_groups={{0,2,4,6},{8,10,12,14},{16,18,20,22},{24,26,28,30},{1,3,5,7},{9,11,13,1..., dimensions={0} | all-to-all | bytes 1048576 | tf_op jit(solution)/shard_map/all_to_all | solution.py:605
  128.8 6.9 %collective-permute-done.21.refs_2_ = bf16[32,4096]{1,0:T(8,128)(2,1)S(1)} collective-permute-done((bf16[32,4096]{1,0:T(8,128)(2,1)S(1)}, bf16[32,4096]{1,0:T(8,128)(2,1)S(1)}, u32[]{:S(2)}, u32[]{:S(2)}) %collective-permute-start.21) | collective-permute-done | bytes 262176 | tf_op jit(solution)/shard_map/ppermute | solution.py:50
  138.4 3.7 %collective-permute-done.24.refs_5_ = bf16[32,4096]{1,0:T(8,128)(2,1)S(1)} collective-permute-done((bf16[32,4096]{1,0:T(8,128)(2,1)S(1)}, bf16[32,4096]{1,0:T(8,128)(2,1)S(1)}, u32[]{:S(2)}, u32[]{:S(2)}) %collective-permute-start.24) | collective-permute-done | bytes 262176 | tf_op jit(solution)/shard_map/ppermute | solution.py:50
  142.2 2.1 %collective-permute-done.22.refs_3_ = bf16[32,4096]{1,0:T(8,128)(2,1)S(1)} collective-permute-done((bf16[32,4096]{1,0:T(8,128)(2,1)S(1)}, bf16[32,4096]{1,0:T(8,128)(2,1)S(1)}, u32[]{:S(2)}, u32[]{:S(2)}) %collective-permute-start.22) | collective-permute-done | bytes 262176 | tf_op jit(solution)/shard_map/ppermute | solution.py:50
  144.3 2.8 %collective-permute-done.25.refs_6_ = bf16[32,4096]{1,0:T(8,128)(2,1)S(1)} collective-permute-done((bf16[32,4096]{1,0:T(8,128)(2,1)S(1)}, bf16[32,4096]{1,0:T(8,128)(2,1)S(1)}, u32[]{:S(2)}, u32[]{:S(2)}) %collective-permute-start.25) | collective-permute-done | bytes 262176 | tf_op jit(solution)/shard_map/ppermute | solution.py:50
  147.1 4.1 %collective-permute-done.26.refs_7_ = bf16[32,4096]{1,0:T(8,128)(2,1)S(1)} collective-permute-done((bf16[32,4096]{1,0:T(8,128)(2,1)S(1)}, bf16[32,4096]{1,0:T(8,128)(2,1)S(1)}, u32[]{:S(2)}, u32[]{:S(2)}) %collective-permute-start.26) | collective-permute-done | bytes 262176 | tf_op jit(solution)/shard_map/ppermute | solution.py:54
  151.2 1.9 run_expert.1
  153.4 3.7 %collective-permute-start.27 = (bf16[32,4096]{1,0:T(8,128)(2,1)S(1)}, bf16[32,4096]{1,0:T(8,128)(2,1)S(1)}, u32[]{:S(2)}, u32[]{:S(2)}) collective-permute-start(bf16[32,4096]{1,0:T(8,128)(2,1)S(1)} %get-tuple-element.89), channel_id=1, source_target_pairs={{0,64},{32,96},{64,128},{96,160},{128,192},{160,224},{192,0},{224,... | collective-permute-start | bytes 786440 | tf_op jit(solution)/shard_map/ppermute | solution.py:50
  157.4 2.9 %collective-permute-done.28 = bf16[32,4096]{1,0:T(8,128)(2,1)S(1)} collective-permute-done((bf16[32,4096]{1,0:T(8,128)(2,1)S(1)}, bf16[32,4096]{1,0:T(8,128)(2,1)S(1)}, u32[]{:S(2)}, u32[]{:S(2)}) %collective-permute-start.28) | collective-permute-done | bytes 262176 | tf_op jit(solution)/shard_map/ppermute | solution.py:54
  160.4 3.4 %collective-permute-done.32 = bf16[32,4096]{1,0:T(8,128)(2,1)S(1)} collective-permute-done((bf16[32,4096]{1,0:T(8,128)(2,1)S(1)}, bf16[32,4096]{1,0:T(8,128)(2,1)S(1)}, u32[]{:S(2)}, u32[]{:S(2)}) %collective-permute-start.32) | collective-permute-done | bytes 262176 | tf_op jit(solution)/shard_map/ppermute | solution.py:50
  163.9 1.8 collective-permute-start.33
  165.7 2.3 %collective-permute-done.29 = bf16[32,4096]{1,0:T(8,128)(2,1)S(1)} collective-permute-done((bf16[32,4096]{1,0:T(8,128)(2,1)S(1)}, bf16[32,4096]{1,0:T(8,128)(2,1)S(1)}, u32[]{:S(2)}, u32[]{:S(2)}) %collective-permute-start.29) | collective-permute-done | bytes 262176 | tf_op jit(solution)/shard_map/ppermute | solution.py:50
  168.2 3.7 %collective-permute-done.33 = bf16[32,4096]{1,0:T(8,128)(2,1)S(1)} collective-permute-done((bf16[32,4096]{1,0:T(8,128)(2,1)S(1)}, bf16[32,4096]{1,0:T(8,128)(2,1)S(1)}, u32[]{:S(2)}, u32[]{:S(2)}) %collective-permute-start.33) | collective-permute-done | bytes 262176 | tf_op jit(solution)/shard_map/ppermute | solution.py:54
  171.9 3.9 %collective-permute-done.31 = bf16[32,4096]{1,0:T(8,128)(2,1)S(1)} collective-permute-done((bf16[32,4096]{1,0:T(8,128)(2,1)S(1)}, bf16[32,4096]{1,0:T(8,128)(2,1)S(1)}, u32[]{:S(2)}, u32[]{:S(2)}) %collective-permute-start.31) | collective-permute-done | bytes 262176 | tf_op jit(solution)/shard_map/ppermute | solution.py:50
  175.9 3.4 %collective-permute-start.36 = (bf16[8,4096]{1,0:T(8,128)(2,1)S(1)}, bf16[8,4096]{1,0:T(8,128)(2,1)S(1)}, u32[]{:S(2)}, u32[]{:S(2)}) collective-permute-start(bf16[8,4096]{1,0:T(8,128)(2,1)S(1)} %get-tuple-element.96), channel_id=1, source_target_pairs={{0,8},{2,10},{4,12},{6,14},{8,16},{10,18},{12,20},{14,22},{16,24},... | collective-permute-start | bytes 196616 | tf_op jit(solution)/shard_map/ppermute | solution.py:45
  179.4 3.6 %collective-permute-start.35 = (bf16[8,4096]{1,0:T(8,128)(2,1)S(1)}, bf16[8,4096]{1,0:T(8,128)(2,1)S(1)}, u32[]{:S(2)}, u32[]{:S(2)}) collective-permute-start(bf16[8,4096]{1,0:T(8,128)(2,1)S(1)} %get-tuple-element.97), channel_id=1, source_target_pairs={{0,16},{2,18},{4,20},{6,22},{8,24},{10,26},{12,28},{14,30},{16,0},... | collective-permute-start | bytes 196616 | tf_op jit(solution)/shard_map/ppermute | solution.py:45
  184.0 3.5 %collective-permute-done.35.refs_2_ = bf16[8,4096]{1,0:T(8,128)(2,1)S(1)} collective-permute-done((bf16[8,4096]{1,0:T(8,128)(2,1)S(1)}, bf16[8,4096]{1,0:T(8,128)(2,1)S(1)}, u32[]{:S(2)}, u32[]{:S(2)}) %collective-permute-start.35) | collective-permute-done | bytes 65568 | tf_op jit(solution)/shard_map/ppermute | solution.py:45
  187.6 2.0 collective-permute-done.34.refs_1_
  190.5 3.4 %all-to-all-start.1 = ((bf16[4,8,4096]{2,1,0:T(8,128)(2,1)}), bf16[4,8,4096]{2,1,0:T(8,128)(2,1)S(1)}, u32[]{:S(2)}, u32[]{:S(2)}) async-start(bf16[4,8,4096]{2,1,0:T(8,128)(2,1)} %regroup.1), calls=%async_computation.1 | async-start | bytes 524288 | tf_op jit(solution)/shard_map/all_to_all | solution.py:605
  194.6 5.9 %all-to-all-done.1.refs_0_ = bf16[4,8,4096]{2,1,0:T(8,128)(2,1)S(1)} async-done(((bf16[4,8,4096]{2,1,0:T(8,128)(2,1)}), bf16[4,8,4096]{2,1,0:T(8,128)(2,1)S(1)}, u32[]{:S(2)}, u32[]{:S(2)}) %all-to-all-start.1) | async-done | bytes 262176 | tf_op jit(solution)/shard_map/all_to_all | solution.py:605
  (81 shorter events, 21.7 us)
Async XLA Ops:
  1.6 8.3 %collective-permute-start = (bf16[1024,128]{1,0:T(8,128)(2,1)S(1)}, bf16[1024,128]{1,0:T(8,128)(2,1)S(1)}, u32[]{:S(2)}, u32[]{:S(2)}) collective-permute-start(bf16[1024,128]{1,0:T(8,128)(2,1)S(1)} %pick_head.1.refs_0_), channel_id=1, source_target_pairs={{0,32},{32,0},{64,96},{96,64},{128,160},{160,128},{192,224},{224,1... | collective-permute-start | bytes 786440 | tf_op jit(solution)/shard_map/ppermute | solution.py:54
  3.7 16.0 %copy-start.4 = (bf16[32,4096]{1,0:T(8,128)(2,1)S(1)}, bf16[32,4096]{1,0:T(8,128)(2,1)}, u32[]{:S(2)}) copy-start(bf16[32,4096]{1,0:T(8,128)(2,1)} %hidden_ref.1) | copy-start | bytes 786436
  3.7 16.0 %copy-start.5 = (s32[32,8]{0,1:T(8,128)S(1)}, s32[32,8]{0,1:T(8,128)}, u32[]{:S(2)}) copy-start(s32[32,8]{0,1:T(8,128)} %param.18) | copy-start | bytes 3076
  3.7 16.7 %copy-start.3 = (bf16[512,512]{1,0:T(8,128)(2,1)S(1)}, bf16[512,512]{1,0:T(8,128)(2,1)}, u32[]{:S(2)}) copy-start(bf16[512,512]{1,0:T(8,128)(2,1)} %refs_1_.7) | copy-start | bytes 1572868
  10.0 15.1 %collective-permute-start.2 = (bf16[2048,128]{1,0:T(8,128)(2,1)S(1)}, bf16[2048,128]{1,0:T(8,128)(2,1)S(1)}, u32[]{:S(2)}, u32[]{:S(2)}) collective-permute-start(bf16[2048,128]{1,0:T(8,128)(2,1)S(1)} %stack.40.refs_2_), channel_id=1, source_target_pairs={{0,192},{32,224},{64,0},{96,32},{128,64},{160,96},{192,128},{224,1... | collective-permute-start | bytes 1572872 | tf_op jit(solution)/shard_map/ppermute | solution.py:50
  10.8 14.3 %collective-permute-start.1 = (bf16[2048,128]{1,0:T(8,128)(2,1)S(1)}, bf16[2048,128]{1,0:T(8,128)(2,1)}, u32[]{:S(2)}, u32[]{:S(2)}) collective-permute-start(bf16[2048,128]{1,0:T(8,128)(2,1)S(1)} %stack.40.refs_2_), channel_id=1, source_target_pairs={{0,64},{32,96},{64,128},{96,160},{128,192},{160,224},{192,0},{224,... | collective-permute-start | bytes 1572872 | tf_op jit(solution)/shard_map/ppermute | solution.py:50
  13.3 23.3 %collective-permute-start.5 = (bf16[256,1024]{1,0:T(8,128)(2,1)}, bf16[256,1024]{1,0:T(8,128)(2,1)S(1)}, u32[]{:S(2)}, u32[]{:S(2)}) collective-permute-start(bf16[256,1024]{1,0:T(8,128)(2,1)} %get-tuple-element.50), channel_id=1, source_target_pairs={{0,2},{2,4},{4,6},{6,0},{8,10},{10,12},{12,14},{14,8},{16,18},{18,... | collective-permute-start | bytes 1572872 | tf_op jit(solution)/shard_map/ppermute | solution.py:40
  14.8 24.6 %collective-permute-start.6 = (bf16[256,1024]{1,0:T(8,128)(2,1)}, bf16[256,1024]{1,0:T(8,128)(2,1)S(1)}, u32[]{:S(2)}, u32[]{:S(2)}) collective-permute-start(bf16[256,1024]{1,0:T(8,128)(2,1)} %get-tuple-element.51), channel_id=1, source_target_pairs={{0,4},{2,6},{4,0},{6,2},{8,12},{10,14},{12,8},{14,10},{16,20},{18,... | collective-permute-start | bytes 1572872 | tf_op jit(solution)/shard_map/ppermute | solution.py:40
  17.5 21.9 %collective-permute-start.7 = (bf16[256,1024]{1,0:T(8,128)(2,1)}, bf16[256,1024]{1,0:T(8,128)(2,1)S(1)}, u32[]{:S(2)}, u32[]{:S(2)}) collective-permute-start(bf16[256,1024]{1,0:T(8,128)(2,1)} %get-tuple-element.52), channel_id=1, source_target_pairs={{0,6},{2,0},{4,2},{6,4},{8,14},{10,8},{12,10},{14,12},{16,22},{18,... | collective-permute-start | bytes 1572872 | tf_op jit(solution)/shard_map/ppermute | solution.py:40
  26.1 13.3 %collective-permute-start.3 = (bf16[1024,128]{1,0:T(8,128)(2,1)S(1)}, bf16[1024,128]{1,0:T(8,128)(2,1)S(1)}, u32[]{:S(2)}, u32[]{:S(2)}) collective-permute-start(bf16[1024,128]{1,0:T(8,128)(2,1)S(1)} %slice.30), channel_id=1, source_target_pairs={{0,64},{32,96},{64,128},{96,160},{128,192},{160,224},{192,0},{224,... | collective-permute-start | bytes 786440 | tf_op jit(solution)/shard_map/ppermute | solution.py:50
  28.4 11.0 %collective-permute-start.4 = (bf16[1024,128]{1,0:T(8,128)(2,1)S(1)}, bf16[1024,128]{1,0:T(8,128)(2,1)S(1)}, u32[]{:S(2)}, u32[]{:S(2)}) collective-permute-start(bf16[1024,128]{1,0:T(8,128)(2,1)S(1)} %slice.31), channel_id=1, source_target_pairs={{0,192},{32,224},{64,0},{96,32},{128,64},{160,96},{192,128},{224,1... | collective-permute-start | bytes 786440 | tf_op jit(solution)/shard_map/ppermute | solution.py:50
  39.5 27.7 %collective-permute-start.12 = (bf16[768,1024]{1,0:T(8,128)(2,1)S(1)}, bf16[768,1024]{1,0:T(8,128)(2,1)S(1)}, u32[]{:S(2)}, u32[]{:S(2)}) collective-permute-start(bf16[768,1024]{1,0:T(8,128)(2,1)S(1)} %stack.41), channel_id=1, source_target_pairs={{0,1},{1,0},{2,3},{3,2},{4,5},{5,4},{6,7},{7,6},{8,9},{9,8},{10,11... | collective-permute-start | bytes 4718600 | tf_op jit(solution)/shard_map/ppermute | solution.py:58
  44.4 19.1 %collective-permute-start.8 = (bf16[672,512]{1,0:T(8,128)(2,1)S(1)}, bf16[672,512]{1,0:T(8,128)(2,1)S(1)}, u32[]{:S(2)}, u32[]{:S(2)}) collective-permute-start(bf16[672,512]{1,0:T(8,128)(2,1)S(1)} %get-tuple-element.65.own_ref), channel_id=1, source_target_pairs={{0,2},{2,4},{4,6},{6,0},{8,10},{10,12},{12,14},{14,8},{16,18},{18,... | collective-permute-start | bytes 2064392 | tf_op jit(solution)/shard_map/ppermute | solution.py:40
  45.8 18.1 %collective-permute-start.10 = (bf16[592,512]{1,0:T(8,128)(2,1)S(1)}, bf16[592,512]{1,0:T(8,128)(2,1)S(1)}, u32[]{:S(2)}, u32[]{:S(2)}) collective-permute-start(bf16[592,512]{1,0:T(8,128)(2,1)S(1)} %get-tuple-element.66), channel_id=1, source_target_pairs={{0,6},{2,0},{4,2},{6,4},{8,14},{10,8},{12,10},{14,12},{16,22},{18,... | collective-permute-start | bytes 1818632 | tf_op jit(solution)/shard_map/ppermute | solution.py:40
  63.6 11.2 %collective-permute-start.9 = (bf16[336,512]{1,0:T(8,128)(2,1)S(1)}, bf16[336,512]{1,0:T(8,128)(2,1)S(1)}, u32[]{:S(2)}, u32[]{:S(2)}) collective-permute-start(bf16[336,512]{1,0:T(8,128)(2,1)S(1)} %forward.2), channel_id=1, source_target_pairs={{0,2},{2,4},{4,6},{6,0},{8,10},{10,12},{12,14},{14,8},{16,18},{18,... | collective-permute-start | bytes 1032200 | tf_op jit(solution)/shard_map/ppermute | solution.py:40
  64.0 8.4 %collective-permute-start.11 = (bf16[256,512]{1,0:T(8,128)(2,1)S(1)}, bf16[256,512]{1,0:T(8,128)(2,1)S(1)}, u32[]{:S(2)}, u32[]{:S(2)}) collective-permute-start(bf16[256,512]{1,0:T(8,128)(2,1)S(1)} %forward.3), channel_id=1, source_target_pairs={{0,6},{2,0},{4,2},{6,4},{8,14},{10,8},{12,10},{14,12},{16,22},{18,... | collective-permute-start | bytes 786440 | tf_op jit(solution)/shard_map/ppermute | solution.py:40
  76.1 9.2 %collective-permute-start.13 = (bf16[128,512]{1,0:T(8,128)(2,1)S(1)}, bf16[128,512]{1,0:T(8,128)(2,1)S(1)}, u32[]{:S(2)}, u32[]{:S(2)}) collective-permute-start(bf16[128,512]{1,0:T(8,128)(2,1)S(1)} %get-tuple-element.75), channel_id=1, source_target_pairs={{0,8},{2,10},{4,12},{6,14},{8,16},{10,18},{12,20},{14,22},{16,24},... | collective-permute-start | bytes 393224 | tf_op jit(solution)/shard_map/ppermute | solution.py:45
  79.4 9.1 %collective-permute-start.14 = (bf16[128,512]{1,0:T(8,128)(2,1)S(1)}, bf16[128,512]{1,0:T(8,128)(2,1)S(1)}, u32[]{:S(2)}, u32[]{:S(2)}) collective-permute-start(bf16[128,512]{1,0:T(8,128)(2,1)S(1)} %get-tuple-element.76), channel_id=1, source_target_pairs={{0,24},{2,26},{4,28},{6,30},{8,0},{10,2},{12,4},{14,6},{16,8},{18,... | collective-permute-start | bytes 393224 | tf_op jit(solution)/shard_map/ppermute | solution.py:45
  88.6 13.6 %collective-permute-start.16 = (bf16[128,1024]{1,0:T(8,128)(2,1)S(1)}, bf16[128,1024]{1,0:T(8,128)(2,1)S(1)}, u32[]{:S(2)}, u32[]{:S(2)}) collective-permute-start(bf16[128,1024]{1,0:T(8,128)(2,1)S(1)} %pad_maximum_fusion.1), channel_id=1, source_target_pairs={{0,24},{2,26},{4,28},{6,30},{8,0},{10,2},{12,4},{14,6},{16,8},{18,... | collective-permute-start | bytes 786440 | tf_op jit(solution)/shard_map/ppermute | solution.py:45
  91.5 12.7 %collective-permute-start.15 = (bf16[128,1024]{1,0:T(8,128)(2,1)S(1)}, bf16[128,1024]{1,0:T(8,128)(2,1)S(1)}, u32[]{:S(2)}, u32[]{:S(2)}) collective-permute-start(bf16[128,1024]{1,0:T(8,128)(2,1)S(1)} %pad_maximum_fusion), channel_id=1, source_target_pairs={{0,8},{2,10},{4,12},{6,14},{8,16},{10,18},{12,20},{14,22},{16,24},... | collective-permute-start | bytes 786440 | tf_op jit(solution)/shard_map/ppermute | solution.py:45
  104.2 22.7 %copy-start.6 = (f32[4096]{0:T(1024)S(1)}, f32[4096]{0:T(1024)}, u32[]{:S(2)}) copy-start(f32[4096]{0:T(1024)} %param.17) | copy-start | bytes 49156
  104.2 47.0 %copy-start.1 = (bf16[1,4096,192]{1,2,0:T(8,128)(2,1)S(1)}, bf16[1,4096,192]{1,2,0:T(8,128)(2,1)}, u32[]{:S(2)}) copy-start(bf16[1,4096,192]{1,2,0:T(8,128)(2,1)} %param.22) | copy-start | bytes 4718596
  104.2 47.0 %copy-start.2 = (bf16[1,192,4096]{2,1,0:T(8,128)(2,1)S(1)}, bf16[1,192,4096]{2,1,0:T(8,128)(2,1)}, u32[]{:S(2)}) copy-start(bf16[1,192,4096]{2,1,0:T(8,128)(2,1)} %param.23) | copy-start | bytes 4718596
  105.1 46.1 %copy-start = (bf16[1,4096,192]{1,2,0:T(8,128)(2,1)S(1)}, bf16[1,4096,192]{1,2,0:T(8,128)(2,1)}, u32[]{:S(2)}) copy-start(bf16[1,4096,192]{1,2,0:T(8,128)(2,1)} %param.21) | copy-start | bytes 4718596
  105.1 8.4 %collective-permute-start.17 = (bf16[32,1024]{1,0:T(8,128)(2,1)S(1)}, bf16[32,1024]{1,0:T(8,128)(2,1)S(1)}, u32[]{:S(2)}, u32[]{:S(2)}) collective-permute-start(bf16[32,1024]{1,0:T(8,128)(2,1)S(1)} %get-tuple-element.81), channel_id=1, source_target_pairs={{0,8},{2,10},{4,12},{6,14},{8,16},{10,18},{12,20},{14,22},{16,24},... | collective-permute-start | bytes 196616 | tf_op jit(solution)/shard_map/ppermute | solution.py:45
  106.5 8.8 %collective-permute-start.18 = (bf16[32,1024]{1,0:T(8,128)(2,1)S(1)}, bf16[32,1024]{1,0:T(8,128)(2,1)S(1)}, u32[]{:S(2)}, u32[]{:S(2)}) collective-permute-start(bf16[32,1024]{1,0:T(8,128)(2,1)S(1)} %get-tuple-element.82), channel_id=1, source_target_pairs={{0,16},{2,18},{4,20},{6,22},{8,24},{10,26},{12,28},{14,30},{16,0},... | collective-permute-start | bytes 196616 | tf_op jit(solution)/shard_map/ppermute | solution.py:45
  109.5 6.9 %collective-permute-start.19 = (bf16[32,1024]{1,0:T(8,128)(2,1)S(1)}, bf16[32,1024]{1,0:T(8,128)(2,1)S(1)}, u32[]{:S(2)}, u32[]{:S(2)}) collective-permute-start(bf16[32,1024]{1,0:T(8,128)(2,1)S(1)} %get-tuple-element.83), channel_id=1, source_target_pairs={{0,24},{2,26},{4,28},{6,30},{8,0},{10,2},{12,4},{14,6},{16,8},{18,... | collective-permute-start | bytes 196616 | tf_op jit(solution)/shard_map/ppermute | solution.py:45
  127.7 7.9 %collective-permute-start.21 = (bf16[32,4096]{1,0:T(8,128)(2,1)S(1)}, bf16[32,4096]{1,0:T(8,128)(2,1)S(1)}, u32[]{:S(2)}, u32[]{:S(2)}) collective-permute-start(bf16[32,4096]{1,0:T(8,128)(2,1)S(1)} %get-tuple-element.87.refs_0_), channel_id=1, source_target_pairs={{0,64},{32,96},{64,128},{96,160},{128,192},{160,224},{192,0},{224,... | collective-permute-start | bytes 786440 | tf_op jit(solution)/shard_map/ppermute | solution.py:50
  127.7 10.6 %collective-permute-start.20 = (bf16[32,4096]{1,0:T(8,128)(2,1)S(1)}, bf16[32,4096]{1,0:T(8,128)(2,1)S(1)}, u32[]{:S(2)}, u32[]{:S(2)}) collective-permute-start(bf16[32,4096]{1,0:T(8,128)(2,1)S(1)} %get-tuple-element.87.refs_0_), channel_id=1, source_target_pairs={{0,32},{32,0},{64,96},{96,64},{128,160},{160,128},{192,224},{224,1... | collective-permute-start | bytes 786440 | tf_op jit(solution)/shard_map/ppermute | solution.py:54
  135.7 6.4 %collective-permute-start.24 = (bf16[32,4096]{1,0:T(8,128)(2,1)S(1)}, bf16[32,4096]{1,0:T(8,128)(2,1)S(1)}, u32[]{:S(2)}, u32[]{:S(2)}) collective-permute-start(bf16[32,4096]{1,0:T(8,128)(2,1)S(1)} %collective-permute-done.21.refs_2_), channel_id=1, source_target_pairs={{0,64},{32,96},{64,128},{96,160},{128,192},{160,224},{192,0},{224,... | collective-permute-start | bytes 786440 | tf_op jit(solution)/shard_map/ppermute | solution.py:50
  136.8 7.6 %collective-permute-start.22 = (bf16[32,4096]{1,0:T(8,128)(2,1)S(1)}, bf16[32,4096]{1,0:T(8,128)(2,1)S(1)}, u32[]{:S(2)}, u32[]{:S(2)}) collective-permute-start(bf16[32,4096]{1,0:T(8,128)(2,1)S(1)} %get-tuple-element.87.refs_0_), channel_id=1, source_target_pairs={{0,192},{32,224},{64,0},{96,32},{128,64},{160,96},{192,128},{224,1... | collective-permute-start | bytes 786440 | tf_op jit(solution)/shard_map/ppermute | solution.py:50
  137.7 6.6 %collective-permute-start.23 = (bf16[32,4096]{1,0:T(8,128)(2,1)S(1)}, bf16[32,4096]{1,0:T(8,128)(2,1)S(1)}, u32[]{:S(2)}, u32[]{:S(2)}) collective-permute-start(bf16[32,4096]{1,0:T(8,128)(2,1)S(1)} %collective-permute-done.21.refs_2_), channel_id=1, source_target_pairs={{0,32},{32,0},{64,96},{96,64},{128,160},{160,128},{192,224},{224,1... | collective-permute-start | bytes 786440 | tf_op jit(solution)/shard_map/ppermute | solution.py:54
  138.4 8.8 %collective-permute-start.25 = (bf16[32,4096]{1,0:T(8,128)(2,1)S(1)}, bf16[32,4096]{1,0:T(8,128)(2,1)S(1)}, u32[]{:S(2)}, u32[]{:S(2)}) collective-permute-start(bf16[32,4096]{1,0:T(8,128)(2,1)S(1)} %collective-permute-done.20.refs_1_), channel_id=1, source_target_pairs={{0,192},{32,224},{64,0},{96,32},{128,64},{160,96},{192,128},{224,1... | collective-permute-start | bytes 786440 | tf_op jit(solution)/shard_map/ppermute | solution.py:50
  142.1 9.2 %collective-permute-start.26 = (bf16[32,4096]{1,0:T(8,128)(2,1)S(1)}, bf16[32,4096]{1,0:T(8,128)(2,1)S(1)}, u32[]{:S(2)}, u32[]{:S(2)}) collective-permute-start(bf16[32,4096]{1,0:T(8,128)(2,1)S(1)} %collective-permute-done.24.refs_5_), channel_id=1, source_target_pairs={{0,32},{32,0},{64,96},{96,64},{128,160},{160,128},{192,224},{224,1... | collective-permute-start | bytes 786440 | tf_op jit(solution)/shard_map/ppermute | solution.py:54
  153.2 7.1 %collective-permute-start.28 = (bf16[32,4096]{1,0:T(8,128)(2,1)S(1)}, bf16[32,4096]{1,0:T(8,128)(2,1)S(1)}, u32[]{:S(2)}, u32[]{:S(2)}) collective-permute-start(bf16[32,4096]{1,0:T(8,128)(2,1)S(1)} %get-tuple-element.92), channel_id=1, source_target_pairs={{0,32},{32,0},{64,96},{96,64},{128,160},{160,128},{192,224},{224,1... | collective-permute-start | bytes 786440 | tf_op jit(solution)/shard_map/ppermute | solution.py:54
  153.4 14.8 %collective-permute-start.27 = (bf16[32,4096]{1,0:T(8,128)(2,1)S(1)}, bf16[32,4096]{1,0:T(8,128)(2,1)S(1)}, u32[]{:S(2)}, u32[]{:S(2)}) collective-permute-start(bf16[32,4096]{1,0:T(8,128)(2,1)S(1)} %get-tuple-element.89), channel_id=1, source_target_pairs={{0,64},{32,96},{64,128},{96,160},{128,192},{160,224},{192,0},{224,... | collective-permute-start | bytes 786440 | tf_op jit(solution)/shard_map/ppermute | solution.py:50
  157.1 8.6 %collective-permute-start.30 = (bf16[32,4096]{1,0:T(8,128)(2,1)S(1)}, bf16[32,4096]{1,0:T(8,128)(2,1)S(1)}, u32[]{:S(2)}, u32[]{:S(2)}) collective-permute-start(bf16[32,4096]{1,0:T(8,128)(2,1)S(1)} %get-tuple-element.93), channel_id=1, source_target_pairs={{0,32},{32,0},{64,96},{96,64},{128,160},{160,128},{192,224},{224,1... | collective-permute-start | bytes 786440 | tf_op jit(solution)/shard_map/ppermute | solution.py:54
  157.4 6.5 %collective-permute-start.32 = (bf16[32,4096]{1,0:T(8,128)(2,1)S(1)}, bf16[32,4096]{1,0:T(8,128)(2,1)S(1)}, u32[]{:S(2)}, u32[]{:S(2)}) collective-permute-start(bf16[32,4096]{1,0:T(8,128)(2,1)S(1)} %get-tuple-element.95), channel_id=1, source_target_pairs={{0,64},{32,96},{64,128},{96,160},{128,192},{160,224},{192,0},{224,... | collective-permute-start | bytes 786440 | tf_op jit(solution)/shard_map/ppermute | solution.py:50
  160.3 7.7 %collective-permute-start.29 = (bf16[32,4096]{1,0:T(8,128)(2,1)S(1)}, bf16[32,4096]{1,0:T(8,128)(2,1)S(1)}, u32[]{:S(2)}, u32[]{:S(2)}) collective-permute-start(bf16[32,4096]{1,0:T(8,128)(2,1)S(1)} %add_convert_fusion.3), channel_id=1, source_target_pairs={{0,192},{32,224},{64,0},{96,32},{128,64},{160,96},{192,128},{224,1... | collective-permute-start | bytes 786440 | tf_op jit(solution)/shard_map/ppermute | solution.py:50
  163.9 8.0 %collective-permute-start.33 = (bf16[32,4096]{1,0:T(8,128)(2,1)S(1)}, bf16[32,4096]{1,0:T(8,128)(2,1)S(1)}, u32[]{:S(2)}, u32[]{:S(2)}) collective-permute-start(bf16[32,4096]{1,0:T(8,128)(2,1)S(1)} %add_convert_fusion.1), channel_id=1, source_target_pairs={{0,32},{32,0},{64,96},{96,64},{128,160},{160,128},{192,224},{224,1... | collective-permute-start | bytes 786440 | tf_op jit(solution)/shard_map/ppermute | solution.py:54
  168.1 25.8 %copy-start.7 = (s32[32,8]{0,1:T(8,128)S(1)}, s32[32,8]{0,1:T(8,128)}, u32[]{:S(2)}) copy-start(s32[32,8]{0,1:T(8,128)} %param.19) | copy-start | bytes 3076
  168.1 7.7 %collective-permute-start.31 = (bf16[32,4096]{1,0:T(8,128)(2,1)S(1)}, bf16[32,4096]{1,0:T(8,128)(2,1)S(1)}, u32[]{:S(2)}, u32[]{:S(2)}) collective-permute-start(bf16[32,4096]{1,0:T(8,128)(2,1)S(1)} %add_convert_fusion.2), channel_id=1, source_target_pairs={{0,192},{32,224},{64,0},{96,32},{128,64},{160,96},{192,128},{224,1... | collective-permute-start | bytes 786440 | tf_op jit(solution)/shard_map/ppermute | solution.py:50
  175.9 8.1 %collective-permute-start.36 = (bf16[8,4096]{1,0:T(8,128)(2,1)S(1)}, bf16[8,4096]{1,0:T(8,128)(2,1)S(1)}, u32[]{:S(2)}, u32[]{:S(2)}) collective-permute-start(bf16[8,4096]{1,0:T(8,128)(2,1)S(1)} %get-tuple-element.96), channel_id=1, source_target_pairs={{0,8},{2,10},{4,12},{6,14},{8,16},{10,18},{12,20},{14,22},{16,24},... | collective-permute-start | bytes 196616 | tf_op jit(solution)/shard_map/ppermute | solution.py:45
  179.4 8.2 %collective-permute-start.35 = (bf16[8,4096]{1,0:T(8,128)(2,1)S(1)}, bf16[8,4096]{1,0:T(8,128)(2,1)S(1)}, u32[]{:S(2)}, u32[]{:S(2)}) collective-permute-start(bf16[8,4096]{1,0:T(8,128)(2,1)S(1)} %get-tuple-element.97), channel_id=1, source_target_pairs={{0,16},{2,18},{4,20},{6,22},{8,24},{10,26},{12,28},{14,30},{16,0},... | collective-permute-start | bytes 196616 | tf_op jit(solution)/shard_map/ppermute | solution.py:45
  183.0 6.6 %collective-permute-start.34 = (bf16[8,4096]{1,0:T(8,128)(2,1)S(1)}, bf16[8,4096]{1,0:T(8,128)(2,1)S(1)}, u32[]{:S(2)}, u32[]{:S(2)}) collective-permute-start(bf16[8,4096]{1,0:T(8,128)(2,1)S(1)} %get-tuple-element.98), channel_id=1, source_target_pairs={{0,24},{2,26},{4,28},{6,30},{8,0},{10,2},{12,4},{14,6},{16,8},{18,... | collective-permute-start | bytes 196616 | tf_op jit(solution)/shard_map/ppermute | solution.py:45
  190.5 10.1 %all-to-all-start.1 = ((bf16[4,8,4096]{2,1,0:T(8,128)(2,1)}), bf16[4,8,4096]{2,1,0:T(8,128)(2,1)S(1)}, u32[]{:S(2)}, u32[]{:S(2)}) async-start(bf16[4,8,4096]{2,1,0:T(8,128)(2,1)} %regroup.1), calls=%async_computation.1 | async-start | bytes 524288 | tf_op jit(solution)/shard_map/all_to_all | solution.py:605

commit v4 on v3

--- a/solution.py
+++ b/solution.py
@@ -608,12 +608,12 @@
 def scatter_ctx(parts):
     own, swapped, below, above, below_swapped, below_two, above_swapped, far = parts
     got_far = swap_l(far)
-    got_below_swapped = swap_l(below_swapped)
+    got_below_swapped = shift_y(below_swapped, -1)
     got_above_swapped = shift_y(above_swapped, 1)
     got_two = shift_y(add(below_two, got_far), -1)
     got_above = shift_y(above, 1)
-    got_swapped = swap_l(add(swapped, got_above_swapped))
-    got_below = shift_y(add(below, got_two, got_below_swapped), -1)
+    got_swapped = swap_l(add(swapped, got_above_swapped, got_below_swapped))
+    got_below = shift_y(add(below, got_two), -1)
     return add(own, got_above, got_below, got_swapped)
 
 
@@ -658,8 +658,8 @@
     riders = pick_hidden(place, live_counts, hidden_in, expert_ids.T)
     below, above = tie((below, above), *state, *riders)
     block = own.shape[0]
-    far_a = shift_y(below[:block], 1)
-    far_b = shift_y(above[block:], -1)
+    far_a = shift_y(forward(below, 0, block, 0), 1)
+    far_b = shift_y(forward(above, block, block, 0), -1)
     state = attend(
         queries, [below, above], spot, [(-1, 0), (-1, 1), (1, 0), (1, 1)], state
     )
@@ -705,7 +705,7 @@
     below = shift_y(block, 1)
     above = shift_y(block, -1)
     below_two = shift_y(below, 1)
-    below_swapped = swap_l(below)
+    below_swapped = shift_y(swapped, 1)
     above_swapped = shift_y(swapped, -1)
     far = swap_l(below_two)
     parts = run_expert(

time: 202 us -> 204 us (level)
    ppermute x12 -> x14, starting transfers between devices: 11.5 us -> 16.8 us  [shift_y(): return lax.ppermute(a, 'ctx', pairs)]
    ppermute x7 -> x5, starting transfers between devices: 6.18 us -> 4.43 us  [swap_l(): return lax.ppermute(a, 'ctx', [(i, i ^ 1) for i in range(2 * N_Y)])]
    ppermute x12 -> x14, waiting for transfers between devices: 25.1 us -> 23.7 us  [shift_y(): return lax.ppermute(a, 'ctx', pairs)]
    ppermute x7 -> x5, waiting for transfers between devices: 13.8 us -> 13.3 us  [swap_l(): return lax.ppermute(a, 'ctx', [(i, i ^ 1) for i in range(2 * N_Y)])]
  transfers between devices with their start and end apart: 38 -> 38, of which waited for: 24 -> 26; matrix products, arithmetic and copies ran while one was open for 1% -> 0% of each run, Pallas kernels for 13% -> 13%
where the time goes in v4:
time: 204 us; the launch traced here: 203 us
  waiting for transfers between devices  91.9 us (45%)
  starting transfers between devices  62.1 us (30%)
  Pallas kernels  36.4 us (18%)
  blocking collectives  10.5 us (5%)
    ppermute x10, waiting for transfers between devices, shift_z(): return lax.ppermute(a, 'exp', pairs)  26 us
    ppermute x10, starting transfers between devices, shift_z(): return lax.ppermute(a, 'exp', pairs)  24.9 us
    ppermute x14, waiting for transfers between devices, shift_y(): return lax.ppermute(a, 'ctx', pairs)  23.7 us
    ppermute x7, waiting for transfers between devices, shift_x(): return lax.ppermute(a, 'exp', pairs)  23 us
    pallas_call x3, Pallas kernels, attend(): pl.pallas_call(kernel, in_specs=[pl.BlockSpec(memory_space=SMEM)] + [whol...  17.6 us
    ppermute x14, starting transfers between devices, shift_y(): return lax.ppermute(a, 'ctx', pairs)  16.8 us
    ppermute x5, waiting for transfers between devices, swap_l(): return lax.ppermute(a, 'ctx', [(i, i ^ 1) for i in range(2 * N_Y)])  13.3 us
    ppermute x7, starting transfers between devices, shift_x(): return lax.ppermute(a, 'exp', pairs)  12.5 us
  transfers between devices with their start and end apart: 38, of which 26 were waited for; matrix products, arithmetic and copies ran while one was open for 0% of the time, Pallas kernels for 13%

profile of v4, /device:TPU:24, one launch (start us, length us, event | category | flops | bytes accessed | tf_op | source)
XLA Modules:
  0.0 203.3 jit_solution(6421772136999910332)
XLA Ops:
  1.6 2.0 collective-permute-start
  3.7 3.1 %pick_weights.1 = (bf16[256,1024]{1,0:T(8,128)(2,1)}, bf16[256,1024]{1,0:T(8,128)(2,1)}, bf16[256,1024]{1,0:T(8,128)(2,1)}) custom-call(s32[2]{0:T(128)S(1)} %pad_add_fusion.2.place_ref, bf16[512,4096]{1,0:T(8,128)(2,1)} %weight_ref.1, bf16[512,4096]{1,0:T(8,128)(2,1)} %weight_ref.1, bf16[512,4096]{1,0:T(8,128)(2,1)} %weight_ref.1), custom_call_target="tpu_custom_call" | custom-call | tf_op jit(solution)/shard_map/pick_weights/pallas_call | solution.py:93
  6.8 3.1 %collective-permute-done.refs_1_ = bf16[1024,128]{1,0:T(8,128)(2,1)S(1)} collective-permute-done((bf16[1024,128]{1,0:T(8,128)(2,1)S(1)}, bf16[1024,128]{1,0:T(8,128)(2,1)S(1)}, u32[]{:S(2)}, u32[]{:S(2)}) %collective-permute-start) | collective-permute-done | bytes 262176 | tf_op jit(solution)/shard_map/ppermute | solution.py:54
  11.5 2.5 %collective-permute-start.1 = (bf16[2048,128]{1,0:T(8,128)(2,1)}, bf16[2048,128]{1,0:T(8,128)(2,1)S(1)}, u32[]{:S(2)}, u32[]{:S(2)}) collective-permute-start(bf16[2048,128]{1,0:T(8,128)(2,1)} %stack.40.refs_2_), channel_id=1, source_target_pairs={{0,64},{32,96},{64,128},{96,160},{128,192},{160,224},{192,0},{224,... | collective-permute-start | bytes 1572872 | tf_op jit(solution)/shard_map/ppermute | solution.py:50
  14.0 1.5 collective-permute-start.5
  15.5 2.7 %collective-permute-start.6 = (bf16[256,1024]{1,0:T(8,128)(2,1)}, bf16[256,1024]{1,0:T(8,128)(2,1)S(1)}, u32[]{:S(2)}, u32[]{:S(2)}) collective-permute-start(bf16[256,1024]{1,0:T(8,128)(2,1)} %get-tuple-element.51), channel_id=1, source_target_pairs={{0,4},{2,6},{4,0},{6,2},{8,12},{10,14},{12,8},{14,10},{16,20},{18,... | collective-permute-start | bytes 1572872 | tf_op jit(solution)/shard_map/ppermute | solution.py:40
  18.2 1.4 collective-permute-start.7
  21.2 5.1 %attend.3 = (f32[4,512,256]{2,1,0:T(8,128)S(1)}, f32[4,512,128]{2,1,0:T(8,128)S(1)}) custom-call(s32[3]{0:T(128)S(1)} %pad_add_fusion.1.refs_0_, bf16[512,512]{1,0:T(8,128)(2,1)S(1)} %copy-done.3, bf16[2048,128]{1,0:T(8,128)(2,1)} %stack.40.refs_2_), custom_call_target="tpu_custom_call" | custom-call | flops 1073741824 | bytes 4194304 | tf_op jit(solution)/shard_map/attend/pallas_call | solution.py:201
  26.4 1.9 collective-permute-start.3
  28.5 7.7 %attend.4 = (f32[4,512,256]{2,1,0:T(8,128)S(1)}, f32[4,512,128]{2,1,0:T(8,128)S(1)}) custom-call(s32[3]{0:T(128)S(1)} %pad_add_fusion.1.refs_0_, bf16[512,512]{1,0:T(8,128)(2,1)S(1)} %copy-done.3, bf16[2048,128]{1,0:T(8,128)(2,1)S(1)} %collective-permute-done.1.message_ref.refs_2_, bf16[2048,128]{1,0:T(8,128)(2,1)S(1)} %collective-permute-done.2.message_ref.refs_3_, ...), custom_call_target="tpu_custom_call" | custom-call | flops 2147483648 | bytes 4194304 | tf_op jit(solution)/shard_map/attend/pallas_call | solution.py:201
  36.2 3.9 %collective-permute-done.6.refs_1_.fetched_ref = bf16[256,1024]{1,0:T(8,128)(2,1)S(1)} collective-permute-done((bf16[256,1024]{1,0:T(8,128)(2,1)}, bf16[256,1024]{1,0:T(8,128)(2,1)S(1)}, u32[]{:S(2)}, u32[]{:S(2)}) %collective-permute-start.6) | collective-permute-done | bytes 524320 | tf_op jit(solution)/shard_map/ppermute | solution.py:40
  40.3 4.8 %attend.5 = (bf16[672,512]{1,0:T(8,128)(2,1)S(1)}, bf16[592,512]{1,0:T(8,128)(2,1)S(1)}) custom-call(s32[3]{0:T(128)S(1)} %pad_add_fusion.1.refs_0_, bf16[512,512]{1,0:T(8,128)(2,1)S(1)} %copy-done.3, bf16[1024,128]{1,0:T(8,128)(2,1)S(1)} %collective-permute-done.3.refs_2_, bf16[1024,128]{1,0:T(8,128)(2,1)S(1)} %collective-permute-done.4.refs_3_, ...), custom_call_target="tpu_custom_call" | custom-call | flops 1073741824 | bytes 4194304 | tf_op jit(solution)/shard_map/attend/pallas_call | solution.py:201
  45.2 1.4 collective-permute-start.8
  46.6 1.9 collective-permute-start.10
  48.5 15.8 %collective-permute-done.8.message_ref.refs_0_.refs_1_.h1 = bf16[672,512]{1,0:T(8,128)(2,1)S(1)} collective-permute-done((bf16[672,512]{1,0:T(8,128)(2,1)S(1)}, bf16[672,512]{1,0:T(8,128)(2,1)S(1)}, u32[]{:S(2)}, u32[]{:S(2)}) %collective-permute-start.8) | collective-permute-done | bytes 688160 | tf_op jit(solution)/shard_map/ppermute | solution.py:40
  64.7 3.2 %collective-permute-start.11 = (bf16[256,512]{1,0:T(8,128)(2,1)S(1)}, bf16[256,512]{1,0:T(8,128)(2,1)S(1)}, u32[]{:S(2)}, u32[]{:S(2)}) collective-permute-start(bf16[256,512]{1,0:T(8,128)(2,1)S(1)} %forward.7), channel_id=1, source_target_pairs={{0,6},{2,0},{4,2},{6,4},{8,14},{10,8},{12,10},{14,12},{16,22},{18,... | collective-permute-start | bytes 786440 | tf_op jit(solution)/shard_map/ppermute | solution.py:40
  67.9 4.2 %project_near.1.refs_0_ = f32[4,128,1024]{2,1,0:T(8,128)S(1)} custom-call(s32[3]{0:T(128)S(1)} %pad_add_fusion.place_ref, bf16[672,512]{1,0:T(8,128)(2,1)S(1)} %get-tuple-element.65.own_ref, bf16[512,4096]{1,0:T(8,128)(2,1)} %weight_ref.1, bf16[672,512]{1,0:T(8,128)(2,1)S(1)} %collective-permute-done.8.message_ref.refs_0_.refs_1_.h1, ...), custom_call_target="tpu_custom_call" | custom-call | flops 1 | bytes 1 | tf_op jit(solution)/shard_map/project_near/pallas_call | solution.py:252
  73.1 2.4 %collective-permute-done.9.upper_ref.refs_2_.h2 = bf16[336,512]{1,0:T(8,128)(2,1)S(1)} collective-permute-done((bf16[336,512]{1,0:T(8,128)(2,1)S(1)}, bf16[336,512]{1,0:T(8,128)(2,1)S(1)}, u32[]{:S(2)}, u32[]{:S(2)}) %collective-permute-start.9) | collective-permute-done | bytes 344096 | tf_op jit(solution)/shard_map/ppermute | solution.py:40
  75.5 1.3 project_far.1
  76.8 3.3 %collective-permute-start.13 = (bf16[128,512]{1,0:T(8,128)(2,1)S(1)}, bf16[128,512]{1,0:T(8,128)(2,1)S(1)}, u32[]{:S(2)}, u32[]{:S(2)}) collective-permute-start(bf16[128,512]{1,0:T(8,128)(2,1)S(1)} %get-tuple-element.75), channel_id=1, source_target_pairs={{0,8},{2,10},{4,12},{6,14},{8,16},{10,18},{12,20},{14,22},{16,24},... | collective-permute-start | bytes 393224 | tf_op jit(solution)/shard_map/ppermute | solution.py:45
  80.1 2.8 %collective-permute-start.14 = (bf16[128,512]{1,0:T(8,128)(2,1)S(1)}, bf16[128,512]{1,0:T(8,128)(2,1)S(1)}, u32[]{:S(2)}, u32[]{:S(2)}) collective-permute-start(bf16[128,512]{1,0:T(8,128)(2,1)S(1)} %get-tuple-element.76), channel_id=1, source_target_pairs={{0,24},{2,26},{4,28},{6,30},{8,0},{10,2},{12,4},{14,6},{16,8},{18,... | collective-permute-start | bytes 393224 | tf_op jit(solution)/shard_map/ppermute | solution.py:45
  83.7 2.4 %collective-permute-done.13 = bf16[128,512]{1,0:T(8,128)(2,1)S(1)} collective-permute-done((bf16[128,512]{1,0:T(8,128)(2,1)S(1)}, bf16[128,512]{1,0:T(8,128)(2,1)S(1)}, u32[]{:S(2)}, u32[]{:S(2)}) %collective-permute-start.13) | collective-permute-done | bytes 131104 | tf_op jit(solution)/shard_map/ppermute | solution.py:45
  86.1 3.2 %collective-permute-done.14 = bf16[128,512]{1,0:T(8,128)(2,1)S(1)} collective-permute-done((bf16[128,512]{1,0:T(8,128)(2,1)S(1)}, bf16[128,512]{1,0:T(8,128)(2,1)S(1)}, u32[]{:S(2)}, u32[]{:S(2)}) %collective-permute-start.14) | collective-permute-done | bytes 131104 | tf_op jit(solution)/shard_map/ppermute | solution.py:45
  89.4 2.9 %collective-permute-start.16 = (bf16[128,1024]{1,0:T(8,128)(2,1)S(1)}, bf16[128,1024]{1,0:T(8,128)(2,1)S(1)}, u32[]{:S(2)}, u32[]{:S(2)}) collective-permute-start(bf16[128,1024]{1,0:T(8,128)(2,1)S(1)} %pad_maximum_fusion.1), channel_id=1, source_target_pairs={{0,24},{2,26},{4,28},{6,30},{8,0},{10,2},{12,4},{14,6},{16,8},{18,... | collective-permute-start | bytes 786440 | tf_op jit(solution)/shard_map/ppermute | solution.py:45
  93.2 9.9 %collective-permute-done.16.s2 = bf16[128,1024]{1,0:T(8,128)(2,1)S(1)} collective-permute-done((bf16[128,1024]{1,0:T(8,128)(2,1)S(1)}, bf16[128,1024]{1,0:T(8,128)(2,1)S(1)}, u32[]{:S(2)}, u32[]{:S(2)}) %collective-permute-start.16) | collective-permute-done | bytes 262176 | tf_op jit(solution)/shard_map/ppermute | solution.py:45
  103.2 2.5 %collective-permute-done.15.s1 = bf16[128,1024]{1,0:T(8,128)(2,1)S(1)} collective-permute-done((bf16[128,1024]{1,0:T(8,128)(2,1)S(1)}, bf16[128,1024]{1,0:T(8,128)(2,1)S(1)}, u32[]{:S(2)}, u32[]{:S(2)}) %collective-permute-start.15) | collective-permute-done | bytes 262176 | tf_op jit(solution)/shard_map/ppermute | solution.py:45
  107.2 3.0 %collective-permute-start.18 = (bf16[32,1024]{1,0:T(8,128)(2,1)S(1)}, bf16[32,1024]{1,0:T(8,128)(2,1)S(1)}, u32[]{:S(2)}, u32[]{:S(2)}) collective-permute-start(bf16[32,1024]{1,0:T(8,128)(2,1)S(1)} %get-tuple-element.82), channel_id=1, source_target_pairs={{0,16},{2,18},{4,20},{6,22},{8,24},{10,26},{12,28},{14,30},{16,0},... | collective-permute-start | bytes 196616 | tf_op jit(solution)/shard_map/ppermute | solution.py:45
  110.2 4.0 %collective-permute-start.19 = (bf16[32,1024]{1,0:T(8,128)(2,1)S(1)}, bf16[32,1024]{1,0:T(8,128)(2,1)S(1)}, u32[]{:S(2)}, u32[]{:S(2)}) collective-permute-start(bf16[32,1024]{1,0:T(8,128)(2,1)S(1)} %get-tuple-element.83), channel_id=1, source_target_pairs={{0,24},{2,26},{4,28},{6,30},{8,0},{10,2},{12,4},{14,6},{16,8},{18,... | collective-permute-start | bytes 196616 | tf_op jit(solution)/shard_map/ppermute | solution.py:45
  116.9 10.5 %all_to_all.10.piece_ref = bf16[4,64,1024]{2,1,0:T(8,128)(2,1)S(1)} all-to-all(bf16[4,64,1024]{2,1,0:T(8,128)(2,1)S(1)} %by_columns.1), channel_id=1, replica_groups={{0,2,4,6},{8,10,12,14},{16,18,20,22},{24,26,28,30},{1,3,5,7},{9,11,13,1..., dimensions={0} | all-to-all | bytes 1048576 | tf_op jit(solution)/shard_map/all_to_all | solution.py:605
  129.3 8.0 %collective-permute-done.21.refs_2_ = bf16[32,4096]{1,0:T(8,128)(2,1)S(1)} collective-permute-done((bf16[32,4096]{1,0:T(8,128)(2,1)S(1)}, bf16[32,4096]{1,0:T(8,128)(2,1)S(1)}, u32[]{:S(2)}, u32[]{:S(2)}) %collective-permute-start.21) | collective-permute-done | bytes 262176 | tf_op jit(solution)/shard_map/ppermute | solution.py:50
  139.4 3.1 %collective-permute-start.23 = (bf16[32,4096]{1,0:T(8,128)(2,1)S(1)}, bf16[32,4096]{1,0:T(8,128)(2,1)S(1)}, u32[]{:S(2)}, u32[]{:S(2)}) collective-permute-start(bf16[32,4096]{1,0:T(8,128)(2,1)S(1)} %collective-permute-done.20.refs_1_), channel_id=1, source_target_pairs={{0,64},{32,96},{64,128},{96,160},{128,192},{160,224},{192,0},{224,... | collective-permute-start | bytes 786440 | tf_op jit(solution)/shard_map/ppermute | solution.py:50
  145.7 2.8 %collective-permute-done.25.refs_6_ = bf16[32,4096]{1,0:T(8,128)(2,1)S(1)} collective-permute-done((bf16[32,4096]{1,0:T(8,128)(2,1)S(1)}, bf16[32,4096]{1,0:T(8,128)(2,1)S(1)}, u32[]{:S(2)}, u32[]{:S(2)}) %collective-permute-start.25) | collective-permute-done | bytes 262176 | tf_op jit(solution)/shard_map/ppermute | solution.py:50
  148.6 3.3 %collective-permute-done.26.refs_7_ = bf16[32,4096]{1,0:T(8,128)(2,1)S(1)} collective-permute-done((bf16[32,4096]{1,0:T(8,128)(2,1)S(1)}, bf16[32,4096]{1,0:T(8,128)(2,1)S(1)}, u32[]{:S(2)}, u32[]{:S(2)}) %collective-permute-start.26) | collective-permute-done | bytes 262176 | tf_op jit(solution)/shard_map/ppermute | solution.py:54
  151.8 1.9 run_expert.1
  154.1 3.0 %collective-permute-start.27 = (bf16[32,4096]{1,0:T(8,128)(2,1)S(1)}, bf16[32,4096]{1,0:T(8,128)(2,1)S(1)}, u32[]{:S(2)}, u32[]{:S(2)}) collective-permute-start(bf16[32,4096]{1,0:T(8,128)(2,1)S(1)} %get-tuple-element.89), channel_id=1, source_target_pairs={{0,64},{32,96},{64,128},{96,160},{128,192},{160,224},{192,0},{224,... | collective-permute-start | bytes 786440 | tf_op jit(solution)/shard_map/ppermute | solution.py:50
  157.2 2.0 collective-permute-start.32
  159.2 2.0 %collective-permute-done.28 = bf16[32,4096]{1,0:T(8,128)(2,1)S(1)} collective-permute-done((bf16[32,4096]{1,0:T(8,128)(2,1)S(1)}, bf16[32,4096]{1,0:T(8,128)(2,1)S(1)}, u32[]{:S(2)}, u32[]{:S(2)}) %collective-permute-start.28) | collective-permute-done | bytes 262176 | tf_op jit(solution)/shard_map/ppermute | solution.py:54
  161.9 2.0 collective-permute-done.31
  163.9 3.6 %collective-permute-done.32 = bf16[32,4096]{1,0:T(8,128)(2,1)S(1)} collective-permute-done((bf16[32,4096]{1,0:T(8,128)(2,1)S(1)}, bf16[32,4096]{1,0:T(8,128)(2,1)S(1)}, u32[]{:S(2)}, u32[]{:S(2)}) %collective-permute-start.32) | collective-permute-done | bytes 262176 | tf_op jit(solution)/shard_map/ppermute | solution.py:50
  167.7 2.7 %collective-permute-done.29 = bf16[32,4096]{1,0:T(8,128)(2,1)S(1)} collective-permute-done((bf16[32,4096]{1,0:T(8,128)(2,1)S(1)}, bf16[32,4096]{1,0:T(8,128)(2,1)S(1)}, u32[]{:S(2)}, u32[]{:S(2)}) %collective-permute-start.29) | collective-permute-done | bytes 262176 | tf_op jit(solution)/shard_map/ppermute | solution.py:50
  170.6 4.9 %collective-permute-done.33 = bf16[32,4096]{1,0:T(8,128)(2,1)S(1)} collective-permute-done((bf16[32,4096]{1,0:T(8,128)(2,1)S(1)}, bf16[32,4096]{1,0:T(8,128)(2,1)S(1)}, u32[]{:S(2)}, u32[]{:S(2)}) %collective-permute-start.33) | collective-permute-done | bytes 262176 | tf_op jit(solution)/shard_map/ppermute | solution.py:54
  175.5 2.7 %collective-permute-done.30 = bf16[32,4096]{1,0:T(8,128)(2,1)S(1)} collective-permute-done((bf16[32,4096]{1,0:T(8,128)(2,1)S(1)}, bf16[32,4096]{1,0:T(8,128)(2,1)S(1)}, u32[]{:S(2)}, u32[]{:S(2)}) %collective-permute-start.30) | collective-permute-done | bytes 262176 | tf_op jit(solution)/shard_map/ppermute | solution.py:50
  178.3 2.7 %collective-permute-start.36 = (bf16[8,4096]{1,0:T(8,128)(2,1)S(1)}, bf16[8,4096]{1,0:T(8,128)(2,1)S(1)}, u32[]{:S(2)}, u32[]{:S(2)}) collective-permute-start(bf16[8,4096]{1,0:T(8,128)(2,1)S(1)} %get-tuple-element.96), channel_id=1, source_target_pairs={{0,8},{2,10},{4,12},{6,14},{8,16},{10,18},{12,20},{14,22},{16,24},... | collective-permute-start | bytes 196616 | tf_op jit(solution)/shard_map/ppermute | solution.py:45
  181.0 3.6 %collective-permute-start.35 = (bf16[8,4096]{1,0:T(8,128)(2,1)S(1)}, bf16[8,4096]{1,0:T(8,128)(2,1)S(1)}, u32[]{:S(2)}, u32[]{:S(2)}) collective-permute-start(bf16[8,4096]{1,0:T(8,128)(2,1)S(1)} %get-tuple-element.97), channel_id=1, source_target_pairs={{0,16},{2,18},{4,20},{6,22},{8,24},{10,26},{12,28},{14,30},{16,0},... | collective-permute-start | bytes 196616 | tf_op jit(solution)/shard_map/ppermute | solution.py:45
  185.6 3.6 %collective-permute-done.35.refs_2_ = bf16[8,4096]{1,0:T(8,128)(2,1)S(1)} collective-permute-done((bf16[8,4096]{1,0:T(8,128)(2,1)S(1)}, bf16[8,4096]{1,0:T(8,128)(2,1)S(1)}, u32[]{:S(2)}, u32[]{:S(2)}) %collective-permute-start.35) | collective-permute-done | bytes 65568 | tf_op jit(solution)/shard_map/ppermute | solution.py:45
  189.2 1.8 collective-permute-done.34.refs_1_
  191.9 3.4 %all-to-all-start.1 = ((bf16[4,8,4096]{2,1,0:T(8,128)(2,1)}), bf16[4,8,4096]{2,1,0:T(8,128)(2,1)S(1)}, u32[]{:S(2)}, u32[]{:S(2)}) async-start(bf16[4,8,4096]{2,1,0:T(8,128)(2,1)} %regroup.1), calls=%async_computation.1 | async-start | bytes 524288 | tf_op jit(solution)/shard_map/all_to_all | solution.py:605
  196.0 5.9 %all-to-all-done.1.refs_0_ = bf16[4,8,4096]{2,1,0:T(8,128)(2,1)S(1)} async-done(((bf16[4,8,4096]{2,1,0:T(8,128)(2,1)}), bf16[4,8,4096]{2,1,0:T(8,128)(2,1)S(1)}, u32[]{:S(2)}, u32[]{:S(2)}) %all-to-all-start.1) | async-done | bytes 262176 | tf_op jit(solution)/shard_map/all_to_all | solution.py:605
  (81 shorter events, 24.1 us)
Async XLA Ops:
  1.6 8.3 %collective-permute-start = (bf16[1024,128]{1,0:T(8,128)(2,1)S(1)}, bf16[1024,128]{1,0:T(8,128)(2,1)S(1)}, u32[]{:S(2)}, u32[]{:S(2)}) collective-permute-start(bf16[1024,128]{1,0:T(8,128)(2,1)S(1)} %pick_head.1.refs_0_), channel_id=1, source_target_pairs={{0,32},{32,0},{64,96},{96,64},{128,160},{160,128},{192,224},{224,1... | collective-permute-start | bytes 786440 | tf_op jit(solution)/shard_map/ppermute | solution.py:54
  3.7 16.7 %copy-start.4 = (bf16[32,4096]{1,0:T(8,128)(2,1)S(1)}, bf16[32,4096]{1,0:T(8,128)(2,1)}, u32[]{:S(2)}) copy-start(bf16[32,4096]{1,0:T(8,128)(2,1)} %hidden_ref.1) | copy-start | bytes 786436
  3.7 16.7 %copy-start.5 = (s32[32,8]{0,1:T(8,128)S(1)}, s32[32,8]{0,1:T(8,128)}, u32[]{:S(2)}) copy-start(s32[32,8]{0,1:T(8,128)} %param.18) | copy-start | bytes 3076
  3.7 17.5 %copy-start.3 = (bf16[512,512]{1,0:T(8,128)(2,1)S(1)}, bf16[512,512]{1,0:T(8,128)(2,1)}, u32[]{:S(2)}) copy-start(bf16[512,512]{1,0:T(8,128)(2,1)} %refs_1_.7) | copy-start | bytes 1572868
  10.8 15.5 %collective-permute-start.2 = (bf16[2048,128]{1,0:T(8,128)(2,1)}, bf16[2048,128]{1,0:T(8,128)(2,1)S(1)}, u32[]{:S(2)}, u32[]{:S(2)}) collective-permute-start(bf16[2048,128]{1,0:T(8,128)(2,1)} %stack.40.refs_2_), channel_id=1, source_target_pairs={{0,192},{32,224},{64,0},{96,32},{128,64},{160,96},{192,128},{224,1... | collective-permute-start | bytes 1572872 | tf_op jit(solution)/shard_map/ppermute | solution.py:50
  11.5 14.8 %collective-permute-start.1 = (bf16[2048,128]{1,0:T(8,128)(2,1)}, bf16[2048,128]{1,0:T(8,128)(2,1)S(1)}, u32[]{:S(2)}, u32[]{:S(2)}) collective-permute-start(bf16[2048,128]{1,0:T(8,128)(2,1)} %stack.40.refs_2_), channel_id=1, source_target_pairs={{0,64},{32,96},{64,128},{96,160},{128,192},{160,224},{192,0},{224,... | collective-permute-start | bytes 1572872 | tf_op jit(solution)/shard_map/ppermute | solution.py:50
  14.0 22.2 %collective-permute-start.5 = (bf16[256,1024]{1,0:T(8,128)(2,1)}, bf16[256,1024]{1,0:T(8,128)(2,1)S(1)}, u32[]{:S(2)}, u32[]{:S(2)}) collective-permute-start(bf16[256,1024]{1,0:T(8,128)(2,1)} %get-tuple-element.50), channel_id=1, source_target_pairs={{0,2},{2,4},{4,6},{6,0},{8,10},{10,12},{12,14},{14,8},{16,18},{18,... | collective-permute-start | bytes 1572872 | tf_op jit(solution)/shard_map/ppermute | solution.py:40
  15.5 24.6 %collective-permute-start.6 = (bf16[256,1024]{1,0:T(8,128)(2,1)}, bf16[256,1024]{1,0:T(8,128)(2,1)S(1)}, u32[]{:S(2)}, u32[]{:S(2)}) collective-permute-start(bf16[256,1024]{1,0:T(8,128)(2,1)} %get-tuple-element.51), channel_id=1, source_target_pairs={{0,4},{2,6},{4,0},{6,2},{8,12},{10,14},{12,8},{14,10},{16,20},{18,... | collective-permute-start | bytes 1572872 | tf_op jit(solution)/shard_map/ppermute | solution.py:40
  18.2 21.9 %collective-permute-start.7 = (bf16[256,1024]{1,0:T(8,128)(2,1)}, bf16[256,1024]{1,0:T(8,128)(2,1)S(1)}, u32[]{:S(2)}, u32[]{:S(2)}) collective-permute-start(bf16[256,1024]{1,0:T(8,128)(2,1)} %get-tuple-element.52), channel_id=1, source_target_pairs={{0,6},{2,0},{4,2},{6,4},{8,14},{10,8},{12,10},{14,12},{16,22},{18,... | collective-permute-start | bytes 1572872 | tf_op jit(solution)/shard_map/ppermute | solution.py:40
  26.4 13.7 %collective-permute-start.3 = (bf16[1024,128]{1,0:T(8,128)(2,1)S(1)}, bf16[1024,128]{1,0:T(8,128)(2,1)S(1)}, u32[]{:S(2)}, u32[]{:S(2)}) collective-permute-start(bf16[1024,128]{1,0:T(8,128)(2,1)S(1)} %forward.4), channel_id=1, source_target_pairs={{0,64},{32,96},{64,128},{96,160},{128,192},{160,224},{192,0},{224,... | collective-permute-start | bytes 786440 | tf_op jit(solution)/shard_map/ppermute | solution.py:50
  28.3 11.8 %collective-permute-start.4 = (bf16[1024,128]{1,0:T(8,128)(2,1)S(1)}, bf16[1024,128]{1,0:T(8,128)(2,1)S(1)}, u32[]{:S(2)}, u32[]{:S(2)}) collective-permute-start(bf16[1024,128]{1,0:T(8,128)(2,1)S(1)} %forward.5), channel_id=1, source_target_pairs={{0,192},{32,224},{64,0},{96,32},{128,64},{160,96},{192,128},{224,1... | collective-permute-start | bytes 786440 | tf_op jit(solution)/shard_map/ppermute | solution.py:50
  40.2 27.7 %collective-permute-start.12 = (bf16[768,1024]{1,0:T(8,128)(2,1)S(1)}, bf16[768,1024]{1,0:T(8,128)(2,1)S(1)}, u32[]{:S(2)}, u32[]{:S(2)}) collective-permute-start(bf16[768,1024]{1,0:T(8,128)(2,1)S(1)} %stack.41), channel_id=1, source_target_pairs={{0,1},{1,0},{2,3},{3,2},{4,5},{5,4},{6,7},{7,6},{8,9},{9,8},{10,11... | collective-permute-start | bytes 4718600 | tf_op jit(solution)/shard_map/ppermute | solution.py:58
  45.2 19.1 %collective-permute-start.8 = (bf16[672,512]{1,0:T(8,128)(2,1)S(1)}, bf16[672,512]{1,0:T(8,128)(2,1)S(1)}, u32[]{:S(2)}, u32[]{:S(2)}) collective-permute-start(bf16[672,512]{1,0:T(8,128)(2,1)S(1)} %get-tuple-element.65.own_ref), channel_id=1, source_target_pairs={{0,2},{2,4},{4,6},{6,0},{8,10},{10,12},{12,14},{14,8},{16,18},{18,... | collective-permute-start | bytes 2064392 | tf_op jit(solution)/shard_map/ppermute | solution.py:40
  46.6 18.1 %collective-permute-start.10 = (bf16[592,512]{1,0:T(8,128)(2,1)S(1)}, bf16[592,512]{1,0:T(8,128)(2,1)S(1)}, u32[]{:S(2)}, u32[]{:S(2)}) collective-permute-start(bf16[592,512]{1,0:T(8,128)(2,1)S(1)} %get-tuple-element.66), channel_id=1, source_target_pairs={{0,6},{2,0},{4,2},{6,4},{8,14},{10,8},{12,10},{14,12},{16,22},{18,... | collective-permute-start | bytes 1818632 | tf_op jit(solution)/shard_map/ppermute | solution.py:40
  64.3 11.2 %collective-permute-start.9 = (bf16[336,512]{1,0:T(8,128)(2,1)S(1)}, bf16[336,512]{1,0:T(8,128)(2,1)S(1)}, u32[]{:S(2)}, u32[]{:S(2)}) collective-permute-start(bf16[336,512]{1,0:T(8,128)(2,1)S(1)} %forward.6), channel_id=1, source_target_pairs={{0,2},{2,4},{4,6},{6,0},{8,10},{10,12},{12,14},{14,8},{16,18},{18,... | collective-permute-start | bytes 1032200 | tf_op jit(solution)/shard_map/ppermute | solution.py:40
  64.7 8.4 %collective-permute-start.11 = (bf16[256,512]{1,0:T(8,128)(2,1)S(1)}, bf16[256,512]{1,0:T(8,128)(2,1)S(1)}, u32[]{:S(2)}, u32[]{:S(2)}) collective-permute-start(bf16[256,512]{1,0:T(8,128)(2,1)S(1)} %forward.7), channel_id=1, source_target_pairs={{0,6},{2,0},{4,2},{6,4},{8,14},{10,8},{12,10},{14,12},{16,22},{18,... | collective-permute-start | bytes 786440 | tf_op jit(solution)/shard_map/ppermute | solution.py:40
  76.8 9.3 %collective-permute-start.13 = (bf16[128,512]{1,0:T(8,128)(2,1)S(1)}, bf16[128,512]{1,0:T(8,128)(2,1)S(1)}, u32[]{:S(2)}, u32[]{:S(2)}) collective-permute-start(bf16[128,512]{1,0:T(8,128)(2,1)S(1)} %get-tuple-element.75), channel_id=1, source_target_pairs={{0,8},{2,10},{4,12},{6,14},{8,16},{10,18},{12,20},{14,22},{16,24},... | collective-permute-start | bytes 393224 | tf_op jit(solution)/shard_map/ppermute | solution.py:45
  80.1 9.1 %collective-permute-start.14 = (bf16[128,512]{1,0:T(8,128)(2,1)S(1)}, bf16[128,512]{1,0:T(8,128)(2,1)S(1)}, u32[]{:S(2)}, u32[]{:S(2)}) collective-permute-start(bf16[128,512]{1,0:T(8,128)(2,1)S(1)} %get-tuple-element.76), channel_id=1, source_target_pairs={{0,24},{2,26},{4,28},{6,30},{8,0},{10,2},{12,4},{14,6},{16,8},{18,... | collective-permute-start | bytes 393224 | tf_op jit(solution)/shard_map/ppermute | solution.py:45
  89.4 13.8 %collective-permute-start.16 = (bf16[128,1024]{1,0:T(8,128)(2,1)S(1)}, bf16[128,1024]{1,0:T(8,128)(2,1)S(1)}, u32[]{:S(2)}, u32[]{:S(2)}) collective-permute-start(bf16[128,1024]{1,0:T(8,128)(2,1)S(1)} %pad_maximum_fusion.1), channel_id=1, source_target_pairs={{0,24},{2,26},{4,28},{6,30},{8,0},{10,2},{12,4},{14,6},{16,8},{18,... | collective-permute-start | bytes 786440 | tf_op jit(solution)/shard_map/ppermute | solution.py:45
  92.3 13.4 %collective-permute-start.15 = (bf16[128,1024]{1,0:T(8,128)(2,1)S(1)}, bf16[128,1024]{1,0:T(8,128)(2,1)S(1)}, u32[]{:S(2)}, u32[]{:S(2)}) collective-permute-start(bf16[128,1024]{1,0:T(8,128)(2,1)S(1)} %pad_maximum_fusion), channel_id=1, source_target_pairs={{0,8},{2,10},{4,12},{6,14},{8,16},{10,18},{12,20},{14,22},{16,24},... | collective-permute-start | bytes 786440 | tf_op jit(solution)/shard_map/ppermute | solution.py:45
  105.7 21.7 %copy-start.6 = (f32[4096]{0:T(1024)S(1)}, f32[4096]{0:T(1024)}, u32[]{:S(2)}) copy-start(f32[4096]{0:T(1024)} %param.17) | copy-start | bytes 49156
  105.7 46.1 %copy-start.1 = (bf16[1,4096,192]{1,2,0:T(8,128)(2,1)S(1)}, bf16[1,4096,192]{1,2,0:T(8,128)(2,1)}, u32[]{:S(2)}) copy-start(bf16[1,4096,192]{1,2,0:T(8,128)(2,1)} %param.22) | copy-start | bytes 4718596
  105.7 46.1 %copy-start.2 = (bf16[1,192,4096]{2,1,0:T(8,128)(2,1)S(1)}, bf16[1,192,4096]{2,1,0:T(8,128)(2,1)}, u32[]{:S(2)}) copy-start(bf16[1,192,4096]{2,1,0:T(8,128)(2,1)} %param.23) | copy-start | bytes 4718596
  106.6 45.2 %copy-start = (bf16[1,4096,192]{1,2,0:T(8,128)(2,1)S(1)}, bf16[1,4096,192]{1,2,0:T(8,128)(2,1)}, u32[]{:S(2)}) copy-start(bf16[1,4096,192]{1,2,0:T(8,128)(2,1)} %param.21) | copy-start | bytes 4718596
  106.6 8.4 %collective-permute-start.17 = (bf16[32,1024]{1,0:T(8,128)(2,1)S(1)}, bf16[32,1024]{1,0:T(8,128)(2,1)S(1)}, u32[]{:S(2)}, u32[]{:S(2)}) collective-permute-start(bf16[32,1024]{1,0:T(8,128)(2,1)S(1)} %get-tuple-element.81), channel_id=1, source_target_pairs={{0,8},{2,10},{4,12},{6,14},{8,16},{10,18},{12,20},{14,22},{16,24},... | collective-permute-start | bytes 196616 | tf_op jit(solution)/shard_map/ppermute | solution.py:45
  107.2 8.3 %collective-permute-start.18 = (bf16[32,1024]{1,0:T(8,128)(2,1)S(1)}, bf16[32,1024]{1,0:T(8,128)(2,1)S(1)}, u32[]{:S(2)}, u32[]{:S(2)}) collective-permute-start(bf16[32,1024]{1,0:T(8,128)(2,1)S(1)} %get-tuple-element.82), channel_id=1, source_target_pairs={{0,16},{2,18},{4,20},{6,22},{8,24},{10,26},{12,28},{14,30},{16,0},... | collective-permute-start | bytes 196616 | tf_op jit(solution)/shard_map/ppermute | solution.py:45
  110.2 6.6 %collective-permute-start.19 = (bf16[32,1024]{1,0:T(8,128)(2,1)S(1)}, bf16[32,1024]{1,0:T(8,128)(2,1)S(1)}, u32[]{:S(2)}, u32[]{:S(2)}) collective-permute-start(bf16[32,1024]{1,0:T(8,128)(2,1)S(1)} %get-tuple-element.83), channel_id=1, source_target_pairs={{0,24},{2,26},{4,28},{6,30},{8,0},{10,2},{12,4},{14,6},{16,8},{18,... | collective-permute-start | bytes 196616 | tf_op jit(solution)/shard_map/ppermute | solution.py:45
  128.2 9.1 %collective-permute-start.21 = (bf16[32,4096]{1,0:T(8,128)(2,1)S(1)}, bf16[32,4096]{1,0:T(8,128)(2,1)S(1)}, u32[]{:S(2)}, u32[]{:S(2)}) collective-permute-start(bf16[32,4096]{1,0:T(8,128)(2,1)S(1)} %get-tuple-element.87.refs_0_), channel_id=1, source_target_pairs={{0,64},{32,96},{64,128},{96,160},{128,192},{160,224},{192,0},{224,... | collective-permute-start | bytes 786440 | tf_op jit(solution)/shard_map/ppermute | solution.py:50
  128.7 10.7 %collective-permute-start.20 = (bf16[32,4096]{1,0:T(8,128)(2,1)S(1)}, bf16[32,4096]{1,0:T(8,128)(2,1)S(1)}, u32[]{:S(2)}, u32[]{:S(2)}) collective-permute-start(bf16[32,4096]{1,0:T(8,128)(2,1)S(1)} %get-tuple-element.87.refs_0_), channel_id=1, source_target_pairs={{0,32},{32,0},{64,96},{96,64},{128,160},{160,128},{192,224},{224,1... | collective-permute-start | bytes 786440 | tf_op jit(solution)/shard_map/ppermute | solution.py:54
  137.3 6.4 %collective-permute-start.24 = (bf16[32,4096]{1,0:T(8,128)(2,1)S(1)}, bf16[32,4096]{1,0:T(8,128)(2,1)S(1)}, u32[]{:S(2)}, u32[]{:S(2)}) collective-permute-start(bf16[32,4096]{1,0:T(8,128)(2,1)S(1)} %collective-permute-done.21.refs_2_), channel_id=1, source_target_pairs={{0,64},{32,96},{64,128},{96,160},{128,192},{160,224},{192,0},{224,... | collective-permute-start | bytes 786440 | tf_op jit(solution)/shard_map/ppermute | solution.py:50
  138.2 7.6 %collective-permute-start.22 = (bf16[32,4096]{1,0:T(8,128)(2,1)S(1)}, bf16[32,4096]{1,0:T(8,128)(2,1)S(1)}, u32[]{:S(2)}, u32[]{:S(2)}) collective-permute-start(bf16[32,4096]{1,0:T(8,128)(2,1)S(1)} %get-tuple-element.87.refs_0_), channel_id=1, source_target_pairs={{0,192},{32,224},{64,0},{96,32},{128,64},{160,96},{192,128},{224,1... | collective-permute-start | bytes 786440 | tf_op jit(solution)/shard_map/ppermute | solution.py:50
  139.3 9.2 %collective-permute-start.25 = (bf16[32,4096]{1,0:T(8,128)(2,1)S(1)}, bf16[32,4096]{1,0:T(8,128)(2,1)S(1)}, u32[]{:S(2)}, u32[]{:S(2)}) collective-permute-start(bf16[32,4096]{1,0:T(8,128)(2,1)S(1)} %collective-permute-done.20.refs_1_), channel_id=1, source_target_pairs={{0,192},{32,224},{64,0},{96,32},{128,64},{160,96},{192,128},{224,1... | collective-permute-start | bytes 786440 | tf_op jit(solution)/shard_map/ppermute | solution.py:50
  139.4 9.1 %collective-permute-start.23 = (bf16[32,4096]{1,0:T(8,128)(2,1)S(1)}, bf16[32,4096]{1,0:T(8,128)(2,1)S(1)}, u32[]{:S(2)}, u32[]{:S(2)}) collective-permute-start(bf16[32,4096]{1,0:T(8,128)(2,1)S(1)} %collective-permute-done.20.refs_1_), channel_id=1, source_target_pairs={{0,64},{32,96},{64,128},{96,160},{128,192},{160,224},{192,0},{224,... | collective-permute-start | bytes 786440 | tf_op jit(solution)/shard_map/ppermute | solution.py:50
  143.7 8.2 %collective-permute-start.26 = (bf16[32,4096]{1,0:T(8,128)(2,1)S(1)}, bf16[32,4096]{1,0:T(8,128)(2,1)S(1)}, u32[]{:S(2)}, u32[]{:S(2)}) collective-permute-start(bf16[32,4096]{1,0:T(8,128)(2,1)S(1)} %collective-permute-done.24.refs_5_), channel_id=1, source_target_pairs={{0,32},{32,0},{64,96},{96,64},{128,160},{160,128},{192,224},{224,1... | collective-permute-start | bytes 786440 | tf_op jit(solution)/shard_map/ppermute | solution.py:54
  153.8 7.5 %collective-permute-start.28 = (bf16[32,4096]{1,0:T(8,128)(2,1)S(1)}, bf16[32,4096]{1,0:T(8,128)(2,1)S(1)}, u32[]{:S(2)}, u32[]{:S(2)}) collective-permute-start(bf16[32,4096]{1,0:T(8,128)(2,1)S(1)} %get-tuple-element.92), channel_id=1, source_target_pairs={{0,32},{32,0},{64,96},{96,64},{128,160},{160,128},{192,224},{224,1... | collective-permute-start | bytes 786440 | tf_op jit(solution)/shard_map/ppermute | solution.py:54
  154.1 16.4 %collective-permute-start.27 = (bf16[32,4096]{1,0:T(8,128)(2,1)S(1)}, bf16[32,4096]{1,0:T(8,128)(2,1)S(1)}, u32[]{:S(2)}, u32[]{:S(2)}) collective-permute-start(bf16[32,4096]{1,0:T(8,128)(2,1)S(1)} %get-tuple-element.89), channel_id=1, source_target_pairs={{0,64},{32,96},{64,128},{96,160},{128,192},{160,224},{192,0},{224,... | collective-permute-start | bytes 786440 | tf_op jit(solution)/shard_map/ppermute | solution.py:50
  157.2 6.7 %collective-permute-start.31 = (bf16[32,4096]{1,0:T(8,128)(2,1)S(1)}, bf16[32,4096]{1,0:T(8,128)(2,1)S(1)}, u32[]{:S(2)}, u32[]{:S(2)}) collective-permute-start(bf16[32,4096]{1,0:T(8,128)(2,1)S(1)} %get-tuple-element.94), channel_id=1, source_target_pairs={{0,64},{32,96},{64,128},{96,160},{128,192},{160,224},{192,0},{224,... | collective-permute-start | bytes 786440 | tf_op jit(solution)/shard_map/ppermute | solution.py:50
  157.2 10.3 %collective-permute-start.32 = (bf16[32,4096]{1,0:T(8,128)(2,1)S(1)}, bf16[32,4096]{1,0:T(8,128)(2,1)S(1)}, u32[]{:S(2)}, u32[]{:S(2)}) collective-permute-start(bf16[32,4096]{1,0:T(8,128)(2,1)S(1)} %get-tuple-element.95), channel_id=1, source_target_pairs={{0,192},{32,224},{64,0},{96,32},{128,64},{160,96},{192,128},{224,1... | collective-permute-start | bytes 786440 | tf_op jit(solution)/shard_map/ppermute | solution.py:50
  161.3 9.1 %collective-permute-start.29 = (bf16[32,4096]{1,0:T(8,128)(2,1)S(1)}, bf16[32,4096]{1,0:T(8,128)(2,1)S(1)}, u32[]{:S(2)}, u32[]{:S(2)}) collective-permute-start(bf16[32,4096]{1,0:T(8,128)(2,1)S(1)} %add_convert_fusion.3), channel_id=1, source_target_pairs={{0,192},{32,224},{64,0},{96,32},{128,64},{160,96},{192,128},{224,1... | collective-permute-start | bytes 786440 | tf_op jit(solution)/shard_map/ppermute | solution.py:50
  167.6 7.9 %collective-permute-start.33 = (bf16[32,4096]{1,0:T(8,128)(2,1)S(1)}, bf16[32,4096]{1,0:T(8,128)(2,1)S(1)}, u32[]{:S(2)}, u32[]{:S(2)}) collective-permute-start(bf16[32,4096]{1,0:T(8,128)(2,1)S(1)} %add_convert_fusion.1), channel_id=1, source_target_pairs={{0,32},{32,0},{64,96},{96,64},{128,160},{160,128},{192,224},{224,1... | collective-permute-start | bytes 786440 | tf_op jit(solution)/shard_map/ppermute | solution.py:54
  170.5 24.8 %copy-start.7 = (s32[32,8]{0,1:T(8,128)S(1)}, s32[32,8]{0,1:T(8,128)}, u32[]{:S(2)}) copy-start(s32[32,8]{0,1:T(8,128)} %param.19) | copy-start | bytes 3076
  170.5 7.7 %collective-permute-start.30 = (bf16[32,4096]{1,0:T(8,128)(2,1)S(1)}, bf16[32,4096]{1,0:T(8,128)(2,1)S(1)}, u32[]{:S(2)}, u32[]{:S(2)}) collective-permute-start(bf16[32,4096]{1,0:T(8,128)(2,1)S(1)} %add_convert_fusion.2), channel_id=1, source_target_pairs={{0,192},{32,224},{64,0},{96,32},{128,64},{160,96},{192,128},{224,1... | collective-permute-start | bytes 786440 | tf_op jit(solution)/shard_map/ppermute | solution.py:50
  178.3 7.3 %collective-permute-start.36 = (bf16[8,4096]{1,0:T(8,128)(2,1)S(1)}, bf16[8,4096]{1,0:T(8,128)(2,1)S(1)}, u32[]{:S(2)}, u32[]{:S(2)}) collective-permute-start(bf16[8,4096]{1,0:T(8,128)(2,1)S(1)} %get-tuple-element.96), channel_id=1, source_target_pairs={{0,8},{2,10},{4,12},{6,14},{8,16},{10,18},{12,20},{14,22},{16,24},... | collective-permute-start | bytes 196616 | tf_op jit(solution)/shard_map/ppermute | solution.py:45
  181.0 8.2 %collective-permute-start.35 = (bf16[8,4096]{1,0:T(8,128)(2,1)S(1)}, bf16[8,4096]{1,0:T(8,128)(2,1)S(1)}, u32[]{:S(2)}, u32[]{:S(2)}) collective-permute-start(bf16[8,4096]{1,0:T(8,128)(2,1)S(1)} %get-tuple-element.97), channel_id=1, source_target_pairs={{0,16},{2,18},{4,20},{6,22},{8,24},{10,26},{12,28},{14,30},{16,0},... | collective-permute-start | bytes 196616 | tf_op jit(solution)/shard_map/ppermute | solution.py:45
  184.6 6.3 %collective-permute-start.34 = (bf16[8,4096]{1,0:T(8,128)(2,1)S(1)}, bf16[8,4096]{1,0:T(8,128)(2,1)S(1)}, u32[]{:S(2)}, u32[]{:S(2)}) collective-permute-start(bf16[8,4096]{1,0:T(8,128)(2,1)S(1)} %get-tuple-element.98), channel_id=1, source_target_pairs={{0,24},{2,26},{4,28},{6,30},{8,0},{10,2},{12,4},{14,6},{16,8},{18,... | collective-permute-start | bytes 196616 | tf_op jit(solution)/shard_map/ppermute | solution.py:45
  191.9 10.1 %all-to-all-start.1 = ((bf16[4,8,4096]{2,1,0:T(8,128)(2,1)}), bf16[4,8,4096]{2,1,0:T(8,128)(2,1)S(1)}, u32[]{:S(2)}, u32[]{:S(2)}) async-start(bf16[4,8,4096]{2,1,0:T(8,128)(2,1)} %regroup.1), calls=%async_computation.1 | async-start | bytes 524288 | tf_op jit(solution)/shard_map/all_to_all | solution.py:605

commit v5 on v3

--- a/solution.py
+++ b/solution.py
@@ -48,6 +48,15 @@
 def shift_y(a, d):
     pairs = [(y * 2 + k, (y + d) % N_Y * 2 + k) for y in range(N_Y) for k in range(2)]
     return lax.ppermute(a, "ctx", pairs)
+
+
+def turn_y(a, d):
+    pairs = []
+    for core in range(2):
+        for y in range(N_Y):
+            to = (y + (d if core == 0 else -d)) % N_Y
+            pairs += [((y * 2 + k) * 2 + core, (to * 2 + k) * 2 + core) for k in range(2)]
+    return lax.ppermute(a, ("ctx", "rep"), pairs)
 
 
 def swap_l(a):
@@ -609,11 +618,11 @@
     own, swapped, below, above, below_swapped, below_two, above_swapped, far = parts
     got_far = swap_l(far)
     got_below_swapped = swap_l(below_swapped)
-    got_above_swapped = shift_y(above_swapped, 1)
-    got_two = shift_y(add(below_two, got_far), -1)
-    got_above = shift_y(above, 1)
+    got_above_swapped = turn_y(above_swapped, 1)
+    got_two = turn_y(add(below_two, got_far), -1)
+    got_above = turn_y(above, 1)
     got_swapped = swap_l(add(swapped, got_above_swapped))
-    got_below = shift_y(add(below, got_two, got_below_swapped), -1)
+    got_below = turn_y(add(below, got_two, got_below_swapped), -1)
     return add(own, got_above, got_below, got_swapped)
 
 
@@ -702,11 +711,11 @@
     by_z = [send[0]] + [shift_z(send[d], d) for d in range(1, N_Z)]
     block, mixed = join_columns(exchange_x(by_columns(by_z, mixed)), norm_gain.reshape(1, D))
     swapped = swap_l(block)
-    below = shift_y(block, 1)
-    above = shift_y(block, -1)
-    below_two = shift_y(below, 1)
+    below = turn_y(block, 1)
+    above = turn_y(block, -1)
+    below_two = turn_y(below, 1)
     below_swapped = swap_l(below)
-    above_swapped = shift_y(swapped, -1)
+    above_swapped = turn_y(swapped, -1)
     far = swap_l(below_two)
     parts = run_expert(
         [block, swapped, below, above, below_swapped, below_two, above_swapped, far],

time: 202 us -> 203 us (level)
    ppermute x12 -> x4, waiting for transfers between devices: 25.1 us -> 0.01 us  [shift_y(): return lax.ppermute(a, 'ctx', pairs)]
    ppermute x0 -> x8, waiting for transfers between devices: none -> 23.3 us  [turn_y(): return lax.ppermute(a, ('ctx', 'rep'), pairs)]
    ppermute x12 -> x4, starting transfers between devices: 11.5 us -> 5.63 us  [shift_y(): return lax.ppermute(a, 'ctx', pairs)]
    ppermute x0 -> x8, starting transfers between devices: none -> 4.56 us  [turn_y(): return lax.ppermute(a, ('ctx', 'rep'), pairs)]
    ppermute x7, waiting for transfers between devices: 13.8 us -> 18.1 us  [swap_l(): return lax.ppermute(a, 'ctx', [(i, i ^ 1) for i in range(2 * N_Y)])]
  transfers between devices with their start and end apart: 38 -> 38, of which waited for: 24 -> 25; matrix products, arithmetic and copies ran while one was open for 1% -> 1% of each run, Pallas kernels for 13% -> 14%
where the time goes in v5:
time: 203 us; the launch traced here: 201 us
  waiting for transfers between devices  93.6 us (46%)
  starting transfers between devices  58.2 us (29%)
  Pallas kernels  35.6 us (18%)
  blocking collectives  10.5 us (5%)
    ppermute x10, starting transfers between devices, shift_z(): return lax.ppermute(a, 'exp', pairs)  26.1 us
    ppermute x10, waiting for transfers between devices, shift_z(): return lax.ppermute(a, 'exp', pairs)  24.4 us
    ppermute x8, waiting for transfers between devices, turn_y(): return lax.ppermute(a, ('ctx', 'rep'), pairs)  23.3 us
    ppermute x7, waiting for transfers between devices, shift_x(): return lax.ppermute(a, 'exp', pairs)  21.8 us
    ppermute x7, waiting for transfers between devices, swap_l(): return lax.ppermute(a, 'ctx', [(i, i ^ 1) for i in range(2 * N_Y)])  18.1 us
    pallas_call x3, Pallas kernels, attend(): pl.pallas_call(kernel, in_specs=[pl.BlockSpec(memory_space=SMEM)] + [whol...  17.6 us
    ppermute x7, starting transfers between devices, shift_x(): return lax.ppermute(a, 'exp', pairs)  12.5 us
    all_to_all x1, blocking collectives, exchange_x(): return lax.all_to_all(a, 'exp', 0, 0, tiled=True, axis_index_groups=groups)  10.5 us
  transfers between devices with their start and end apart: 38, of which 25 were waited for; matrix products, arithmetic and copies ran while one was open for 1% of the time, Pallas kernels for 14%

profile of v5, /device:TPU:24, one launch (start us, length us, event | category | flops | bytes accessed | tf_op | source)
XLA Modules:
  0.0 201.2 jit_solution(12921204195802534619)
XLA Ops:
  1.6 2.0 collective-permute-start
  3.7 3.1 %pick_weights.1 = (bf16[256,1024]{1,0:T(8,128)(2,1)}, bf16[256,1024]{1,0:T(8,128)(2,1)}, bf16[256,1024]{1,0:T(8,128)(2,1)}) custom-call(s32[2]{0:T(128)S(1)} %pad_add_fusion.2.place_ref, bf16[512,4096]{1,0:T(8,128)(2,1)} %weight_ref.1, bf16[512,4096]{1,0:T(8,128)(2,1)} %weight_ref.1, bf16[512,4096]{1,0:T(8,128)(2,1)} %weight_ref.1), custom_call_target="tpu_custom_call" | custom-call | tf_op jit(solution)/shard_map/pick_weights/pallas_call | solution.py:102
  6.8 3.1 %collective-permute-done.refs_1_ = bf16[1024,128]{1,0:T(8,128)(2,1)S(1)} collective-permute-done((bf16[1024,128]{1,0:T(8,128)(2,1)S(1)}, bf16[1024,128]{1,0:T(8,128)(2,1)S(1)}, u32[]{:S(2)}, u32[]{:S(2)}) %collective-permute-start) | collective-permute-done | bytes 262176 | tf_op jit(solution)/shard_map/ppermute | solution.py:63
  10.8 2.5 %collective-permute-start.1 = (bf16[2048,128]{1,0:T(8,128)(2,1)S(1)}, bf16[2048,128]{1,0:T(8,128)(2,1)}, u32[]{:S(2)}, u32[]{:S(2)}) collective-permute-start(bf16[2048,128]{1,0:T(8,128)(2,1)S(1)} %stack.40.refs_2_), channel_id=1, source_target_pairs={{0,64},{32,96},{64,128},{96,160},{128,192},{160,224},{192,0},{224,... | collective-permute-start | bytes 1572872 | tf_op jit(solution)/shard_map/ppermute | solution.py:50
  13.3 1.5 collective-permute-start.5
  14.8 2.7 %collective-permute-start.6 = (bf16[256,1024]{1,0:T(8,128)(2,1)}, bf16[256,1024]{1,0:T(8,128)(2,1)S(1)}, u32[]{:S(2)}, u32[]{:S(2)}) collective-permute-start(bf16[256,1024]{1,0:T(8,128)(2,1)} %get-tuple-element.51), channel_id=1, source_target_pairs={{0,4},{2,6},{4,0},{6,2},{8,12},{10,14},{12,8},{14,10},{16,20},{18,... | collective-permute-start | bytes 1572872 | tf_op jit(solution)/shard_map/ppermute | solution.py:40
  17.5 1.4 collective-permute-start.7
  20.5 4.6 %attend.3 = (f32[4,512,256]{2,1,0:T(8,128)S(1)}, f32[4,512,128]{2,1,0:T(8,128)S(1)}) custom-call(s32[3]{0:T(128)S(1)} %pad_add_fusion.1.refs_0_, bf16[512,512]{1,0:T(8,128)(2,1)S(1)} %copy-done.3, bf16[2048,128]{1,0:T(8,128)(2,1)S(1)} %stack.40.refs_2_), custom_call_target="tpu_custom_call" | custom-call | flops 1073741824 | bytes 4194304 | tf_op jit(solution)/shard_map/attend/pallas_call | solution.py:210
  26.1 2.3 %collective-permute-start.3 = (bf16[1024,128]{1,0:T(8,128)(2,1)S(1)}, bf16[1024,128]{1,0:T(8,128)(2,1)S(1)}, u32[]{:S(2)}, u32[]{:S(2)}) collective-permute-start(bf16[1024,128]{1,0:T(8,128)(2,1)S(1)} %slice.30), channel_id=1, source_target_pairs={{0,64},{32,96},{64,128},{96,160},{128,192},{160,224},{192,0},{224,... | collective-permute-start | bytes 786440 | tf_op jit(solution)/shard_map/ppermute | solution.py:50
  28.4 8.2 %attend.4 = (f32[4,512,256]{2,1,0:T(8,128)S(1)}, f32[4,512,128]{2,1,0:T(8,128)S(1)}) custom-call(s32[3]{0:T(128)S(1)} %pad_add_fusion.1.refs_0_, bf16[512,512]{1,0:T(8,128)(2,1)S(1)} %copy-done.3, bf16[2048,128]{1,0:T(8,128)(2,1)} %collective-permute-done.1.refs_2_, bf16[2048,128]{1,0:T(8,128)(2,1)S(1)} %collective-permute-done.2.refs_3_, ...), custom_call_target="tpu_custom_call" | custom-call | flops 2147483648 | bytes 4194304 | tf_op jit(solution)/shard_map/attend/pallas_call | solution.py:210
  36.7 2.7 %collective-permute-done.6.refs_1_.fetched_ref = bf16[256,1024]{1,0:T(8,128)(2,1)S(1)} collective-permute-done((bf16[256,1024]{1,0:T(8,128)(2,1)}, bf16[256,1024]{1,0:T(8,128)(2,1)S(1)}, u32[]{:S(2)}, u32[]{:S(2)}) %collective-permute-start.6) | collective-permute-done | bytes 524320 | tf_op jit(solution)/shard_map/ppermute | solution.py:40
  39.6 4.8 %attend.5 = (bf16[672,512]{1,0:T(8,128)(2,1)S(1)}, bf16[592,512]{1,0:T(8,128)(2,1)S(1)}) custom-call(s32[3]{0:T(128)S(1)} %pad_add_fusion.1.refs_0_, bf16[512,512]{1,0:T(8,128)(2,1)S(1)} %copy-done.3, bf16[1024,128]{1,0:T(8,128)(2,1)S(1)} %collective-permute-done.3.refs_2_, bf16[1024,128]{1,0:T(8,128)(2,1)S(1)} %collective-permute-done.4.refs_3_, ...), custom_call_target="tpu_custom_call" | custom-call | flops 1073741824 | bytes 4194304 | tf_op jit(solution)/shard_map/attend/pallas_call | solution.py:210
  44.4 1.4 collective-permute-start.8
  45.8 1.9 collective-permute-start.10
  47.7 15.8 %collective-permute-done.8.message_ref.refs_0_.refs_1_.h1 = bf16[672,512]{1,0:T(8,128)(2,1)S(1)} collective-permute-done((bf16[672,512]{1,0:T(8,128)(2,1)S(1)}, bf16[672,512]{1,0:T(8,128)(2,1)S(1)}, u32[]{:S(2)}, u32[]{:S(2)}) %collective-permute-start.8) | collective-permute-done | bytes 688160 | tf_op jit(solution)/shard_map/ppermute | solution.py:40
  64.0 3.2 %collective-permute-start.11 = (bf16[256,512]{1,0:T(8,128)(2,1)S(1)}, bf16[256,512]{1,0:T(8,128)(2,1)S(1)}, u32[]{:S(2)}, u32[]{:S(2)}) collective-permute-start(bf16[256,512]{1,0:T(8,128)(2,1)S(1)} %forward.3), channel_id=1, source_target_pairs={{0,6},{2,0},{4,2},{6,4},{8,14},{10,8},{12,10},{14,12},{16,22},{18,... | collective-permute-start | bytes 786440 | tf_op jit(solution)/shard_map/ppermute | solution.py:40
  67.2 4.3 %project_near.1.refs_0_ = f32[4,128,1024]{2,1,0:T(8,128)S(1)} custom-call(s32[3]{0:T(128)S(1)} %pad_add_fusion.place_ref, bf16[672,512]{1,0:T(8,128)(2,1)S(1)} %get-tuple-element.65.own_ref, bf16[512,4096]{1,0:T(8,128)(2,1)} %weight_ref.1, bf16[672,512]{1,0:T(8,128)(2,1)S(1)} %collective-permute-done.8.message_ref.refs_0_.refs_1_.h1, ...), custom_call_target="tpu_custom_call" | custom-call | flops 1 | bytes 1 | tf_op jit(solution)/shard_map/project_near/pallas_call | solution.py:261
  72.3 2.4 %collective-permute-done.9.upper_ref.refs_2_.h2 = bf16[336,512]{1,0:T(8,128)(2,1)S(1)} collective-permute-done((bf16[336,512]{1,0:T(8,128)(2,1)S(1)}, bf16[336,512]{1,0:T(8,128)(2,1)S(1)}, u32[]{:S(2)}, u32[]{:S(2)}) %collective-permute-start.9) | collective-permute-done | bytes 344096 | tf_op jit(solution)/shard_map/ppermute | solution.py:40
  74.7 1.3 project_far.1
  76.1 3.4 %collective-permute-start.13 = (bf16[128,512]{1,0:T(8,128)(2,1)S(1)}, bf16[128,512]{1,0:T(8,128)(2,1)S(1)}, u32[]{:S(2)}, u32[]{:S(2)}) collective-permute-start(bf16[128,512]{1,0:T(8,128)(2,1)S(1)} %get-tuple-element.75), channel_id=1, source_target_pairs={{0,8},{2,10},{4,12},{6,14},{8,16},{10,18},{12,20},{14,22},{16,24},... | collective-permute-start | bytes 393224 | tf_op jit(solution)/shard_map/ppermute | solution.py:45
  79.4 2.7 %collective-permute-start.14 = (bf16[128,512]{1,0:T(8,128)(2,1)S(1)}, bf16[128,512]{1,0:T(8,128)(2,1)S(1)}, u32[]{:S(2)}, u32[]{:S(2)}) collective-permute-start(bf16[128,512]{1,0:T(8,128)(2,1)S(1)} %get-tuple-element.76), channel_id=1, source_target_pairs={{0,24},{2,26},{4,28},{6,30},{8,0},{10,2},{12,4},{14,6},{16,8},{18,... | collective-permute-start | bytes 393224 | tf_op jit(solution)/shard_map/ppermute | solution.py:45
  83.0 2.3 %collective-permute-done.13 = bf16[128,512]{1,0:T(8,128)(2,1)S(1)} collective-permute-done((bf16[128,512]{1,0:T(8,128)(2,1)S(1)}, bf16[128,512]{1,0:T(8,128)(2,1)S(1)}, u32[]{:S(2)}, u32[]{:S(2)}) %collective-permute-start.13) | collective-permute-done | bytes 131104 | tf_op jit(solution)/shard_map/ppermute | solution.py:45
  85.3 3.2 %collective-permute-done.14 = bf16[128,512]{1,0:T(8,128)(2,1)S(1)} collective-permute-done((bf16[128,512]{1,0:T(8,128)(2,1)S(1)}, bf16[128,512]{1,0:T(8,128)(2,1)S(1)}, u32[]{:S(2)}, u32[]{:S(2)}) %collective-permute-start.14) | collective-permute-done | bytes 131104 | tf_op jit(solution)/shard_map/ppermute | solution.py:45
  88.6 2.8 %collective-permute-start.16 = (bf16[128,1024]{1,0:T(8,128)(2,1)S(1)}, bf16[128,1024]{1,0:T(8,128)(2,1)S(1)}, u32[]{:S(2)}, u32[]{:S(2)}) collective-permute-start(bf16[128,1024]{1,0:T(8,128)(2,1)S(1)} %pad_maximum_fusion.1), channel_id=1, source_target_pairs={{0,24},{2,26},{4,28},{6,30},{8,0},{10,2},{12,4},{14,6},{16,8},{18,... | collective-permute-start | bytes 786440 | tf_op jit(solution)/shard_map/ppermute | solution.py:45
  92.5 9.8 %collective-permute-done.16.s2 = bf16[128,1024]{1,0:T(8,128)(2,1)S(1)} collective-permute-done((bf16[128,1024]{1,0:T(8,128)(2,1)S(1)}, bf16[128,1024]{1,0:T(8,128)(2,1)S(1)}, u32[]{:S(2)}, u32[]{:S(2)}) %collective-permute-start.16) | collective-permute-done | bytes 262176 | tf_op jit(solution)/shard_map/ppermute | solution.py:45
  102.2 2.0 collective-permute-done.15.s1
  105.1 1.4 collective-permute-start.17
  106.5 3.0 %collective-permute-start.18 = (bf16[32,1024]{1,0:T(8,128)(2,1)S(1)}, bf16[32,1024]{1,0:T(8,128)(2,1)S(1)}, u32[]{:S(2)}, u32[]{:S(2)}) collective-permute-start(bf16[32,1024]{1,0:T(8,128)(2,1)S(1)} %get-tuple-element.82), channel_id=1, source_target_pairs={{0,16},{2,18},{4,20},{6,22},{8,24},{10,26},{12,28},{14,30},{16,0},... | collective-permute-start | bytes 196616 | tf_op jit(solution)/shard_map/ppermute | solution.py:45
  109.5 4.0 %collective-permute-start.19 = (bf16[32,1024]{1,0:T(8,128)(2,1)S(1)}, bf16[32,1024]{1,0:T(8,128)(2,1)S(1)}, u32[]{:S(2)}, u32[]{:S(2)}) collective-permute-start(bf16[32,1024]{1,0:T(8,128)(2,1)S(1)} %get-tuple-element.83), channel_id=1, source_target_pairs={{0,24},{2,26},{4,28},{6,30},{8,0},{10,2},{12,4},{14,6},{16,8},{18,... | collective-permute-start | bytes 196616 | tf_op jit(solution)/shard_map/ppermute | solution.py:45
  113.5 1.8 collective-permute-done.18.refs_2_
  116.4 10.5 %all_to_all.10.piece_ref = bf16[4,64,1024]{2,1,0:T(8,128)(2,1)S(1)} all-to-all(bf16[4,64,1024]{2,1,0:T(8,128)(2,1)S(1)} %by_columns.1), channel_id=1, replica_groups={{0,2,4,6},{8,10,12,14},{16,18,20,22},{24,26,28,30},{1,3,5,7},{9,11,13,1..., dimensions={0} | all-to-all | bytes 1048576 | tf_op jit(solution)/shard_map/all_to_all | solution.py:614
  128.8 8.1 %collective-permute-done.21.refs_2_ = bf16[32,4096]{1,0:T(8,128)(2,1)S(1)} collective-permute-done((bf16[32,4096]{1,0:T(8,128)(2,1)S(1)}, bf16[32,4096]{1,0:T(8,128)(2,1)S(1)}, u32[]{:S(2)}, u32[]{:S(2)}) %collective-permute-start.21) | collective-permute-done | bytes 262176 | tf_op jit(solution)/shard_map/ppermute | solution.py:59
  136.9 2.0 %collective-permute-start.22 = (bf16[32,4096]{1,0:T(8,128)(2,1)S(1)}, bf16[32,4096]{1,0:T(8,128)(2,1)S(1)}, u32[]{:S(2)}, u32[]{:S(2)}) collective-permute-start(bf16[32,4096]{1,0:T(8,128)(2,1)S(1)} %get-tuple-element.87.refs_0_), channel_id=1, source_target_pairs={{0,192},{32,224},{64,0},{96,32},{128,64},{160,96},{192,128},{224,1... | collective-permute-start | bytes 786440 | tf_op jit(solution)/shard_map/ppermute | solution.py:59
  139.3 4.0 %collective-permute-done.24.refs_5_ = bf16[32,4096]{1,0:T(8,128)(2,1)S(1)} collective-permute-done((bf16[32,4096]{1,0:T(8,128)(2,1)S(1)}, bf16[32,4096]{1,0:T(8,128)(2,1)S(1)}, u32[]{:S(2)}, u32[]{:S(2)}) %collective-permute-start.24) | collective-permute-done | bytes 262176 | tf_op jit(solution)/shard_map/ppermute | solution.py:59
  145.3 2.7 %collective-permute-done.25.refs_6_ = bf16[32,4096]{1,0:T(8,128)(2,1)S(1)} collective-permute-done((bf16[32,4096]{1,0:T(8,128)(2,1)S(1)}, bf16[32,4096]{1,0:T(8,128)(2,1)S(1)}, u32[]{:S(2)}, u32[]{:S(2)}) %collective-permute-start.25) | collective-permute-done | bytes 262176 | tf_op jit(solution)/shard_map/ppermute | solution.py:59
  148.0 4.5 %collective-permute-done.26.refs_7_ = bf16[32,4096]{1,0:T(8,128)(2,1)S(1)} collective-permute-done((bf16[32,4096]{1,0:T(8,128)(2,1)S(1)}, bf16[32,4096]{1,0:T(8,128)(2,1)S(1)}, u32[]{:S(2)}, u32[]{:S(2)}) %collective-permute-start.26) | collective-permute-done | bytes 262176 | tf_op jit(solution)/shard_map/ppermute | solution.py:63
  152.6 1.9 run_expert.1
  154.7 1.4 collective-permute-start.27
  156.2 1.6 collective-permute-start.30
  157.8 3.3 %collective-permute-done.28 = bf16[32,4096]{1,0:T(8,128)(2,1)S(1)} collective-permute-done((bf16[32,4096]{1,0:T(8,128)(2,1)S(1)}, bf16[32,4096]{1,0:T(8,128)(2,1)S(1)}, u32[]{:S(2)}, u32[]{:S(2)}) %collective-permute-start.28) | collective-permute-done | bytes 262176 | tf_op jit(solution)/shard_map/ppermute | solution.py:63
  162.1 4.5 %collective-permute-done.32 = bf16[32,4096]{1,0:T(8,128)(2,1)S(1)} collective-permute-done((bf16[32,4096]{1,0:T(8,128)(2,1)S(1)}, bf16[32,4096]{1,0:T(8,128)(2,1)S(1)}, u32[]{:S(2)}, u32[]{:S(2)}) %collective-permute-start.32) | collective-permute-done | bytes 262176 | tf_op jit(solution)/shard_map/ppermute | solution.py:59
  167.1 1.8 collective-permute-done.29
  169.1 6.3 %collective-permute-done.33 = bf16[32,4096]{1,0:T(8,128)(2,1)S(1)} collective-permute-done((bf16[32,4096]{1,0:T(8,128)(2,1)S(1)}, bf16[32,4096]{1,0:T(8,128)(2,1)S(1)}, u32[]{:S(2)}, u32[]{:S(2)}) %collective-permute-start.33) | collective-permute-done | bytes 262176 | tf_op jit(solution)/shard_map/ppermute | solution.py:63
  176.8 3.7 %collective-permute-start.36 = (bf16[8,4096]{1,0:T(8,128)(2,1)S(1)}, bf16[8,4096]{1,0:T(8,128)(2,1)S(1)}, u32[]{:S(2)}, u32[]{:S(2)}) collective-permute-start(bf16[8,4096]{1,0:T(8,128)(2,1)S(1)} %get-tuple-element.96), channel_id=1, source_target_pairs={{0,8},{2,10},{4,12},{6,14},{8,16},{10,18},{12,20},{14,22},{16,24},... | collective-permute-start | bytes 196616 | tf_op jit(solution)/shard_map/ppermute | solution.py:45
  180.4 3.2 %collective-permute-start.35 = (bf16[8,4096]{1,0:T(8,128)(2,1)S(1)}, bf16[8,4096]{1,0:T(8,128)(2,1)S(1)}, u32[]{:S(2)}, u32[]{:S(2)}) collective-permute-start(bf16[8,4096]{1,0:T(8,128)(2,1)S(1)} %get-tuple-element.97), channel_id=1, source_target_pairs={{0,16},{2,18},{4,20},{6,22},{8,24},{10,26},{12,28},{14,30},{16,0},... | collective-permute-start | bytes 196616 | tf_op jit(solution)/shard_map/ppermute | solution.py:45
  184.7 4.0 %collective-permute-done.35.refs_2_ = bf16[8,4096]{1,0:T(8,128)(2,1)S(1)} collective-permute-done((bf16[8,4096]{1,0:T(8,128)(2,1)S(1)}, bf16[8,4096]{1,0:T(8,128)(2,1)S(1)}, u32[]{:S(2)}, u32[]{:S(2)}) %collective-permute-start.35) | collective-permute-done | bytes 65568 | tf_op jit(solution)/shard_map/ppermute | solution.py:45
  189.8 3.4 %all-to-all-start.1 = ((bf16[4,8,4096]{2,1,0:T(8,128)(2,1)}), bf16[4,8,4096]{2,1,0:T(8,128)(2,1)S(1)}, u32[]{:S(2)}, u32[]{:S(2)}) async-start(bf16[4,8,4096]{2,1,0:T(8,128)(2,1)} %regroup.1), calls=%async_computation.1 | async-start | bytes 524288 | tf_op jit(solution)/shard_map/all_to_all | solution.py:614
  193.9 5.9 %all-to-all-done.1.refs_0_ = bf16[4,8,4096]{2,1,0:T(8,128)(2,1)S(1)} async-done(((bf16[4,8,4096]{2,1,0:T(8,128)(2,1)}), bf16[4,8,4096]{2,1,0:T(8,128)(2,1)S(1)}, u32[]{:S(2)}, u32[]{:S(2)}) %all-to-all-start.1) | async-done | bytes 262176 | tf_op jit(solution)/shard_map/all_to_all | solution.py:614
  (81 shorter events, 21.0 us)
Async XLA Ops:
  1.6 8.3 %collective-permute-start = (bf16[1024,128]{1,0:T(8,128)(2,1)S(1)}, bf16[1024,128]{1,0:T(8,128)(2,1)S(1)}, u32[]{:S(2)}, u32[]{:S(2)}) collective-permute-start(bf16[1024,128]{1,0:T(8,128)(2,1)S(1)} %pick_head.1.refs_0_), channel_id=1, source_target_pairs={{0,32},{32,0},{64,96},{96,64},{128,160},{160,128},{192,224},{224,1... | collective-permute-start | bytes 786440 | tf_op jit(solution)/shard_map/ppermute | solution.py:63
  3.7 16.0 %copy-start.4 = (bf16[32,4096]{1,0:T(8,128)(2,1)S(1)}, bf16[32,4096]{1,0:T(8,128)(2,1)}, u32[]{:S(2)}) copy-start(bf16[32,4096]{1,0:T(8,128)(2,1)} %hidden_ref.1) | copy-start | bytes 786436
  3.7 16.0 %copy-start.5 = (s32[32,8]{0,1:T(8,128)S(1)}, s32[32,8]{0,1:T(8,128)}, u32[]{:S(2)}) copy-start(s32[32,8]{0,1:T(8,128)} %param.18) | copy-start | bytes 3076
  3.7 16.7 %copy-start.3 = (bf16[512,512]{1,0:T(8,128)(2,1)S(1)}, bf16[512,512]{1,0:T(8,128)(2,1)}, u32[]{:S(2)}) copy-start(bf16[512,512]{1,0:T(8,128)(2,1)} %refs_1_.7) | copy-start | bytes 1572868
  10.0 15.1 %collective-permute-start.2 = (bf16[2048,128]{1,0:T(8,128)(2,1)S(1)}, bf16[2048,128]{1,0:T(8,128)(2,1)S(1)}, u32[]{:S(2)}, u32[]{:S(2)}) collective-permute-start(bf16[2048,128]{1,0:T(8,128)(2,1)S(1)} %stack.40.refs_2_), channel_id=1, source_target_pairs={{0,192},{32,224},{64,0},{96,32},{128,64},{160,96},{192,128},{224,1... | collective-permute-start | bytes 1572872 | tf_op jit(solution)/shard_map/ppermute | solution.py:50
  10.8 14.3 %collective-permute-start.1 = (bf16[2048,128]{1,0:T(8,128)(2,1)S(1)}, bf16[2048,128]{1,0:T(8,128)(2,1)}, u32[]{:S(2)}, u32[]{:S(2)}) collective-permute-start(bf16[2048,128]{1,0:T(8,128)(2,1)S(1)} %stack.40.refs_2_), channel_id=1, source_target_pairs={{0,64},{32,96},{64,128},{96,160},{128,192},{160,224},{192,0},{224,... | collective-permute-start | bytes 1572872 | tf_op jit(solution)/shard_map/ppermute | solution.py:50
  13.3 23.3 %collective-permute-start.5 = (bf16[256,1024]{1,0:T(8,128)(2,1)}, bf16[256,1024]{1,0:T(8,128)(2,1)S(1)}, u32[]{:S(2)}, u32[]{:S(2)}) collective-permute-start(bf16[256,1024]{1,0:T(8,128)(2,1)} %get-tuple-element.50), channel_id=1, source_target_pairs={{0,2},{2,4},{4,6},{6,0},{8,10},{10,12},{12,14},{14,8},{16,18},{18,... | collective-permute-start | bytes 1572872 | tf_op jit(solution)/shard_map/ppermute | solution.py:40
  14.8 24.6 %collective-permute-start.6 = (bf16[256,1024]{1,0:T(8,128)(2,1)}, bf16[256,1024]{1,0:T(8,128)(2,1)S(1)}, u32[]{:S(2)}, u32[]{:S(2)}) collective-permute-start(bf16[256,1024]{1,0:T(8,128)(2,1)} %get-tuple-element.51), channel_id=1, source_target_pairs={{0,4},{2,6},{4,0},{6,2},{8,12},{10,14},{12,8},{14,10},{16,20},{18,... | collective-permute-start | bytes 1572872 | tf_op jit(solution)/shard_map/ppermute | solution.py:40
  17.5 21.9 %collective-permute-start.7 = (bf16[256,1024]{1,0:T(8,128)(2,1)}, bf16[256,1024]{1,0:T(8,128)(2,1)S(1)}, u32[]{:S(2)}, u32[]{:S(2)}) collective-permute-start(bf16[256,1024]{1,0:T(8,128)(2,1)} %get-tuple-element.52), channel_id=1, source_target_pairs={{0,6},{2,0},{4,2},{6,4},{8,14},{10,8},{12,10},{14,12},{16,22},{18,... | collective-permute-start | bytes 1572872 | tf_op jit(solution)/shard_map/ppermute | solution.py:40
  26.1 13.3 %collective-permute-start.3 = (bf16[1024,128]{1,0:T(8,128)(2,1)S(1)}, bf16[1024,128]{1,0:T(8,128)(2,1)S(1)}, u32[]{:S(2)}, u32[]{:S(2)}) collective-permute-start(bf16[1024,128]{1,0:T(8,128)(2,1)S(1)} %slice.30), channel_id=1, source_target_pairs={{0,64},{32,96},{64,128},{96,160},{128,192},{160,224},{192,0},{224,... | collective-permute-start | bytes 786440 | tf_op jit(solution)/shard_map/ppermute | solution.py:50
  28.4 11.0 %collective-permute-start.4 = (bf16[1024,128]{1,0:T(8,128)(2,1)S(1)}, bf16[1024,128]{1,0:T(8,128)(2,1)S(1)}, u32[]{:S(2)}, u32[]{:S(2)}) collective-permute-start(bf16[1024,128]{1,0:T(8,128)(2,1)S(1)} %slice.31), channel_id=1, source_target_pairs={{0,192},{32,224},{64,0},{96,32},{128,64},{160,96},{192,128},{224,1... | collective-permute-start | bytes 786440 | tf_op jit(solution)/shard_map/ppermute | solution.py:50
  39.5 27.7 %collective-permute-start.12 = (bf16[768,1024]{1,0:T(8,128)(2,1)S(1)}, bf16[768,1024]{1,0:T(8,128)(2,1)S(1)}, u32[]{:S(2)}, u32[]{:S(2)}) collective-permute-start(bf16[768,1024]{1,0:T(8,128)(2,1)S(1)} %stack.41), channel_id=1, source_target_pairs={{0,1},{1,0},{2,3},{3,2},{4,5},{5,4},{6,7},{7,6},{8,9},{9,8},{10,11... | collective-permute-start | bytes 4718600 | tf_op jit(solution)/shard_map/ppermute | solution.py:67
  44.4 19.1 %collective-permute-start.8 = (bf16[672,512]{1,0:T(8,128)(2,1)S(1)}, bf16[672,512]{1,0:T(8,128)(2,1)S(1)}, u32[]{:S(2)}, u32[]{:S(2)}) collective-permute-start(bf16[672,512]{1,0:T(8,128)(2,1)S(1)} %get-tuple-element.65.own_ref), channel_id=1, source_target_pairs={{0,2},{2,4},{4,6},{6,0},{8,10},{10,12},{12,14},{14,8},{16,18},{18,... | collective-permute-start | bytes 2064392 | tf_op jit(solution)/shard_map/ppermute | solution.py:40
  45.8 18.1 %collective-permute-start.10 = (bf16[592,512]{1,0:T(8,128)(2,1)S(1)}, bf16[592,512]{1,0:T(8,128)(2,1)S(1)}, u32[]{:S(2)}, u32[]{:S(2)}) collective-permute-start(bf16[592,512]{1,0:T(8,128)(2,1)S(1)} %get-tuple-element.66), channel_id=1, source_target_pairs={{0,6},{2,0},{4,2},{6,4},{8,14},{10,8},{12,10},{14,12},{16,22},{18,... | collective-permute-start | bytes 1818632 | tf_op jit(solution)/shard_map/ppermute | solution.py:40
  63.6 11.2 %collective-permute-start.9 = (bf16[336,512]{1,0:T(8,128)(2,1)S(1)}, bf16[336,512]{1,0:T(8,128)(2,1)S(1)}, u32[]{:S(2)}, u32[]{:S(2)}) collective-permute-start(bf16[336,512]{1,0:T(8,128)(2,1)S(1)} %forward.2), channel_id=1, source_target_pairs={{0,2},{2,4},{4,6},{6,0},{8,10},{10,12},{12,14},{14,8},{16,18},{18,... | collective-permute-start | bytes 1032200 | tf_op jit(solution)/shard_map/ppermute | solution.py:40
  64.0 8.4 %collective-permute-start.11 = (bf16[256,512]{1,0:T(8,128)(2,1)S(1)}, bf16[256,512]{1,0:T(8,128)(2,1)S(1)}, u32[]{:S(2)}, u32[]{:S(2)}) collective-permute-start(bf16[256,512]{1,0:T(8,128)(2,1)S(1)} %forward.3), channel_id=1, source_target_pairs={{0,6},{2,0},{4,2},{6,4},{8,14},{10,8},{12,10},{14,12},{16,22},{18,... | collective-permute-start | bytes 786440 | tf_op jit(solution)/shard_map/ppermute | solution.py:40
  76.1 9.2 %collective-permute-start.13 = (bf16[128,512]{1,0:T(8,128)(2,1)S(1)}, bf16[128,512]{1,0:T(8,128)(2,1)S(1)}, u32[]{:S(2)}, u32[]{:S(2)}) collective-permute-start(bf16[128,512]{1,0:T(8,128)(2,1)S(1)} %get-tuple-element.75), channel_id=1, source_target_pairs={{0,8},{2,10},{4,12},{6,14},{8,16},{10,18},{12,20},{14,22},{16,24},... | collective-permute-start | bytes 393224 | tf_op jit(solution)/shard_map/ppermute | solution.py:45
  79.4 9.1 %collective-permute-start.14 = (bf16[128,512]{1,0:T(8,128)(2,1)S(1)}, bf16[128,512]{1,0:T(8,128)(2,1)S(1)}, u32[]{:S(2)}, u32[]{:S(2)}) collective-permute-start(bf16[128,512]{1,0:T(8,128)(2,1)S(1)} %get-tuple-element.76), channel_id=1, source_target_pairs={{0,24},{2,26},{4,28},{6,30},{8,0},{10,2},{12,4},{14,6},{16,8},{18,... | collective-permute-start | bytes 393224 | tf_op jit(solution)/shard_map/ppermute | solution.py:45
  88.6 13.6 %collective-permute-start.16 = (bf16[128,1024]{1,0:T(8,128)(2,1)S(1)}, bf16[128,1024]{1,0:T(8,128)(2,1)S(1)}, u32[]{:S(2)}, u32[]{:S(2)}) collective-permute-start(bf16[128,1024]{1,0:T(8,128)(2,1)S(1)} %pad_maximum_fusion.1), channel_id=1, source_target_pairs={{0,24},{2,26},{4,28},{6,30},{8,0},{10,2},{12,4},{14,6},{16,8},{18,... | collective-permute-start | bytes 786440 | tf_op jit(solution)/shard_map/ppermute | solution.py:45
  91.5 12.7 %collective-permute-start.15 = (bf16[128,1024]{1,0:T(8,128)(2,1)S(1)}, bf16[128,1024]{1,0:T(8,128)(2,1)S(1)}, u32[]{:S(2)}, u32[]{:S(2)}) collective-permute-start(bf16[128,1024]{1,0:T(8,128)(2,1)S(1)} %pad_maximum_fusion), channel_id=1, source_target_pairs={{0,8},{2,10},{4,12},{6,14},{8,16},{10,18},{12,20},{14,22},{16,24},... | collective-permute-start | bytes 786440 | tf_op jit(solution)/shard_map/ppermute | solution.py:45
  104.2 22.7 %copy-start.6 = (f32[4096]{0:T(1024)S(1)}, f32[4096]{0:T(1024)}, u32[]{:S(2)}) copy-start(f32[4096]{0:T(1024)} %param.17) | copy-start | bytes 49156
  104.2 48.3 %copy-start.1 = (bf16[1,4096,192]{1,2,0:T(8,128)(2,1)S(1)}, bf16[1,4096,192]{1,2,0:T(8,128)(2,1)}, u32[]{:S(2)}) copy-start(bf16[1,4096,192]{1,2,0:T(8,128)(2,1)} %param.22) | copy-start | bytes 4718596
  104.2 48.3 %copy-start.2 = (bf16[1,192,4096]{2,1,0:T(8,128)(2,1)S(1)}, bf16[1,192,4096]{2,1,0:T(8,128)(2,1)}, u32[]{:S(2)}) copy-start(bf16[1,192,4096]{2,1,0:T(8,128)(2,1)} %param.23) | copy-start | bytes 4718596
  105.1 47.4 %copy-start = (bf16[1,4096,192]{1,2,0:T(8,128)(2,1)S(1)}, bf16[1,4096,192]{1,2,0:T(8,128)(2,1)}, u32[]{:S(2)}) copy-start(bf16[1,4096,192]{1,2,0:T(8,128)(2,1)} %param.21) | copy-start | bytes 4718596
  105.1 8.4 %collective-permute-start.17 = (bf16[32,1024]{1,0:T(8,128)(2,1)S(1)}, bf16[32,1024]{1,0:T(8,128)(2,1)S(1)}, u32[]{:S(2)}, u32[]{:S(2)}) collective-permute-start(bf16[32,1024]{1,0:T(8,128)(2,1)S(1)} %get-tuple-element.81), channel_id=1, source_target_pairs={{0,8},{2,10},{4,12},{6,14},{8,16},{10,18},{12,20},{14,22},{16,24},... | collective-permute-start | bytes 196616 | tf_op jit(solution)/shard_map/ppermute | solution.py:45
  106.5 8.8 %collective-permute-start.18 = (bf16[32,1024]{1,0:T(8,128)(2,1)S(1)}, bf16[32,1024]{1,0:T(8,128)(2,1)S(1)}, u32[]{:S(2)}, u32[]{:S(2)}) collective-permute-start(bf16[32,1024]{1,0:T(8,128)(2,1)S(1)} %get-tuple-element.82), channel_id=1, source_target_pairs={{0,16},{2,18},{4,20},{6,22},{8,24},{10,26},{12,28},{14,30},{16,0},... | collective-permute-start | bytes 196616 | tf_op jit(solution)/shard_map/ppermute | solution.py:45
  109.5 6.9 %collective-permute-start.19 = (bf16[32,1024]{1,0:T(8,128)(2,1)S(1)}, bf16[32,1024]{1,0:T(8,128)(2,1)S(1)}, u32[]{:S(2)}, u32[]{:S(2)}) collective-permute-start(bf16[32,1024]{1,0:T(8,128)(2,1)S(1)} %get-tuple-element.83), channel_id=1, source_target_pairs={{0,24},{2,26},{4,28},{6,30},{8,0},{10,2},{12,4},{14,6},{16,8},{18,... | collective-permute-start | bytes 196616 | tf_op jit(solution)/shard_map/ppermute | solution.py:45
  127.7 9.2 %collective-permute-start.21 = (bf16[32,4096]{1,0:T(8,128)(2,1)S(1)}, bf16[32,4096]{1,0:T(8,128)(2,1)S(1)}, u32[]{:S(2)}, u32[]{:S(2)}) collective-permute-start(bf16[32,4096]{1,0:T(8,128)(2,1)S(1)} %get-tuple-element.87.refs_0_), channel_id=1, source_target_pairs={{0,64},{32,96},{64,128},{96,160},{128,192},{160,224},{192,0},{224,... | collective-permute-start | bytes 786440 | tf_op jit(solution)/shard_map/ppermute | solution.py:59
  127.7 11.4 %collective-permute-start.20 = (bf16[32,4096]{1,0:T(8,128)(2,1)S(1)}, bf16[32,4096]{1,0:T(8,128)(2,1)S(1)}, u32[]{:S(2)}, u32[]{:S(2)}) collective-permute-start(bf16[32,4096]{1,0:T(8,128)(2,1)S(1)} %get-tuple-element.87.refs_0_), channel_id=1, source_target_pairs={{0,32},{32,0},{64,96},{96,64},{128,160},{160,128},{192,224},{224,1... | collective-permute-start | bytes 786440 | tf_op jit(solution)/shard_map/ppermute | solution.py:63
  136.9 6.4 %collective-permute-start.24 = (bf16[32,4096]{1,0:T(8,128)(2,1)S(1)}, bf16[32,4096]{1,0:T(8,128)(2,1)S(1)}, u32[]{:S(2)}, u32[]{:S(2)}) collective-permute-start(bf16[32,4096]{1,0:T(8,128)(2,1)S(1)} %collective-permute-done.21.refs_2_), channel_id=1, source_target_pairs={{0,64},{32,96},{64,128},{96,160},{128,192},{160,224},{192,0},{224,... | collective-permute-start | bytes 786440 | tf_op jit(solution)/shard_map/ppermute | solution.py:59
  136.9 7.6 %collective-permute-start.22 = (bf16[32,4096]{1,0:T(8,128)(2,1)S(1)}, bf16[32,4096]{1,0:T(8,128)(2,1)S(1)}, u32[]{:S(2)}, u32[]{:S(2)}) collective-permute-start(bf16[32,4096]{1,0:T(8,128)(2,1)S(1)} %get-tuple-element.87.refs_0_), channel_id=1, source_target_pairs={{0,192},{32,224},{64,0},{96,32},{128,64},{160,96},{192,128},{224,1... | collective-permute-start | bytes 786440 | tf_op jit(solution)/shard_map/ppermute | solution.py:59
  138.9 6.4 %collective-permute-start.23 = (bf16[32,4096]{1,0:T(8,128)(2,1)S(1)}, bf16[32,4096]{1,0:T(8,128)(2,1)S(1)}, u32[]{:S(2)}, u32[]{:S(2)}) collective-permute-start(bf16[32,4096]{1,0:T(8,128)(2,1)S(1)} %collective-permute-done.21.refs_2_), channel_id=1, source_target_pairs={{0,32},{32,0},{64,96},{96,64},{128,160},{160,128},{192,224},{224,1... | collective-permute-start | bytes 786440 | tf_op jit(solution)/shard_map/ppermute | solution.py:63
  139.1 8.9 %collective-permute-start.25 = (bf16[32,4096]{1,0:T(8,128)(2,1)S(1)}, bf16[32,4096]{1,0:T(8,128)(2,1)S(1)}, u32[]{:S(2)}, u32[]{:S(2)}) collective-permute-start(bf16[32,4096]{1,0:T(8,128)(2,1)S(1)} %collective-permute-done.20.refs_1_), channel_id=1, source_target_pairs={{0,192},{32,224},{64,0},{96,32},{128,64},{160,96},{192,128},{224,1... | collective-permute-start | bytes 786440 | tf_op jit(solution)/shard_map/ppermute | solution.py:59
  143.3 9.2 %collective-permute-start.26 = (bf16[32,4096]{1,0:T(8,128)(2,1)S(1)}, bf16[32,4096]{1,0:T(8,128)(2,1)S(1)}, u32[]{:S(2)}, u32[]{:S(2)}) collective-permute-start(bf16[32,4096]{1,0:T(8,128)(2,1)S(1)} %collective-permute-done.24.refs_5_), channel_id=1, source_target_pairs={{0,32},{32,0},{64,96},{96,64},{128,160},{160,128},{192,224},{224,1... | collective-permute-start | bytes 786440 | tf_op jit(solution)/shard_map/ppermute | solution.py:63
  154.5 6.6 %collective-permute-start.28 = (bf16[32,4096]{1,0:T(8,128)(2,1)S(1)}, bf16[32,4096]{1,0:T(8,128)(2,1)S(1)}, u32[]{:S(2)}, u32[]{:S(2)}) collective-permute-start(bf16[32,4096]{1,0:T(8,128)(2,1)S(1)} %get-tuple-element.92), channel_id=1, source_target_pairs={{0,32},{32,0},{64,96},{96,64},{128,160},{160,128},{192,224},{224,1... | collective-permute-start | bytes 786440 | tf_op jit(solution)/shard_map/ppermute | solution.py:63
  154.7 14.3 %collective-permute-start.27 = (bf16[32,4096]{1,0:T(8,128)(2,1)S(1)}, bf16[32,4096]{1,0:T(8,128)(2,1)S(1)}, u32[]{:S(2)}, u32[]{:S(2)}) collective-permute-start(bf16[32,4096]{1,0:T(8,128)(2,1)S(1)} %get-tuple-element.89), channel_id=1, source_target_pairs={{0,64},{32,96},{64,128},{96,160},{128,192},{160,224},{192,0},{224,... | collective-permute-start | bytes 786440 | tf_op jit(solution)/shard_map/ppermute | solution.py:59
  156.2 10.9 %collective-permute-start.30 = (bf16[32,4096]{1,0:T(8,128)(2,1)S(1)}, bf16[32,4096]{1,0:T(8,128)(2,1)S(1)}, u32[]{:S(2)}, u32[]{:S(2)}) collective-permute-start(bf16[32,4096]{1,0:T(8,128)(2,1)S(1)} %get-tuple-element.93), channel_id=1, source_target_pairs={{0,32},{32,0},{64,96},{96,64},{128,160},{160,128},{192,224},{224,1... | collective-permute-start | bytes 786440 | tf_op jit(solution)/shard_map/ppermute | solution.py:63
  157.8 8.7 %collective-permute-start.32 = (bf16[32,4096]{1,0:T(8,128)(2,1)S(1)}, bf16[32,4096]{1,0:T(8,128)(2,1)S(1)}, u32[]{:S(2)}, u32[]{:S(2)}) collective-permute-start(bf16[32,4096]{1,0:T(8,128)(2,1)S(1)} %get-tuple-element.95), channel_id=1, source_target_pairs={{0,64},{32,96},{64,128},{96,160},{128,192},{160,224},{192,0},{224,... | collective-permute-start | bytes 786440 | tf_op jit(solution)/shard_map/ppermute | solution.py:59
  161.2 7.7 %collective-permute-start.29 = (bf16[32,4096]{1,0:T(8,128)(2,1)S(1)}, bf16[32,4096]{1,0:T(8,128)(2,1)S(1)}, u32[]{:S(2)}, u32[]{:S(2)}) collective-permute-start(bf16[32,4096]{1,0:T(8,128)(2,1)S(1)} %add_convert_fusion.3), channel_id=1, source_target_pairs={{0,192},{32,224},{64,0},{96,32},{128,64},{160,96},{192,128},{224,1... | collective-permute-start | bytes 786440 | tf_op jit(solution)/shard_map/ppermute | solution.py:59
  166.6 8.8 %collective-permute-start.33 = (bf16[32,4096]{1,0:T(8,128)(2,1)S(1)}, bf16[32,4096]{1,0:T(8,128)(2,1)S(1)}, u32[]{:S(2)}, u32[]{:S(2)}) collective-permute-start(bf16[32,4096]{1,0:T(8,128)(2,1)S(1)} %add_convert_fusion.1), channel_id=1, source_target_pairs={{0,32},{32,0},{64,96},{96,64},{128,160},{160,128},{192,224},{224,1... | collective-permute-start | bytes 786440 | tf_op jit(solution)/shard_map/ppermute | solution.py:63
  168.9 24.3 %copy-start.7 = (s32[32,8]{0,1:T(8,128)S(1)}, s32[32,8]{0,1:T(8,128)}, u32[]{:S(2)}) copy-start(s32[32,8]{0,1:T(8,128)} %param.19) | copy-start | bytes 3076
  169.0 7.7 %collective-permute-start.31 = (bf16[32,4096]{1,0:T(8,128)(2,1)S(1)}, bf16[32,4096]{1,0:T(8,128)(2,1)S(1)}, u32[]{:S(2)}, u32[]{:S(2)}) collective-permute-start(bf16[32,4096]{1,0:T(8,128)(2,1)S(1)} %add_convert_fusion.2), channel_id=1, source_target_pairs={{0,192},{32,224},{64,0},{96,32},{128,64},{160,96},{192,128},{224,1... | collective-permute-start | bytes 786440 | tf_op jit(solution)/shard_map/ppermute | solution.py:59
  176.8 7.9 %collective-permute-start.36 = (bf16[8,4096]{1,0:T(8,128)(2,1)S(1)}, bf16[8,4096]{1,0:T(8,128)(2,1)S(1)}, u32[]{:S(2)}, u32[]{:S(2)}) collective-permute-start(bf16[8,4096]{1,0:T(8,128)(2,1)S(1)} %get-tuple-element.96), channel_id=1, source_target_pairs={{0,8},{2,10},{4,12},{6,14},{8,16},{10,18},{12,20},{14,22},{16,24},... | collective-permute-start | bytes 196616 | tf_op jit(solution)/shard_map/ppermute | solution.py:45
  180.4 8.2 %collective-permute-start.35 = (bf16[8,4096]{1,0:T(8,128)(2,1)S(1)}, bf16[8,4096]{1,0:T(8,128)(2,1)S(1)}, u32[]{:S(2)}, u32[]{:S(2)}) collective-permute-start(bf16[8,4096]{1,0:T(8,128)(2,1)S(1)} %get-tuple-element.97), channel_id=1, source_target_pairs={{0,16},{2,18},{4,20},{6,22},{8,24},{10,26},{12,28},{14,30},{16,0},... | collective-permute-start | bytes 196616 | tf_op jit(solution)/shard_map/ppermute | solution.py:45
  183.6 5.3 %collective-permute-start.34 = (bf16[8,4096]{1,0:T(8,128)(2,1)S(1)}, bf16[8,4096]{1,0:T(8,128)(2,1)S(1)}, u32[]{:S(2)}, u32[]{:S(2)}) collective-permute-start(bf16[8,4096]{1,0:T(8,128)(2,1)S(1)} %get-tuple-element.98), channel_id=1, source_target_pairs={{0,24},{2,26},{4,28},{6,30},{8,0},{10,2},{12,4},{14,6},{16,8},{18,... | collective-permute-start | bytes 196616 | tf_op jit(solution)/shard_map/ppermute | solution.py:45
  189.8 10.1 %all-to-all-start.1 = ((bf16[4,8,4096]{2,1,0:T(8,128)(2,1)}), bf16[4,8,4096]{2,1,0:T(8,128)(2,1)S(1)}, u32[]{:S(2)}, u32[]{:S(2)}) async-start(bf16[4,8,4096]{2,1,0:T(8,128)(2,1)} %regroup.1), calls=%async_computation.1 | async-start | bytes 524288 | tf_op jit(solution)/shard_map/all_to_all | solution.py:614

commit v6 on v5

--- a/solution.py
+++ b/solution.py
@@ -617,12 +617,12 @@
 def scatter_ctx(parts):
     own, swapped, below, above, below_swapped, below_two, above_swapped, far = parts
     got_far = swap_l(far)
-    got_below_swapped = swap_l(below_swapped)
+    got_below_swapped = turn_y(below_swapped, -1)
     got_above_swapped = turn_y(above_swapped, 1)
     got_two = turn_y(add(below_two, got_far), -1)
     got_above = turn_y(above, 1)
-    got_swapped = swap_l(add(swapped, got_above_swapped))
-    got_below = turn_y(add(below, got_two, got_below_swapped), -1)
+    got_swapped = swap_l(add(swapped, got_above_swapped, got_below_swapped))
+    got_below = turn_y(add(below, got_two), -1)
     return add(own, got_above, got_below, got_swapped)
 
 
@@ -714,7 +714,7 @@
     below = turn_y(block, 1)
     above = turn_y(block, -1)
     below_two = turn_y(below, 1)
-    below_swapped = swap_l(below)
+    below_swapped = turn_y(swapped, 1)
     above_swapped = turn_y(swapped, -1)
     far = swap_l(below_two)
     parts = run_expert(

time: 203 us -> 202 us (level)
  starting transfers between devices: 58.2 us -> 60.9 us
  waiting for transfers between devices: 93.6 us -> 91.4 us
    ppermute x8 -> x10, starting transfers between devices: 4.56 us -> 8.83 us  [turn_y(): return lax.ppermute(a, ('ctx', 'rep'), pairs)]
    ppermute x7 -> x5, waiting for transfers between devices: 18.1 us -> 15.6 us  [swap_l(): return lax.ppermute(a, 'ctx', [(i, i ^ 1) for i in range(2 * N_Y)])]
    ppermute x7 -> x5, starting transfers between devices: 5.8 us -> 4.79 us  [swap_l(): return lax.ppermute(a, 'ctx', [(i, i ^ 1) for i in range(2 * N_Y)])]
    ppermute x8 -> x10, waiting for transfers between devices: 23.3 us -> 22.6 us  [turn_y(): return lax.ppermute(a, ('ctx', 'rep'), pairs)]
  transfers between devices with their start and end apart: 38 -> 38, of which waited for: 25 -> 23; matrix products, arithmetic and copies ran while one was open for 1% -> 1% of each run, Pallas kernels for 14% -> 13%
where the time goes in v6:
time: 202 us
  waiting for transfers between devices  91.4 us (45%)
  starting transfers between devices  60.9 us (30%)
  Pallas kernels  35.6 us (18%)
  blocking collectives  10.5 us (5%)
    ppermute x10, starting transfers between devices, shift_z(): return lax.ppermute(a, 'exp', pairs)  25.6 us
    ppermute x10, waiting for transfers between devices, shift_z(): return lax.ppermute(a, 'exp', pairs)  25.4 us
    ppermute x10, waiting for transfers between devices, turn_y(): return lax.ppermute(a, ('ctx', 'rep'), pairs)  22.6 us
    ppermute x7, waiting for transfers between devices, shift_x(): return lax.ppermute(a, 'exp', pairs)  21.8 us
    pallas_call x3, Pallas kernels, attend(): pl.pallas_call(kernel, in_specs=[pl.BlockSpec(memory_space=SMEM)] + [whol...  17.6 us
    ppermute x5, waiting for transfers between devices, swap_l(): return lax.ppermute(a, 'ctx', [(i, i ^ 1) for i in range(2 * N_Y)])  15.6 us
    ppermute x7, starting transfers between devices, shift_x(): return lax.ppermute(a, 'exp', pairs)  12.5 us
    all_to_all x1, blocking collectives, exchange_x(): return lax.all_to_all(a, 'exp', 0, 0, tiled=True, axis_index_groups=groups)  10.5 us
  transfers between devices with their start and end apart: 38, of which 23 were waited for; matrix products, arithmetic and copies ran while one was open for 1% of the time, Pallas kernels for 13%

profile of v6, /device:TPU:24, one launch (start us, length us, event | category | flops | bytes accessed | tf_op | source)
XLA Modules:
  0.0 201.6 jit_solution(12567285886381493217)
XLA Ops:
  1.6 2.0 collective-permute-start
  3.7 3.1 %pick_weights.1 = (bf16[256,1024]{1,0:T(8,128)(2,1)}, bf16[256,1024]{1,0:T(8,128)(2,1)}, bf16[256,1024]{1,0:T(8,128)(2,1)}) custom-call(s32[2]{0:T(128)S(1)} %pad_add_fusion.2.place_ref, bf16[512,4096]{1,0:T(8,128)(2,1)} %weight_ref.1, bf16[512,4096]{1,0:T(8,128)(2,1)} %weight_ref.1, bf16[512,4096]{1,0:T(8,128)(2,1)} %weight_ref.1), custom_call_target="tpu_custom_call" | custom-call | tf_op jit(solution)/shard_map/pick_weights/pallas_call | solution.py:102
  6.8 3.1 %collective-permute-done.refs_1_ = bf16[1024,128]{1,0:T(8,128)(2,1)S(1)} collective-permute-done((bf16[1024,128]{1,0:T(8,128)(2,1)S(1)}, bf16[1024,128]{1,0:T(8,128)(2,1)S(1)}, u32[]{:S(2)}, u32[]{:S(2)}) %collective-permute-start) | collective-permute-done | bytes 262176 | tf_op jit(solution)/shard_map/ppermute | solution.py:63
  10.8 2.5 %collective-permute-start.1 = (bf16[2048,128]{1,0:T(8,128)(2,1)S(1)}, bf16[2048,128]{1,0:T(8,128)(2,1)}, u32[]{:S(2)}, u32[]{:S(2)}) collective-permute-start(bf16[2048,128]{1,0:T(8,128)(2,1)S(1)} %stack.40.refs_2_), channel_id=1, source_target_pairs={{0,64},{32,96},{64,128},{96,160},{128,192},{160,224},{192,0},{224,... | collective-permute-start | bytes 1572872 | tf_op jit(solution)/shard_map/ppermute | solution.py:50
  13.3 1.5 collective-permute-start.5
  14.8 2.7 %collective-permute-start.6 = (bf16[256,1024]{1,0:T(8,128)(2,1)}, bf16[256,1024]{1,0:T(8,128)(2,1)S(1)}, u32[]{:S(2)}, u32[]{:S(2)}) collective-permute-start(bf16[256,1024]{1,0:T(8,128)(2,1)} %get-tuple-element.51), channel_id=1, source_target_pairs={{0,4},{2,6},{4,0},{6,2},{8,12},{10,14},{12,8},{14,10},{16,20},{18,... | collective-permute-start | bytes 1572872 | tf_op jit(solution)/shard_map/ppermute | solution.py:40
  17.5 1.4 collective-permute-start.7
  20.5 4.6 %attend.3 = (f32[4,512,256]{2,1,0:T(8,128)S(1)}, f32[4,512,128]{2,1,0:T(8,128)S(1)}) custom-call(s32[3]{0:T(128)S(1)} %pad_add_fusion.1.refs_0_, bf16[512,512]{1,0:T(8,128)(2,1)S(1)} %copy-done.3, bf16[2048,128]{1,0:T(8,128)(2,1)S(1)} %stack.40.refs_2_), custom_call_target="tpu_custom_call" | custom-call | flops 1073741824 | bytes 4194304 | tf_op jit(solution)/shard_map/attend/pallas_call | solution.py:210
  26.1 2.3 %collective-permute-start.3 = (bf16[1024,128]{1,0:T(8,128)(2,1)S(1)}, bf16[1024,128]{1,0:T(8,128)(2,1)S(1)}, u32[]{:S(2)}, u32[]{:S(2)}) collective-permute-start(bf16[1024,128]{1,0:T(8,128)(2,1)S(1)} %slice.30), channel_id=1, source_target_pairs={{0,64},{32,96},{64,128},{96,160},{128,192},{160,224},{192,0},{224,... | collective-permute-start | bytes 786440 | tf_op jit(solution)/shard_map/ppermute | solution.py:50
  28.4 8.2 %attend.4 = (f32[4,512,256]{2,1,0:T(8,128)S(1)}, f32[4,512,128]{2,1,0:T(8,128)S(1)}) custom-call(s32[3]{0:T(128)S(1)} %pad_add_fusion.1.refs_0_, bf16[512,512]{1,0:T(8,128)(2,1)S(1)} %copy-done.3, bf16[2048,128]{1,0:T(8,128)(2,1)} %collective-permute-done.1.refs_2_, bf16[2048,128]{1,0:T(8,128)(2,1)S(1)} %collective-permute-done.2.refs_3_, ...), custom_call_target="tpu_custom_call" | custom-call | flops 2147483648 | bytes 4194304 | tf_op jit(solution)/shard_map/attend/pallas_call | solution.py:210
  36.7 2.7 %collective-permute-done.6.refs_1_.fetched_ref = bf16[256,1024]{1,0:T(8,128)(2,1)S(1)} collective-permute-done((bf16[256,1024]{1,0:T(8,128)(2,1)}, bf16[256,1024]{1,0:T(8,128)(2,1)S(1)}, u32[]{:S(2)}, u32[]{:S(2)}) %collective-permute-start.6) | collective-permute-done | bytes 524320 | tf_op jit(solution)/shard_map/ppermute | solution.py:40
  39.6 4.8 %attend.5 = (bf16[672,512]{1,0:T(8,128)(2,1)S(1)}, bf16[592,512]{1,0:T(8,128)(2,1)S(1)}) custom-call(s32[3]{0:T(128)S(1)} %pad_add_fusion.1.refs_0_, bf16[512,512]{1,0:T(8,128)(2,1)S(1)} %copy-done.3, bf16[1024,128]{1,0:T(8,128)(2,1)S(1)} %collective-permute-done.3.refs_2_, bf16[1024,128]{1,0:T(8,128)(2,1)S(1)} %collective-permute-done.4.refs_3_, ...), custom_call_target="tpu_custom_call" | custom-call | flops 1073741824 | bytes 4194304 | tf_op jit(solution)/shard_map/attend/pallas_call | solution.py:210
  44.4 1.4 collective-permute-start.8
  45.8 1.9 collective-permute-start.10
  47.7 15.8 %collective-permute-done.8.message_ref.refs_0_.refs_1_.h1 = bf16[672,512]{1,0:T(8,128)(2,1)S(1)} collective-permute-done((bf16[672,512]{1,0:T(8,128)(2,1)S(1)}, bf16[672,512]{1,0:T(8,128)(2,1)S(1)}, u32[]{:S(2)}, u32[]{:S(2)}) %collective-permute-start.8) | collective-permute-done | bytes 688160 | tf_op jit(solution)/shard_map/ppermute | solution.py:40
  64.0 3.2 %collective-permute-start.11 = (bf16[256,512]{1,0:T(8,128)(2,1)S(1)}, bf16[256,512]{1,0:T(8,128)(2,1)S(1)}, u32[]{:S(2)}, u32[]{:S(2)}) collective-permute-start(bf16[256,512]{1,0:T(8,128)(2,1)S(1)} %forward.3), channel_id=1, source_target_pairs={{0,6},{2,0},{4,2},{6,4},{8,14},{10,8},{12,10},{14,12},{16,22},{18,... | collective-permute-start | bytes 786440 | tf_op jit(solution)/shard_map/ppermute | solution.py:40
  67.2 4.3 %project_near.1.refs_0_ = f32[4,128,1024]{2,1,0:T(8,128)S(1)} custom-call(s32[3]{0:T(128)S(1)} %pad_add_fusion.place_ref, bf16[672,512]{1,0:T(8,128)(2,1)S(1)} %get-tuple-element.65.own_ref, bf16[512,4096]{1,0:T(8,128)(2,1)} %weight_ref.1, bf16[672,512]{1,0:T(8,128)(2,1)S(1)} %collective-permute-done.8.message_ref.refs_0_.refs_1_.h1, ...), custom_call_target="tpu_custom_call" | custom-call | flops 1 | bytes 1 | tf_op jit(solution)/shard_map/project_near/pallas_call | solution.py:261
  72.3 2.4 %collective-permute-done.9.upper_ref.refs_2_.h2 = bf16[336,512]{1,0:T(8,128)(2,1)S(1)} collective-permute-done((bf16[336,512]{1,0:T(8,128)(2,1)S(1)}, bf16[336,512]{1,0:T(8,128)(2,1)S(1)}, u32[]{:S(2)}, u32[]{:S(2)}) %collective-permute-start.9) | collective-permute-done | bytes 344096 | tf_op jit(solution)/shard_map/ppermute | solution.py:40
  74.7 1.3 project_far.1
  76.1 3.4 %collective-permute-start.13 = (bf16[128,512]{1,0:T(8,128)(2,1)S(1)}, bf16[128,512]{1,0:T(8,128)(2,1)S(1)}, u32[]{:S(2)}, u32[]{:S(2)}) collective-permute-start(bf16[128,512]{1,0:T(8,128)(2,1)S(1)} %get-tuple-element.75), channel_id=1, source_target_pairs={{0,8},{2,10},{4,12},{6,14},{8,16},{10,18},{12,20},{14,22},{16,24},... | collective-permute-start | bytes 393224 | tf_op jit(solution)/shard_map/ppermute | solution.py:45
  79.4 2.7 %collective-permute-start.14 = (bf16[128,512]{1,0:T(8,128)(2,1)S(1)}, bf16[128,512]{1,0:T(8,128)(2,1)S(1)}, u32[]{:S(2)}, u32[]{:S(2)}) collective-permute-start(bf16[128,512]{1,0:T(8,128)(2,1)S(1)} %get-tuple-element.76), channel_id=1, source_target_pairs={{0,24},{2,26},{4,28},{6,30},{8,0},{10,2},{12,4},{14,6},{16,8},{18,... | collective-permute-start | bytes 393224 | tf_op jit(solution)/shard_map/ppermute | solution.py:45
  83.0 2.3 %collective-permute-done.13 = bf16[128,512]{1,0:T(8,128)(2,1)S(1)} collective-permute-done((bf16[128,512]{1,0:T(8,128)(2,1)S(1)}, bf16[128,512]{1,0:T(8,128)(2,1)S(1)}, u32[]{:S(2)}, u32[]{:S(2)}) %collective-permute-start.13) | collective-permute-done | bytes 131104 | tf_op jit(solution)/shard_map/ppermute | solution.py:45
  85.3 3.2 %collective-permute-done.14 = bf16[128,512]{1,0:T(8,128)(2,1)S(1)} collective-permute-done((bf16[128,512]{1,0:T(8,128)(2,1)S(1)}, bf16[128,512]{1,0:T(8,128)(2,1)S(1)}, u32[]{:S(2)}, u32[]{:S(2)}) %collective-permute-start.14) | collective-permute-done | bytes 131104 | tf_op jit(solution)/shard_map/ppermute | solution.py:45
  88.6 2.8 %collective-permute-start.16 = (bf16[128,1024]{1,0:T(8,128)(2,1)S(1)}, bf16[128,1024]{1,0:T(8,128)(2,1)S(1)}, u32[]{:S(2)}, u32[]{:S(2)}) collective-permute-start(bf16[128,1024]{1,0:T(8,128)(2,1)S(1)} %pad_maximum_fusion.1), channel_id=1, source_target_pairs={{0,24},{2,26},{4,28},{6,30},{8,0},{10,2},{12,4},{14,6},{16,8},{18,... | collective-permute-start | bytes 786440 | tf_op jit(solution)/shard_map/ppermute | solution.py:45
  92.5 9.8 %collective-permute-done.16.s2 = bf16[128,1024]{1,0:T(8,128)(2,1)S(1)} collective-permute-done((bf16[128,1024]{1,0:T(8,128)(2,1)S(1)}, bf16[128,1024]{1,0:T(8,128)(2,1)S(1)}, u32[]{:S(2)}, u32[]{:S(2)}) %collective-permute-start.16) | collective-permute-done | bytes 262176 | tf_op jit(solution)/shard_map/ppermute | solution.py:45
  102.2 2.0 collective-permute-done.15.s1
  105.1 1.4 collective-permute-start.17
  106.5 3.0 %collective-permute-start.18 = (bf16[32,1024]{1,0:T(8,128)(2,1)S(1)}, bf16[32,1024]{1,0:T(8,128)(2,1)S(1)}, u32[]{:S(2)}, u32[]{:S(2)}) collective-permute-start(bf16[32,1024]{1,0:T(8,128)(2,1)S(1)} %get-tuple-element.82), channel_id=1, source_target_pairs={{0,16},{2,18},{4,20},{6,22},{8,24},{10,26},{12,28},{14,30},{16,0},... | collective-permute-start | bytes 196616 | tf_op jit(solution)/shard_map/ppermute | solution.py:45
  109.5 4.0 %collective-permute-start.19 = (bf16[32,1024]{1,0:T(8,128)(2,1)S(1)}, bf16[32,1024]{1,0:T(8,128)(2,1)S(1)}, u32[]{:S(2)}, u32[]{:S(2)}) collective-permute-start(bf16[32,1024]{1,0:T(8,128)(2,1)S(1)} %get-tuple-element.83), channel_id=1, source_target_pairs={{0,24},{2,26},{4,28},{6,30},{8,0},{10,2},{12,4},{14,6},{16,8},{18,... | collective-permute-start | bytes 196616 | tf_op jit(solution)/shard_map/ppermute | solution.py:45
  113.5 1.8 collective-permute-done.18.refs_2_
  116.4 10.5 %all_to_all.10.piece_ref = bf16[4,64,1024]{2,1,0:T(8,128)(2,1)S(1)} all-to-all(bf16[4,64,1024]{2,1,0:T(8,128)(2,1)S(1)} %by_columns.1), channel_id=1, replica_groups={{0,2,4,6},{8,10,12,14},{16,18,20,22},{24,26,28,30},{1,3,5,7},{9,11,13,1..., dimensions={0} | all-to-all | bytes 1048576 | tf_op jit(solution)/shard_map/all_to_all | solution.py:614
  128.8 8.1 %collective-permute-done.21.refs_2_ = bf16[32,4096]{1,0:T(8,128)(2,1)S(1)} collective-permute-done((bf16[32,4096]{1,0:T(8,128)(2,1)S(1)}, bf16[32,4096]{1,0:T(8,128)(2,1)S(1)}, u32[]{:S(2)}, u32[]{:S(2)}) %collective-permute-start.21) | collective-permute-done | bytes 262176 | tf_op jit(solution)/shard_map/ppermute | solution.py:59
  136.9 2.0 %collective-permute-start.22 = (bf16[32,4096]{1,0:T(8,128)(2,1)S(1)}, bf16[32,4096]{1,0:T(8,128)(2,1)S(1)}, u32[]{:S(2)}, u32[]{:S(2)}) collective-permute-start(bf16[32,4096]{1,0:T(8,128)(2,1)S(1)} %get-tuple-element.87.refs_0_), channel_id=1, source_target_pairs={{0,192},{32,224},{64,0},{96,32},{128,64},{160,96},{192,128},{224,1... | collective-permute-start | bytes 786440 | tf_op jit(solution)/shard_map/ppermute | solution.py:59
  139.0 3.2 %collective-permute-start.23 = (bf16[32,4096]{1,0:T(8,128)(2,1)S(1)}, bf16[32,4096]{1,0:T(8,128)(2,1)S(1)}, u32[]{:S(2)}, u32[]{:S(2)}) collective-permute-start(bf16[32,4096]{1,0:T(8,128)(2,1)S(1)} %collective-permute-done.20.refs_1_), channel_id=1, source_target_pairs={{0,64},{32,96},{64,128},{96,160},{128,192},{160,224},{192,0},{224,... | collective-permute-start | bytes 786440 | tf_op jit(solution)/shard_map/ppermute | solution.py:59
  144.5 3.6 %collective-permute-done.25.refs_6_ = bf16[32,4096]{1,0:T(8,128)(2,1)S(1)} collective-permute-done((bf16[32,4096]{1,0:T(8,128)(2,1)S(1)}, bf16[32,4096]{1,0:T(8,128)(2,1)S(1)}, u32[]{:S(2)}, u32[]{:S(2)}) %collective-permute-start.25) | collective-permute-done | bytes 262176 | tf_op jit(solution)/shard_map/ppermute | solution.py:59
  148.1 2.8 %collective-permute-done.26.refs_7_ = bf16[32,4096]{1,0:T(8,128)(2,1)S(1)} collective-permute-done((bf16[32,4096]{1,0:T(8,128)(2,1)S(1)}, bf16[32,4096]{1,0:T(8,128)(2,1)S(1)}, u32[]{:S(2)}, u32[]{:S(2)}) %collective-permute-start.26) | collective-permute-done | bytes 262176 | tf_op jit(solution)/shard_map/ppermute | solution.py:63
  150.9 1.9 run_expert.1
  154.5 1.7 collective-permute-start.32
  156.1 5.0 %collective-permute-done.28 = bf16[32,4096]{1,0:T(8,128)(2,1)S(1)} collective-permute-done((bf16[32,4096]{1,0:T(8,128)(2,1)S(1)}, bf16[32,4096]{1,0:T(8,128)(2,1)S(1)}, u32[]{:S(2)}, u32[]{:S(2)}) %collective-permute-start.28) | collective-permute-done | bytes 262176 | tf_op jit(solution)/shard_map/ppermute | solution.py:63
  161.7 3.4 %collective-permute-done.31 = bf16[32,4096]{1,0:T(8,128)(2,1)S(1)} collective-permute-done((bf16[32,4096]{1,0:T(8,128)(2,1)S(1)}, bf16[32,4096]{1,0:T(8,128)(2,1)S(1)}, u32[]{:S(2)}, u32[]{:S(2)}) %collective-permute-start.31) | collective-permute-done | bytes 262176 | tf_op jit(solution)/shard_map/ppermute | solution.py:59
  166.4 2.4 %collective-permute-done.29 = bf16[32,4096]{1,0:T(8,128)(2,1)S(1)} collective-permute-done((bf16[32,4096]{1,0:T(8,128)(2,1)S(1)}, bf16[32,4096]{1,0:T(8,128)(2,1)S(1)}, u32[]{:S(2)}, u32[]{:S(2)}) %collective-permute-start.29) | collective-permute-done | bytes 262176 | tf_op jit(solution)/shard_map/ppermute | solution.py:59
  169.1 4.7 %collective-permute-done.33 = bf16[32,4096]{1,0:T(8,128)(2,1)S(1)} collective-permute-done((bf16[32,4096]{1,0:T(8,128)(2,1)S(1)}, bf16[32,4096]{1,0:T(8,128)(2,1)S(1)}, u32[]{:S(2)}, u32[]{:S(2)}) %collective-permute-start.33) | collective-permute-done | bytes 262176 | tf_op jit(solution)/shard_map/ppermute | solution.py:63
  173.7 2.9 %collective-permute-done.30 = bf16[32,4096]{1,0:T(8,128)(2,1)S(1)} collective-permute-done((bf16[32,4096]{1,0:T(8,128)(2,1)S(1)}, bf16[32,4096]{1,0:T(8,128)(2,1)S(1)}, u32[]{:S(2)}, u32[]{:S(2)}) %collective-permute-start.30) | collective-permute-done | bytes 262176 | tf_op jit(solution)/shard_map/ppermute | solution.py:59
  176.8 3.7 %collective-permute-start.36 = (bf16[8,4096]{1,0:T(8,128)(2,1)S(1)}, bf16[8,4096]{1,0:T(8,128)(2,1)S(1)}, u32[]{:S(2)}, u32[]{:S(2)}) collective-permute-start(bf16[8,4096]{1,0:T(8,128)(2,1)S(1)} %get-tuple-element.96), channel_id=1, source_target_pairs={{0,8},{2,10},{4,12},{6,14},{8,16},{10,18},{12,20},{14,22},{16,24},... | collective-permute-start | bytes 196616 | tf_op jit(solution)/shard_map/ppermute | solution.py:45
  180.5 3.2 %collective-permute-start.35 = (bf16[8,4096]{1,0:T(8,128)(2,1)S(1)}, bf16[8,4096]{1,0:T(8,128)(2,1)S(1)}, u32[]{:S(2)}, u32[]{:S(2)}) collective-permute-start(bf16[8,4096]{1,0:T(8,128)(2,1)S(1)} %get-tuple-element.97), channel_id=1, source_target_pairs={{0,16},{2,18},{4,20},{6,22},{8,24},{10,26},{12,28},{14,30},{16,0},... | collective-permute-start | bytes 196616 | tf_op jit(solution)/shard_map/ppermute | solution.py:45
  184.1 5.2 %collective-permute-done.35.refs_2_ = bf16[8,4096]{1,0:T(8,128)(2,1)S(1)} collective-permute-done((bf16[8,4096]{1,0:T(8,128)(2,1)S(1)}, bf16[8,4096]{1,0:T(8,128)(2,1)S(1)}, u32[]{:S(2)}, u32[]{:S(2)}) %collective-permute-start.35) | collective-permute-done | bytes 65568 | tf_op jit(solution)/shard_map/ppermute | solution.py:45
  190.3 3.4 %all-to-all-start.1 = ((bf16[4,8,4096]{2,1,0:T(8,128)(2,1)}), bf16[4,8,4096]{2,1,0:T(8,128)(2,1)S(1)}, u32[]{:S(2)}, u32[]{:S(2)}) async-start(bf16[4,8,4096]{2,1,0:T(8,128)(2,1)} %regroup.1), calls=%async_computation.1 | async-start | bytes 524288 | tf_op jit(solution)/shard_map/all_to_all | solution.py:614
  194.4 5.9 %all-to-all-done.1.refs_0_ = bf16[4,8,4096]{2,1,0:T(8,128)(2,1)S(1)} async-done(((bf16[4,8,4096]{2,1,0:T(8,128)(2,1)}), bf16[4,8,4096]{2,1,0:T(8,128)(2,1)S(1)}, u32[]{:S(2)}, u32[]{:S(2)}) %all-to-all-start.1) | async-done | bytes 262176 | tf_op jit(solution)/shard_map/all_to_all | solution.py:614
  (81 shorter events, 20.7 us)
Async XLA Ops:
  1.6 8.3 %collective-permute-start = (bf16[1024,128]{1,0:T(8,128)(2,1)S(1)}, bf16[1024,128]{1,0:T(8,128)(2,1)S(1)}, u32[]{:S(2)}, u32[]{:S(2)}) collective-permute-start(bf16[1024,128]{1,0:T(8,128)(2,1)S(1)} %pick_head.1.refs_0_), channel_id=1, source_target_pairs={{0,32},{32,0},{64,96},{96,64},{128,160},{160,128},{192,224},{224,1... | collective-permute-start | bytes 786440 | tf_op jit(solution)/shard_map/ppermute | solution.py:63
  3.7 16.0 %copy-start.4 = (bf16[32,4096]{1,0:T(8,128)(2,1)S(1)}, bf16[32,4096]{1,0:T(8,128)(2,1)}, u32[]{:S(2)}) copy-start(bf16[32,4096]{1,0:T(8,128)(2,1)} %hidden_ref.1) | copy-start | bytes 786436
  3.7 16.0 %copy-start.5 = (s32[32,8]{0,1:T(8,128)S(1)}, s32[32,8]{0,1:T(8,128)}, u32[]{:S(2)}) copy-start(s32[32,8]{0,1:T(8,128)} %param.18) | copy-start | bytes 3076
  3.7 16.7 %copy-start.3 = (bf16[512,512]{1,0:T(8,128)(2,1)S(1)}, bf16[512,512]{1,0:T(8,128)(2,1)}, u32[]{:S(2)}) copy-start(bf16[512,512]{1,0:T(8,128)(2,1)} %refs_1_.7) | copy-start | bytes 1572868
  10.0 15.1 %collective-permute-start.2 = (bf16[2048,128]{1,0:T(8,128)(2,1)S(1)}, bf16[2048,128]{1,0:T(8,128)(2,1)S(1)}, u32[]{:S(2)}, u32[]{:S(2)}) collective-permute-start(bf16[2048,128]{1,0:T(8,128)(2,1)S(1)} %stack.40.refs_2_), channel_id=1, source_target_pairs={{0,192},{32,224},{64,0},{96,32},{128,64},{160,96},{192,128},{224,1... | collective-permute-start | bytes 1572872 | tf_op jit(solution)/shard_map/ppermute | solution.py:50
  10.8 14.3 %collective-permute-start.1 = (bf16[2048,128]{1,0:T(8,128)(2,1)S(1)}, bf16[2048,128]{1,0:T(8,128)(2,1)}, u32[]{:S(2)}, u32[]{:S(2)}) collective-permute-start(bf16[2048,128]{1,0:T(8,128)(2,1)S(1)} %stack.40.refs_2_), channel_id=1, source_target_pairs={{0,64},{32,96},{64,128},{96,160},{128,192},{160,224},{192,0},{224,... | collective-permute-start | bytes 1572872 | tf_op jit(solution)/shard_map/ppermute | solution.py:50
  13.3 23.3 %collective-permute-start.5 = (bf16[256,1024]{1,0:T(8,128)(2,1)}, bf16[256,1024]{1,0:T(8,128)(2,1)S(1)}, u32[]{:S(2)}, u32[]{:S(2)}) collective-permute-start(bf16[256,1024]{1,0:T(8,128)(2,1)} %get-tuple-element.50), channel_id=1, source_target_pairs={{0,2},{2,4},{4,6},{6,0},{8,10},{10,12},{12,14},{14,8},{16,18},{18,... | collective-permute-start | bytes 1572872 | tf_op jit(solution)/shard_map/ppermute | solution.py:40
  14.8 24.6 %collective-permute-start.6 = (bf16[256,1024]{1,0:T(8,128)(2,1)}, bf16[256,1024]{1,0:T(8,128)(2,1)S(1)}, u32[]{:S(2)}, u32[]{:S(2)}) collective-permute-start(bf16[256,1024]{1,0:T(8,128)(2,1)} %get-tuple-element.51), channel_id=1, source_target_pairs={{0,4},{2,6},{4,0},{6,2},{8,12},{10,14},{12,8},{14,10},{16,20},{18,... | collective-permute-start | bytes 1572872 | tf_op jit(solution)/shard_map/ppermute | solution.py:40
  17.5 21.9 %collective-permute-start.7 = (bf16[256,1024]{1,0:T(8,128)(2,1)}, bf16[256,1024]{1,0:T(8,128)(2,1)S(1)}, u32[]{:S(2)}, u32[]{:S(2)}) collective-permute-start(bf16[256,1024]{1,0:T(8,128)(2,1)} %get-tuple-element.52), channel_id=1, source_target_pairs={{0,6},{2,0},{4,2},{6,4},{8,14},{10,8},{12,10},{14,12},{16,22},{18,... | collective-permute-start | bytes 1572872 | tf_op jit(solution)/shard_map/ppermute | solution.py:40
  26.1 13.3 %collective-permute-start.3 = (bf16[1024,128]{1,0:T(8,128)(2,1)S(1)}, bf16[1024,128]{1,0:T(8,128)(2,1)S(1)}, u32[]{:S(2)}, u32[]{:S(2)}) collective-permute-start(bf16[1024,128]{1,0:T(8,128)(2,1)S(1)} %slice.30), channel_id=1, source_target_pairs={{0,64},{32,96},{64,128},{96,160},{128,192},{160,224},{192,0},{224,... | collective-permute-start | bytes 786440 | tf_op jit(solution)/shard_map/ppermute | solution.py:50
  28.4 11.0 %collective-permute-start.4 = (bf16[1024,128]{1,0:T(8,128)(2,1)S(1)}, bf16[1024,128]{1,0:T(8,128)(2,1)S(1)}, u32[]{:S(2)}, u32[]{:S(2)}) collective-permute-start(bf16[1024,128]{1,0:T(8,128)(2,1)S(1)} %slice.31), channel_id=1, source_target_pairs={{0,192},{32,224},{64,0},{96,32},{128,64},{160,96},{192,128},{224,1... | collective-permute-start | bytes 786440 | tf_op jit(solution)/shard_map/ppermute | solution.py:50
  39.5 27.7 %collective-permute-start.12 = (bf16[768,1024]{1,0:T(8,128)(2,1)S(1)}, bf16[768,1024]{1,0:T(8,128)(2,1)S(1)}, u32[]{:S(2)}, u32[]{:S(2)}) collective-permute-start(bf16[768,1024]{1,0:T(8,128)(2,1)S(1)} %stack.41), channel_id=1, source_target_pairs={{0,1},{1,0},{2,3},{3,2},{4,5},{5,4},{6,7},{7,6},{8,9},{9,8},{10,11... | collective-permute-start | bytes 4718600 | tf_op jit(solution)/shard_map/ppermute | solution.py:67
  44.4 19.1 %collective-permute-start.8 = (bf16[672,512]{1,0:T(8,128)(2,1)S(1)}, bf16[672,512]{1,0:T(8,128)(2,1)S(1)}, u32[]{:S(2)}, u32[]{:S(2)}) collective-permute-start(bf16[672,512]{1,0:T(8,128)(2,1)S(1)} %get-tuple-element.65.own_ref), channel_id=1, source_target_pairs={{0,2},{2,4},{4,6},{6,0},{8,10},{10,12},{12,14},{14,8},{16,18},{18,... | collective-permute-start | bytes 2064392 | tf_op jit(solution)/shard_map/ppermute | solution.py:40
  45.8 18.1 %collective-permute-start.10 = (bf16[592,512]{1,0:T(8,128)(2,1)S(1)}, bf16[592,512]{1,0:T(8,128)(2,1)S(1)}, u32[]{:S(2)}, u32[]{:S(2)}) collective-permute-start(bf16[592,512]{1,0:T(8,128)(2,1)S(1)} %get-tuple-element.66), channel_id=1, source_target_pairs={{0,6},{2,0},{4,2},{6,4},{8,14},{10,8},{12,10},{14,12},{16,22},{18,... | collective-permute-start | bytes 1818632 | tf_op jit(solution)/shard_map/ppermute | solution.py:40
  63.6 11.2 %collective-permute-start.9 = (bf16[336,512]{1,0:T(8,128)(2,1)S(1)}, bf16[336,512]{1,0:T(8,128)(2,1)S(1)}, u32[]{:S(2)}, u32[]{:S(2)}) collective-permute-start(bf16[336,512]{1,0:T(8,128)(2,1)S(1)} %forward.2), channel_id=1, source_target_pairs={{0,2},{2,4},{4,6},{6,0},{8,10},{10,12},{12,14},{14,8},{16,18},{18,... | collective-permute-start | bytes 1032200 | tf_op jit(solution)/shard_map/ppermute | solution.py:40
  64.0 8.4 %collective-permute-start.11 = (bf16[256,512]{1,0:T(8,128)(2,1)S(1)}, bf16[256,512]{1,0:T(8,128)(2,1)S(1)}, u32[]{:S(2)}, u32[]{:S(2)}) collective-permute-start(bf16[256,512]{1,0:T(8,128)(2,1)S(1)} %forward.3), channel_id=1, source_target_pairs={{0,6},{2,0},{4,2},{6,4},{8,14},{10,8},{12,10},{14,12},{16,22},{18,... | collective-permute-start | bytes 786440 | tf_op jit(solution)/shard_map/ppermute | solution.py:40
  76.1 9.2 %collective-permute-start.13 = (bf16[128,512]{1,0:T(8,128)(2,1)S(1)}, bf16[128,512]{1,0:T(8,128)(2,1)S(1)}, u32[]{:S(2)}, u32[]{:S(2)}) collective-permute-start(bf16[128,512]{1,0:T(8,128)(2,1)S(1)} %get-tuple-element.75), channel_id=1, source_target_pairs={{0,8},{2,10},{4,12},{6,14},{8,16},{10,18},{12,20},{14,22},{16,24},... | collective-permute-start | bytes 393224 | tf_op jit(solution)/shard_map/ppermute | solution.py:45
  79.4 9.1 %collective-permute-start.14 = (bf16[128,512]{1,0:T(8,128)(2,1)S(1)}, bf16[128,512]{1,0:T(8,128)(2,1)S(1)}, u32[]{:S(2)}, u32[]{:S(2)}) collective-permute-start(bf16[128,512]{1,0:T(8,128)(2,1)S(1)} %get-tuple-element.76), channel_id=1, source_target_pairs={{0,24},{2,26},{4,28},{6,30},{8,0},{10,2},{12,4},{14,6},{16,8},{18,... | collective-permute-start | bytes 393224 | tf_op jit(solution)/shard_map/ppermute | solution.py:45
  88.6 13.6 %collective-permute-start.16 = (bf16[128,1024]{1,0:T(8,128)(2,1)S(1)}, bf16[128,1024]{1,0:T(8,128)(2,1)S(1)}, u32[]{:S(2)}, u32[]{:S(2)}) collective-permute-start(bf16[128,1024]{1,0:T(8,128)(2,1)S(1)} %pad_maximum_fusion.1), channel_id=1, source_target_pairs={{0,24},{2,26},{4,28},{6,30},{8,0},{10,2},{12,4},{14,6},{16,8},{18,... | collective-permute-start | bytes 786440 | tf_op jit(solution)/shard_map/ppermute | solution.py:45
  91.5 12.7 %collective-permute-start.15 = (bf16[128,1024]{1,0:T(8,128)(2,1)S(1)}, bf16[128,1024]{1,0:T(8,128)(2,1)S(1)}, u32[]{:S(2)}, u32[]{:S(2)}) collective-permute-start(bf16[128,1024]{1,0:T(8,128)(2,1)S(1)} %pad_maximum_fusion), channel_id=1, source_target_pairs={{0,8},{2,10},{4,12},{6,14},{8,16},{10,18},{12,20},{14,22},{16,24},... | collective-permute-start | bytes 786440 | tf_op jit(solution)/shard_map/ppermute | solution.py:45
  104.2 22.7 %copy-start.6 = (f32[4096]{0:T(1024)S(1)}, f32[4096]{0:T(1024)}, u32[]{:S(2)}) copy-start(f32[4096]{0:T(1024)} %param.17) | copy-start | bytes 49156
  104.2 46.6 %copy-start.1 = (bf16[1,4096,192]{1,2,0:T(8,128)(2,1)S(1)}, bf16[1,4096,192]{1,2,0:T(8,128)(2,1)}, u32[]{:S(2)}) copy-start(bf16[1,4096,192]{1,2,0:T(8,128)(2,1)} %param.22) | copy-start | bytes 4718596
  104.2 46.6 %copy-start.2 = (bf16[1,192,4096]{2,1,0:T(8,128)(2,1)S(1)}, bf16[1,192,4096]{2,1,0:T(8,128)(2,1)}, u32[]{:S(2)}) copy-start(bf16[1,192,4096]{2,1,0:T(8,128)(2,1)} %param.23) | copy-start | bytes 4718596
  105.1 45.8 %copy-start = (bf16[1,4096,192]{1,2,0:T(8,128)(2,1)S(1)}, bf16[1,4096,192]{1,2,0:T(8,128)(2,1)}, u32[]{:S(2)}) copy-start(bf16[1,4096,192]{1,2,0:T(8,128)(2,1)} %param.21) | copy-start | bytes 4718596
  105.1 8.4 %collective-permute-start.17 = (bf16[32,1024]{1,0:T(8,128)(2,1)S(1)}, bf16[32,1024]{1,0:T(8,128)(2,1)S(1)}, u32[]{:S(2)}, u32[]{:S(2)}) collective-permute-start(bf16[32,1024]{1,0:T(8,128)(2,1)S(1)} %get-tuple-element.81), channel_id=1, source_target_pairs={{0,8},{2,10},{4,12},{6,14},{8,16},{10,18},{12,20},{14,22},{16,24},... | collective-permute-start | bytes 196616 | tf_op jit(solution)/shard_map/ppermute | solution.py:45
  106.5 8.8 %collective-permute-start.18 = (bf16[32,1024]{1,0:T(8,128)(2,1)S(1)}, bf16[32,1024]{1,0:T(8,128)(2,1)S(1)}, u32[]{:S(2)}, u32[]{:S(2)}) collective-permute-start(bf16[32,1024]{1,0:T(8,128)(2,1)S(1)} %get-tuple-element.82), channel_id=1, source_target_pairs={{0,16},{2,18},{4,20},{6,22},{8,24},{10,26},{12,28},{14,30},{16,0},... | collective-permute-start | bytes 196616 | tf_op jit(solution)/shard_map/ppermute | solution.py:45
  109.5 6.9 %collective-permute-start.19 = (bf16[32,1024]{1,0:T(8,128)(2,1)S(1)}, bf16[32,1024]{1,0:T(8,128)(2,1)S(1)}, u32[]{:S(2)}, u32[]{:S(2)}) collective-permute-start(bf16[32,1024]{1,0:T(8,128)(2,1)S(1)} %get-tuple-element.83), channel_id=1, source_target_pairs={{0,24},{2,26},{4,28},{6,30},{8,0},{10,2},{12,4},{14,6},{16,8},{18,... | collective-permute-start | bytes 196616 | tf_op jit(solution)/shard_map/ppermute | solution.py:45
  127.7 9.2 %collective-permute-start.21 = (bf16[32,4096]{1,0:T(8,128)(2,1)S(1)}, bf16[32,4096]{1,0:T(8,128)(2,1)S(1)}, u32[]{:S(2)}, u32[]{:S(2)}) collective-permute-start(bf16[32,4096]{1,0:T(8,128)(2,1)S(1)} %get-tuple-element.87.refs_0_), channel_id=1, source_target_pairs={{0,64},{32,96},{64,128},{96,160},{128,192},{160,224},{192,0},{224,... | collective-permute-start | bytes 786440 | tf_op jit(solution)/shard_map/ppermute | solution.py:59
  127.7 11.2 %collective-permute-start.20 = (bf16[32,4096]{1,0:T(8,128)(2,1)S(1)}, bf16[32,4096]{1,0:T(8,128)(2,1)S(1)}, u32[]{:S(2)}, u32[]{:S(2)}) collective-permute-start(bf16[32,4096]{1,0:T(8,128)(2,1)S(1)} %get-tuple-element.87.refs_0_), channel_id=1, source_target_pairs={{0,32},{32,0},{64,96},{96,64},{128,160},{160,128},{192,224},{224,1... | collective-permute-start | bytes 786440 | tf_op jit(solution)/shard_map/ppermute | solution.py:63
  136.9 6.4 %collective-permute-start.24 = (bf16[32,4096]{1,0:T(8,128)(2,1)S(1)}, bf16[32,4096]{1,0:T(8,128)(2,1)S(1)}, u32[]{:S(2)}, u32[]{:S(2)}) collective-permute-start(bf16[32,4096]{1,0:T(8,128)(2,1)S(1)} %collective-permute-done.21.refs_2_), channel_id=1, source_target_pairs={{0,64},{32,96},{64,128},{96,160},{128,192},{160,224},{192,0},{224,... | collective-permute-start | bytes 786440 | tf_op jit(solution)/shard_map/ppermute | solution.py:59
  136.9 7.6 %collective-permute-start.22 = (bf16[32,4096]{1,0:T(8,128)(2,1)S(1)}, bf16[32,4096]{1,0:T(8,128)(2,1)S(1)}, u32[]{:S(2)}, u32[]{:S(2)}) collective-permute-start(bf16[32,4096]{1,0:T(8,128)(2,1)S(1)} %get-tuple-element.87.refs_0_), channel_id=1, source_target_pairs={{0,192},{32,224},{64,0},{96,32},{128,64},{160,96},{192,128},{224,1... | collective-permute-start | bytes 786440 | tf_op jit(solution)/shard_map/ppermute | solution.py:59
  138.9 9.1 %collective-permute-start.25 = (bf16[32,4096]{1,0:T(8,128)(2,1)S(1)}, bf16[32,4096]{1,0:T(8,128)(2,1)S(1)}, u32[]{:S(2)}, u32[]{:S(2)}) collective-permute-start(bf16[32,4096]{1,0:T(8,128)(2,1)S(1)} %collective-permute-done.20.refs_1_), channel_id=1, source_target_pairs={{0,192},{32,224},{64,0},{96,32},{128,64},{160,96},{192,128},{224,1... | collective-permute-start | bytes 786440 | tf_op jit(solution)/shard_map/ppermute | solution.py:59
  139.0 9.1 %collective-permute-start.23 = (bf16[32,4096]{1,0:T(8,128)(2,1)S(1)}, bf16[32,4096]{1,0:T(8,128)(2,1)S(1)}, u32[]{:S(2)}, u32[]{:S(2)}) collective-permute-start(bf16[32,4096]{1,0:T(8,128)(2,1)S(1)} %collective-permute-done.20.refs_1_), channel_id=1, source_target_pairs={{0,64},{32,96},{64,128},{96,160},{128,192},{160,224},{192,0},{224,... | collective-permute-start | bytes 786440 | tf_op jit(solution)/shard_map/ppermute | solution.py:59
  143.3 7.6 %collective-permute-start.26 = (bf16[32,4096]{1,0:T(8,128)(2,1)S(1)}, bf16[32,4096]{1,0:T(8,128)(2,1)S(1)}, u32[]{:S(2)}, u32[]{:S(2)}) collective-permute-start(bf16[32,4096]{1,0:T(8,128)(2,1)S(1)} %collective-permute-done.24.refs_5_), channel_id=1, source_target_pairs={{0,32},{32,0},{64,96},{96,64},{128,160},{160,128},{192,224},{224,1... | collective-permute-start | bytes 786440 | tf_op jit(solution)/shard_map/ppermute | solution.py:63
  152.8 8.4 %collective-permute-start.28 = (bf16[32,4096]{1,0:T(8,128)(2,1)S(1)}, bf16[32,4096]{1,0:T(8,128)(2,1)S(1)}, u32[]{:S(2)}, u32[]{:S(2)}) collective-permute-start(bf16[32,4096]{1,0:T(8,128)(2,1)S(1)} %get-tuple-element.92), channel_id=1, source_target_pairs={{0,32},{32,0},{64,96},{96,64},{128,160},{160,128},{192,224},{224,1... | collective-permute-start | bytes 786440 | tf_op jit(solution)/shard_map/ppermute | solution.py:63
  153.2 15.9 %collective-permute-start.27 = (bf16[32,4096]{1,0:T(8,128)(2,1)S(1)}, bf16[32,4096]{1,0:T(8,128)(2,1)S(1)}, u32[]{:S(2)}, u32[]{:S(2)}) collective-permute-start(bf16[32,4096]{1,0:T(8,128)(2,1)S(1)} %get-tuple-element.89), channel_id=1, source_target_pairs={{0,64},{32,96},{64,128},{96,160},{128,192},{160,224},{192,0},{224,... | collective-permute-start | bytes 786440 | tf_op jit(solution)/shard_map/ppermute | solution.py:59
  154.1 11.1 %collective-permute-start.31 = (bf16[32,4096]{1,0:T(8,128)(2,1)S(1)}, bf16[32,4096]{1,0:T(8,128)(2,1)S(1)}, u32[]{:S(2)}, u32[]{:S(2)}) collective-permute-start(bf16[32,4096]{1,0:T(8,128)(2,1)S(1)} %get-tuple-element.94), channel_id=1, source_target_pairs={{0,64},{32,96},{64,128},{96,160},{128,192},{160,224},{192,0},{224,... | collective-permute-start | bytes 786440 | tf_op jit(solution)/shard_map/ppermute | solution.py:59
  154.5 10.7 %collective-permute-start.32 = (bf16[32,4096]{1,0:T(8,128)(2,1)S(1)}, bf16[32,4096]{1,0:T(8,128)(2,1)S(1)}, u32[]{:S(2)}, u32[]{:S(2)}) collective-permute-start(bf16[32,4096]{1,0:T(8,128)(2,1)S(1)} %get-tuple-element.95), channel_id=1, source_target_pairs={{0,192},{32,224},{64,0},{96,32},{128,64},{160,96},{192,128},{224,1... | collective-permute-start | bytes 786440 | tf_op jit(solution)/shard_map/ppermute | solution.py:59
  161.2 7.7 %collective-permute-start.29 = (bf16[32,4096]{1,0:T(8,128)(2,1)S(1)}, bf16[32,4096]{1,0:T(8,128)(2,1)S(1)}, u32[]{:S(2)}, u32[]{:S(2)}) collective-permute-start(bf16[32,4096]{1,0:T(8,128)(2,1)S(1)} %add_convert_fusion.3), channel_id=1, source_target_pairs={{0,192},{32,224},{64,0},{96,32},{128,64},{160,96},{192,128},{224,1... | collective-permute-start | bytes 786440 | tf_op jit(solution)/shard_map/ppermute | solution.py:59
  165.3 8.4 %collective-permute-start.33 = (bf16[32,4096]{1,0:T(8,128)(2,1)S(1)}, bf16[32,4096]{1,0:T(8,128)(2,1)S(1)}, u32[]{:S(2)}, u32[]{:S(2)}) collective-permute-start(bf16[32,4096]{1,0:T(8,128)(2,1)S(1)} %add_convert_fusion.1), channel_id=1, source_target_pairs={{0,32},{32,0},{64,96},{96,64},{128,160},{160,128},{192,224},{224,1... | collective-permute-start | bytes 786440 | tf_op jit(solution)/shard_map/ppermute | solution.py:63
  169.0 24.7 %copy-start.7 = (s32[32,8]{0,1:T(8,128)S(1)}, s32[32,8]{0,1:T(8,128)}, u32[]{:S(2)}) copy-start(s32[32,8]{0,1:T(8,128)} %param.19) | copy-start | bytes 3076
  169.0 7.7 %collective-permute-start.30 = (bf16[32,4096]{1,0:T(8,128)(2,1)S(1)}, bf16[32,4096]{1,0:T(8,128)(2,1)S(1)}, u32[]{:S(2)}, u32[]{:S(2)}) collective-permute-start(bf16[32,4096]{1,0:T(8,128)(2,1)S(1)} %add_convert_fusion.2), channel_id=1, source_target_pairs={{0,192},{32,224},{64,0},{96,32},{128,64},{160,96},{192,128},{224,1... | collective-permute-start | bytes 786440 | tf_op jit(solution)/shard_map/ppermute | solution.py:59
  176.8 7.3 %collective-permute-start.36 = (bf16[8,4096]{1,0:T(8,128)(2,1)S(1)}, bf16[8,4096]{1,0:T(8,128)(2,1)S(1)}, u32[]{:S(2)}, u32[]{:S(2)}) collective-permute-start(bf16[8,4096]{1,0:T(8,128)(2,1)S(1)} %get-tuple-element.96), channel_id=1, source_target_pairs={{0,8},{2,10},{4,12},{6,14},{8,16},{10,18},{12,20},{14,22},{16,24},... | collective-permute-start | bytes 196616 | tf_op jit(solution)/shard_map/ppermute | solution.py:45
  180.5 8.9 %collective-permute-start.35 = (bf16[8,4096]{1,0:T(8,128)(2,1)S(1)}, bf16[8,4096]{1,0:T(8,128)(2,1)S(1)}, u32[]{:S(2)}, u32[]{:S(2)}) collective-permute-start(bf16[8,4096]{1,0:T(8,128)(2,1)S(1)} %get-tuple-element.97), channel_id=1, source_target_pairs={{0,16},{2,18},{4,20},{6,22},{8,24},{10,26},{12,28},{14,30},{16,0},... | collective-permute-start | bytes 196616 | tf_op jit(solution)/shard_map/ppermute | solution.py:45
  183.6 5.7 %collective-permute-start.34 = (bf16[8,4096]{1,0:T(8,128)(2,1)S(1)}, bf16[8,4096]{1,0:T(8,128)(2,1)S(1)}, u32[]{:S(2)}, u32[]{:S(2)}) collective-permute-start(bf16[8,4096]{1,0:T(8,128)(2,1)S(1)} %get-tuple-element.98), channel_id=1, source_target_pairs={{0,24},{2,26},{4,28},{6,30},{8,0},{10,2},{12,4},{14,6},{16,8},{18,... | collective-permute-start | bytes 196616 | tf_op jit(solution)/shard_map/ppermute | solution.py:45
  190.3 10.1 %all-to-all-start.1 = ((bf16[4,8,4096]{2,1,0:T(8,128)(2,1)}), bf16[4,8,4096]{2,1,0:T(8,128)(2,1)S(1)}, u32[]{:S(2)}, u32[]{:S(2)}) async-start(bf16[4,8,4096]{2,1,0:T(8,128)(2,1)} %regroup.1), calls=%async_computation.1 | async-start | bytes 524288 | tf_op jit(solution)/shard_map/all_to_all | solution.py:614
